TPU v7x, 32 devices: a whole 2x2x4 slice. The times are simulated.
32 devices in a mesh: ctx: 8 (over y, x, core), fsdp: 4 (over z).
Axes of the slice: x: 2, y: 2, z: 4, core: 2. Of those that a mesh axis runs over, the one named last changes fastest.
Arguments:
- inputs: bfloat16 [2, 8, 2, 128, 2048], P(None, 'ctx', None, 'fsdp'), may hold values from -6 to 6
- w_qkv: float32 [2048, 2304], P('fsdp'), may hold values from -0.1875 to 0.1875
- w_out: float32 [2048, 2048], P('fsdp'), may hold values from -0.75 to 0.75
- w_fc: float32 [2048, 8192], P('fsdp'), may hold values from -0.125 to 0.125
- w_proj: float32 [8192, 2048], P('fsdp'), may hold values from -0.0625 to 0.0625
- ln1_gain: float32 [2048], P('fsdp'), may hold values from 0.5 to 1.5
- ln1_bias: float32 [2048], P('fsdp'), may hold values from -1.8 to 1.8
- bias_q: float32 [2048], P('fsdp'), may hold values from -1.8 to 1.8
- bias_v: float32 [128], P('fsdp'), may hold values from -1.8 to 1.8
- bias_out: float32 [2048], P('fsdp'), may hold values from -1.8 to 1.8
- ln2_gain: float32 [2048], P('fsdp'), may hold values from 0.5 to 1.5
- ln2_bias: float32 [2048], P('fsdp'), may hold values from -1.8 to 1.8
- bias_fc: float32 [8192], P('fsdp'), may hold values from -1.8 to 1.8
- bias_proj: float32 [2048], P('fsdp'), may hold values from -1.8 to 1.8
- cotangent: bfloat16 [2, 8, 2, 128, 2048], P(None, 'ctx', None, 'fsdp'), may hold values from -6 to 6
- lengths: int32 [2, 2], replicated, may hold values from 512 to 1536, as said below
- pair_table: int32 [8], replicated, may hold values from 0 to 7, each once
Outputs:
- result: bfloat16 [2, 8, 2, 128, 2048], P(None, 'ctx', None, 'fsdp')
- grad_inputs: float32 [2, 8, 2, 128, 2048], P(None, 'ctx', None, 'fsdp')
- grad_w_qkv: float32 [2048, 2304], P('fsdp')
- grad_w_out: float32 [2048, 2048], P('fsdp')
- grad_w_fc: float32 [2048, 8192], P('fsdp')
- grad_w_proj: float32 [8192, 2048], P('fsdp')
- grad_ln1_gain: float32 [2048], P('fsdp')
- grad_ln1_bias: float32 [2048], P('fsdp')
- grad_bias_q: float32 [2048], P('fsdp')
- grad_bias_v: float32 [128], P('fsdp')
- grad_bias_out: float32 [2048], P('fsdp')
- grad_ln2_gain: float32 [2048], P('fsdp')
- grad_ln2_bias: float32 [2048], P('fsdp')
- grad_bias_fc: float32 [8192], P('fsdp')
- grad_bias_proj: float32 [2048], P('fsdp')
Inputs may be any that keep to these rules, and one draw needn't show every extreme that they name: Each slot's two lengths are each at least 512 and add up to at most 2048; in every draw one slot holds exactly 512 and 1536, in some order. A permutation of the ctx indices' block pairs: index c holds blocks pair_table[c] and 15 - pair_table[c].
All inputs are finite; a program needn't handle non-finite values.
Results may differ from a plain program's by a relative error of at most 0.02.
Values may be sent and summed in bfloat16 or wider, within the bound.
No kernel may reach another device: no remote copies, remote signals or barrier semaphores. Data moves between devices by JAX's collectives and lax.ppermute only.
A program may use at most 448 MiB of HBM per device.

v0:
```python
import math

import jax
import jax.numpy as jnp
from jax import lax
from jax.sharding import PartitionSpec as P

HEADS = 16
HD = 128


norm_eps = 1e-05
masked_score = -1e30


def layer_norm(values, gain_vec, shift_vec):
    centred = values - jnp.mean(values, axis=-1, keepdims=True)
    inverse = lax.rsqrt(jnp.mean(centred * centred, axis=-1, keepdims=True) + norm_eps)
    normed = centred * inverse
    return (normed * gain_vec + shift_vec, normed, inverse)


def norm_backward(grad_norm, normed, inverse, gain_vec):
    scaled = grad_norm * gain_vec
    centred = scaled - jnp.mean(scaled, axis=-1, keepdims=True)
    centred = centred - normed * jnp.mean(scaled * normed, axis=-1, keepdims=True)
    return (centred * inverse, jnp.sum(grad_norm * normed, axis=0), jnp.sum(grad_norm, axis=0))


def gelu_tanh(values):
    return jax.nn.gelu(values, approximate=True)


def times_transposed(left_side, right_side):
    return lax.dot_general(
        left_side, right_side, (((1,), (1,)), ((), ())), preferred_element_type=jnp.float32
    )


def over_rows(left_side, right_side):
    return lax.dot_general(
        left_side, right_side, (((0,), (0,)), ((), ())), preferred_element_type=jnp.float32
    )


def outer_rows(left_side, right_side):
    return over_rows(left_side, right_side)


def column_sum(values):
    return jnp.sum(values, axis=0, dtype=jnp.float32)


def pick_block(pair_table, ctx_at, half_bit):
    ctx_total = pair_table.shape[0]
    chosen = jnp.sum(jnp.where(jnp.arange(ctx_total, dtype=jnp.int32) == ctx_at, pair_table, 0))
    return jnp.where(half_bit == 0, chosen, 2 * ctx_total - 1 - chosen)


def doc_ids(positions, lengths):
    doc_start = lengths[:, 0:1]
    doc_end = doc_start + lengths[:, 1:2]
    doc_index = (positions[None, :] >= doc_start).astype(jnp.int32) + (
        positions[None, :] >= doc_end
    ).astype(jnp.int32)
    return (doc_index, positions[None, :] < doc_end)


def body(
    inputs,
    w_qkv,
    w_out,
    w_fc,
    w_proj,
    ln1_gain,
    ln1_bias,
    bias_q,
    bias_v,
    bias_out,
    ln2_gain,
    ln2_bias,
    bias_fc,
    bias_proj,
    cotangent,
    lengths,
    pair_table,
):
    slot_count = inputs.shape[0]
    row_count = inputs.shape[3]
    model_width = inputs.shape[4]
    ctx_count = lax.axis_size("ctx")
    fsdp_count = lax.axis_size("fsdp")
    ctx_at = lax.axis_index("ctx")
    fsdp_at = lax.axis_index("fsdp")
    block_len = row_count * fsdp_count
    pair_rows = 2 * row_count
    group_len = fsdp_count * pair_rows
    token_count = slot_count * pair_rows
    score_scale = 1.0 / math.sqrt(HD)
    offsets = jnp.arange(pair_rows, dtype=jnp.int32)
    query_pos = (
        pick_block(pair_table, ctx_at, offsets // row_count) * block_len
        + fsdp_at * row_count
        + offsets % row_count
    )
    query_doc, query_live = doc_ids(query_pos, lengths)
    query_doc_tiles = query_doc.reshape(slot_count, 2, row_count)
    query_pos_tiles = query_pos.reshape(2, row_count)
    block_offsets = jnp.arange(block_len, dtype=jnp.int32)
    lowered = [
        member.astype(jnp.bfloat16)
        for member in (
            w_qkv,
            w_out,
            w_fc,
            w_proj,
            ln1_gain,
            ln1_bias,
            bias_q,
            bias_v,
            bias_out,
            ln2_gain,
            ln2_bias,
            bias_fc,
            bias_proj,
        )
    ]
    fetched = (
        lax.all_gather(lowered[0], "fsdp", axis=0, tiled=True),
        lax.all_gather(lowered[1], "fsdp", axis=0, tiled=True),
        lax.all_gather(lowered[4], "fsdp", axis=0, tiled=True),
        lax.all_gather(lowered[5], "fsdp", axis=0, tiled=True),
        lax.all_gather(lowered[6], "fsdp", axis=0, tiled=True),
        lax.all_gather(lowered[7], "fsdp", axis=0, tiled=True),
        lax.all_gather(lowered[8], "fsdp", axis=0, tiled=True),
        lax.all_gather(lowered[9], "fsdp", axis=0, tiled=True),
        lax.all_gather(lowered[10], "fsdp", axis=0, tiled=True),
        lax.all_gather(lowered[11], "fsdp", axis=0, tiled=True),
        lax.all_gather(lowered[12], "fsdp", axis=0, tiled=True),
    )
    full_qkv = fetched[0]
    full_out = fetched[1]
    vectors = [member.astype(jnp.float32) for member in fetched[2:]]
    (
        gain_one,
        shift_one,
        query_bias,
        value_bias,
        out_bias,
        gain_two,
        shift_two,
        fc_bias,
        proj_bias,
    ) = vectors
    live_rows = query_live.reshape(token_count, 1).astype(jnp.float32)
    grad_out = cotangent.reshape(token_count, model_width).astype(jnp.float32) * live_rows
    grad_mlp = grad_out.astype(jnp.bfloat16)
    rows_in = inputs.reshape(token_count, model_width).astype(jnp.float32)
    first_norm, normed_one, inverse_one = layer_norm(rows_in, gain_one, shift_one)
    first_low = first_norm.astype(jnp.bfloat16)
    projected = jnp.dot(first_low, full_qkv, preferred_element_type=jnp.float32)
    query_rows = (projected[:, :model_width] + query_bias).astype(jnp.bfloat16)
    key_value = jnp.concatenate(
        [
            projected[:, model_width : model_width + HD],
            projected[:, model_width + HD :] + value_bias,
        ],
        axis=1,
    ).astype(jnp.bfloat16)
    query_five = query_rows.reshape(slot_count, 2, row_count, HEADS, HD)
    kv_all = lax.all_gather(
        key_value.reshape(slot_count, pair_rows, 2 * HD), ("ctx", "fsdp"), axis=1, tiled=True
    )
    kv_six = kv_all.reshape(slot_count, ctx_count, fsdp_count, 2, row_count, 2 * HD)

    def key_tile(group_at, slot_at, key_half):
        kv_group = lax.dynamic_index_in_dim(kv_six[slot_at], group_at, 0, keepdims=False)
        kv_block = kv_group[:, key_half].reshape(block_len, 2 * HD)
        key_pos = pick_block(pair_table, group_at, key_half) * block_len + block_offsets
        key_doc = doc_ids(key_pos, lengths)[0][slot_at]
        return (kv_block[:, :HD], kv_block[:, HD:], key_pos, key_doc)

    def tile_mask(slot_at, query_half, key_pos, key_doc):
        same_doc = query_doc_tiles[slot_at, query_half][:, None] == key_doc[None, :]
        return same_doc & (key_pos[None, :] <= query_pos_tiles[query_half][:, None])

    def tile_scores(slot_at, query_half, key_part, allowed):
        scores = (
            jnp.einsum(
                "rhd,kd->rhk",
                query_five[slot_at, query_half],
                key_part,
                preferred_element_type=jnp.float32,
            )
            * score_scale
        )
        return jnp.where(allowed[:, None, :], scores, masked_score)

    def forward_group(group_at, loop_state):
        peaks, totals, sums = loop_state
        for slot_at in range(slot_count):
            for key_half in range(2):
                key_part, value_part, key_pos, key_doc = key_tile(group_at, slot_at, key_half)
                for query_half in range(2):
                    allowed = tile_mask(slot_at, query_half, key_pos, key_doc)

                    def forward_update(
                        tile_state,
                        allowed=allowed,
                        key_part=key_part,
                        value_part=value_part,
                        slot_at=slot_at,
                        query_half=query_half,
                    ):
                        run_peak, run_total, run_sum = tile_state
                        scores = tile_scores(slot_at, query_half, key_part, allowed)
                        new_peak = jnp.maximum(run_peak, jnp.max(scores, axis=-1))
                        fade_factor = jnp.exp(run_peak - new_peak)
                        weights = jnp.where(
                            allowed[:, None, :], jnp.exp(scores - new_peak[..., None]), 0.0
                        )
                        gathered = jnp.einsum(
                            "rhk,kd->rhd",
                            weights.astype(jnp.bfloat16),
                            value_part,
                            preferred_element_type=jnp.float32,
                        )
                        return (
                            new_peak,
                            run_total * fade_factor + jnp.sum(weights, axis=-1),
                            run_sum * fade_factor[..., None] + gathered,
                        )

                    tile_state = (
                        peaks[slot_at, query_half],
                        totals[slot_at, query_half],
                        sums[slot_at, query_half],
                    )
                    new_state = forward_update(tile_state)
                    peaks = peaks.at[slot_at, query_half].set(new_state[0])
                    totals = totals.at[slot_at, query_half].set(new_state[1])
                    sums = sums.at[slot_at, query_half].set(new_state[2])
        return (peaks, totals, sums)

    start_state = (
        jnp.full((slot_count, 2, row_count, HEADS), masked_score, jnp.float32),
        jnp.zeros((slot_count, 2, row_count, HEADS), jnp.float32),
        jnp.zeros((slot_count, 2, row_count, HEADS, HD), jnp.float32),
    )
    run_peak, run_total, run_sum = lax.fori_loop(0, ctx_count, forward_group, start_state)
    attended = run_sum / run_total[..., None]
    log_total = run_peak + jnp.log(run_total)
    attended_low = attended.reshape(token_count, model_width).astype(jnp.bfloat16)
    branch = jnp.dot(attended_low, full_out, preferred_element_type=jnp.float32) + out_bias
    middle = rows_in + branch
    second_norm, normed_two, inverse_two = layer_norm(middle, gain_two, shift_two)
    second_low = second_norm.astype(jnp.bfloat16)
    mlp_full = (
        lax.all_gather(lowered[2], "fsdp", axis=0, tiled=True),
        lax.all_gather(lowered[3], "fsdp", axis=0, tiled=True),
    )
    full_fc = mlp_full[0]
    full_proj = mlp_full[1]
    hidden = jnp.dot(second_low, full_fc, preferred_element_type=jnp.float32) + fc_bias
    activated, gelu_pull = jax.vjp(gelu_tanh, hidden)
    activated_low = activated.astype(jnp.bfloat16)
    result = middle + (
        jnp.dot(activated_low, full_proj, preferred_element_type=jnp.float32) + proj_bias
    )
    grad_proj_w = lax.psum_scatter(
        outer_rows(activated_low, grad_mlp).astype(jnp.bfloat16),
        "fsdp",
        scatter_dimension=0,
        tiled=True,
    )
    grad_act = times_transposed(grad_mlp, full_proj)
    grad_hidden = gelu_pull(grad_act)[0].astype(jnp.bfloat16)
    grad_fc_w = lax.psum_scatter(
        outer_rows(second_low, grad_hidden).astype(jnp.bfloat16),
        "fsdp",
        scatter_dimension=0,
        tiled=True,
    )
    grad_second = times_transposed(grad_hidden, full_fc)
    fc_bias_term = column_sum(grad_hidden)
    grad_mid_norm, grad_gain_two, grad_shift_two = norm_backward(
        grad_second, normed_two, inverse_two, gain_two
    )
    grad_middle = grad_out + grad_mid_norm
    grad_branch = grad_middle.astype(jnp.bfloat16)
    grad_attended = times_transposed(grad_branch, full_out).astype(jnp.bfloat16)
    grad_five = grad_attended.reshape(slot_count, 2, row_count, HEADS, HD)
    delta_rows = jnp.sum(grad_five.astype(jnp.float32) * attended, axis=-1)

    def backward_group(group_at, loop_state):
        query_acc, term_six = loop_state
        slot_terms = []
        for slot_at in range(slot_count):
            half_terms = []
            for key_half in range(2):
                key_part, value_part, key_pos, key_doc = key_tile(group_at, slot_at, key_half)
                kv_sum = jnp.zeros((block_len, 2 * HD), jnp.float32)
                for query_half in range(2):
                    allowed = tile_mask(slot_at, query_half, key_pos, key_doc)

                    def backward_update(
                        tile_state,
                        allowed=allowed,
                        key_part=key_part,
                        value_part=value_part,
                        slot_at=slot_at,
                        query_half=query_half,
                    ):
                        query_tile, kv_tile = tile_state
                        scores = tile_scores(slot_at, query_half, key_part, allowed)
                        prob_rows = jnp.where(
                            allowed[:, None, :],
                            jnp.exp(scores - log_total[slot_at, query_half][..., None]),
                            0.0,
                        )
                        grad_tile = grad_five[slot_at, query_half]
                        prob_grad = jnp.einsum(
                            "rhd,kd->rhk", grad_tile, value_part, preferred_element_type=jnp.float32
                        )
                        score_grad = (
                            prob_rows * (prob_grad - delta_rows[slot_at, query_half][..., None])
                        ).astype(jnp.bfloat16)
                        query_tile = (
                            query_tile
                            + jnp.einsum(
                                "rhk,kd->rhd",
                                score_grad,
                                key_part,
                                preferred_element_type=jnp.float32,
                            )
                            * score_scale
                        )
                        key_grad = (
                            jnp.einsum(
                                "rhk,rhd->kd",
                                score_grad,
                                query_five[slot_at, query_half],
                                preferred_element_type=jnp.float32,
                            )
                            * score_scale
                        )
                        value_grad = jnp.einsum(
                            "rhk,rhd->kd",
                            prob_rows.astype(jnp.bfloat16),
                            grad_tile,
                            preferred_element_type=jnp.float32,
                        )
                        return (
                            query_tile,
                            kv_tile + jnp.concatenate([key_grad, value_grad], axis=-1),
                        )

                    tile_state = (query_acc[slot_at, query_half], kv_sum)
                    new_state = backward_update(tile_state)
                    query_acc = query_acc.at[slot_at, query_half].set(new_state[0])
                    kv_sum = new_state[1]
                half_terms.append(kv_sum.reshape(fsdp_count, row_count, 2 * HD))
            slot_terms.append(jnp.stack(half_terms, axis=1))
        group_term = jnp.stack(slot_terms, axis=0)[:, None]
        term_six = lax.dynamic_update_slice_in_dim(term_six, group_term, group_at, 1)
        return (query_acc, term_six)

    back_start = (
        jnp.zeros((slot_count, 2, row_count, HEADS, HD), jnp.float32),
        jnp.zeros((slot_count, ctx_count, fsdp_count, 2, row_count, 2 * HD), jnp.float32),
    )
    query_acc, term_six = lax.fori_loop(0, ctx_count, backward_group, back_start)
    kv_term = term_six.reshape(slot_count, ctx_count * group_len, 2 * HD)
    kv_grad = lax.psum_scatter(kv_term, ("ctx", "fsdp"), scatter_dimension=1, tiled=True)
    grad_kv_low = kv_grad.reshape(token_count, 2 * HD).astype(jnp.bfloat16)
    grad_query_low = query_acc.reshape(token_count, model_width).astype(jnp.bfloat16)
    grad_projected = jnp.concatenate([grad_query_low, grad_kv_low], axis=1)
    attn_sums = lax.psum_scatter(
        jnp.concatenate(
            [outer_rows(first_low, grad_projected), outer_rows(attended_low, grad_branch)], axis=1
        ).astype(jnp.bfloat16),
        "fsdp",
        scatter_dimension=0,
        tiled=True,
    ).astype(jnp.float32)
    grad_qkv_w = attn_sums[:, : model_width + 2 * HD]
    grad_out_w = attn_sums[:, model_width + 2 * HD :]
    grad_first = times_transposed(grad_projected, full_qkv)
    grad_in_norm, grad_gain_one, grad_shift_one = norm_backward(
        grad_first, normed_one, inverse_one, gain_one
    )
    grad_inputs = grad_middle + grad_in_norm
    vector_sums = (
        lax.psum_scatter(
            grad_gain_one.astype(jnp.bfloat16), "fsdp", scatter_dimension=0, tiled=True
        ).astype(jnp.float32),
        lax.psum_scatter(
            grad_shift_one.astype(jnp.bfloat16), "fsdp", scatter_dimension=0, tiled=True
        ).astype(jnp.float32),
        lax.psum_scatter(
            column_sum(grad_query_low).astype(jnp.bfloat16), "fsdp", scatter_dimension=0, tiled=True
        ).astype(jnp.float32),
        lax.psum_scatter(
            column_sum(grad_kv_low[:, HD:]).astype(jnp.bfloat16),
            "fsdp",
            scatter_dimension=0,
            tiled=True,
        ).astype(jnp.float32),
        lax.psum_scatter(
            column_sum(grad_branch).astype(jnp.bfloat16), "fsdp", scatter_dimension=0, tiled=True
        ).astype(jnp.float32),
        lax.psum_scatter(
            grad_gain_two.astype(jnp.bfloat16), "fsdp", scatter_dimension=0, tiled=True
        ).astype(jnp.float32),
        lax.psum_scatter(
            grad_shift_two.astype(jnp.bfloat16), "fsdp", scatter_dimension=0, tiled=True
        ).astype(jnp.float32),
        lax.psum_scatter(
            fc_bias_term.astype(jnp.bfloat16), "fsdp", scatter_dimension=0, tiled=True
        ).astype(jnp.float32),
        lax.psum_scatter(
            column_sum(grad_mlp).astype(jnp.bfloat16), "fsdp", scatter_dimension=0, tiled=True
        ).astype(jnp.float32),
    )
    summed_all = (
        lax.psum(grad_qkv_w.astype(jnp.bfloat16), "ctx").astype(jnp.float32),
        lax.psum(grad_out_w.astype(jnp.bfloat16), "ctx").astype(jnp.float32),
        lax.psum(grad_fc_w, "ctx").astype(jnp.float32),
        lax.psum(grad_proj_w, "ctx").astype(jnp.float32),
        lax.psum(vector_sums[0].astype(jnp.bfloat16), "ctx").astype(jnp.float32),
        lax.psum(vector_sums[1].astype(jnp.bfloat16), "ctx").astype(jnp.float32),
        lax.psum(vector_sums[2].astype(jnp.bfloat16), "ctx").astype(jnp.float32),
        lax.psum(vector_sums[3].astype(jnp.bfloat16), "ctx").astype(jnp.float32),
        lax.psum(vector_sums[4].astype(jnp.bfloat16), "ctx").astype(jnp.float32),
        lax.psum(vector_sums[5].astype(jnp.bfloat16), "ctx").astype(jnp.float32),
        lax.psum(vector_sums[6].astype(jnp.bfloat16), "ctx").astype(jnp.float32),
        lax.psum(vector_sums[7].astype(jnp.bfloat16), "ctx").astype(jnp.float32),
        lax.psum(vector_sums[8].astype(jnp.bfloat16), "ctx").astype(jnp.float32),
    )
    return (
        result.astype(jnp.bfloat16).reshape(inputs.shape),
        grad_inputs.reshape(inputs.shape),
        summed_all[0],
        summed_all[1],
        summed_all[2],
        summed_all[3],
        summed_all[4],
        summed_all[5],
        summed_all[6],
        summed_all[7],
        summed_all[8],
        summed_all[9],
        summed_all[10],
        summed_all[11],
        summed_all[12],
    )


def solution(mesh):
    placed = (
        P(None, "ctx", None, "fsdp", None),
        P("fsdp", None),
        P("fsdp", None),
        P("fsdp", None),
        P("fsdp", None),
        P("fsdp"),
        P("fsdp"),
        P("fsdp"),
        P("fsdp"),
        P("fsdp"),
        P("fsdp"),
        P("fsdp"),
        P("fsdp"),
        P("fsdp"),
        P(None, "ctx", None, "fsdp", None),
        P(),
        P(),
    )
    return jax.shard_map(
        body,
        mesh=mesh,
        in_specs=placed,
        out_specs=(
            P(None, "ctx", None, "fsdp", None),
            P(None, "ctx", None, "fsdp", None),
            P("fsdp", None),
            P("fsdp", None),
            P("fsdp", None),
            P("fsdp", None),
            P("fsdp"),
            P("fsdp"),
            P("fsdp"),
            P("fsdp"),
            P("fsdp"),
            P("fsdp"),
            P("fsdp"),
            P("fsdp"),
            P("fsdp"),
        ),
        check_vma=False,
    )
```

profile of v0, /device:TPU:0, one launch (start us, length us, event | category | flops | bytes accessed | tf_op | source)
XLA Modules:
  0.0 4026.6 jit_solution(9942491713067840299)
XLA Ops:
  7.3 4.0 convert_element_type.628
  12.1 13.5 all-gather
  25.7 15.7 all-gather.1
  42.9 13.5 all-reduce
  56.8 124.4 %all-gather.13.cloned.1.call-done = bf16[2048,2304]{1,0:T(8,128)(2,1)} async-done(((bf16[512,2304]{1,0:T(8,128)(2,1)}), bf16[2048,2304]{1,0:T(8,128)(2,1)}) %all-gather.13.cloned.1.call-update) | async-done | bytes 9437200 | tf_op jit(solution)/shard_map/all_gather | solution.py:129
  181.3 5.1 fusion.359
  187.2 3.8 convert_element_type.636
  191.1 9.1 convert_element_type.648
  200.2 8.9 convert_element_type.644
  215.2 11.9 all-gather.2
  227.1 11.9 all-gather.3
  240.4 11.9 all-gather.4
  252.9 15.8 all-gather.5
  269.3 13.9 all_gather.53
  289.2 436.0 %while.74 = (s32[]{:T(128)}, f32[2,2,32,16]{2,3,1,0:T(8,128)S(1)}, f32[2,2,32,16]{2,3,1,0:T(8,128)S(1)}, f32[2,2,32,16,128]{4,3,2,1,0:T(8,128)S(1)}, s32[2,2,32]...) while((s32[]{:T(128)}, f32[2,2,32,16]{2,3,1,0:T(8,128)S(1)}, ...), condition=%wide.region_21.22_spmd.clone.clone, body=%wide.region_3.21_spmd.clone.clone.sunk | while | flops 273256224 | bytes 22487640 | solution.py:250
  314.0 2.1 fusion.582
  641.0 2.1 fusion.582
  695.5 2.1 fusion.582
  726.5 5.0 fusion.358
  733.4 221.4 %all-gather.21.cloned.1.call-done = bf16[8192,2048]{1,0:T(8,128)(2,1)} async-done(((bf16[2048,2048]{1,0:T(8,128)(2,1)}), bf16[8192,2048]{1,0:T(8,128)(2,1)}) %all-gather.21.cloned.1.call-update) | async-done | bytes 33554448 | tf_op jit(solution)/shard_map/all_gather | solution.py:260
  954.8 21.1 fusion.360
  975.9 540.5 %all-gather.19.cloned.1.call-done = bf16[2048,8192]{1,0:T(8,128)(2,1)} async-done(((bf16[512,8192]{1,0:T(8,128)(2,1)}), bf16[2048,8192]{1,0:T(8,128)(2,1)}) %all-gather.19.cloned.1.call-update) | async-done | bytes 33554448 | tf_op jit(solution)/shard_map/all_gather | solution.py:259
  1516.4 19.4 fusion.338
  1535.8 19.8 multiply_reduce_fusion
  1555.6 2.8 convert_reduce_fusion.1
  1558.4 6.7 fusion.312
  1567.6 586.4 %while.75 = (s32[]{:T(128)}, f32[2,2,32,16,128]{4,3,2,1,0:T(8,128)S(1)}, f32[2,8,4,2,32,256]{5,4,3,2,1,0:T(8,128)}, s32[2,2,32]{2,1,0:T(2,128)}, s32[8]{0:T(128)...) while((s32[]{:T(128)}, ...), condition=%wide.region_29.30_spmd.clone.clone, body=%wide.region_27.29_spmd.clone.clone.sunk | while | flops 678857472 | bytes 58006420 | solution.py:372
  2155.3 5.8 convolution_convert_fusion.3
  2161.1 138.8 %reduce-scatter.9.cloned.1.call-done = f32[2,64,256]{2,1,0:T(8,128)} async-done(((f32[2,2048,256]{2,1,0:T(8,128)}), f32[2,64,256]{2,1,0:T(8,128)}) %reduce-scatter.9.cloned.1.call-update) | async-done | bytes 131088 | tf_op jit(solution)/shard_map/reduce_scatter | solution.py:374
  2300.9 3.3 convolution_convert_fusion.2
  2304.2 6.8 pad_maximum_fusion
  2312.3 15.5 convolution_convert_fusion
  2328.9 16.2 convolution_convert_fusion.1
  2345.2 262.1 %reduce-scatter.11.cloned.1.call-done = bf16[512,4352]{1,0:T(8,128)(2,1)} async-done(((bf16[2048,4352]{1,0:T(8,128)(2,1)}), bf16[512,4352]{1,0:T(8,128)(2,1)}) %reduce-scatter.11.cloned.1.call-update) | async-done | bytes 4456464 | tf_op jit(solution)/shard_map/reduce_scatter | solution.py:378
  2607.2 3.2 slice.3344
  2610.5 3.2 slice.3345
  2613.6 549.1 %reduce-scatter.13.cloned.1.call-done = bf16[512,8192]{1,0:T(8,128)(2,1)} async-done(((bf16[2048,8192]{1,0:T(8,128)(2,1)}), bf16[512,8192]{1,0:T(8,128)(2,1)}) %reduce-scatter.13.cloned.1.call-update) | async-done | bytes 8388624
  3162.7 555.2 %reduce-scatter.15.cloned.1.call-done = bf16[2048,2048]{1,0:T(8,128)(2,1)} async-done(((bf16[8192,2048]{1,0:T(8,128)(2,1)}), bf16[2048,2048]{1,0:T(8,128)(2,1)}) %reduce-scatter.15.cloned.1.call-update) | async-done | bytes 8388624
  3720.0 12.8 all-gather.6
  3733.8 18.5 fusion.311
  3752.4 7.4 multiply_reduce_fusion.1
  3759.9 16.3 all-reduce.14
  3776.8 24.0 all-reduce.12
  3807.5 183.4 %all-reduce.17.cloned.1.call-done = (bf16[512,2304]{1,0:T(8,128)(2,1)}, bf16[512,2048]{1,0:T(8,128)(2,1)}, bf16[512,8192]{1,0:T(8,128)(2,1)}, bf16[2048,2048]{1,0:T(8,128)(2,1)}) async-done(((bf16[512,2304]{1,0:T(8,128)(2,1)}, bf16[512,2048]{1,0:T(8,128)(2,1)}, bf16[512,8192]{1,0:T(8,128)(2,1)}, bf16[2048,2048]{1,0:T(8,128)(2,1)}), (bf16[512,2304]{1,0:T(8,128)(2,1)}, bf16[512,2048]{1,0:T(8,128)(2,1)}, ...) | async-done | bytes 21233680 | tf_op jit(solution)/shard_map/psum | solution.py:426
  3990.8 11.7 convert_element_type.668
  4002.6 11.8 convert_element_type.670
  4014.4 2.5 convert_element_type.665
  4016.9 2.5 convert_element_type.666
  (2104 shorter events, 1021.1 us)
Async XLA Ops:
  7.2 34.3 copy-start.78
  7.2 18.4 copy-start.80
  7.2 34.2 copy-start.87
  7.2 174.1 %all-gather.13.cloned.1.call-start = ((), (), s32[]{:S(2)}) async-start(), calls=%async_computation.4 | async-start | bytes 11796480 | tf_op jit(solution)/shard_map/all_gather | solution.py:129
  11.3 276.0 %all-gather.15.cloned.1.call-start = ((), (), s32[]{:S(2)}) async-start(), calls=%async_computation.5 | async-start | bytes 2162688 | tf_op jit(solution)/shard_map/all_gather | solution.py:171
  11.6 174.7 %copy-start.72 = (f32[128]{0:T(128)}, f32[128]{0:T(128)S(1)}, u32[]{:S(2)}) copy-start(f32[128]{0:T(128)S(1)} %div.58) | copy-start | bytes 1540
  12.0 174.3 %copy-start.74 = (f32[128]{0:T(128)}, f32[128]{0:T(128)S(1)}, u32[]{:S(2)}) copy-start(f32[128]{0:T(128)S(1)} %rsqrt.20) | copy-start | bytes 1540
  25.6 160.8 %copy-start.58 = (f32[4,1,512]{2,1,0:T(1,128)}, f32[4,1,512]{2,1,0:T(1,128)S(1)}, u32[]{:S(2)}) copy-start(f32[4,1,512]{2,1,0:T(1,128)S(1)} %convert_element_type.722) | copy-start | bytes 24580
  56.8 129.6 %copy-start.11 = (bf16[128,2048]{1,0:T(8,128)(2,1)}, bf16[128,2048]{1,0:T(8,128)(2,1)S(1)}, u32[]{:S(2)}) copy-start(bf16[128,2048]{1,0:T(8,128)(2,1)S(1)} %add_convert_fusion.1) | copy-start | bytes 1572868
  187.1 539.4 %all-gather.17.cloned.1.call-start = ((), (), s32[]{:S(2)}) async-start(), calls=%async_computation.6 | async-start | bytes 10485760 | tf_op jit(solution)/shard_map/all_gather | solution.py:130
  191.0 763.8 %all-gather.21.cloned.1.call-start = ((), (), s32[]{:S(2)}) async-start(), calls=%async_computation.8 | async-start | bytes 41943040 | tf_op jit(solution)/shard_map/all_gather | solution.py:260
  200.2 1316.2 %all-gather.19.cloned.1.call-start = ((), (), s32[]{:S(2)}) async-start(), calls=%async_computation.7 | async-start | bytes 41943040 | tf_op jit(solution)/shard_map/all_gather | solution.py:259
  209.2 17.9 copy-start.82
  209.2 31.2 copy-start.83
  209.2 43.7 %copy-start.84 = (f32[512]{0:T(512)S(1)}, f32[512]{0:T(512)}, u32[]{:S(2)}) copy-start(f32[512]{0:T(512)} %param.96) | copy-start | bytes 6148
  209.2 60.2 %copy-start.71 = (f32[2048]{0:T(1024)S(1)}, f32[2048]{0:T(1024)}, u32[]{:S(2)}) copy-start(f32[2048]{0:T(1024)} %param.97) | copy-start | bytes 24580
  209.2 76.0 %copy-start.20 = (bf16[2,1,2,32,2048]{4,3,2,1,0:T(8,128)(2,1)S(1)}, bf16[2,1,2,32,2048]{4,3,2,1,0:T(8,128)(2,1)}, u32[]{:S(2)}) copy-start(bf16[2,1,2,32,2048]{4,3,2,1,0:T(8,128)(2,1)} %param.99) | copy-start | bytes 1572868
  209.2 2090.7 %reduce-scatter.9.cloned.1.call-start = ((), (), s32[]{:S(2)}) async-start(), calls=%async_computation.9 | async-start | bytes 4325376 | tf_op jit(solution)/shard_map/reduce_scatter | solution.py:374
  212.6 73.6 %copy-start.69 = (s32[2,32]{1,0:T(2,128)}, s32[2,32]{1,0:T(2,128)S(1)}, u32[]{:S(2)}) copy-start(s32[2,32]{1,0:T(2,128)S(1)} %get-tuple-element.1907) | copy-start | bytes 772
  240.4 45.7 %copy-start.76 = (f32[128]{0:T(128)}, f32[128]{0:T(128)S(1)}, u32[]{:S(2)}) copy-start(f32[128]{0:T(128)S(1)} %reshape.4574) | copy-start | bytes 1540
  731.5 824.1 %copy-start.61 = (f32[128]{0:T(128)}, f32[128]{0:T(128)S(1)}, u32[]{:S(2)}) copy-start(f32[128]{0:T(128)S(1)} %broadcast_multiply_fusion.5) | copy-start | bytes 1540
  732.7 822.9 %copy-start.63 = (f32[128]{0:T(128)}, f32[128]{0:T(128)S(1)}, u32[]{:S(2)}) copy-start(f32[128]{0:T(128)S(1)} %add_rsqrt_fusion.1) | copy-start | bytes 1540
  733.3 783.0 %copy-start.41 = (f32[4,1,512]{2,1,0:T(1,128)S(1)}, f32[4,1,512]{2,1,0:T(1,128)}, u32[]{:S(2)}) copy-start(f32[4,1,512]{2,1,0:T(1,128)} %convert_element_type.726) | copy-start | bytes 24580
  733.4 783.0 %copy-start.42 = (f32[4,1,512]{2,1,0:T(1,128)S(1)}, f32[4,1,512]{2,1,0:T(1,128)}, u32[]{:S(2)}) copy-start(f32[4,1,512]{2,1,0:T(1,128)} %convert_element_type.727) | copy-start | bytes 24580
  733.4 783.0 %copy-start.60 = (f32[8192]{0:T(1024)S(1)}, f32[8192]{0:T(1024)}, u32[]{:S(2)}) copy-start(f32[8192]{0:T(1024)} %convert_element_type.646) | copy-start | bytes 98308
  1535.8 19.9 copy-start.77
  1575.1 25.6 copy-start.15
  1599.2 12.1 copy-start.43
  1648.4 25.6 copy-start.15
  1672.5 12.1 copy-start.43
  1721.6 25.6 copy-start.15
  1745.8 12.1 copy-start.43
  1794.9 25.6 copy-start.15
  1868.2 25.6 copy-start.15
  1941.5 25.6 copy-start.15
  2014.7 25.6 copy-start.15
  2088.0 25.6 copy-start.15
  2154.0 453.2 %reduce-scatter.11.cloned.1.call-start = ((), (), s32[]{:S(2)}) async-start(), calls=%async_computation.10 | async-start | bytes 22282240 | tf_op jit(solution)/shard_map/reduce_scatter | solution.py:378
  2155.3 145.5 %copy-start.12 = (bf16[128,2048]{1,0:T(8,128)(2,1)S(1)}, bf16[128,2048]{1,0:T(8,128)(2,1)}, u32[]{:S(2)}) copy-start(bf16[128,2048]{1,0:T(8,128)(2,1)} %copy-done.11) | copy-start | bytes 1572868
  2311.1 851.6 %reduce-scatter.13.cloned.1.call-start = ((), (), s32[]{:S(2)}) async-start(), calls=%async_computation.11 | async-start | bytes 41943040
  2327.8 1390.1 %reduce-scatter.15.cloned.1.call-start = ((), (), s32[]{:S(2)}) async-start(), calls=%async_computation.12 | async-start | bytes 41943040
  2345.1 1645.7 %all-reduce.17.cloned.1.call-start = ((), (), s32[]{:S(2)}) async-start(), calls=%async_computation.13 | async-start | bytes 42467328 | tf_op jit(solution)/shard_map/psum | solution.py:426
  3717.9 14.9 copy-start.70
  3717.9 15.6 copy-start.21
  3733.7 18.6 copy-start.9
  3733.7 18.6 copy-start.59
  3733.7 18.6 copy-start.73
  3733.8 18.6 copy-start.75
  (337 other events, 2276.2 us)
Sparse Core Ops, SparseCore 0:
  11.4 169.7 all-gather.12
  187.2 54.8 all-gather.14
  244.2 148.8 all-gather.16
  395.2 559.5 all-gather.20
  956.8 559.5 all-gather.18
  2154.1 145.7 reduce-scatter.8
  2311.2 295.9 reduce-scatter.10
  2609.7 552.9 reduce-scatter.12
  3165.1 552.7 reduce-scatter.14
  3723.2 267.6 all-reduce.16
where the time goes:
time: 4050 us; the launch traced here: 4030 us
  waiting for transfers between devices  2580 us (64%)
  matrix products  593 us (15%)
  other arithmetic  339 us (8%)
  local copies, waits for them, and re-layouts  310 us (8%)
  blocking collectives  161 us (4%)
    unnamed x12, waiting for transfers between devices  1100 us
    all_gather x1, waiting for transfers between devices, body(): lax.all_gather(lowered[2], 'fsdp', axis=0, tiled=True)  540 us
    reduce_scatter x1, waiting for transfers between devices, body(): lax.psum_scatter(jnp.concatenate([outer_rows(first_low, grad_projected),...  262 us
    all_gather x1, waiting for transfers between devices, body(): lax.all_gather(lowered[3], 'fsdp', axis=0, tiled=True)  221 us
    psum x1, waiting for transfers between devices, body(): lax.psum(grad_qkv_w.astype(jnp.bfloat16), 'ctx').astype(jnp.float32)  183 us
    reduce_scatter x1, waiting for transfers between devices, body(): lax.psum_scatter(kv_term, ('ctx', 'fsdp'), scatter_dimension=1, tiled=True)  139 us
    dot_general x128, matrix products, tile_scores(): jnp.einsum('rhd,kd->rhk', query_five[slot_at, query_half], key_part, pref...  138 us
    another operation x98, local copies, waits for them, and re-layouts  128 us
  transfers between devices with their start and end apart: 10, of which 8 were waited for; matrix products, arithmetic and copies ran while one was open for 14% of the time, Pallas kernels for 0%

commit v1 on v0

v1 whole, which is shorter than its diff:
```python
import functools
import math

import jax
import jax.numpy as jnp
from jax import lax
from jax.experimental import pallas as pl
from jax.experimental.pallas import tpu as pltpu
from jax.sharding import PartitionSpec as P

HEADS = 16
HD = 128
NORM_EPS = 1e-05
MASKED = -1e30
KEY_TILE = 512
LANE_ROWS = 256
SCALE = 1.0 / math.sqrt(HD)
F32 = jnp.float32
BF16 = jnp.bfloat16


def layer_norm(values, gain_vec, shift_vec):
    centred = values - jnp.mean(values, axis=-1, keepdims=True)
    inverse = lax.rsqrt(jnp.mean(centred * centred, axis=-1, keepdims=True) + NORM_EPS)
    normed = centred * inverse
    return (normed * gain_vec + shift_vec, normed, inverse)


def norm_backward(grad_norm, normed, inverse, gain_vec):
    scaled = grad_norm * gain_vec
    centred = scaled - jnp.mean(scaled, axis=-1, keepdims=True)
    centred = centred - normed * jnp.mean(scaled * normed, axis=-1, keepdims=True)
    return (centred * inverse, jnp.sum(grad_norm * normed, axis=0), jnp.sum(grad_norm, axis=0))


def gelu_tanh(values):
    return jax.nn.gelu(values, approximate=True)


def mm(left, right):
    return jnp.dot(left, right, preferred_element_type=F32)


def mm_t(left, right):
    return lax.dot_general(left, right, (((1,), (1,)), ((), ())), preferred_element_type=F32)


def mm_rows(left, right):
    return lax.dot_general(left, right, (((0,), (0,)), ((), ())), preferred_element_type=F32)


def ctx_swap(values, mask):
    count = lax.axis_size("ctx")
    return lax.ppermute(values, "ctx", [(at, at ^ mask) for at in range(count)])


def ctx_gather(values):
    chips = lax.axis_size("ctx") // 2
    mine = jnp.concatenate([values] + [ctx_swap(values, 2 * at) for at in range(1, chips)], axis=0)
    return mine, ctx_swap(mine, 1)


def ctx_scatter(even, odd):
    chips = lax.axis_size("ctx") // 2
    rows = even.shape[0] // chips
    both = even.astype(F32) + ctx_swap(odd.astype(BF16), 1).astype(F32)
    total = both[:rows]
    low = both.astype(BF16)
    for at in range(1, chips):
        total = total + ctx_swap(low[at * rows : (at + 1) * rows], 2 * at).astype(F32)
    return total


def z_masks(count):
    masks = []
    while count > 1:
        masks.append(count - 1)
        count //= 2
    return masks


def z_offsets(count):
    offsets = [0]
    for mask in z_masks(count):
        offsets = offsets + [at ^ mask for at in offsets]
    return offsets


def z_swap(values, mask):
    count = lax.axis_size("fsdp")
    return lax.ppermute(values, "fsdp", [(at, at ^ mask) for at in range(count)])


def z_gather_relative(values):
    blocks = [values]
    for mask in z_masks(lax.axis_size("fsdp")):
        blocks = blocks + [z_swap(block, mask) for block in blocks]
    return blocks


def z_gather(values, z_at):
    count = lax.axis_size("fsdp")
    blocks = z_gather_relative(values)
    out = jnp.zeros((count,) + values.shape, values.dtype)
    for offset, block in zip(z_offsets(count), blocks):
        out = lax.dynamic_update_index_in_dim(out, block, z_at ^ offset, 0)
    return out


def z_scatter(partial, z_at):
    count = lax.axis_size("fsdp")
    blocks = {
        offset: lax.dynamic_index_in_dim(partial, z_at ^ offset, 0, keepdims=False)
        for offset in z_offsets(count)
    }
    return z_scatter_relative(blocks)


def z_scatter_relative(blocks):
    count = lax.axis_size("fsdp")
    held = z_offsets(count)
    for mask in reversed(z_masks(count)):
        held = held[: len(held) // 2]
        blocks = {
            offset: blocks[offset].astype(F32)
            + z_swap(blocks[offset ^ mask].astype(BF16), mask).astype(F32)
            for offset in held
        }
    return blocks[0].astype(F32)


def z_broadcast(values, z_at, source_of):
    ctx_count, count = lax.axis_size("ctx"), lax.axis_size("fsdp")
    source = source_of(lax.axis_index("ctx"))
    known = [0]
    for mask in z_masks(count):
        pairs = [
            (c * count + (source_of(c) ^ at), c * count + (source_of(c) ^ at ^ mask))
            for c in range(ctx_count)
            for at in known
        ]
        got = lax.ppermute(values, ("ctx", "fsdp"), pairs)
        held = functools.reduce(jnp.logical_or, [z_at == (source ^ at) for at in known])
        values = jnp.where(held, values, got)
        known = known + [at ^ mask for at in known]
    return values


class Shape:
    def __init__(self, ctx_count, fsdp_count, slots, rows):
        self.ctx_count, self.fsdp_count, self.slots, self.rows = ctx_count, fsdp_count, slots, rows
        self.heads = HEADS // ctx_count
        self.block = rows * fsdp_count
        self.blocks = 2 * ctx_count
        self.keys = self.block * self.blocks
        self.tokens = slots * 2 * rows
        self.q_blocks = LANE_ROWS // (self.heads * rows)
        self.head_rows = self.q_blocks * rows
        self.q_tiles = self.blocks // self.q_blocks
        self.q_rows = self.q_tiles * LANE_ROWS
        self.chips = ctx_count // 2
        self.offsets = z_offsets(fsdp_count)


def for_blocks(shape, meta, act):
    me = meta[0]

    def step(chip, carry):
        for parity in range(2):
            first = meta[6 + (me ^ (2 * chip + parity))]
            for slot in range(shape.slots):
                for half in range(2):
                    block = first if half == 0 else shape.blocks - 1 - first
                    act(parity, chip, slot, half, block)
        return carry

    lax.fori_loop(0, shape.chips, step, 0)


def at_rows(start, size, unit):
    return pl.ds(pl.multiple_of(start, unit), size)


def q_source(shape, chip, slot, half):
    return at_rows(chip * shape.tokens + (slot * 2 + half) * shape.rows, shape.rows, shape.rows)


def q_target(shape, block, head):
    start = (block // shape.q_blocks) * LANE_ROWS + (block % shape.q_blocks) * shape.rows
    return at_rows(start + head * shape.head_rows, shape.rows, shape.rows)


def kv_source(shape, chip, order, slot, half):
    start = (chip * shape.fsdp_count + order) * shape.tokens + (slot * 2 + half) * shape.rows
    return at_rows(start, shape.rows, shape.rows)


def kv_target(shape, meta, block, order):
    start = block * shape.block + (meta[1] ^ shape.offsets[order]) * shape.rows
    return at_rows(start, shape.rows, shape.rows)


def query_bounds(shape, meta, slot, tile):
    lane = lax.broadcasted_iota(jnp.int32, (1, LANE_ROWS), 1)
    row = lane % shape.head_rows
    pos = (tile * shape.q_blocks + row // shape.rows) * shape.block + meta[1] * shape.rows + row % shape.rows
    first_end = meta[2 + 2 * slot]
    second_end = first_end + meta[3 + 2 * slot]

    def start_of(at):
        return jnp.where(at < first_end, 0, jnp.where(at < second_end, first_end, second_end))

    first_pos = tile * shape.q_blocks * shape.block + meta[1] * shape.rows
    last_pos = first_pos + (shape.q_blocks - 1) * shape.block + shape.rows - 1
    return pos, start_of(pos), start_of(first_pos) // KEY_TILE, last_pos // KEY_TILE + 1


def visible(pos, start, tile):
    key_pos = tile * KEY_TILE + lax.broadcasted_iota(jnp.int32, (KEY_TILE, LANE_ROWS), 0)
    return (key_pos <= pos) & (key_pos >= start)


def attend_kernel(shape, meta, q_even, q_odd, kv_even, kv_odd, o_even, o_odd, q_all, kv_all, o_t, lse, o_rows):
    queries, keys, outs = (q_even, q_odd), (kv_even, kv_odd), (o_even, o_odd)

    def place(parity, chip, slot, half, block):
        for head in range(shape.heads):
            q_all[slot, q_target(shape, block, head), :] = queries[parity][
                q_source(shape, chip, slot, half), head * HD : (head + 1) * HD
            ]
        for order in range(shape.fsdp_count):
            kv_all[slot, kv_target(shape, meta, block, order), :] = keys[parity][
                kv_source(shape, chip, order, slot, half), :
            ]

    for_blocks(shape, meta, place)

    def tile_step(item, carry):
        slot, tile = item // shape.q_tiles, item % shape.q_tiles
        pos, start, low, high = query_bounds(shape, meta, slot, tile)
        q_tile = q_all[slot, at_rows(tile * LANE_ROWS, LANE_ROWS, LANE_ROWS), :]

        def key_step(at, state):
            peak, total, acc = state
            part = at_rows(at * KEY_TILE, KEY_TILE, KEY_TILE)
            scores = mm_t(kv_all[slot, part, :HD], q_tile) * SCALE
            scores = jnp.where(visible(pos, start, at), scores, MASKED)
            new_peak = jnp.maximum(peak, jnp.max(scores, axis=0, keepdims=True))
            fade = jnp.exp(peak - new_peak)
            weights = jnp.exp(scores - new_peak)
            total = total * fade + jnp.sum(weights, axis=0, keepdims=True)
            acc = acc * fade + mm_rows(kv_all[slot, part, HD:], weights.astype(BF16))
            return new_peak, total, acc

        begin = (
            jnp.full((1, LANE_ROWS), MASKED, F32),
            jnp.zeros((1, LANE_ROWS), F32),
            jnp.zeros((HD, LANE_ROWS), F32),
        )
        peak, total, acc = lax.fori_loop(low, high, key_step, begin)
        acc = acc / total
        o_t[item] = acc
        lse[item] = peak + jnp.log(total)
        o_rows[slot, at_rows(tile * LANE_ROWS, LANE_ROWS, LANE_ROWS), :] = acc.T.astype(BF16)
        return carry

    lax.fori_loop(0, shape.slots * shape.q_tiles, tile_step, 0)

    def put_back(parity, chip, slot, half, block):
        for head in range(shape.heads):
            outs[parity][q_source(shape, chip, slot, half), head * HD : (head + 1) * HD] = o_rows[
                slot, q_target(shape, block, head), :
            ]

    for_blocks(shape, meta, put_back)


def attend_grad_kernel(
    shape, meta, q_all, kv_all, o_t, lse, go_even, go_odd, gq_even, gq_odd, gkv_even, gkv_odd, go_all, gq_all, gkv_all
):
    grads, g_queries, g_keys = (go_even, go_odd), (gq_even, gq_odd), (gkv_even, gkv_odd)

    def place(parity, chip, slot, half, block):
        for head in range(shape.heads):
            go_all[slot, q_target(shape, block, head), :] = grads[parity][
                q_source(shape, chip, slot, half), head * HD : (head + 1) * HD
            ]

    for_blocks(shape, meta, place)
    gkv_all[...] = jnp.zeros_like(gkv_all)

    def tile_step(item, carry):
        slot, tile = item // shape.q_tiles, item % shape.q_tiles
        pos, start, low, high = query_bounds(shape, meta, slot, tile)
        rows = at_rows(tile * LANE_ROWS, LANE_ROWS, LANE_ROWS)
        q_tile = q_all[slot, rows, :]
        go_tile = go_all[slot, rows, :]
        delta = jnp.sum(go_tile.astype(F32).T * o_t[item], axis=0, keepdims=True)
        lse_row = lse[item]

        def key_step(at, acc):
            part = at_rows(at * KEY_TILE, KEY_TILE, KEY_TILE)
            key_part, value_part = kv_all[slot, part, :HD], kv_all[slot, part, HD:]
            scores = mm_t(key_part, q_tile) * SCALE
            probs = jnp.where(visible(pos, start, at), jnp.exp(scores - lse_row), 0.0)
            g_scores = (probs * (mm_t(value_part, go_tile) - delta)).astype(BF16)
            gkv_all[slot, part, :HD] += mm(g_scores, q_tile)
            gkv_all[slot, part, HD:] += mm(probs.astype(BF16), go_tile)
            return acc + mm_rows(key_part, g_scores)

        acc = lax.fori_loop(low, high, key_step, jnp.zeros((HD, LANE_ROWS), F32))
        gq_all[slot, rows, :] = (acc * SCALE).T.astype(BF16)
        return carry

    lax.fori_loop(0, shape.slots * shape.q_tiles, tile_step, 0)

    def put_back(parity, chip, slot, half, block):
        for head in range(shape.heads):
            g_queries[parity][q_source(shape, chip, slot, half), head * HD : (head + 1) * HD] = gq_all[
                slot, q_target(shape, block, head), :
            ]
        for order in range(shape.fsdp_count):
            target = kv_target(shape, meta, block, order)
            source = kv_source(shape, chip, order, slot, half)
            g_keys[parity][source, :HD] = (gkv_all[slot, target, :HD] * SCALE).astype(BF16)
            g_keys[parity][source, HD:] = gkv_all[slot, target, HD:].astype(BF16)

    for_blocks(shape, meta, put_back)


def attend(shape, meta, q_even, q_odd, kv_even, kv_odd):
    items = shape.slots * shape.q_tiles
    q_like = jax.ShapeDtypeStruct(q_even.shape, BF16)
    pairs = items * LANE_ROWS * shape.keys // 2
    return pl.pallas_call(
        functools.partial(attend_kernel, shape),
        grid_spec=pltpu.PrefetchScalarGridSpec(
            num_scalar_prefetch=1,
            grid=(1,),
            in_specs=[pl.BlockSpec(memory_space=pltpu.VMEM)] * 4,
            out_specs=[pl.BlockSpec(memory_space=pltpu.VMEM)] * 6,
            scratch_shapes=[pltpu.VMEM((shape.slots, shape.q_rows, HD), BF16)],
        ),
        out_shape=[
            q_like,
            q_like,
            jax.ShapeDtypeStruct((shape.slots, shape.q_rows, HD), BF16),
            jax.ShapeDtypeStruct((shape.slots, shape.keys, 2 * HD), BF16),
            jax.ShapeDtypeStruct((items, HD, LANE_ROWS), F32),
            jax.ShapeDtypeStruct((items, 1, LANE_ROWS), F32),
        ],
        compiler_params=pltpu.CompilerParams(vmem_limit_bytes=56 * 2**20),
        cost_estimate=pl.CostEstimate(flops=pairs * HD * 4, transcendentals=pairs, bytes_accessed=8 * 2**20),
        name="attend",
    )(meta, q_even, q_odd, kv_even, kv_odd)


def attend_grad(shape, meta, q_all, kv_all, o_t, lse, go_even, go_odd):
    items = shape.slots * shape.q_tiles
    q_like = jax.ShapeDtypeStruct(go_even.shape, BF16)
    kv_like = jax.ShapeDtypeStruct((shape.chips * shape.fsdp_count * shape.tokens, 2 * HD), BF16)
    pairs = items * LANE_ROWS * shape.keys // 2
    return pl.pallas_call(
        functools.partial(attend_grad_kernel, shape),
        grid_spec=pltpu.PrefetchScalarGridSpec(
            num_scalar_prefetch=1,
            grid=(1,),
            in_specs=[pl.BlockSpec(memory_space=pltpu.VMEM)] * 6,
            out_specs=[pl.BlockSpec(memory_space=pltpu.VMEM)] * 4,
            scratch_shapes=[
                pltpu.VMEM((shape.slots, shape.q_rows, HD), BF16),
                pltpu.VMEM((shape.slots, shape.q_rows, HD), BF16),
                pltpu.VMEM((shape.slots, shape.keys, 2 * HD), F32),
            ],
        ),
        out_shape=[q_like, q_like, kv_like, kv_like],
        compiler_params=pltpu.CompilerParams(vmem_limit_bytes=56 * 2**20),
        cost_estimate=pl.CostEstimate(flops=pairs * HD * 10, transcendentals=pairs, bytes_accessed=10 * 2**20),
        name="attend_grad",
    )(meta, q_all, kv_all, o_t, lse, go_even, go_odd)


def spread_kernel(by_rows, meta, even_ref, odd_ref, out_ref):
    swapped = meta[0] % 2 == 1
    even, odd = even_ref[0].astype(F32), odd_ref[0].astype(F32)
    first = jnp.where(swapped, odd, even)
    second = jnp.where(swapped, even, odd)
    if by_rows:
        out_ref[0], out_ref[1] = first, second
    else:
        width = even.shape[1]
        out_ref[:, :width] = first
        out_ref[:, width:] = second


def spread_rows(meta, even, odd):
    chips, rows, columns = even.shape
    tile = min(rows, 128)
    out = pl.pallas_call(
        functools.partial(spread_kernel, True),
        grid_spec=pltpu.PrefetchScalarGridSpec(
            num_scalar_prefetch=1,
            grid=(chips, rows // tile),
            in_specs=[pl.BlockSpec((1, tile, columns), lambda k, i, m: (k ^ (m[0] // 2), i, 0))] * 2,
            out_specs=pl.BlockSpec((2, tile, columns), lambda k, i, m: (k, i, 0)),
        ),
        out_shape=jax.ShapeDtypeStruct((2 * chips, rows, columns), F32),
        compiler_params=pltpu.CompilerParams(vmem_limit_bytes=32 * 2**20),
        name="spread_rows",
    )(meta, even, odd)
    return out.reshape(2 * chips * rows, columns)


def spread_columns(meta, even, odd, groups):
    chips, rows, columns = even.shape
    width = columns // groups
    if width % 128:
        out = jnp.zeros((2 * chips, rows, groups, width), F32)
        for at in range(2 * chips):
            block = (even, odd)[at % 2][at // 2].reshape(rows, groups, width).astype(F32)
            out = lax.dynamic_update_index_in_dim(out, block, meta[0] ^ at, 0)
        return jnp.transpose(out, (1, 2, 0, 3)).reshape(rows, 2 * chips * columns)
    return pl.pallas_call(
        functools.partial(spread_kernel, False),
        grid_spec=pltpu.PrefetchScalarGridSpec(
            num_scalar_prefetch=1,
            grid=(groups, chips),
            in_specs=[pl.BlockSpec((1, rows, width), lambda g, k, m: (k ^ (m[0] // 2), 0, g))] * 2,
            out_specs=pl.BlockSpec((rows, 2 * width), lambda g, k, m: (0, g * chips + k)),
        ),
        out_shape=jax.ShapeDtypeStruct((rows, 2 * chips * columns), F32),
        compiler_params=pltpu.CompilerParams(vmem_limit_bytes=32 * 2**20),
        name="spread_columns",
    )(meta, even, odd)


def pick_block(pair_table, ctx_at, half_bit):
    ctx_total = pair_table.shape[0]
    chosen = jnp.sum(jnp.where(jnp.arange(ctx_total, dtype=jnp.int32) == ctx_at, pair_table, 0))
    return jnp.where(half_bit == 0, chosen, 2 * ctx_total - 1 - chosen)


def body(
    inputs,
    w_qkv,
    w_out,
    w_fc,
    w_proj,
    ln1_gain,
    ln1_bias,
    bias_q,
    bias_v,
    bias_out,
    ln2_gain,
    ln2_bias,
    bias_fc,
    bias_proj,
    cotangent,
    lengths,
    pair_table,
):
    slots, _, _, rows, width = inputs.shape
    ctx_count, fsdp_count = lax.axis_size("ctx"), lax.axis_size("fsdp")
    c_at, z_at = lax.axis_index("ctx"), lax.axis_index("fsdp")
    shape = Shape(ctx_count, fsdp_count, slots, rows)
    tokens, chips = shape.tokens, shape.chips
    q_width = width // ctx_count
    hidden_width = w_fc.shape[1]
    unit = hidden_width // (fsdp_count * ctx_count)
    meta = jnp.concatenate(
        [jnp.stack([c_at, z_at]).astype(jnp.int32), lengths.reshape(-1), pair_table]
    ).astype(jnp.int32)

    offsets = jnp.arange(2 * rows, dtype=jnp.int32)
    pos = (
        pick_block(pair_table, c_at, offsets // rows) * shape.block + z_at * rows + offsets % rows
    )
    live = (pos[None, :] < lengths[:, 0:1] + lengths[:, 1:2]).reshape(tokens, 1).astype(F32)

    x_low = inputs.reshape(tokens, width)
    x_even, x_odd = ctx_gather(x_low)
    vectors = [ln1_gain, ln1_bias, bias_q, bias_v, bias_out, ln2_gain, ln2_bias, bias_fc, bias_proj]
    sizes = [member.shape[0] for member in vectors]
    packed = z_gather(jnp.concatenate([member.astype(BF16) for member in vectors]), z_at)
    full, start = [], 0
    for size in sizes:
        full.append(packed[:, start : start + size].reshape(-1).astype(F32))
        start += size
    gain_one, shift_one, q_bias, v_bias, out_bias, gain_two, shift_two, fc_bias, proj_bias = full
    q_bias = lax.dynamic_slice_in_dim(q_bias, c_at * q_width, q_width)
    fc_bias = lax.dynamic_index_in_dim(
        fc_bias.reshape(fsdp_count, ctx_count, unit), c_at, 1, keepdims=False
    ).reshape(-1)

    w_kv = z_gather(w_qkv[:, width:].astype(BF16), z_at).reshape(width, 2 * HD)
    w_q = z_gather(
        lax.dynamic_slice_in_dim(w_qkv, c_at * q_width, q_width, axis=1).astype(BF16), z_at
    ).reshape(width, q_width)
    per_plane = ctx_count // fsdp_count
    w_o = z_broadcast(
        lax.dynamic_slice_in_dim(w_out, (c_at % per_plane) * q_width, q_width, axis=0).astype(BF16),
        z_at,
        lambda c: c // per_plane,
    )
    w_f = z_gather(
        lax.dynamic_index_in_dim(
            w_fc.reshape(-1, fsdp_count, ctx_count, unit), c_at, 2, keepdims=False
        )
        .reshape(-1, fsdp_count * unit)
        .astype(BF16),
        z_at,
    ).reshape(width, fsdp_count * unit)
    w_p = z_gather(
        lax.dynamic_slice_in_dim(w_proj, c_at * unit, unit, axis=0).astype(BF16), z_at
    ).reshape(fsdp_count * unit, width)

    x_own = x_low.astype(F32)
    first_norm, normed_one, inverse_one = layer_norm(x_own, gain_one, shift_one)
    kv_own = mm(first_norm.astype(BF16), w_kv)
    kv_own = jnp.concatenate([kv_own[:, :HD], kv_own[:, HD:] + v_bias], axis=1).astype(BF16)
    kv_even, kv_odd = ctx_gather(jnp.concatenate(z_gather_relative(kv_own), axis=0))
    a_even = layer_norm(x_even.astype(F32), gain_one, shift_one)[0].astype(BF16)
    a_odd = layer_norm(x_odd.astype(F32), gain_one, shift_one)[0].astype(BF16)
    q_even = (mm(a_even, w_q) + q_bias).astype(BF16)
    q_odd = (mm(a_odd, w_q) + q_bias).astype(BF16)
    o_even, o_odd, q_all, kv_all, o_t, lse = attend(shape, meta, q_even, q_odd, kv_even, kv_odd)
    branch = ctx_scatter(mm(o_even, w_o), mm(o_odd, w_o)) + out_bias
    middle = x_own + branch
    second_norm, normed_two, inverse_two = layer_norm(middle, gain_two, shift_two)

    grad_out = cotangent.reshape(tokens, width).astype(F32) * live
    grad_mlp = grad_out.astype(BF16)
    gm_even, gm_odd = ctx_gather(grad_mlp)
    cn_even, cn_odd = ctx_gather(second_norm.astype(BF16))
    acts, g_hidden, g_second, mlp = [], [], [], []
    for cn_part, gm_part in ((cn_even, gm_even), (cn_odd, gm_odd)):
        hidden = mm(cn_part, w_f) + fc_bias
        activated, pull = jax.vjp(gelu_tanh, hidden)
        acts.append(activated.astype(BF16))
        g_hidden.append(pull(mm_t(gm_part, w_p))[0].astype(BF16))
        g_second.append(mm_t(g_hidden[-1], w_f).astype(BF16))
        mlp.append(mm(acts[-1], w_p).astype(BF16))
    grad_second = ctx_scatter(*g_second)
    result = (middle + (ctx_scatter(*mlp) + proj_bias)).astype(BF16)

    def over_plane(left, right):
        return mm_rows(left[0], right[0]) + mm_rows(left[1], right[1])

    d_proj = over_plane(acts, (gm_even, gm_odd)).astype(BF16)
    d_fc = over_plane((cn_even, cn_odd), g_hidden).astype(BF16)
    d_proj = z_scatter(d_proj.reshape(fsdp_count, unit, width), z_at).astype(BF16)
    d_fc = z_scatter(d_fc.reshape(fsdp_count, -1, fsdp_count * unit), z_at).astype(BF16)

    def spread(values, by_rows, groups=1):
        even, odd = ctx_gather(values)
        even, odd = even.reshape((chips,) + values.shape), odd.reshape((chips,) + values.shape)
        return spread_rows(meta, even, odd) if by_rows else spread_columns(meta, even, odd, groups)

    grad_w_proj = spread(d_proj, True)
    grad_w_fc = spread(d_fc, False, fsdp_count)

    grad_mid_norm, grad_gain_two, grad_shift_two = norm_backward(
        grad_second, normed_two, inverse_two, gain_two
    )
    grad_middle = grad_out + grad_mid_norm
    grad_branch = grad_middle.astype(BF16)
    ga_even, ga_odd = ctx_gather(grad_branch)

    def o_blocks(from_mask):
        got = (o_even, o_odd)
        if from_mask:
            got = (ctx_swap(o_even, from_mask), ctx_swap(o_odd, from_mask))
        order = []
        for parity in range(2):
            for at in range(chips):
                source = (2 * at + parity) ^ from_mask
                part = got[source % 2]
                order.append(part[(source // 2) * tokens : (source // 2 + 1) * tokens])
        return jnp.concatenate(order, axis=0)

    ga_all = jnp.concatenate([ga_even, ga_odd], axis=0)
    ga_columns = lax.dynamic_slice_in_dim(ga_all, c_at * q_width, q_width, axis=1)
    o_full = jnp.zeros((ctx_count, ctx_count * tokens, q_width), BF16)
    for mask in range(ctx_count):
        o_full = lax.dynamic_update_index_in_dim(o_full, o_blocks(mask), c_at ^ mask, 0)
    d_out = lax.dot_general(
        o_full, ga_columns, (((1,), (0,)), ((), ())), preferred_element_type=F32
    ).astype(BF16)
    d_out = z_scatter(d_out.reshape(fsdp_count, -1, q_width), z_at).astype(BF16)
    grad_w_out = spread(d_out, False)

    go_even = mm_t(ga_even, w_o).astype(BF16)
    go_odd = mm_t(ga_odd, w_o).astype(BF16)
    gq_even, gq_odd, gkv_even, gkv_odd = attend_grad(
        shape, meta, q_all, kv_all, o_t, lse, go_even, go_odd
    )
    gkv_plane = ctx_scatter(gkv_even, gkv_odd).reshape(fsdp_count, tokens, 2 * HD)
    gkv_low = z_scatter_relative(
        {offset: gkv_plane[at] for at, offset in enumerate(shape.offsets)}
    ).astype(BF16)
    gkv_parts = ctx_gather(gkv_low)
    grad_first = ctx_scatter(mm_t(gq_even, w_q), mm_t(gq_odd, w_q)) + mm_t(gkv_low, w_kv)
    grad_in_norm, grad_gain_one, grad_shift_one = norm_backward(
        grad_first, normed_one, inverse_one, gain_one
    )
    grad_inputs = grad_middle + grad_in_norm
    d_q = over_plane((a_even, a_odd), (gq_even, gq_odd)).astype(BF16)
    d_q = z_scatter(d_q.reshape(fsdp_count, -1, q_width), z_at).astype(BF16)
    d_kv = over_plane((a_even, a_odd), gkv_parts).astype(BF16)
    d_kv = z_scatter(d_kv.reshape(fsdp_count, -1, 2 * HD), z_at).astype(BF16).astype(F32)
    grad_w_qkv = jnp.concatenate([spread(d_q, False), d_kv], axis=1)

    def column_sum(*parts):
        return sum(jnp.sum(part, axis=0, dtype=F32) for part in parts)

    g_bias_q = lax.dynamic_update_index_in_dim(
        jnp.zeros((ctx_count, q_width), F32), column_sum(gq_even, gq_odd), c_at, 0
    ).reshape(-1)
    g_bias_fc = lax.dynamic_update_index_in_dim(
        jnp.zeros((fsdp_count, ctx_count, unit), F32),
        column_sum(*g_hidden).reshape(fsdp_count, unit),
        c_at,
        1,
    ).reshape(-1)
    g_vectors = [
        grad_gain_one,
        grad_shift_one,
        g_bias_q,
        column_sum(gkv_low[:, HD:]),
        column_sum(grad_branch),
        grad_gain_two,
        grad_shift_two,
        g_bias_fc,
        column_sum(grad_mlp),
    ]
    stacked = jnp.concatenate(
        [member.reshape(fsdp_count, -1) for member in g_vectors], axis=1
    ).astype(BF16)
    own = z_scatter(stacked[:, None, :], z_at).astype(BF16)
    all_even, all_odd = ctx_gather(own)
    summed = column_sum(all_even, all_odd)
    vector_grads, start = [], 0
    for size in sizes:
        vector_grads.append(summed[start : start + size].astype(BF16).astype(F32))
        start += size
    return (
        result.reshape(inputs.shape),
        grad_inputs.reshape(inputs.shape),
        grad_w_qkv,
        grad_w_out,
        grad_w_fc,
        grad_w_proj,
        *vector_grads,
    )


def solution(mesh):
    rows_placed = P(None, "ctx", None, "fsdp", None)
    matrix, vector = P("fsdp", None), P("fsdp")
    return jax.shard_map(
        body,
        mesh=mesh,
        in_specs=(rows_placed,) + (matrix,) * 4 + (vector,) * 9 + (rows_placed, P(), P()),
        out_specs=(rows_placed, rows_placed) + (matrix,) * 4 + (vector,) * 9,
        check_vma=False,
    )
```

time: 4050 us -> 950 us (0.23)
  waiting for transfers between devices: 2580 us -> 415 us
  matrix products: 593 us -> 115 us
  other arithmetic: 339 us -> 70.1 us
  local copies, waits for them, and re-layouts: 310 us -> 117 us
  blocking collectives: 161 us -> 0 us
  starting transfers between devices: 0.42 us -> 161 us
  Pallas kernels: 0 us -> 61.3 us
    unnamed x12 -> x0, waiting for transfers between devices: 1100 us -> none
    all_gather x5 -> x0, waiting for transfers between devices: 886 us -> none  [the longest x1 540 us: body(): lax.all_gather(lowered[2], 'fsdp', axis=0, tiled=True)]
    dot_general x460 -> x27, matrix products: 593 us -> 115 us  [the longest x9 44.5 us: mm_t(): lax.dot_general(left, right, (((1,), (1,)), ((), ())), preferred_element_...]
    ppermute x0 -> x119, waiting for transfers between devices: none -> 415 us  [the longest x78 207 us: ctx_swap(): return lax.ppermute(values, 'ctx', [(at, at ^ mask) for at in range(count)])]
    reduce_scatter x2 -> x0, waiting for transfers between devices: 401 us -> none  [the longest x1 262 us: body(): lax.psum_scatter(jnp.concatenate([outer_rows(first_low, grad_projected),...]
    psum x1 -> x0, waiting for transfers between devices: 183 us -> none  [body(): lax.psum(grad_qkv_w.astype(jnp.bfloat16), 'ctx').astype(jnp.float32)]
    ppermute x0 -> x119, starting transfers between devices: none -> 161 us  [the longest x39 80.9 us: z_swap(): lax.ppermute(values, 'fsdp', [(at, at ^ mask) for at in range(count)])]
    another operation x98 -> x3, local copies, waits for them, and re-layouts: 128 us -> 0.16 us
  transfers between devices with their start and end apart: 10 -> 119, of which waited for: 8 -> 53; matrix products, arithmetic and copies ran while one was open for 14% -> 29% of each run, Pallas kernels for 0% -> 5%
where the time goes in v1:
time: 950 us; the launch traced here: 943 us
  waiting for transfers between devices  415 us (44%)
  starting transfers between devices  161 us (17%)
  local copies, waits for them, and re-layouts  117 us (12%)
  matrix products  115 us (12%)
  other arithmetic  70.1 us (7%)
  Pallas kernels  61.3 us (6%)
    ppermute x78, waiting for transfers between devices, ctx_swap(): return lax.ppermute(values, 'ctx', [(at, at ^ mask) for at in range(count)])  207 us
    ppermute x39, waiting for transfers between devices, z_swap(): lax.ppermute(values, 'fsdp', [(at, at ^ mask) for at in range(count)])  192 us
    ppermute x39, starting transfers between devices, z_swap(): lax.ppermute(values, 'fsdp', [(at, at ^ mask) for at in range(count)])  80.9 us
    ppermute x78, starting transfers between devices, ctx_swap(): return lax.ppermute(values, 'ctx', [(at, at ^ mask) for at in range(count)])  69.5 us
    dot_general x9, matrix products, mm_t(): lax.dot_general(left, right, (((1,), (1,)), ((), ())), preferred_element_...  44.5 us
    unnamed x205, local copies, waits for them, and re-layouts  43 us
    dot_general x8, matrix products, mm_rows(): lax.dot_general(left, right, (((0,), (0,)), ((), ())), preferred_element_...  35.9 us
    dot_general x9, matrix products, mm(): return jnp.dot(left, right, preferred_element_type=F32)  30.9 us
  transfers between devices with their start and end apart: 119, of which 53 were waited for; matrix products, arithmetic and copies ran while one was open for 29% of the time, Pallas kernels for 5%

profile of v1, /device:TPU:0, one launch (start us, length us, event | category | flops | bytes accessed | tf_op | source)
XLA Modules:
  0.0 943.0 jit_solution(17711433042310742133)
XLA Ops:
  23.5 13.8 %copy.67 = bf16[512,8192]{0,1:T(8,128)(2,1)} copy(f32[512,8192]{1,0:T(8,128)} %param.20) | data formatting | bytes 25165824 | tf_op args[3]
  61.0 7.6 collective-permute-done.6
  90.8 7.9 collective-permute-done.12
  112.3 5.4 collective-permute-start.20
  119.3 7.5 collective-permute-done.17
  128.8 5.3 collective-permute-done.18
  134.1 43.1 %collective-permute-done.30 = bf16[512,1024]{0,1:T(8,128)(2,1)S(1)} collective-permute-done((bf16[512,1024]{0,1:T(8,128)(2,1)S(1)}, bf16[512,1024]{0,1:T(8,128)(2,1)S(1)}, u32[]{:S(2)}, u32[]{:S(2)}) %collective-permute-start.30) | collective-permute-done | bytes 1048608 | tf_op jit(solution)/shard_map/ppermute | solution.py:91
  183.6 21.0 %collective-permute-start.31 = (bf16[512,1024]{0,1:T(8,128)(2,1)}, bf16[512,1024]{0,1:T(8,128)(2,1)S(1)}, u32[]{:S(2)}, u32[]{:S(2)}) collective-permute-start(bf16[512,1024]{0,1:T(8,128)(2,1)} %collective-permute-done.29), channel_id=1, source_target_pairs={{0,1},{1,0},{2,3},{3,2},{4,5},{5,4},{6,7},{7,6},{8,9},{9,8},{10,11... | collective-permute-start | bytes 3145736 | tf_op jit(solution)/shard_map/ppermute | solution.py:91
  208.5 13.0 %collective-permute-start.34 = (bf16[256,2048]{1,0:T(8,128)(2,1)}, bf16[256,2048]{1,0:T(8,128)(2,1)}, u32[]{:S(2)}, u32[]{:S(2)}) collective-permute-start(bf16[256,2048]{1,0:T(8,128)(2,1)} %collective-permute-done.32), channel_id=1, source_target_pairs={{0,1},{1,0},{2,3},{3,2},{4,5},{5,4},{6,7},{7,6},{8,9},{9,8},{10,11... | collective-permute-start | bytes 3145736 | tf_op jit(solution)/shard_map/ppermute | solution.py:91
  224.5 5.6 collective-permute-start.21
  232.5 14.5 %collective-permute-done.31 = bf16[512,1024]{0,1:T(8,128)(2,1)S(1)} collective-permute-done((bf16[512,1024]{0,1:T(8,128)(2,1)}, bf16[512,1024]{0,1:T(8,128)(2,1)S(1)}, u32[]{:S(2)}, u32[]{:S(2)}) %collective-permute-start.31) | collective-permute-done | bytes 1048608 | tf_op jit(solution)/shard_map/ppermute | solution.py:91
  250.5 19.0 %collective-permute-done.34 = bf16[256,2048]{1,0:T(8,128)(2,1)} collective-permute-done((bf16[256,2048]{1,0:T(8,128)(2,1)}, bf16[256,2048]{1,0:T(8,128)(2,1)}, u32[]{:S(2)}, u32[]{:S(2)}) %collective-permute-start.34) | collective-permute-done | bytes 1048608 | tf_op jit(solution)/shard_map/ppermute | solution.py:91
  271.8 15.5 %collective-permute-done.21 = bf16[256,2048]{1,0:T(8,128)(2,1)} collective-permute-done((bf16[256,2048]{1,0:T(8,128)(2,1)}, bf16[256,2048]{1,0:T(8,128)(2,1)}, u32[]{:S(2)}, u32[]{:S(2)}) %collective-permute-start.21) | collective-permute-done | bytes 1048608 | tf_op jit(solution)/shard_map/ppermute | solution.py:142
  294.0 14.3 %attend.1 = (bf16[512,256]{1,0:T(8,128)(2,1)}, bf16[512,256]{1,0:T(8,128)(2,1)}, bf16[2,1024,128]{2,1,0:T(8,128)(2,1)}, bf16[2,2048,256]{2,1,0:T(8,128)(2,1)}, f...) custom-call(s32[14]{0:T(128)} %pad_add_fusion.meta, bf16[512,256]{1,0:T(8,128)(2,1)} %fusion.36.q_even, ...), custom_call_target="tpu_custom_call" | custom-call | flops 1073741824 | bytes 8388608 | tf_op jit(solution)/shard_map/attend/pallas_call | solution.py:335
  335.2 5.2 collective-permute-done.89
  341.2 8.3 collective-permute-done.80
  393.0 6.9 collective-permute-done.23
  399.9 11.1 %collective-permute-done.25 = bf16[128,2048]{1,0:T(8,128)(2,1)S(1)} collective-permute-done((bf16[128,2048]{1,0:T(8,128)(2,1)S(1)}, bf16[128,2048]{1,0:T(8,128)(2,1)S(1)}, u32[]{:S(2)}, u32[]{:S(2)}) %collective-permute-start.25) | collective-permute-done | bytes 524320 | tf_op jit(solution)/shard_map/ppermute | solution.py:54
  411.0 13.0 %collective-permute-done.24 = bf16[128,2048]{1,0:T(8,128)(2,1)S(1)} collective-permute-done((bf16[128,2048]{1,0:T(8,128)(2,1)S(1)}, bf16[128,2048]{1,0:T(8,128)(2,1)S(1)}, u32[]{:S(2)}, u32[]{:S(2)}) %collective-permute-start.24) | collective-permute-done | bytes 524320 | tf_op jit(solution)/shard_map/ppermute | solution.py:54
  436.3 5.5 collective-permute-done.27
  451.0 5.3 fusion.93
  456.4 15.8 %convert_reduce_fusion.3 = (f32[1024]{0:T(1024)S(1)}, bf16[512,1024]{1,0:T(8,128)(2,1)S(1)}) fusion(f32[512,1024]{1,0:T(8,128)S(1)} %fusion.93, f32[1024]{0:T(1024)S(1)} %bitcast.279, bf16[1024,2048]{1,0:T(8,128)(2,1)} %bitcast.26, bf16[128,2048]{1,0:T(8,128)(2,1)S(1)} %copy-done.55, bf16[128,2048]{1,0:T(8,128)(2,1)S(1)} %copy-done.57, ...), kind=kOutput, calls=%fused_computation.69 | convolution fusion | flops 2167929856 | bytes 9445376 | tf_op jit(solution)/shard_map/dot_general | solution.py:45
  476.5 6.1 convolution_convert_fusion.3
  482.6 6.4 convert_reduce_fusion.2
  493.2 7.7 fusion.91
  500.9 5.7 add_convert_fusion
  509.5 7.4 fusion.120
  516.8 6.4 add_convert_fusion.1
  524.9 4.8 convolution_convert_fusion.4
  534.7 21.2 %collective-permute-done.99 = bf16[512,1024]{1,0:T(8,128)(2,1)S(1)} collective-permute-done((bf16[512,1024]{1,0:T(8,128)(2,1)S(1)}, bf16[512,1024]{1,0:T(8,128)(2,1)S(1)}, u32[]{:S(2)}, u32[]{:S(2)}) %collective-permute-start.99) | collective-permute-done | bytes 1048608 | tf_op jit(solution)/shard_map/ppermute | solution.py:91
  556.4 6.0 fusion.114
  567.1 11.1 %collective-permute-done.105 = bf16[256,2048]{1,0:T(8,128)(2,1)S(1)} collective-permute-done((bf16[256,2048]{1,0:T(8,128)(2,1)S(1)}, bf16[256,2048]{1,0:T(8,128)(2,1)S(1)}, u32[]{:S(2)}, u32[]{:S(2)}) %collective-permute-start.105) | collective-permute-done | bytes 1048608 | tf_op jit(solution)/shard_map/ppermute | solution.py:91
  580.4 21.3 %collective-permute-done.107 = bf16[256,2048]{1,0:T(8,128)(2,1)S(1)} collective-permute-done((bf16[256,2048]{1,0:T(8,128)(2,1)S(1)}, bf16[256,2048]{1,0:T(8,128)(2,1)S(1)}, u32[]{:S(2)}, u32[]{:S(2)}) %collective-permute-start.107) | collective-permute-done | bytes 1048608 | tf_op jit(solution)/shard_map/ppermute | solution.py:91
  609.7 10.2 %collective-permute-done.37 = bf16[128,2048]{1,0:T(8,128)(2,1)S(1)} collective-permute-done((bf16[128,2048]{1,0:T(8,128)(2,1)S(1)}, bf16[128,2048]{1,0:T(8,128)(2,1)S(1)}, u32[]{:S(2)}, u32[]{:S(2)}) %collective-permute-start.37) | collective-permute-done | bytes 524320 | tf_op jit(solution)/shard_map/ppermute | solution.py:54
  621.4 10.3 %collective-permute-done.39 = bf16[128,2048]{1,0:T(8,128)(2,1)S(1)} collective-permute-done((bf16[128,2048]{1,0:T(8,128)(2,1)S(1)}, bf16[128,2048]{1,0:T(8,128)(2,1)S(1)}, u32[]{:S(2)}, u32[]{:S(2)}) %collective-permute-start.39) | collective-permute-done | bytes 524320 | tf_op jit(solution)/shard_map/ppermute | solution.py:54
  632.3 28.2 %collective-permute-done.38 = bf16[128,2048]{1,0:T(8,128)(2,1)S(1)} collective-permute-done((bf16[128,2048]{1,0:T(8,128)(2,1)S(1)}, bf16[128,2048]{1,0:T(8,128)(2,1)S(1)}, u32[]{:S(2)}, u32[]{:S(2)}) %collective-permute-start.38) | collective-permute-done | bytes 524320 | tf_op jit(solution)/shard_map/ppermute | solution.py:54
  672.4 8.6 collective-permute-done.50
  682.4 35.4 %collective-permute-done.49 = bf16[128,2048]{1,0:T(8,128)(2,1)S(1)} collective-permute-done((bf16[128,2048]{1,0:T(8,128)(2,1)S(1)}, bf16[128,2048]{1,0:T(8,128)(2,1)S(1)}, u32[]{:S(2)}, u32[]{:S(2)}) %collective-permute-start.49) | collective-permute-done | bytes 524320 | tf_op jit(solution)/shard_map/ppermute | solution.py:54
  728.7 14.9 %collective-permute-done.102 = bf16[512,1024]{1,0:T(8,128)(2,1)} collective-permute-done((bf16[512,1024]{1,0:T(8,128)(2,1)}, bf16[512,1024]{1,0:T(8,128)(2,1)}, u32[]{:S(2)}, u32[]{:S(2)}) %collective-permute-start.102) | collective-permute-done | bytes 1048608 | tf_op jit(solution)/shard_map/ppermute | solution.py:54
  752.2 16.0 %attend_grad.1 = (bf16[512,256]{1,0:T(8,128)(2,1)}, bf16[512,256]{1,0:T(8,128)(2,1)}, bf16[2048,256]{1,0:T(8,128)(2,1)}, bf16[2048,256]{1,0:T(8,128)(2,1)}) custom-call(s32[14]{0:T(128)} %pad_add_fusion.meta, bf16[2,1024,128]{2,1,0:T(8,128)(2,1)} %get-tuple-element.27.q_all, bf16[2,2048,256]{2,1,0:T(8,128)(2,1)} %get-tuple-element.28.kv_all, ...), custom_call_target="tpu_custom_call" | custom-call | flops 2684354560 | bytes 10485760 | tf_op jit(solution)/shard_map/attend_grad/pallas_call | solution.py:363
  786.6 5.4 collective-permute-done.59
  794.3 6.9 collective-permute-done.61
  807.2 5.3 collective-permute-done.62
  845.7 5.2 collective-permute-done.67
  865.4 7.3 collective-permute-done.75
  889.8 14.4 %spread_columns.5 = f32[512,8192]{1,0:T(8,128)} custom-call(s32[14]{0:T(128)S(1)} %copy-done.3, bf16[4,512,1024]{2,1,0:T(8,128)(2,1)} %bitcast.65.even_ref, bf16[4,512,1024]{2,1,0:T(8,128)(2,1)} %bitcast.66.odd_ref), custom_call_target="tpu_custom_call" | custom-call | tf_op jit(solution)/shard_map/spread_columns/pallas_call | solution.py:423
  904.2 11.2 %spread_rows.1 = f32[8,256,2048]{2,1,0:T(8,128)} custom-call(s32[14]{0:T(128)S(1)} %copy-done.3, bf16[4,256,2048]{2,1,0:T(8,128)(2,1)} %bitcast.72.even_ref, bf16[4,256,2048]{2,1,0:T(8,128)(2,1)} %bitcast.73.odd_ref), custom_call_target="tpu_custom_call" | custom-call | tf_op jit(solution)/shard_map/spread_rows/pallas_call | solution.py:399
  921.1 4.7 pad_maximum_fusion
  (616 shorter events, 386.8 us)
Async XLA Ops:
  6.9 50.4 %collective-permute-start.4 = (bf16[5664]{0:T(1024)(128)(2,1)S(1)}, bf16[5664]{0:T(1024)(128)(2,1)S(1)}, u32[]{:S(2)}, u32[]{:S(2)}) collective-permute-start(bf16[5664]{0:T(1024)(128)(2,1)S(1)} %concatenate.88), channel_id=1, source_target_pairs={{0,1},{1,0},{2,3},{3,2},{4,5},{5,4},{6,7},{7,6},{8,9},{9,8},{10,11... | collective-permute-start | bytes 33992 | tf_op jit(solution)/shard_map/ppermute | solution.py:91
  10.0 45.5 %collective-permute-start.3 = (bf16[5664]{0:T(1024)(128)(2,1)S(1)}, bf16[5664]{0:T(1024)(128)(2,1)S(1)}, u32[]{:S(2)}, u32[]{:S(2)}) collective-permute-start(bf16[5664]{0:T(1024)(128)(2,1)S(1)} %concatenate.88), channel_id=1, source_target_pairs={{0,3},{1,2},{2,1},{3,0},{4,7},{5,6},{6,5},{7,4},{8,11},{9,10},{10,... | collective-permute-start | bytes 33992 | tf_op jit(solution)/shard_map/ppermute | solution.py:91
  12.4 71.8 %collective-permute-start.2 = (bf16[128,2048]{1,0:T(8,128)(2,1)}, bf16[128,2048]{1,0:T(8,128)(2,1)}, u32[]{:S(2)}, u32[]{:S(2)}) collective-permute-start(bf16[128,2048]{1,0:T(8,128)(2,1)} %bitcast.212), channel_id=1, source_target_pairs={{0,24},{4,28},{8,16},{12,20},{16,8},{20,12},{24,0},{28,4},{1,25},{... | collective-permute-start | bytes 1572872 | tf_op jit(solution)/shard_map/ppermute | solution.py:54
  14.9 70.9 %collective-permute-start.1 = (bf16[128,2048]{1,0:T(8,128)(2,1)}, bf16[128,2048]{1,0:T(8,128)(2,1)}, u32[]{:S(2)}, u32[]{:S(2)}) collective-permute-start(bf16[128,2048]{1,0:T(8,128)(2,1)} %bitcast.213), channel_id=1, source_target_pairs={{0,16},{4,20},{8,24},{12,28},{16,0},{20,4},{24,8},{28,12},{1,17},{... | collective-permute-start | bytes 1572872 | tf_op jit(solution)/shard_map/ppermute | solution.py:54
  15.4 70.8 %collective-permute-start = (bf16[128,2048]{1,0:T(8,128)(2,1)}, bf16[128,2048]{1,0:T(8,128)(2,1)}, u32[]{:S(2)}, u32[]{:S(2)}) collective-permute-start(bf16[128,2048]{1,0:T(8,128)(2,1)} %bitcast.214), channel_id=1, source_target_pairs={{0,8},{4,12},{8,0},{12,4},{16,24},{20,28},{24,16},{28,20},{1,9},{5... | collective-permute-start | bytes 1572872 | tf_op jit(solution)/shard_map/ppermute | solution.py:54
  78.1 34.1 %collective-permute-start.42 = (bf16[128,2048]{1,0:T(8,128)(2,1)}, bf16[128,2048]{1,0:T(8,128)(2,1)S(1)}, u32[]{:S(2)}, u32[]{:S(2)}) collective-permute-start(bf16[128,2048]{1,0:T(8,128)(2,1)} %fusion.63), channel_id=1, source_target_pairs={{0,24},{4,28},{8,16},{12,20},{16,8},{20,12},{24,0},{28,4},{1,25},{... | collective-permute-start | bytes 1572872 | tf_op jit(solution)/shard_map/ppermute | solution.py:54
  82.7 35.0 %collective-permute-start.41 = (bf16[128,2048]{1,0:T(8,128)(2,1)}, bf16[128,2048]{1,0:T(8,128)(2,1)S(1)}, u32[]{:S(2)}, u32[]{:S(2)}) collective-permute-start(bf16[128,2048]{1,0:T(8,128)(2,1)} %fusion.63), channel_id=1, source_target_pairs={{0,16},{4,20},{8,24},{12,28},{16,0},{20,4},{24,8},{28,12},{1,17},{... | collective-permute-start | bytes 1572872 | tf_op jit(solution)/shard_map/ppermute | solution.py:54
  84.2 33.4 %collective-permute-start.40 = (bf16[128,2048]{1,0:T(8,128)(2,1)S(1)}, bf16[128,2048]{1,0:T(8,128)(2,1)S(1)}, u32[]{:S(2)}, u32[]{:S(2)}) collective-permute-start(bf16[128,2048]{1,0:T(8,128)(2,1)S(1)} %copy-done.39), channel_id=1, source_target_pairs={{0,8},{4,12},{8,0},{12,4},{16,24},{20,28},{24,16},{28,20},{1,9},{5... | collective-permute-start | bytes 1572872 | tf_op jit(solution)/shard_map/ppermute | solution.py:54
  108.8 68.4 %collective-permute-start.30 = (bf16[512,1024]{0,1:T(8,128)(2,1)S(1)}, bf16[512,1024]{0,1:T(8,128)(2,1)S(1)}, u32[]{:S(2)}, u32[]{:S(2)}) collective-permute-start(bf16[512,1024]{0,1:T(8,128)(2,1)S(1)} %bitcast.231), channel_id=1, source_target_pairs={{0,1},{1,0},{2,3},{3,2},{4,5},{5,4},{6,7},{7,6},{8,9},{9,8},{10,11... | collective-permute-start | bytes 3145736 | tf_op jit(solution)/shard_map/ppermute | solution.py:91
  110.9 69.7 %collective-permute-start.29 = (bf16[512,1024]{0,1:T(8,128)(2,1)S(1)}, bf16[512,1024]{0,1:T(8,128)(2,1)}, u32[]{:S(2)}, u32[]{:S(2)}) collective-permute-start(bf16[512,1024]{0,1:T(8,128)(2,1)S(1)} %bitcast.232), channel_id=1, source_target_pairs={{0,3},{1,2},{2,1},{3,0},{4,7},{5,6},{6,5},{7,4},{8,11},{9,10},{10,... | collective-permute-start | bytes 3145736 | tf_op jit(solution)/shard_map/ppermute | solution.py:91
  112.3 71.3 %collective-permute-start.20 = (bf16[256,2048]{1,0:T(8,128)(2,1)}, bf16[256,2048]{1,0:T(8,128)(2,1)}, u32[]{:S(2)}, u32[]{:S(2)}) collective-permute-start(bf16[256,2048]{1,0:T(8,128)(2,1)} %dynamic-slice_convert_fusion.2), channel_id=1, source_target_pairs={{0,3},{4,7},{9,10},{13,14},{18,17},{22,21},{27,24},{31,28}} | collective-permute-start | bytes 3145736 | tf_op jit(solution)/shard_map/ppermute | solution.py:142
  126.9 81.7 %collective-permute-start.32 = (bf16[256,2048]{1,0:T(8,128)(2,1)}, bf16[256,2048]{1,0:T(8,128)(2,1)}, u32[]{:S(2)}, u32[]{:S(2)}) collective-permute-start(bf16[256,2048]{1,0:T(8,128)(2,1)} %get-tuple-element.116), channel_id=1, source_target_pairs={{0,3},{1,2},{2,1},{3,0},{4,7},{5,6},{6,5},{7,4},{8,11},{9,10},{10,... | collective-permute-start | bytes 3145736 | tf_op jit(solution)/shard_map/ppermute | solution.py:91
  134.1 90.4 %collective-permute-start.33 = (bf16[256,2048]{1,0:T(8,128)(2,1)}, bf16[256,2048]{1,0:T(8,128)(2,1)}, u32[]{:S(2)}, u32[]{:S(2)}) collective-permute-start(bf16[256,2048]{1,0:T(8,128)(2,1)} %get-tuple-element.116), channel_id=1, source_target_pairs={{0,1},{1,0},{2,3},{3,2},{4,5},{5,4},{6,7},{7,6},{8,9},{9,8},{10,11... | collective-permute-start | bytes 3145736 | tf_op jit(solution)/shard_map/ppermute | solution.py:91
  178.3 110.4 %collective-permute-start.9 = (bf16[512,2048]{1,0:T(8,128)(2,1)}, bf16[512,2048]{1,0:T(8,128)(2,1)S(1)}, u32[]{:S(2)}, u32[]{:S(2)}) collective-permute-start(bf16[512,2048]{1,0:T(8,128)(2,1)} %get-tuple-element.120), channel_id=1, source_target_pairs={{0,4},{4,0},{8,12},{12,8},{16,20},{20,16},{24,28},{28,24},{1,5},{5... | collective-permute-start | bytes 6291464 | tf_op jit(solution)/shard_map/ppermute | solution.py:54
  180.6 113.4 %collective-permute-start.19 = (bf16[2048,256]{1,0:T(8,128)(2,1)}, bf16[2048,256]{1,0:T(8,128)(2,1)}, u32[]{:S(2)}, u32[]{:S(2)}) collective-permute-start(bf16[2048,256]{1,0:T(8,128)(2,1)} %copy-done.72), channel_id=1, source_target_pairs={{0,4},{4,0},{8,12},{12,8},{16,20},{20,16},{24,28},{28,24},{1,5},{5... | collective-permute-start | bytes 3145736 | tf_op jit(solution)/shard_map/ppermute | solution.py:54
  183.6 63.4 %collective-permute-start.31 = (bf16[512,1024]{0,1:T(8,128)(2,1)}, bf16[512,1024]{0,1:T(8,128)(2,1)S(1)}, u32[]{:S(2)}, u32[]{:S(2)}) collective-permute-start(bf16[512,1024]{0,1:T(8,128)(2,1)} %collective-permute-done.29), channel_id=1, source_target_pairs={{0,1},{1,0},{2,3},{3,2},{4,5},{5,4},{6,7},{7,6},{8,9},{9,8},{10,11... | collective-permute-start | bytes 3145736 | tf_op jit(solution)/shard_map/ppermute | solution.py:91
  208.5 61.0 %collective-permute-start.34 = (bf16[256,2048]{1,0:T(8,128)(2,1)}, bf16[256,2048]{1,0:T(8,128)(2,1)}, u32[]{:S(2)}, u32[]{:S(2)}) collective-permute-start(bf16[256,2048]{1,0:T(8,128)(2,1)} %collective-permute-done.32), channel_id=1, source_target_pairs={{0,1},{1,0},{2,3},{3,2},{4,5},{5,4},{6,7},{7,6},{8,9},{9,8},{10,11... | collective-permute-start | bytes 3145736 | tf_op jit(solution)/shard_map/ppermute | solution.py:91
  224.5 62.8 %collective-permute-start.21 = (bf16[256,2048]{1,0:T(8,128)(2,1)}, bf16[256,2048]{1,0:T(8,128)(2,1)}, u32[]{:S(2)}, u32[]{:S(2)}) collective-permute-start(bf16[256,2048]{1,0:T(8,128)(2,1)} %broadcast_select_fusion), channel_id=1, source_target_pairs={{0,1},{3,2},{4,5},{7,6},{9,8},{10,11},{13,12},{14,15},{18,19},{17,... | collective-permute-start | bytes 3145736 | tf_op jit(solution)/shard_map/ppermute | solution.py:142
  308.4 47.6 %collective-permute-start.87 = (bf16[512,256]{1,0:T(8,128)(2,1)}, bf16[512,256]{1,0:T(8,128)(2,1)}, u32[]{:S(2)}, u32[]{:S(2)}) collective-permute-start(bf16[512,256]{1,0:T(8,128)(2,1)} %get-tuple-element.25), channel_id=1, source_target_pairs={{0,24},{4,28},{8,16},{12,20},{16,8},{20,12},{24,0},{28,4},{1,25},{... | collective-permute-start | bytes 786440 | tf_op jit(solution)/shard_map/ppermute | solution.py:54
  308.4 81.1 %collective-permute-start.86 = (bf16[512,256]{1,0:T(8,128)(2,1)}, bf16[512,256]{1,0:T(8,128)(2,1)}, u32[]{:S(2)}, u32[]{:S(2)}) collective-permute-start(bf16[512,256]{1,0:T(8,128)(2,1)} %get-tuple-element.25), channel_id=1, source_target_pairs={{0,20},{4,16},{8,28},{12,24},{16,4},{20,0},{24,12},{28,8},{1,21},{... | collective-permute-start | bytes 786440 | tf_op jit(solution)/shard_map/ppermute | solution.py:54
  308.4 61.7 %collective-permute-start.83 = (bf16[512,256]{1,0:T(8,128)(2,1)}, bf16[512,256]{1,0:T(8,128)(2,1)}, u32[]{:S(2)}, u32[]{:S(2)}) collective-permute-start(bf16[512,256]{1,0:T(8,128)(2,1)} %get-tuple-element.25), channel_id=1, source_target_pairs={{0,16},{4,20},{8,24},{12,28},{16,0},{20,4},{24,8},{28,12},{1,17},{... | collective-permute-start | bytes 786440 | tf_op jit(solution)/shard_map/ppermute | solution.py:54
  386.9 37.1 %collective-permute-start.24 = (bf16[128,2048]{1,0:T(8,128)(2,1)S(1)}, bf16[128,2048]{1,0:T(8,128)(2,1)S(1)}, u32[]{:S(2)}, u32[]{:S(2)}) collective-permute-start(bf16[128,2048]{1,0:T(8,128)(2,1)S(1)} %get-tuple-element.142), channel_id=1, source_target_pairs={{0,16},{4,20},{8,24},{12,28},{16,0},{20,4},{24,8},{28,12},{1,17},{... | collective-permute-start | bytes 1572872 | tf_op jit(solution)/shard_map/ppermute | solution.py:54
  389.4 93.2 %collective-permute-start.43 = (bf16[512,2048]{1,0:T(8,128)(2,1)}, bf16[512,2048]{1,0:T(8,128)(2,1)}, u32[]{:S(2)}, u32[]{:S(2)}) collective-permute-start(bf16[512,2048]{1,0:T(8,128)(2,1)} %pad_maximum_fusion.5), channel_id=1, source_target_pairs={{0,4},{4,0},{8,12},{12,8},{16,20},{20,16},{24,28},{28,24},{1,5},{5... | collective-permute-start | bytes 6291464 | tf_op jit(solution)/shard_map/ppermute | solution.py:54
  390.4 43.3 %collective-permute-start.90 = (bf16[512,256]{1,0:T(8,128)(2,1)S(1)}, bf16[512,256]{1,0:T(8,128)(2,1)}, u32[]{:S(2)}, u32[]{:S(2)}) collective-permute-start(bf16[512,256]{1,0:T(8,128)(2,1)S(1)} %copy-done.47), channel_id=1, source_target_pairs={{0,28},{4,24},{8,20},{12,16},{16,12},{20,8},{24,4},{28,0},{1,29},{... | collective-permute-start | bytes 786440 | tf_op jit(solution)/shard_map/ppermute | solution.py:54
  492.7 63.6 %collective-permute-start.44 = (bf16[512,2048]{1,0:T(8,128)(2,1)}, bf16[512,2048]{1,0:T(8,128)(2,1)}, u32[]{:S(2)}, u32[]{:S(2)}) collective-permute-start(bf16[512,2048]{1,0:T(8,128)(2,1)} %convolution_convert_fusion.1), channel_id=1, source_target_pairs={{0,4},{4,0},{8,12},{12,8},{16,20},{20,16},{24,28},{28,24},{1,5},{5... | collective-permute-start | bytes 6291464 | tf_op jit(solution)/shard_map/ppermute | solution.py:54
  493.2 72.2 %collective-permute-start.36 = (bf16[512,2048]{1,0:T(8,128)(2,1)}, bf16[512,2048]{1,0:T(8,128)(2,1)S(1)}, u32[]{:S(2)}, u32[]{:S(2)}) collective-permute-start(bf16[512,2048]{1,0:T(8,128)(2,1)} %convolution_convert_fusion.3), channel_id=1, source_target_pairs={{0,4},{4,0},{8,12},{12,8},{16,20},{20,16},{24,28},{28,24},{1,5},{5... | collective-permute-start | bytes 6291464 | tf_op jit(solution)/shard_map/ppermute | solution.py:54
  529.7 48.5 %collective-permute-start.105 = (bf16[256,2048]{1,0:T(8,128)(2,1)S(1)}, bf16[256,2048]{1,0:T(8,128)(2,1)S(1)}, u32[]{:S(2)}, u32[]{:S(2)}) collective-permute-start(bf16[256,2048]{1,0:T(8,128)(2,1)S(1)} %get-tuple-element.123), channel_id=1, source_target_pairs={{0,1},{1,0},{2,3},{3,2},{4,5},{5,4},{6,7},{7,6},{8,9},{9,8},{10,11... | collective-permute-start | bytes 3145736 | tf_op jit(solution)/shard_map/ppermute | solution.py:91
  533.9 67.7 %collective-permute-start.107 = (bf16[256,2048]{1,0:T(8,128)(2,1)S(1)}, bf16[256,2048]{1,0:T(8,128)(2,1)S(1)}, u32[]{:S(2)}, u32[]{:S(2)}) collective-permute-start(bf16[256,2048]{1,0:T(8,128)(2,1)S(1)} %fusion.28), channel_id=1, source_target_pairs={{0,3},{1,2},{2,1},{3,0},{4,7},{5,6},{6,5},{7,4},{8,11},{9,10},{10,... | collective-permute-start | bytes 3145736 | tf_op jit(solution)/shard_map/ppermute | solution.py:91
  562.5 42.2 %collective-permute-start.45 = (bf16[128,2048]{1,0:T(8,128)(2,1)S(1)}, bf16[128,2048]{1,0:T(8,128)(2,1)S(1)}, u32[]{:S(2)}, u32[]{:S(2)}) collective-permute-start(bf16[128,2048]{1,0:T(8,128)(2,1)S(1)} %get-tuple-element.134), channel_id=1, source_target_pairs={{0,8},{4,12},{8,0},{12,4},{16,24},{20,28},{24,16},{28,20},{1,9},{5... | collective-permute-start | bytes 1572872 | tf_op jit(solution)/shard_map/ppermute | solution.py:54
  563.9 42.2 %collective-permute-start.47 = (bf16[128,2048]{1,0:T(8,128)(2,1)S(1)}, bf16[128,2048]{1,0:T(8,128)(2,1)S(1)}, u32[]{:S(2)}, u32[]{:S(2)}) collective-permute-start(bf16[128,2048]{1,0:T(8,128)(2,1)S(1)} %get-tuple-element.135), channel_id=1, source_target_pairs={{0,24},{4,28},{8,16},{12,20},{16,8},{20,12},{24,0},{28,4},{1,25},{... | collective-permute-start | bytes 1572872 | tf_op jit(solution)/shard_map/ppermute | solution.py:54
  565.4 42.2 %collective-permute-start.46 = (bf16[128,2048]{1,0:T(8,128)(2,1)S(1)}, bf16[128,2048]{1,0:T(8,128)(2,1)S(1)}, u32[]{:S(2)}, u32[]{:S(2)}) collective-permute-start(bf16[128,2048]{1,0:T(8,128)(2,1)S(1)} %get-tuple-element.136), channel_id=1, source_target_pairs={{0,16},{4,20},{8,24},{12,28},{16,0},{20,4},{24,8},{28,12},{1,17},{... | collective-permute-start | bytes 1572872 | tf_op jit(solution)/shard_map/ppermute | solution.py:54
  578.2 88.3 %collective-permute-start.98 = (bf16[512,1024]{1,0:T(8,128)(2,1)S(1)}, bf16[512,1024]{1,0:T(8,128)(2,1)S(1)}, u32[]{:S(2)}, u32[]{:S(2)}) collective-permute-start(bf16[512,1024]{1,0:T(8,128)(2,1)S(1)} %get-tuple-element.125), channel_id=1, source_target_pairs={{0,1},{1,0},{2,3},{3,2},{4,5},{5,4},{6,7},{7,6},{8,9},{9,8},{10,11... | collective-permute-start | bytes 3145736 | tf_op jit(solution)/shard_map/ppermute | solution.py:91
  601.6 65.6 %collective-permute-start.100 = (bf16[512,1024]{1,0:T(8,128)(2,1)S(1)}, bf16[512,1024]{1,0:T(8,128)(2,1)S(1)}, u32[]{:S(2)}, u32[]{:S(2)}) collective-permute-start(bf16[512,1024]{1,0:T(8,128)(2,1)S(1)} %fusion.31), channel_id=1, source_target_pairs={{0,3},{1,2},{2,1},{3,0},{4,7},{5,6},{6,5},{7,4},{8,11},{9,10},{10,... | collective-permute-start | bytes 3145736 | tf_op jit(solution)/shard_map/ppermute | solution.py:91
  607.6 52.9 %collective-permute-start.38 = (bf16[128,2048]{1,0:T(8,128)(2,1)S(1)}, bf16[128,2048]{1,0:T(8,128)(2,1)S(1)}, u32[]{:S(2)}, u32[]{:S(2)}) collective-permute-start(bf16[128,2048]{1,0:T(8,128)(2,1)S(1)} %get-tuple-element.139), channel_id=1, source_target_pairs={{0,16},{4,20},{8,24},{12,28},{16,0},{20,4},{24,8},{28,12},{1,17},{... | collective-permute-start | bytes 1572872 | tf_op jit(solution)/shard_map/ppermute | solution.py:54
  619.9 50.1 %collective-permute-start.110 = (bf16[256,2048]{1,0:T(8,128)(2,1)}, bf16[256,2048]{1,0:T(8,128)(2,1)S(1)}, u32[]{:S(2)}, u32[]{:S(2)}) collective-permute-start(bf16[256,2048]{1,0:T(8,128)(2,1)} %fusion.30), channel_id=1, source_target_pairs={{0,24},{4,28},{8,16},{12,20},{16,8},{20,12},{24,0},{28,4},{1,25},{... | collective-permute-start | bytes 3145736 | tf_op jit(solution)/shard_map/ppermute | solution.py:54
  631.8 91.8 %collective-permute-start.109 = (bf16[256,2048]{1,0:T(8,128)(2,1)}, bf16[256,2048]{1,0:T(8,128)(2,1)}, u32[]{:S(2)}, u32[]{:S(2)}) collective-permute-start(bf16[256,2048]{1,0:T(8,128)(2,1)} %fusion.30), channel_id=1, source_target_pairs={{0,16},{4,20},{8,24},{12,28},{16,0},{20,4},{24,8},{28,12},{1,17},{... | collective-permute-start | bytes 3145736 | tf_op jit(solution)/shard_map/ppermute | solution.py:54
  666.5 51.3 %collective-permute-start.49 = (bf16[128,2048]{1,0:T(8,128)(2,1)S(1)}, bf16[128,2048]{1,0:T(8,128)(2,1)S(1)}, u32[]{:S(2)}, u32[]{:S(2)}) collective-permute-start(bf16[128,2048]{1,0:T(8,128)(2,1)S(1)} %get-tuple-element.108), channel_id=1, source_target_pairs={{0,16},{4,20},{8,24},{12,28},{16,0},{20,4},{24,8},{28,12},{1,17},{... | collective-permute-start | bytes 1572872 | tf_op jit(solution)/shard_map/ppermute | solution.py:54
  667.2 51.3 %collective-permute-start.48 = (bf16[128,2048]{1,0:T(8,128)(2,1)S(1)}, bf16[128,2048]{1,0:T(8,128)(2,1)S(1)}, u32[]{:S(2)}, u32[]{:S(2)}) collective-permute-start(bf16[128,2048]{1,0:T(8,128)(2,1)S(1)} %get-tuple-element.108), channel_id=1, source_target_pairs={{0,8},{4,12},{8,0},{12,4},{16,24},{20,28},{24,16},{28,20},{1,9},{5... | collective-permute-start | bytes 1572872 | tf_op jit(solution)/shard_map/ppermute | solution.py:54
  670.1 54.5 %collective-permute-start.108 = (bf16[256,2048]{1,0:T(8,128)(2,1)}, bf16[256,2048]{1,0:T(8,128)(2,1)}, u32[]{:S(2)}, u32[]{:S(2)}) collective-permute-start(bf16[256,2048]{1,0:T(8,128)(2,1)} %fusion.30), channel_id=1, source_target_pairs={{0,8},{4,12},{8,0},{12,4},{16,24},{20,28},{24,16},{28,20},{1,9},{5... | collective-permute-start | bytes 3145736 | tf_op jit(solution)/shard_map/ppermute | solution.py:54
  681.0 47.7 %collective-permute-start.103 = (bf16[512,1024]{1,0:T(8,128)(2,1)}, bf16[512,1024]{1,0:T(8,128)(2,1)}, u32[]{:S(2)}, u32[]{:S(2)}) collective-permute-start(bf16[512,1024]{1,0:T(8,128)(2,1)} %fusion.33), channel_id=1, source_target_pairs={{0,24},{4,28},{8,16},{12,20},{16,8},{20,12},{24,0},{28,4},{1,25},{... | collective-permute-start | bytes 3145736 | tf_op jit(solution)/shard_map/ppermute | solution.py:54
  728.6 153.6 %collective-permute-start.111 = (bf16[1024,2048]{1,0:T(8,128)(2,1)}, bf16[1024,2048]{1,0:T(8,128)(2,1)}, u32[]{:S(2)}, u32[]{:S(2)}) collective-permute-start(bf16[1024,2048]{1,0:T(8,128)(2,1)} %pad_maximum_fusion.2), channel_id=1, source_target_pairs={{0,4},{4,0},{8,12},{12,8},{16,20},{20,16},{24,28},{28,24},{1,5},{5... | collective-permute-start | bytes 12582920 | tf_op jit(solution)/shard_map/ppermute | solution.py:54
  747.2 136.6 %collective-permute-start.104 = (bf16[2048,1024]{1,0:T(8,128)(2,1)}, bf16[2048,1024]{1,0:T(8,128)(2,1)}, u32[]{:S(2)}, u32[]{:S(2)}) collective-permute-start(bf16[2048,1024]{1,0:T(8,128)(2,1)} %pad_maximum_fusion.1), channel_id=1, source_target_pairs={{0,4},{4,0},{8,12},{12,8},{16,20},{20,16},{24,28},{28,24},{1,5},{5... | collective-permute-start | bytes 12582920 | tf_op jit(solution)/shard_map/ppermute | solution.py:54
  833.2 40.3 %collective-permute-start.52 = (bf16[512,2048]{1,0:T(8,128)(2,1)}, bf16[512,2048]{1,0:T(8,128)(2,1)}, u32[]{:S(2)}, u32[]{:S(2)}) collective-permute-start(bf16[512,2048]{1,0:T(8,128)(2,1)} %convolution_convert_fusion), channel_id=1, source_target_pairs={{0,4},{4,0},{8,12},{12,8},{16,20},{20,16},{24,28},{28,24},{1,5},{5... | collective-permute-start | bytes 6291464 | tf_op jit(solution)/shard_map/ppermute | solution.py:54
  873.5 42.0 %collective-permute-start.74 = (bf16[512,256]{1,0:T(8,128)(2,1)}, bf16[512,256]{1,0:T(8,128)(2,1)}, u32[]{:S(2)}, u32[]{:S(2)}) collective-permute-start(bf16[512,256]{1,0:T(8,128)(2,1)} %get-tuple-element.147), channel_id=1, source_target_pairs={{0,1},{1,0},{2,3},{3,2},{4,5},{5,4},{6,7},{7,6},{8,9},{9,8},{10,11... | collective-permute-start | bytes 786440 | tf_op jit(solution)/shard_map/ppermute | solution.py:91
  879.4 36.1 %collective-permute-start.76 = (bf16[512,256]{1,0:T(8,128)(2,1)}, bf16[512,256]{1,0:T(8,128)(2,1)}, u32[]{:S(2)}, u32[]{:S(2)}) collective-permute-start(bf16[512,256]{1,0:T(8,128)(2,1)} %fusion.70), channel_id=1, source_target_pairs={{0,3},{1,2},{2,1},{3,0},{4,7},{5,6},{6,5},{7,4},{8,11},{9,10},{10,... | collective-permute-start | bytes 786440 | tf_op jit(solution)/shard_map/ppermute | solution.py:91
  880.6 36.0 %collective-permute-start.53 = (bf16[128,2048]{1,0:T(8,128)(2,1)}, bf16[128,2048]{1,0:T(8,128)(2,1)}, u32[]{:S(2)}, u32[]{:S(2)}) collective-permute-start(bf16[128,2048]{1,0:T(8,128)(2,1)} %get-tuple-element.129), channel_id=1, source_target_pairs={{0,8},{4,12},{8,0},{12,4},{16,24},{20,28},{24,16},{28,20},{1,9},{5... | collective-permute-start | bytes 1572872 | tf_op jit(solution)/shard_map/ppermute | solution.py:54
  882.2 34.5 %collective-permute-start.55 = (bf16[128,2048]{1,0:T(8,128)(2,1)}, bf16[128,2048]{1,0:T(8,128)(2,1)}, u32[]{:S(2)}, u32[]{:S(2)}) collective-permute-start(bf16[128,2048]{1,0:T(8,128)(2,1)} %get-tuple-element.130), channel_id=1, source_target_pairs={{0,24},{4,28},{8,16},{12,20},{16,8},{20,12},{24,0},{28,4},{1,25},{... | collective-permute-start | bytes 1572872 | tf_op jit(solution)/shard_map/ppermute | solution.py:54
  883.8 32.9 %collective-permute-start.54 = (bf16[128,2048]{1,0:T(8,128)(2,1)}, bf16[128,2048]{1,0:T(8,128)(2,1)}, u32[]{:S(2)}, u32[]{:S(2)}) collective-permute-start(bf16[128,2048]{1,0:T(8,128)(2,1)} %get-tuple-element.131), channel_id=1, source_target_pairs={{0,16},{4,20},{8,24},{12,28},{16,0},{20,4},{24,8},{28,12},{1,17},{... | collective-permute-start | bytes 1572872 | tf_op jit(solution)/shard_map/ppermute | solution.py:54
  (150 other events, 1875.4 us)

commit v2 on v1

v2 whole, which is shorter than its diff:
```python
import functools
import math

import jax
import jax.numpy as jnp
from jax import lax
from jax.experimental import pallas as pl
from jax.experimental.pallas import tpu as pltpu
from jax.sharding import PartitionSpec as P

HEADS = 16
HD = 128
NORM_EPS = 1e-05
MASKED = -1e30
KEY_TILE = 512
LANE_ROWS = 256
SCALE = 1.0 / math.sqrt(HD)
F32 = jnp.float32
BF16 = jnp.bfloat16


def layer_norm(values, gain_vec, shift_vec):
    centred = values - jnp.mean(values, axis=-1, keepdims=True)
    inverse = lax.rsqrt(jnp.mean(centred * centred, axis=-1, keepdims=True) + NORM_EPS)
    normed = centred * inverse
    return (normed * gain_vec + shift_vec, normed, inverse)


def norm_backward(grad_norm, normed, inverse, gain_vec):
    scaled = grad_norm * gain_vec
    centred = scaled - jnp.mean(scaled, axis=-1, keepdims=True)
    centred = centred - normed * jnp.mean(scaled * normed, axis=-1, keepdims=True)
    return (centred * inverse, jnp.sum(grad_norm * normed, axis=0), jnp.sum(grad_norm, axis=0))


def gelu_tanh(values):
    return jax.nn.gelu(values, approximate=True)


def mm(left, right):
    return jnp.dot(left, right, preferred_element_type=F32)


def mm_t(left, right):
    return lax.dot_general(left, right, (((1,), (1,)), ((), ())), preferred_element_type=F32)


def mm_rows(left, right):
    return lax.dot_general(left, right, (((0,), (0,)), ((), ())), preferred_element_type=F32)


def after(values, *ready):
    return lax.optimization_barrier((values, *ready))[0] if ready else values


def ctx_swap(values, mask):
    count = lax.axis_size("ctx")
    return lax.ppermute(values, "ctx", [(at, at ^ mask) for at in range(count)])


def ctx_gather(values, ready=()):
    chips = lax.axis_size("ctx") // 2
    mine = jnp.concatenate([values] + [ctx_swap(values, 2 * at) for at in range(1, chips)], axis=0)
    mine = after(mine, *ready)
    return mine, ctx_swap(mine, 1)


def ctx_gather_all(values):
    return jnp.concatenate(ctx_gather(values), axis=0)


def ctx_scatter(even, odd, ready=(), finish=()):
    chips = lax.axis_size("ctx") // 2
    rows = even.shape[0] // chips
    both = even.astype(F32) + ctx_swap(odd.astype(BF16), 1).astype(F32)
    total = both[:rows]
    low = after(both.astype(BF16), *ready)
    for at in range(1, chips):
        got = ctx_swap(low[at * rows : (at + 1) * rows], 2 * at)
        total = total + after(got, *finish).astype(F32)
    return total


def ctx_gather_small(values):
    chips = lax.axis_size("ctx") // 2
    held, mask = values, 2
    while mask < 2 * chips:
        held = jnp.concatenate([held, ctx_swap(held, mask)], axis=0)
        mask *= 2
    return held, ctx_swap(held, 1)


def chip_masks(side):
    masks, mask = [], lax.axis_size("ctx") // 2
    while mask > 1:
        masks.append(mask)
        mask //= 2
    return masks[1:] + masks[:1] if side else masks


def ctx_gather_halves(first, second, wait=lambda values: values, last=lambda values: values):
    held, offsets = [first[None], second[None]], [[0], [0]]
    steps = len(chip_masks(0))
    for step in range(steps):
        sent = []
        for side in range(2):
            mask = chip_masks(side)[step]
            sent.append((ctx_swap(held[side], mask), [at ^ mask for at in offsets[side]]))
        if step < steps - 1:
            for side in range(2):
                held[side] = jnp.concatenate([held[side], wait(sent[side][0])], axis=0)
                offsets[side] = offsets[side] + sent[side][1]
    gathered = []
    for side in range(2):
        parts = [(held[side], offsets[side]), (last(sent[side][0]), sent[side][1])]
        gathered.append(
            parts + [(ctx_swap(block, 1), [at ^ 1 for at in order]) for block, order in parts]
        )
    return gathered


def in_order(parts, parity):
    blocks = {
        offset: values[at]
        for values, order in parts
        for at, offset in enumerate(order)
        if offset % 2 == parity
    }
    return jnp.concatenate([blocks[offset] for offset in sorted(blocks)], axis=0)


def ctx_exchange(values):
    return lax.all_to_all(values, "ctx", 0, 0, tiled=True)


def z_masks(count):
    masks = []
    while count > 1:
        masks.append(count - 1)
        count //= 2
    return masks


def z_offsets(count):
    offsets = [0]
    for mask in z_masks(count):
        offsets = offsets + [at ^ mask for at in offsets]
    return offsets


def z_swap(values, mask):
    count = lax.axis_size("fsdp")
    return lax.ppermute(values, "fsdp", [(at, at ^ mask) for at in range(count)])


def z_gather_steps(values):
    held = values[None]
    own = z_swap(held, 1)
    for mask in z_masks(lax.axis_size("fsdp"))[:-1]:
        held = jnp.concatenate([held, z_swap(held, mask)], axis=0)
    return held, own


def z_gather_finish(held, own):
    if held.shape[0] == 1:
        return [held, own]
    return [held, own, z_swap(held[1:], 1)]


def z_gather_parts(values):
    return z_gather_finish(*z_gather_steps(values))


def z_gather_held(values):
    held = values[None]
    for mask in z_masks(lax.axis_size("fsdp"))[:-1]:
        held = jnp.concatenate([held, z_swap(held, mask)], axis=0)
    return held


def z_scatter_stacked(stacked):
    for mask in reversed(z_masks(lax.axis_size("fsdp"))):
        half = stacked.shape[0] // 2
        sent = z_swap(stacked[half:].astype(BF16), mask)
        stacked = stacked[:half].astype(F32) + sent.astype(F32)
    return stacked[0]


def z_gather_queued(values):
    return lax.all_gather(values, "fsdp", axis=0, tiled=True)


def z_scatter_queued(values):
    return lax.psum_scatter(values, "fsdp", scatter_dimension=0, tiled=True)


def place_kernel(plan, n_in, meta, *refs):
    ins, outs = refs[:n_in], refs[n_in:]
    for source, rows_in, target, rows_out in plan(meta):
        outs[target][rows_out] = ins[source][rows_in]


def place_blocks(meta, sources, outs, plan, name):
    return pl.pallas_call(
        functools.partial(place_kernel, plan, len(sources)),
        grid_spec=pltpu.PrefetchScalarGridSpec(
            num_scalar_prefetch=1,
            grid=(1,),
            in_specs=[pl.BlockSpec(memory_space=pltpu.VMEM)] * len(sources),
            out_specs=[pl.BlockSpec(memory_space=pltpu.VMEM)] * len(outs),
        ),
        out_shape=[jax.ShapeDtypeStruct(out, sources[0].dtype) for out in outs],
        compiler_params=pltpu.CompilerParams(vmem_limit_bytes=56 * 2**20),
        name=name,
    )(meta, *sources)


class Shape:
    def __init__(self, ctx_count, fsdp_count, slots, rows):
        self.ctx_count, self.fsdp_count, self.slots, self.rows = ctx_count, fsdp_count, slots, rows
        self.heads = HEADS // ctx_count
        self.block = rows * fsdp_count
        self.blocks = 2 * ctx_count
        self.keys = self.block * self.blocks
        self.tokens = slots * 2 * rows
        self.q_blocks = LANE_ROWS // (self.heads * rows)
        self.head_rows = self.q_blocks * rows
        self.q_tiles = self.blocks // self.q_blocks
        self.q_rows = self.q_tiles * LANE_ROWS
        self.chips = ctx_count // 2
        self.offsets = z_offsets(fsdp_count)


    def part_starts(self, count):
        half = self.fsdp_count // 2
        return [0, half, half + 1][:count]

    def part_of(self, at, count):
        starts = self.part_starts(count)
        part = max(index for index, start in enumerate(starts) if at >= start)
        return part, at - starts[part]


def for_blocks(shape, meta, act):
    me = meta[0]

    def step(chip, carry):
        for parity in range(2):
            first = meta[6 + (me ^ (2 * chip + parity))]
            for slot in range(shape.slots):
                for half in range(2):
                    block = first if half == 0 else shape.blocks - 1 - first
                    act(parity, chip, slot, half, block)
        return carry

    lax.fori_loop(0, shape.chips, step, 0)


def at_rows(start, size, unit):
    return pl.ds(pl.multiple_of(start, unit), size)


def q_source(shape, chip, slot, half):
    return at_rows(chip * shape.tokens + (slot * 2 + half) * shape.rows, shape.rows, shape.rows)


def q_target(shape, block, head):
    start = (block // shape.q_blocks) * LANE_ROWS + (block % shape.q_blocks) * shape.rows
    return at_rows(start + head * shape.head_rows, shape.rows, shape.rows)


def kv_source(shape, chip, order, slot, half):
    start = (chip * shape.fsdp_count + order) * shape.tokens + (slot * 2 + half) * shape.rows
    return at_rows(start, shape.rows, shape.rows)


def kv_target(shape, meta, block, order):
    start = block * shape.block + (meta[1] ^ shape.offsets[order]) * shape.rows
    return at_rows(start, shape.rows, shape.rows)


def query_bounds(shape, meta, slot, tile):
    lane = lax.broadcasted_iota(jnp.int32, (1, LANE_ROWS), 1)
    row = lane % shape.head_rows
    pos = (tile * shape.q_blocks + row // shape.rows) * shape.block + meta[1] * shape.rows + row % shape.rows
    first_end = meta[2 + 2 * slot]
    second_end = first_end + meta[3 + 2 * slot]

    def start_of(at):
        return jnp.where(at < first_end, 0, jnp.where(at < second_end, first_end, second_end))

    first_pos = tile * shape.q_blocks * shape.block + meta[1] * shape.rows
    last_pos = first_pos + (shape.q_blocks - 1) * shape.block + shape.rows - 1
    return pos, start_of(pos), start_of(first_pos) // KEY_TILE, last_pos // KEY_TILE + 1


def visible(pos, start, tile):
    key_pos = tile * KEY_TILE + lax.broadcasted_iota(jnp.int32, (KEY_TILE, LANE_ROWS), 0)
    return (key_pos <= pos) & (key_pos >= start)


def device_rows(shape, meta, parity, chip, slot, half):
    device = meta[0] ^ (2 * chip + parity)
    return at_rows(device * shape.tokens + (slot * 2 + half) * shape.rows, shape.rows, shape.rows)


def attend_kernel(shape, meta, q_even, q_odd, kv_even, kv_odd, o_out, q_all, kv_all, o_t, lse, o_rows):
    queries, keys = (q_even, q_odd), (kv_even, kv_odd)

    def place(parity, chip, slot, half, block):
        for head in range(shape.heads):
            q_all[slot, q_target(shape, block, head), :] = queries[parity][
                q_source(shape, chip, slot, half), head * HD : (head + 1) * HD
            ]
        for order in range(shape.fsdp_count):
            kv_all[slot, kv_target(shape, meta, block, order), :] = keys[parity][
                kv_source(shape, chip, order, slot, half), :
            ]

    for_blocks(shape, meta, place)

    def tile_step(item, carry):
        slot, tile = item // shape.q_tiles, item % shape.q_tiles
        pos, start, low, high = query_bounds(shape, meta, slot, tile)
        q_tile = q_all[slot, at_rows(tile * LANE_ROWS, LANE_ROWS, LANE_ROWS), :]

        def key_step(at, state):
            peak, total, acc = state
            part = at_rows(at * KEY_TILE, KEY_TILE, KEY_TILE)
            scores = mm_t(kv_all[slot, part, :HD], q_tile) * SCALE
            scores = jnp.where(visible(pos, start, at), scores, MASKED)
            new_peak = jnp.maximum(peak, jnp.max(scores, axis=0, keepdims=True))
            fade = jnp.exp(peak - new_peak)
            weights = jnp.exp(scores - new_peak)
            total = total * fade + jnp.sum(weights, axis=0, keepdims=True)
            acc = acc * fade + mm_rows(kv_all[slot, part, HD:], weights.astype(BF16))
            return new_peak, total, acc

        begin = (
            jnp.full((1, LANE_ROWS), MASKED, F32),
            jnp.zeros((1, LANE_ROWS), F32),
            jnp.zeros((HD, LANE_ROWS), F32),
        )
        peak, total, acc = lax.fori_loop(low, high, key_step, begin)
        acc = acc / total
        o_t[item] = acc
        lse[item] = peak + jnp.log(total)
        o_rows[slot, at_rows(tile * LANE_ROWS, LANE_ROWS, LANE_ROWS), :] = acc.T.astype(BF16)
        return carry

    lax.fori_loop(0, shape.slots * shape.q_tiles, tile_step, 0)

    def put_back(parity, chip, slot, half, block):
        for head in range(shape.heads):
            o_out[device_rows(shape, meta, parity, chip, slot, half), head * HD : (head + 1) * HD] = o_rows[
                slot, q_target(shape, block, head), :
            ]

    for_blocks(shape, meta, put_back)


def attend_grad_kernel(
    shape, meta, q_all, kv_all, o_t, lse, grads, gq_even, gq_odd, gkv_even, gkv_odd, ga_even, ga_odd, go_all, gq_all, gkv_all
):
    g_queries, g_keys, g_branch = (gq_even, gq_odd), (gkv_even, gkv_odd), (ga_even, ga_odd)

    def place(parity, chip, slot, half, block):
        source = device_rows(shape, meta, parity, chip, slot, half)
        for head in range(shape.heads):
            go_all[slot, q_target(shape, block, head), :] = grads[source, head * HD : (head + 1) * HD]
        g_branch[parity][q_source(shape, chip, slot, half), :] = grads[source, shape.heads * HD :]

    for_blocks(shape, meta, place)
    gkv_all[...] = jnp.zeros_like(gkv_all)

    def tile_step(item, carry):
        slot, tile = item // shape.q_tiles, item % shape.q_tiles
        pos, start, low, high = query_bounds(shape, meta, slot, tile)
        rows = at_rows(tile * LANE_ROWS, LANE_ROWS, LANE_ROWS)
        q_tile = q_all[slot, rows, :]
        go_tile = go_all[slot, rows, :]
        delta = jnp.sum(go_tile.astype(F32).T * o_t[item], axis=0, keepdims=True)
        lse_row = lse[item]

        def key_step(at, acc):
            part = at_rows(at * KEY_TILE, KEY_TILE, KEY_TILE)
            key_part, value_part = kv_all[slot, part, :HD], kv_all[slot, part, HD:]
            scores = mm_t(key_part, q_tile) * SCALE
            probs = jnp.where(visible(pos, start, at), jnp.exp(scores - lse_row), 0.0)
            g_scores = (probs * (mm_t(value_part, go_tile) - delta)).astype(BF16)
            gkv_all[slot, part, :HD] += mm(g_scores, q_tile)
            gkv_all[slot, part, HD:] += mm(probs.astype(BF16), go_tile)
            return acc + mm_rows(key_part, g_scores)

        acc = lax.fori_loop(low, high, key_step, jnp.zeros((HD, LANE_ROWS), F32))
        gq_all[slot, rows, :] = (acc * SCALE).T.astype(BF16)
        return carry

    lax.fori_loop(0, shape.slots * shape.q_tiles, tile_step, 0)

    def put_back(parity, chip, slot, half, block):
        for head in range(shape.heads):
            g_queries[parity][q_source(shape, chip, slot, half), head * HD : (head + 1) * HD] = gq_all[
                slot, q_target(shape, block, head), :
            ]
        for order in range(shape.fsdp_count):
            target = kv_target(shape, meta, block, order)
            source = kv_source(shape, chip, order, slot, half)
            g_keys[parity][source, :HD] = (gkv_all[slot, target, :HD] * SCALE).astype(BF16)
            g_keys[parity][source, HD:] = gkv_all[slot, target, HD:].astype(BF16)

    for_blocks(shape, meta, put_back)


def attend(shape, meta, q_even, q_odd, kv_even, kv_odd):
    items = shape.slots * shape.q_tiles
    pairs = items * LANE_ROWS * shape.keys // 2
    return pl.pallas_call(
        functools.partial(attend_kernel, shape),
        grid_spec=pltpu.PrefetchScalarGridSpec(
            num_scalar_prefetch=1,
            grid=(1,),
            in_specs=[pl.BlockSpec(memory_space=pltpu.VMEM)] * 4,
            out_specs=[pl.BlockSpec(memory_space=pltpu.VMEM)] * 5,
            scratch_shapes=[pltpu.VMEM((shape.slots, shape.q_rows, HD), BF16)],
        ),
        out_shape=[
            jax.ShapeDtypeStruct((shape.ctx_count * shape.tokens, shape.heads * HD), BF16),
            jax.ShapeDtypeStruct((shape.slots, shape.q_rows, HD), BF16),
            jax.ShapeDtypeStruct((shape.slots, shape.keys, 2 * HD), BF16),
            jax.ShapeDtypeStruct((items, HD, LANE_ROWS), F32),
            jax.ShapeDtypeStruct((items, 1, LANE_ROWS), F32),
        ],
        compiler_params=pltpu.CompilerParams(vmem_limit_bytes=56 * 2**20),
        cost_estimate=pl.CostEstimate(flops=pairs * HD * 4, transcendentals=pairs, bytes_accessed=8 * 2**20),
        name="attend",
    )(meta, q_even, q_odd, kv_even, kv_odd)


def attend_grad(shape, meta, q_all, kv_all, o_t, lse, grads):
    items = shape.slots * shape.q_tiles
    q_like = jax.ShapeDtypeStruct((shape.chips * shape.tokens, shape.heads * HD), BF16)
    kv_like = jax.ShapeDtypeStruct((shape.chips * shape.fsdp_count * shape.tokens, 2 * HD), BF16)
    pairs = items * LANE_ROWS * shape.keys // 2
    return pl.pallas_call(
        functools.partial(attend_grad_kernel, shape),
        grid_spec=pltpu.PrefetchScalarGridSpec(
            num_scalar_prefetch=1,
            grid=(1,),
            in_specs=[pl.BlockSpec(memory_space=pltpu.VMEM)] * 5,
            out_specs=[pl.BlockSpec(memory_space=pltpu.VMEM)] * 6,
            scratch_shapes=[
                pltpu.VMEM((shape.slots, shape.q_rows, HD), BF16),
                pltpu.VMEM((shape.slots, shape.q_rows, HD), BF16),
                pltpu.VMEM((shape.slots, shape.keys, 2 * HD), F32),
            ],
        ),
        out_shape=[q_like, q_like, kv_like, kv_like, q_like, q_like],
        compiler_params=pltpu.CompilerParams(vmem_limit_bytes=56 * 2**20),
        cost_estimate=pl.CostEstimate(flops=pairs * HD * 10, transcendentals=pairs, bytes_accessed=10 * 2**20),
        name="attend_grad",
    )(meta, q_all, kv_all, o_t, lse, grads)


def block_of(shape, parts, at):
    part, block = shape.part_of(at, len(parts))
    return parts[part][block]


def gelu_parts(values):
    root = math.sqrt(2.0 / math.pi)
    return jnp.tanh(root * (values + 0.044715 * (values * values * values)))


def hidden_kernel(shape, meta, rows_ref, bias_ref, *refs):
    parts, (hidden_ref, act_ref) = refs[:-2], refs[-2:]
    depth = parts[0].shape[1]
    total = bias_ref[...]
    for at, offset in enumerate(shape.offsets):
        part = pl.ds(pl.multiple_of((meta[1] ^ offset) * depth, depth), depth)
        total = total + mm(rows_ref[:, part], block_of(shape, parts, at))
    hidden_ref[...] = total
    act_ref[...] = (0.5 * total * (1.0 + gelu_parts(total))).astype(BF16)


def feed_hidden(shape, meta, rows, parts, bias):
    count, width = rows.shape
    _, depth, columns = parts[0].shape
    tile = 256
    weights = [
        pl.BlockSpec((part.shape[0], depth, tile), lambda i, m: (0, 0, i)) for part in parts
    ]
    out = pl.BlockSpec((count, tile), lambda i, m: (0, i))
    return pl.pallas_call(
        functools.partial(hidden_kernel, shape),
        grid_spec=pltpu.PrefetchScalarGridSpec(
            num_scalar_prefetch=1,
            grid=(columns // tile,),
            in_specs=[
                pl.BlockSpec((count, width), lambda i, m: (0, 0)),
                pl.BlockSpec((1, tile), lambda i, m: (0, i)),
                *weights,
            ],
            out_specs=[out, out],
        ),
        out_shape=[
            jax.ShapeDtypeStruct((count, columns), F32),
            jax.ShapeDtypeStruct((count, columns), BF16),
        ],
        compiler_params=pltpu.CompilerParams(vmem_limit_bytes=56 * 2**20),
        cost_estimate=pl.CostEstimate(
            flops=2 * count * width * columns,
            transcendentals=count * columns,
            bytes_accessed=2 * (count * width + width * columns) + 6 * count * columns,
        ),
        name="feed_hidden",
    )(meta, rows, bias, *parts)


def hidden_grad_kernel(shape, meta, grads_ref, hidden_ref, *refs):
    parts, (out_ref, sum_ref) = refs[:-2], refs[-2:]
    at = pl.program_id(0)
    weights = parts[0][0]
    for part, start in zip(parts[1:], shape.part_starts(len(parts))[1:]):
        weights = jnp.where(at < start, weights, part[0])
    values = hidden_ref[...]
    tanh = gelu_parts(values)
    root = math.sqrt(2.0 / math.pi)
    slope = 0.5 * (1.0 + tanh) + (0.5 * root) * values * (1.0 - tanh * tanh) * (
        1.0 + (3.0 * 0.044715) * (values * values)
    )
    low = (mm_t(grads_ref[...], weights) * slope).astype(BF16)
    out_ref[...] = low
    sum_ref[...] = jnp.sum(low.astype(F32), axis=0, keepdims=True)


def relative(shape, meta, at):
    place = shape.offsets[0]
    for index, offset in enumerate(shape.offsets):
        place = jnp.where(at == index, offset, place)
    return meta[1] ^ place


def feed_hidden_grad(shape, meta, grads, hidden, parts):
    count, width = grads.shape
    half, unit, _ = parts[0].shape
    if unit % 128:
        weights = jnp.zeros((2 * half, unit, width), BF16)
        for at, offset in enumerate(shape.offsets):
            weights = lax.dynamic_update_index_in_dim(
                weights, block_of(shape, parts, at), meta[1] ^ offset, 0
            )
        pull = jax.vjp(gelu_tanh, hidden)[1]
        out = pull(mm_t(grads, weights.reshape(-1, width)))[0].astype(BF16)
        return out, jnp.sum(out, axis=0, dtype=F32, keepdims=True)
    columns = 2 * half * unit
    place = lambda i, m: (0, relative(shape, m, i))
    return pl.pallas_call(
        functools.partial(hidden_grad_kernel, shape),
        grid_spec=pltpu.PrefetchScalarGridSpec(
            num_scalar_prefetch=1,
            grid=(2 * half,),
            in_specs=[
                pl.BlockSpec((count, width), lambda i, m: (0, 0)),
                pl.BlockSpec((count, unit), place),
                *[
                    pl.BlockSpec(
                        (1, unit, width),
                        lambda i, m, start=start, last=part.shape[0] - 1: (
                            jnp.clip(i - start, 0, last),
                            0,
                            0,
                        ),
                    )
                    for part, start in zip(parts, shape.part_starts(len(parts)))
                ],
            ],
            out_specs=[pl.BlockSpec((count, unit), place), pl.BlockSpec((1, unit), place)],
        ),
        out_shape=[
            jax.ShapeDtypeStruct((count, columns), BF16),
            jax.ShapeDtypeStruct((1, columns), F32),
        ],
        compiler_params=pltpu.CompilerParams(vmem_limit_bytes=56 * 2**20),
        cost_estimate=pl.CostEstimate(
            flops=2 * count * width * columns,
            transcendentals=count * columns,
            bytes_accessed=2 * (count * width + width * columns) + 6 * count * columns,
        ),
        name="feed_hidden_grad",
    )(meta, grads, hidden, *parts)


def feed_blocks_kernel(shape, grad, meta, rows_ref, *refs):
    parts, out_ref = refs[:-1], refs[-1]
    for at, offset in enumerate(shape.offsets):
        block = block_of(shape, parts, at)
        size = block.shape[0]
        part = pl.ds(pl.multiple_of((meta[1] ^ offset) * size, size), size)
        if grad:
            out_ref[:, part] = mm_t(rows_ref[...], block).astype(BF16)
        elif at == 0:
            total = mm(rows_ref[:, part], block)
        else:
            total = total + mm(rows_ref[:, part], block)
    if not grad:
        out_ref[...] = total.astype(BF16)


def feed_blocks(shape, meta, rows, parts, side, count, grad):
    half, size, columns = parts[0].shape
    width = 2 * half * size if grad else columns
    tile = 256
    if not grad and size % 128:
        weights = jnp.zeros((2 * half, size, columns), BF16)
        for at, offset in enumerate(shape.offsets):
            weights = lax.dynamic_update_index_in_dim(
                weights, block_of(shape, parts, at), meta[1] ^ offset, 0
            )
        rows = rows[side * count : (side + 1) * count]
        return mm(rows, weights.reshape(-1, columns)).astype(BF16)
    steps = count // tile
    weights = [pl.BlockSpec(part.shape, lambda i, m: (0, 0, 0)) for part in parts]
    return pl.pallas_call(
        functools.partial(feed_blocks_kernel, shape, grad),
        grid_spec=pltpu.PrefetchScalarGridSpec(
            num_scalar_prefetch=1,
            grid=(steps,),
            in_specs=[
                pl.BlockSpec((tile, rows.shape[1]), lambda i, m: (side * steps + i, 0)),
                *weights,
            ],
            out_specs=pl.BlockSpec((tile, width), lambda i, m: (i, 0)),
        ),
        out_shape=jax.ShapeDtypeStruct((count, width), BF16),
        compiler_params=pltpu.CompilerParams(vmem_limit_bytes=56 * 2**20),
        cost_estimate=pl.CostEstimate(
            flops=2 * count * rows.shape[1] * width,
            transcendentals=0,
            bytes_accessed=2 * (count + width) * rows.shape[1] + 2 * count * width,
        ),
        name="feed_grad_rows" if grad else "feed_rows",
    )(meta, rows, *parts)


def branch_kernel(layout, grad, meta, rows_ref, *refs):
    parts, out_ref = refs[:-1], refs[-1]
    out_ref[...] = jnp.zeros_like(out_ref)
    for part, (ctx_order, z_order) in zip(parts, layout):
        depth, columns = part.shape[2], part.shape[3]
        for at, ctx_offset in enumerate(ctx_order):
            column = pl.ds(pl.multiple_of((meta[0] ^ ctx_offset) * columns, columns), columns)
            for order, z_offset in enumerate(z_order):
                row = pl.ds(pl.multiple_of((meta[1] ^ z_offset) * depth, depth), depth)
                if grad:
                    out_ref[:, row] += mm_t(rows_ref[:, column], part[at, order])
                else:
                    out_ref[:, column] += mm(rows_ref[:, row], part[at, order])


def times_blocks(meta, rows, parts, layout, grad):
    return pl.pallas_call(
        functools.partial(branch_kernel, layout, grad),
        grid_spec=pltpu.PrefetchScalarGridSpec(
            num_scalar_prefetch=1,
            grid=(1,),
            in_specs=[pl.BlockSpec(memory_space=pltpu.VMEM)] * (1 + len(parts)),
            out_specs=pl.BlockSpec(memory_space=pltpu.VMEM),
        ),
        out_shape=jax.ShapeDtypeStruct(rows.shape, F32),
        compiler_params=pltpu.CompilerParams(vmem_limit_bytes=56 * 2**20),
        cost_estimate=pl.CostEstimate(
            flops=2 * rows.shape[0] * rows.shape[1] ** 2,
            transcendentals=0,
            bytes_accessed=2 * rows.shape[1] ** 2,
        ),
        name="branch_grad" if grad else "branch",
    )(meta, rows, *parts)


def spread_rows_kernel(pieces, steps, meta, *refs):
    out_ref = refs[-1]
    for piece, blocks in enumerate(pieces):

        @pl.when(pl.program_id(0) // steps == piece)
        def _(blocks=blocks):
            for source, block, offset in blocks:
                rows = refs[source].shape[1]
                start = pl.multiple_of((meta[0] ^ offset) * rows, rows)
                out_ref[pl.ds(start, rows), :] = refs[source][block].astype(F32)


def spread_rows(meta, gathered):
    tile = 256
    members, specs, pieces = [], [], []
    for piece, parts in enumerate(gathered):
        blocks = []
        for values, order in parts:
            count, rows, columns = values.shape
            steps = columns // tile
            blocks += [(len(members), at, offset) for at, offset in enumerate(order)]
            members.append(values)

            def place(i, m, piece=piece, steps=steps):
                return (0, 0, jnp.clip(i - piece * steps, 0, steps - 1))

            specs.append(pl.BlockSpec((count, rows, tile), place))
        pieces.append(blocks)
    total = len(pieces[0]) * rows
    return pl.pallas_call(
        functools.partial(spread_rows_kernel, pieces, steps),
        grid_spec=pltpu.PrefetchScalarGridSpec(
            num_scalar_prefetch=1,
            grid=(len(pieces) * steps,),
            in_specs=specs,
            out_specs=pl.BlockSpec((total, tile), lambda i, m: (0, i)),
        ),
        out_shape=jax.ShapeDtypeStruct((total, len(pieces) * columns), F32),
        compiler_params=pltpu.CompilerParams(vmem_limit_bytes=48 * 2**20),
        name="spread_rows",
    )(meta, *members)


def spread_kernel(moves, extras, outs, meta, *refs):
    outs = refs[len(refs) - outs :]
    for source, block, columns, offset, out, start, step, size in moves:
        target = pl.multiple_of(start + (meta[0] ^ offset) * step, size)
        outs[out][:, pl.ds(target, size)] = refs[source][block, :, columns].astype(F32)
    for source, out in extras:
        width = refs[source].shape[1]
        outs[out][:, outs[out].shape[1] - width :] = refs[source][...]


def spread_columns(meta, gathered, groups, joined, extra=None):
    pieces = len(gathered)
    rows = gathered[0][0][0].shape[1]
    width = gathered[0][0][0].shape[2] // groups
    count = sum(len(order) for _, order in gathered[0])
    if width % 128:
        results = []
        for parts in gathered:
            out = jnp.zeros((count, rows, groups, width), F32)
            for values, order in parts:
                for at, offset in enumerate(order):
                    block = values[at].reshape(rows, groups, width).astype(F32)
                    out = lax.dynamic_update_index_in_dim(out, block, meta[0] ^ offset, 0)
            results.append(jnp.transpose(out, (1, 2, 0, 3)).reshape(rows, -1))
        return [jnp.concatenate(results, axis=1)]
    members, moves = [], []
    for piece, parts in enumerate(gathered):
        for values, order in parts:
            for at, offset in enumerate(order):
                for group in range(groups):
                    start = ((piece if joined else 0) * groups + group) * count * width
                    columns = slice(group * width, (group + 1) * width)
                    out = 0 if joined else piece
                    moves.append((len(members), at, columns, offset, out, start, width, width))
            members.append(values)
    sizes = [groups * count * width * pieces] if joined else [groups * count * width] * pieces
    tile = min(rows, 64)
    in_specs = [
        pl.BlockSpec((member.shape[0], tile, groups * width), lambda i, m: (0, i, 0))
        for member in members
    ]
    extras = []
    if extra is not None:
        extras = [(len(members), 0)]
        members.append(extra)
        in_specs.append(pl.BlockSpec((tile, extra.shape[1]), lambda i, m: (i, 0)))
        sizes[0] += extra.shape[1]
    return pl.pallas_call(
        functools.partial(spread_kernel, moves, extras, len(sizes)),
        grid_spec=pltpu.PrefetchScalarGridSpec(
            num_scalar_prefetch=1,
            grid=(rows // tile,),
            in_specs=in_specs,
            out_specs=[pl.BlockSpec((tile, size), lambda i, m: (i, 0)) for size in sizes],
        ),
        out_shape=[jax.ShapeDtypeStruct((rows, size), F32) for size in sizes],
        compiler_params=pltpu.CompilerParams(vmem_limit_bytes=48 * 2**20),
        name="spread_columns",
    )(meta, *members)


def pick_block(pair_table, ctx_at, half_bit):
    ctx_total = pair_table.shape[0]
    chosen = jnp.sum(jnp.where(jnp.arange(ctx_total, dtype=jnp.int32) == ctx_at, pair_table, 0))
    return jnp.where(half_bit == 0, chosen, 2 * ctx_total - 1 - chosen)


def body(
    inputs,
    w_qkv,
    w_out,
    w_fc,
    w_proj,
    ln1_gain,
    ln1_bias,
    bias_q,
    bias_v,
    bias_out,
    ln2_gain,
    ln2_bias,
    bias_fc,
    bias_proj,
    cotangent,
    lengths,
    pair_table,
):
    slots, _, _, rows, width = inputs.shape
    ctx_count, fsdp_count = lax.axis_size("ctx"), lax.axis_size("fsdp")
    c_at, z_at = lax.axis_index("ctx"), lax.axis_index("fsdp")
    shape = Shape(ctx_count, fsdp_count, slots, rows)
    tokens, chips = shape.tokens, shape.chips
    q_width = width // ctx_count
    shard = width // fsdp_count
    hidden_width = w_fc.shape[1]
    unit = hidden_width // (fsdp_count * ctx_count)
    meta = jnp.concatenate(
        [jnp.stack([c_at, z_at]).astype(jnp.int32), lengths.reshape(-1), pair_table]
    ).astype(jnp.int32)

    offsets = jnp.arange(2 * rows, dtype=jnp.int32)
    pos = (
        pick_block(pair_table, c_at, offsets // rows) * shape.block + z_at * rows + offsets % rows
    )
    live = (pos[None, :] < lengths[:, 0:1] + lengths[:, 1:2]).reshape(tokens, 1).astype(F32)

    x_low = inputs.reshape(tokens, width)
    grad_out = cotangent.reshape(tokens, width).astype(F32) * live
    grad_mlp = grad_out.astype(BF16)
    pack_width = q_width + 2 * HD
    w_first = jnp.concatenate(
        [lax.dynamic_slice_in_dim(w_qkv, c_at * q_width, q_width, axis=1), w_qkv[:, width:]], axis=1
    ).astype(BF16)
    vectors = [ln1_gain, ln1_bias, bias_q, bias_v, bias_out, ln2_gain, ln2_bias, bias_fc, bias_proj]
    sizes = [member.shape[0] for member in vectors]
    vector_rows = 16 * math.ceil(sum(sizes) / (16 * HD))
    packed = jnp.concatenate(
        [member.astype(BF16) for member in vectors]
        + [jnp.zeros((vector_rows * HD - sum(sizes),), BF16)]
    ).reshape(vector_rows, HD)
    x_even, x_odd = ctx_gather(after(x_low, w_first))
    half = fsdp_count // 2
    first_held, first_own = z_gather_steps(w_first)
    first_blocks = z_gather_finish(first_held, first_own)
    vector_held = z_gather_held(after(packed, first_held))
    vector_blocks = [vector_held, z_swap(vector_held, 1)]

    def first_plan(ref):
        moves = []
        for at, offset in enumerate(shape.offsets):
            owner, (part, block) = ref[1] ^ offset, shape.part_of(at, len(first_blocks))
            weight_rows = pl.ds(pl.multiple_of(owner * shard, shard), shard)
            q_part, kv_part = pl.ds(0, q_width), pl.ds(q_width, 2 * HD)
            moves += [
                (part, (block, slice(None), q_part), 0, (weight_rows, slice(None))),
                (part, (block, slice(None), kv_part), 1, (weight_rows, slice(None))),
                (len(first_blocks) + at // half, (at % half,), 2, (owner,)),
            ]
        return moves

    w_q, w_kv, packed = place_blocks(
        meta,
        [*first_blocks, *vector_blocks],
        [(width, q_width), (width, 2 * HD), (fsdp_count, vector_rows, HD)],
        first_plan,
        "place_first",
    )
    packed = packed.reshape(fsdp_count, -1)
    full, start = [], 0
    for size in sizes:
        full.append(packed[:, start : start + size].reshape(-1).astype(F32))
        start += size
    gain_one, shift_one, q_bias, v_bias, out_bias, gain_two, shift_two, fc_bias, proj_bias = full
    q_bias = lax.dynamic_slice_in_dim(q_bias, c_at * q_width, q_width)
    fc_bias = lax.dynamic_index_in_dim(
        fc_bias.reshape(fsdp_count, ctx_count, unit), c_at, 1, keepdims=False
    )

    x_own = x_low.astype(F32)
    first_norm, normed_one, inverse_one = layer_norm(x_own, gain_one, shift_one)
    kv_own = mm(first_norm.astype(BF16), w_kv)
    kv_own = jnp.concatenate([kv_own[:, :HD], kv_own[:, HD:] + v_bias], axis=1).astype(BF16)
    kv_z = jnp.concatenate(z_gather_parts(kv_own), axis=0).reshape(fsdp_count * tokens, 2 * HD)
    kv_even, kv_odd = ctx_gather(kv_z)

    out_parts = z_gather_parts(
        after(lax.dynamic_slice_in_dim(w_out, c_at * q_width, q_width, axis=1).astype(BF16), kv_z)
    )

    fc_own = jnp.concatenate(
        [
            lax.dynamic_slice_in_dim(
                w_fc, group * (hidden_width // fsdp_count) + c_at * unit, unit, axis=1
            )
            for group in range(fsdp_count)
        ],
        axis=1,
    ).astype(BF16)
    proj_own = lax.dynamic_slice_in_dim(w_proj, c_at * unit, unit, axis=0).astype(BF16)
    out_halves = out_parts[0], jnp.concatenate(out_parts[1:], axis=0)
    fc_steps = z_gather_steps(after(fc_own, *out_parts))

    a_even = layer_norm(x_even.astype(F32), gain_one, shift_one)[0].astype(BF16)
    a_odd = layer_norm(x_odd.astype(F32), gain_one, shift_one)[0].astype(BF16)
    q_even = (mm(a_even, w_q) + q_bias).astype(BF16)
    q_odd = (mm(a_odd, w_q) + q_bias).astype(BF16)
    o_heads, q_all, kv_all, o_t, lse = attend(shape, meta, q_even, q_odd, kv_even, kv_odd)
    out_gathered = ctx_gather_halves(
        *[after(side, kv_even) for side in out_halves],
        wait=lambda part: after(part, kv_odd),
        last=lambda part: after(part, o_heads),
    )
    out_blocks, out_layout = [], []
    for side, parts in enumerate(out_gathered):
        z_order = shape.offsets[side * half : (side + 1) * half]
        for values, order in parts:
            out_blocks.append(values)
            out_layout.append((order, z_order))
    o_own = ctx_exchange(o_heads.reshape(ctx_count, tokens, q_width))
    o_own = jnp.transpose(o_own, (1, 0, 2)).reshape(tokens, width)
    fc_parts = z_gather_finish(*fc_steps)
    proj_held = z_gather_held(after(proj_own, fc_parts[-1]))
    o_own = after(o_own, *fc_steps)
    middle = x_own + (times_blocks(meta, o_own, out_blocks, out_layout, False) + out_bias)
    second_norm, normed_two, inverse_two = layer_norm(middle, gain_two, shift_two)

    cn_even, cn_odd = ctx_gather(after(second_norm.astype(BF16), fc_parts[-1]))
    o_parts, gm_parts = ctx_gather_halves(
        after(o_own, cn_even), after(grad_mlp, cn_even), wait=lambda part: after(part, cn_odd)
    )
    o_even, o_odd = in_order(o_parts, 0), in_order(o_parts, 1)
    gm_all = jnp.concatenate([in_order(gm_parts, 0), in_order(gm_parts, 1)], axis=0)
    gm_all, o_even, o_odd = lax.optimization_barrier((gm_all, o_even, o_odd))
    cn_all = after(jnp.concatenate([cn_even, cn_odd], axis=0), proj_held)
    proj_parts = [proj_held, z_swap(proj_held, 1)]
    half_rows = chips * tokens
    hidden, act = feed_hidden(shape, meta, cn_all, fc_parts, fc_bias.reshape(1, -1))
    act_ready = after(act, *proj_parts)
    parts = [slice(at * width // 2, (at + 1) * width // 2) for at in range(2)]
    d_proj = [z_scatter_queued(mm_rows(act_ready, gm_all[:, part]).astype(BF16)) for part in parts]
    g_hidden, g_bias_fc = feed_hidden_grad(
        shape, meta, gm_all, hidden, proj_parts
    )
    g_odd = feed_blocks(shape, meta, g_hidden, fc_parts, 1, half_rows, True)
    g_even = feed_blocks(shape, meta, after(g_hidden, g_odd), fc_parts, 0, half_rows, True)
    grad_second = ctx_scatter(g_even, g_odd)
    cn_late, act_late = after(cn_all, g_even), after(act, g_even)
    own_width = fsdp_count * unit
    parts = [slice(at * own_width // 2, (at + 1) * own_width // 2) for at in range(2)]
    d_fc = [z_scatter_queued(mm_rows(cn_late, g_hidden[:, part]).astype(BF16)) for part in parts]
    mlp = [feed_blocks(shape, meta, act_late, proj_parts, side, half_rows, False) for side in range(2)]

    grad_mid_norm, grad_gain_two, grad_shift_two = norm_backward(
        grad_second, normed_two, inverse_two, gain_two
    )
    grad_middle = grad_out + grad_mid_norm
    grad_branch = grad_middle.astype(BF16)
    go_own = times_blocks(meta, grad_branch, out_blocks, out_layout, True).astype(BF16)
    grads = jnp.concatenate(
        [
            go_own.reshape(tokens, ctx_count, q_width),
            grad_branch.reshape(tokens, ctx_count, q_width),
        ],
        axis=2,
    )
    grads = ctx_exchange(jnp.transpose(grads, (1, 0, 2))).reshape(ctx_count * tokens, 2 * q_width)

    gq_even, gq_odd, gkv_even, gkv_odd, ga_even, ga_odd = attend_grad(
        shape, meta, q_all, kv_all, o_t, lse, grads
    )
    result = ctx_scatter(*mlp, [grad_second], [gq_even])
    result = (middle + (result + proj_bias)).astype(BF16)
    gkv_plane = ctx_scatter(gkv_even, gkv_odd).reshape(fsdp_count, tokens, 2 * HD)
    gkv_low = z_scatter_stacked(gkv_plane).astype(BF16)
    gkv_even, gkv_odd = ctx_gather_small(gkv_low)
    grad_first = ctx_scatter(
        mm_t(gq_even, w_q), mm_t(gq_odd, w_q), [gkv_plane, result], [gkv_even, gkv_odd]
    )
    grad_in_norm, grad_gain_one, grad_shift_one = norm_backward(
        grad_first + mm_t(gkv_low, w_kv), normed_one, inverse_one, gain_one
    )
    grad_inputs = grad_middle + grad_in_norm

    d_proj = ctx_gather_halves(
        *[after(part, grads) for part in d_proj], wait=lambda part: after(part, gkv_plane)
    )
    grad_w_proj = spread_rows(meta, d_proj)
    d_fc = ctx_gather_halves(
        *[after(part, gkv_low) for part in d_fc], wait=lambda part: after(part, grad_first)
    )
    (grad_w_fc,) = spread_columns(meta, d_fc, fsdp_count // 2, True)
    d_q = mm_rows(a_even, gq_even) + mm_rows(a_odd, gq_odd)
    d_out = mm_rows(o_even, ga_even) + mm_rows(o_odd, ga_odd)
    d_pair = z_scatter_queued(jnp.concatenate([d_q, d_out], axis=1).astype(BF16))
    d_kv = (mm_rows(a_even, gkv_even) + mm_rows(a_odd, gkv_odd)).astype(BF16)
    d_kv = z_scatter_queued(d_kv).astype(F32)
    d_pair = ctx_gather_halves(
        d_pair[:, :q_width], d_pair[:, q_width:], wait=lambda part: after(part, grad_w_proj)
    )
    grad_w_qkv, grad_w_out = spread_columns(meta, d_pair, 1, False, d_kv)

    def column_sum(*parts):
        return sum(jnp.sum(part, axis=0, dtype=F32) for part in parts)

    g_bias_q = lax.dynamic_update_index_in_dim(
        jnp.zeros((ctx_count, q_width), F32), column_sum(gq_even, gq_odd), c_at, 0
    ).reshape(-1)
    g_bias_fc = lax.dynamic_update_index_in_dim(
        jnp.zeros((fsdp_count, ctx_count, unit), F32), g_bias_fc.reshape(fsdp_count, unit), c_at, 1
    ).reshape(-1)
    g_vectors = [
        grad_gain_one,
        grad_shift_one,
        g_bias_q,
        column_sum(gkv_low[:, HD:]),
        column_sum(grad_branch),
        grad_gain_two,
        grad_shift_two,
        g_bias_fc,
        column_sum(grad_mlp),
    ]
    stacked = jnp.concatenate(
        [member.reshape(fsdp_count, -1) for member in g_vectors], axis=1
    ).astype(BF16)
    stacked = jnp.stack(
        [lax.dynamic_index_in_dim(stacked, z_at ^ at, 0, keepdims=True) for at in shape.offsets]
    )
    own = z_scatter_stacked(stacked).astype(BF16)
    summed = column_sum(*ctx_gather_small(own))
    vector_grads, start = [], 0
    for size in sizes:
        vector_grads.append(summed[start : start + size].astype(BF16).astype(F32))
        start += size
    return (
        result.reshape(inputs.shape),
        grad_inputs.reshape(inputs.shape),
        grad_w_qkv,
        grad_w_out,
        grad_w_fc,
        grad_w_proj,
        *vector_grads,
    )


def solution(mesh):
    rows_placed = P(None, "ctx", None, "fsdp", None)
    matrix, vector = P("fsdp", None), P("fsdp")
    return jax.shard_map(
        body,
        mesh=mesh,
        in_specs=(rows_placed,) + (matrix,) * 4 + (vector,) * 9 + (rows_placed, P(), P()),
        out_specs=(rows_placed, rows_placed) + (matrix,) * 4 + (vector,) * 9,
        check_vma=False,
    )
```

time: 950 us -> 680 us (0.72)
  waiting for transfers between devices: 415 us -> 234 us
  local copies, waits for them, and re-layouts: 117 us -> 43.2 us
  matrix products: 115 us -> 46.2 us
  Pallas kernels: 61.3 us -> 127 us
  starting transfers between devices: 161 us -> 136 us
  between operations: 3.28 us -> 16.8 us
    ppermute x39 -> x20, waiting for transfers between devices: 192 us -> 77.7 us  [z_swap(): lax.ppermute(values, 'fsdp', [(at, at ^ mask) for at in range(count)])]
    pallas_call x4 -> x12, Pallas kernels: 30.9 us -> 96.6 us  [the longest x4 26.7 us: feed_blocks(): pl.pallas_call(functools.partial(feed_blocks_kernel, shape, grad), grid_s...]
    ppermute x78 -> x74, waiting for transfers between devices: 207 us -> 148 us  [ctx_swap(): return lax.ppermute(values, 'ctx', [(at, at ^ mask) for at in range(count)])]
    dot_general x9 -> x3, matrix products: 44.5 us -> 8.55 us  [mm_t(): lax.dot_general(left, right, (((1,), (1,)), ((), ())), preferred_element_...]
    dynamic_update_slice x28 -> x0, local copies, waits for them, and re-layouts: 28.7 us -> none  [the longest x20 19 us: z_gather(): out = lax.dynamic_update_index_in_dim(out, block, z_at ^ offset, 0)]
    dot_general x9 -> x3, matrix products: 30.9 us -> 4.73 us  [mm(): return jnp.dot(left, right, preferred_element_type=F32)]
    unnamed x205 -> x177, local copies, waits for them, and re-layouts: 43 us -> 17.1 us
    broadcast_in_dim x19 -> x3, local copies, waits for them, and re-layouts: 26.9 us -> 1.08 us  [the longest x1 1.07 us: ctx_gather_halves(): held, offsets = ([first[None], second[None]], [[0], [0]])]
  transfers between devices with their start and end apart: 119 -> 102, of which waited for: 53 -> 43; matrix products, arithmetic and copies ran while one was open for 29% -> 21% of each run, Pallas kernels for 5% -> 18%
where the time goes in v2:
time: 680 us; the launch traced here: 670 us
  waiting for transfers between devices  234 us (34%)
  starting transfers between devices  136 us (20%)
  Pallas kernels  127 us (19%)
  other arithmetic  66 us (10%)
  matrix products  46.2 us (7%)
  local copies, waits for them, and re-layouts  43.2 us (6%)
  between operations  16.8 us (2%)
    ppermute x74, waiting for transfers between devices, ctx_swap(): return lax.ppermute(values, 'ctx', [(at, at ^ mask) for at in range(count)])  148 us
    ppermute x20, waiting for transfers between devices, z_swap(): lax.ppermute(values, 'fsdp', [(at, at ^ mask) for at in range(count)])  77.7 us
    ppermute x20, starting transfers between devices, z_swap(): lax.ppermute(values, 'fsdp', [(at, at ^ mask) for at in range(count)])  61.1 us
    ppermute x74, starting transfers between devices, ctx_swap(): return lax.ppermute(values, 'ctx', [(at, at ^ mask) for at in range(count)])  55 us
    dot_general x10, matrix products, mm_rows(): lax.dot_general(left, right, (((0,), (0,)), ((), ())), preferred_element_...  32.9 us
    pallas_call x4, Pallas kernels, feed_blocks(): pl.pallas_call(functools.partial(feed_blocks_kernel, shape, grad), grid_s...  26.7 us
    pallas_call x2, Pallas kernels, spread_columns(): pl.pallas_call(functools.partial(spread_kernel, moves, extras, len(sizes)...  18 us
    unnamed x177, local copies, waits for them, and re-layouts  17.1 us
  transfers between devices with their start and end apart: 102, of which 43 were waited for; matrix products, arithmetic and copies ran while one was open for 21% of the time, Pallas kernels for 18%

profile of v2, /device:TPU:0, one launch (start us, length us, event | category | flops | bytes accessed | tf_op | source)
XLA Modules:
  0.0 670.2 jit_solution(12914281250653276718)
XLA Ops:
  8.8 5.1 collective-permute-start.3
  17.3 9.5 %collective-permute-done.3 = bf16[1,512,512]{2,1,0:T(8,128)(2,1)} collective-permute-done((bf16[1,512,512]{2,1,0:T(8,128)(2,1)S(1)}, bf16[1,512,512]{2,1,0:T(8,128)(2,1)}, u32[]{:S(2)}, u32[]{:S(2)}) %collective-permute-start.3) | collective-permute-done | bytes 524320 | tf_op jit(solution)/shard_map/ppermute | solution.py:153
  26.8 10.0 %collective-permute-start.5 = (bf16[1,512,512]{2,1,0:T(8,128)(2,1)}, bf16[1,512,512]{2,1,0:T(8,128)(2,1)S(1)}, u32[]{:S(2)}, u32[]{:S(2)}) collective-permute-start(bf16[1,512,512]{2,1,0:T(8,128)(2,1)} %collective-permute-done.3), channel_id=1, source_target_pairs={{0,1},{1,0},{2,3},{3,2},{4,5},{5,4},{6,7},{7,6},{8,9},{9,8},{10,11... | collective-permute-start | bytes 1572872 | tf_op jit(solution)/shard_map/ppermute | solution.py:153
  43.5 7.1 %collective-permute-done.6 = bf16[1,48,128]{2,1,0:T(8,128)(2,1)S(1)} collective-permute-done((bf16[1,48,128]{2,1,0:T(8,128)(2,1)S(1)}, bf16[1,48,128]{2,1,0:T(8,128)(2,1)S(1)}, u32[]{:S(2)}, u32[]{:S(2)}) %collective-permute-start.6) | collective-permute-done | bytes 12320 | tf_op jit(solution)/shard_map/ppermute | solution.py:153
  78.8 4.0 collective-permute-done.14
  96.0 5.4 collective-permute-done.18
  108.2 7.1 %collective-permute-done.25 = bf16[1,2,512,256]{3,2,1,0:T(8,128)(2,1)S(1)} collective-permute-done((bf16[1,2,512,256]{3,2,1,0:T(8,128)(2,1)S(1)}, bf16[1,2,512,256]{3,2,1,0:T(8,128)(2,1)S(1)}, u32[]{:S(2)}, u32[]{:S(2)}) %collective-permute-start.25) | collective-permute-done | bytes 524320 | tf_op jit(solution)/shard_map/ppermute | solution.py:58
  121.9 14.4 %attend.1 = (bf16[1024,256]{1,0:T(8,128)(2,1)}, bf16[2,1024,128]{2,1,0:T(8,128)(2,1)}, bf16[2,2048,256]{2,1,0:T(8,128)(2,1)}, f32[8,128,256]{2,1,0:T(8,128)}, f32[8,1,256]{2,1,0:T(1,128)}) custom-call(s32[14]{0:T(128)} %pad_add_fusion.meta, bf16[512,256]{1,0:T(8,128)(2,1)} %fusion.25.q_even, bf16[512,256]{1,0:T(8,128)(2,1)} %fusion.26.q_odd, ...), custom_call_target="tpu_custom_call" | custom-call | flops 1073741824 | bytes 8388608 | tf_op jit(solution)/shard_map/attend/pallas_call | solution.py:418
  136.3 5.8 collective-permute-done.26.refs_5_
  142.6 10.8 %collective-permute-done.19 = bf16[1,512,1024]{2,1,0:T(8,128)(2,1)} collective-permute-done((bf16[1,512,1024]{2,1,0:T(8,128)(2,1)}, bf16[1,512,1024]{2,1,0:T(8,128)(2,1)}, u32[]{:S(2)}, u32[]{:S(2)}) %collective-permute-start.19) | collective-permute-done | bytes 1048608 | tf_op jit(solution)/shard_map/ppermute | solution.py:153
  153.4 4.2 all-to-all-start
  161.0 6.3 all-to-all-done
  169.8 6.8 %branch.1 = f32[128,2048]{1,0:T(8,128)} custom-call(s32[14]{0:T(128)} %pad_add_fusion.meta, bf16[128,2048]{1,0:T(8,128)(2,1)} %bitcast.177, bf16[2,2,512,256]{3,2,1,0:T(8,128)(2,1)} %copy-done.7, bf16[2,2,512,256]{3,2,1,0:T(8,128)(2,1)} %collective-permute-done.22.refs_1_, bf16[2,2,512,256]{3,2,1,0:T(8,128)(2,1)} %collective-permute-done.23.refs_2_, ...), custom_call_target="tpu_custom_call" | custom-call | flops 1073741824 | bytes 8388608 | tf_op jit(solution)/shard_map/branch/pallas_call | solution.py:662
  178.6 13.4 %collective-permute-done.29.refs_2_ = bf16[1,512,1024]{2,1,0:T(8,128)(2,1)S(1)} collective-permute-done((bf16[1,512,1024]{2,1,0:T(8,128)(2,1)}, bf16[1,512,1024]{2,1,0:T(8,128)(2,1)S(1)}, u32[]{:S(2)}, u32[]{:S(2)}) %collective-permute-start.29) | collective-permute-done | bytes 1048608 | tf_op jit(solution)/shard_map/ppermute | solution.py:153
  202.5 5.4 collective-permute-done.30
  209.0 10.1 %collective-permute-done.31 = bf16[128,2048]{1,0:T(8,128)(2,1)S(1)} collective-permute-done((bf16[128,2048]{1,0:T(8,128)(2,1)S(1)}, bf16[128,2048]{1,0:T(8,128)(2,1)S(1)}, u32[]{:S(2)}, u32[]{:S(2)}) %collective-permute-start.31) | collective-permute-done | bytes 524320 | tf_op jit(solution)/shard_map/ppermute | solution.py:58
  227.1 21.2 %collective-permute-start.43 = (bf16[2,256,2048]{2,1,0:T(8,128)(2,1)}, bf16[2,256,2048]{2,1,0:T(8,128)(2,1)}, u32[]{:S(2)}, u32[]{:S(2)}) collective-permute-start(bf16[2,256,2048]{2,1,0:T(8,128)(2,1)} %pad_maximum_fusion.2.refs_0_), channel_id=1, source_target_pairs={{0,1},{1,0},{2,3},{3,2},{4,5},{5,4},{6,7},{7,6},{8,9},{9,8},{10,11... | collective-permute-start | bytes 6291464 | tf_op jit(solution)/shard_map/ppermute | solution.py:153
  255.0 5.4 collective-permute-done.39
  268.4 10.7 %feed_hidden.1 = (f32[1024,1024]{1,0:T(8,128)}, bf16[1024,1024]{1,0:T(8,128)(2,1)}) custom-call(s32[14]{0:T(128)} %pad_add_fusion.meta, bf16[1024,2048]{1,0:T(8,128)(2,1)} %constant_dynamic-update-slice_fusion.4.rows_ref, f32[1,1024]{1,0:T(1,128)} %bitcast.239, bf16[2,512,1024]{2,1,0:T(8,128)(2,1)} %pad_maximum_fusion.1.refs_0_, ...), custom_call_target="tpu_custom_call" | custom-call | flops 4294967296 | bytes 14680064 | tf_op jit(solution)/shard_map/feed_hidden/pallas_call | solution.py:494
  279.1 13.4 %collective-permute-done.43.refs_1_ = bf16[2,256,2048]{2,1,0:T(8,128)(2,1)} collective-permute-done((bf16[2,256,2048]{2,1,0:T(8,128)(2,1)}, bf16[2,256,2048]{2,1,0:T(8,128)(2,1)}, u32[]{:S(2)}, u32[]{:S(2)}) %collective-permute-start.43) | collective-permute-done | bytes 2097184 | tf_op jit(solution)/shard_map/ppermute | solution.py:153
  305.6 5.3 fusion.22
  311.0 5.9 fusion.19
  317.0 10.9 %reduce-scatter.17.cloned.1.call-start = ((), (), s32[]{:S(2)}) async-start(), calls=%async_computation.13 | async-start | bytes 2621440 | tf_op jit(solution)/shard_map/reduce_scatter | solution.py:194
  327.9 12.1 %feed_hidden_grad.1 = (bf16[1024,1024]{1,0:T(8,128)(2,1)}, f32[1,1024]{1,0:T(1,128)}) custom-call(s32[14]{0:T(128)} %pad_add_fusion.meta, bf16[1024,2048]{1,0:T(8,128)(2,1)} %fusion.58.grads_ref, f32[1024,1024]{1,0:T(8,128)} %get-tuple-element.100.hidden_ref, bf16[2,256,2048]{2,1,0:T(8,128)(2,1)} %pad_maximum_fusion.2.refs_0_, ...), custom_call_target="tpu_custom_call" | custom-call | flops 4294967296 | bytes 14680064 | tf_op jit(solution)/shard_map/feed_hidden_grad/pallas_call | solution.py:558
  339.9 6.6 feed_grad_rows.2
  346.5 6.8 %feed_grad_rows.3 = bf16[512,2048]{1,0:T(8,128)(2,1)} custom-call(s32[14]{0:T(128)} %pad_add_fusion.meta, bf16[1024,1024]{1,0:T(8,128)(2,1)} %get-tuple-element.102.rows_ref, bf16[2,512,1024]{2,1,0:T(8,128)(2,1)} %pad_maximum_fusion.1.refs_0_, bf16[1,512,1024]{2,1,0:T(8,128)(2,1)} %collective-permute-done.20.refs_1_, bf16[1,512,1024]{2,1,0:T(8,128)(2,1)} %copy-done.21), custom_call_target="tpu_custom_call" | custom-call | flops 2147483648 | bytes 7340032 | tf_op jit(solution)/shard_map/feed_grad_rows/pallas_call | solution.py:624
  353.3 6.0 convolution_convert_fusion
  362.0 6.7 %feed_rows.3 = bf16[512,2048]{1,0:T(8,128)(2,1)} custom-call(s32[14]{0:T(128)} %pad_add_fusion.meta, bf16[1024,1024]{1,0:T(8,128)(2,1)} %get-tuple-element.124.rows_ref, bf16[2,256,2048]{2,1,0:T(8,128)(2,1)} %pad_maximum_fusion.2.refs_0_, bf16[2,256,2048]{2,1,0:T(8,128)(2,1)} %collective-permute-done.43.refs_1_), custom_call_target="tpu_custom_call" | custom-call | flops 2147483648 | bytes 7340032 | tf_op jit(solution)/shard_map/feed_rows/pallas_call | solution.py:624
  369.2 4.7 convert_add_fusion.1
  378.6 6.0 convolution_convert_fusion.1
  385.8 6.6 feed_rows.2
  392.4 9.4 %collective-permute-done.48 = bf16[128,2048]{1,0:T(8,128)(2,1)} collective-permute-done((bf16[128,2048]{1,0:T(8,128)(2,1)}, bf16[128,2048]{1,0:T(8,128)(2,1)}, u32[]{:S(2)}, u32[]{:S(2)}) %collective-permute-start.48) | collective-permute-done | bytes 524320 | tf_op jit(solution)/shard_map/ppermute | solution.py:58
  407.3 8.1 %branch_grad.1 = f32[128,2048]{1,0:T(8,128)} custom-call(s32[14]{0:T(128)} %pad_add_fusion.meta, bf16[128,2048]{1,0:T(8,128)(2,1)} %get-tuple-element.195.rows_ref, bf16[2,2,512,256]{3,2,1,0:T(8,128)(2,1)} %copy-done.7, bf16[2,2,512,256]{3,2,1,0:T(8,128)(2,1)} %collective-permute-done.22.refs_1_, bf16[2,2,512,256]{3,2,1,0:T(8,128)(2,1)} %collective-permute-done.23.refs_2_, ...), custom_call_target="tpu_custom_call" | custom-call | flops 1073741824 | bytes 8388608 | tf_op jit(solution)/shard_map/branch_grad/pallas_call | solution.py:662
  418.0 4.2 all-to-all-start.1
  422.5 6.0 fusion.84
  438.0 16.3 %attend_grad.1 = (bf16[512,256]{1,0:T(8,128)(2,1)}, bf16[512,256]{1,0:T(8,128)(2,1)}, bf16[2048,256]{1,0:T(8,128)(2,1)}, bf16[2048,256]{1,0:T(8,128)(2,1)}, bf16...) custom-call(s32[14]{0:T(128)} %pad_add_fusion.meta, bf16[2,1024,128]{2,1,0:T(8,128)(2,1)} %get-tuple-element.105.q_all, ...), custom_call_target="tpu_custom_call" | custom-call | flops 2684354560 | bytes 10485760 | tf_op jit(solution)/shard_map/attend_grad/pallas_call | solution.py:445
  470.4 4.8 collective-permute-done.54
  475.3 5.1 collective-permute-done.56
  484.7 5.8 collective-permute-done.58
  503.3 4.3 fusion.96
  527.1 10.8 %collective-permute-done.64 = bf16[128,2048]{1,0:T(8,128)(2,1)} collective-permute-done((bf16[128,2048]{1,0:T(8,128)(2,1)}, bf16[128,2048]{1,0:T(8,128)(2,1)}, u32[]{:S(2)}, u32[]{:S(2)}) %collective-permute-start.64) | collective-permute-done | bytes 524320 | tf_op jit(solution)/shard_map/ppermute | solution.py:58
  545.5 23.2 %collective-permute-done.85 = bf16[1,512,512]{2,1,0:T(8,128)(2,1)} collective-permute-done((bf16[1,512,512]{2,1,0:T(8,128)(2,1)}, bf16[1,512,512]{2,1,0:T(8,128)(2,1)}, u32[]{:S(2)}, u32[]{:S(2)}) %collective-permute-start.85) | collective-permute-done | bytes 524320 | tf_op jit(solution)/shard_map/ppermute | solution.py:58
  573.9 5.9 collective-permute-done.81
  590.8 19.0 %collective-permute-done.92 = bf16[2,5664]{1,0:T(2,128)(2,1)S(1)} collective-permute-done((bf16[2,5664]{1,0:T(2,128)(2,1)S(1)}, bf16[2,5664]{1,0:T(2,128)(2,1)S(1)}, u32[]{:S(2)}, u32[]{:S(2)}) %collective-permute-start.92) | collective-permute-done | bytes 22688 | tf_op jit(solution)/shard_map/ppermute | solution.py:58
  613.1 10.6 %spread_rows.1 = f32[2048,2048]{1,0:T(8,128)} custom-call(s32[14]{0:T(128)S(1)} %copy-done, bf16[2,256,1024]{2,1,0:T(8,128)(2,1)S(1)} %pad_maximum_fusion.13.refs_0_, bf16[2,256,1024]{2,1,0:T(8,128)(2,1)} %collective-permute-done.67.refs_1_, bf16[2,256,1024]{2,1,0:T(8,128)(2,1)} %collective-permute-done.68.refs_2_, ...), custom_call_target="tpu_custom_call" | custom-call | tf_op jit(solution)/shard_map/spread_rows/pallas_call | solution.py:710
  631.7 9.8 %collective-permute-done.74.refs_1_ = bf16[2,512,256]{2,1,0:T(8,128)(2,1)} collective-permute-done((bf16[2,512,256]{2,1,0:T(8,128)(2,1)S(1)}, bf16[2,512,256]{2,1,0:T(8,128)(2,1)}, u32[]{:S(2)}, u32[]{:S(2)}) %collective-permute-start.74) | collective-permute-done | bytes 524320 | tf_op jit(solution)/shard_map/ppermute | solution.py:58
  644.8 10.3 %spread_columns.3 = f32[512,8192]{1,0:T(8,128)} custom-call(s32[14]{0:T(128)S(1)} %copy-done, bf16[2,512,512]{2,1,0:T(8,128)(2,1)} %pad_maximum_fusion.15.refs_0_, bf16[2,512,512]{2,1,0:T(8,128)(2,1)} %collective-permute-done.82.refs_1_, bf16[2,512,512]{2,1,0:T(8,128)(2,1)} %collective-permute-done.83.refs_2_, ...), custom_call_target="tpu_custom_call" | custom-call | tf_op jit(solution)/shard_map/spread_columns/pallas_call | solution.py:771
  655.2 7.7 %spread_columns.2 = (f32[512,2304]{1,0:T(8,128)}, f32[512,2048]{1,0:T(8,128)}) custom-call(s32[14]{0:T(128)S(1)} %copy-done, bf16[2,512,256]{2,1,0:T(8,128)(2,1)S(1)} %pad_maximum_fusion.20.refs_0_, bf16[2,512,256]{2,1,0:T(8,128)(2,1)} %collective-permute-done.74.refs_1_, bf16[2,512,256]{2,1,0:T(8,128)(2,1)} %collective-permute-done.75.refs_2_, ...), custom_call_target="tpu_custom_call" | custom-call | tf_op jit(solution)/shard_map/spread_columns/pallas_call | solution.py:771
  (515 shorter events, 238.4 us)
Async XLA Ops:
  13.9 37.5 %collective-permute-start.4 = (bf16[1,512,512]{2,1,0:T(8,128)(2,1)S(1)}, bf16[1,512,512]{2,1,0:T(8,128)(2,1)S(1)}, u32[]{:S(2)}, u32[]{:S(2)}) collective-permute-start(bf16[1,512,512]{2,1,0:T(8,128)(2,1)S(1)} %pad_maximum_fusion.17), channel_id=1, source_target_pairs={{0,1},{1,0},{2,3},{3,2},{4,5},{5,4},{6,7},{7,6},{8,9},{9,8},{10,11... | collective-permute-start | bytes 1572872 | tf_op jit(solution)/shard_map/ppermute | solution.py:153
  13.9 54.4 %collective-permute-start.2 = (bf16[128,2048]{1,0:T(8,128)(2,1)S(1)}, bf16[128,2048]{1,0:T(8,128)(2,1)}, u32[]{:S(2)}, u32[]{:S(2)}) collective-permute-start(bf16[128,2048]{1,0:T(8,128)(2,1)S(1)} %bitcast.172), channel_id=1, source_target_pairs={{0,24},{4,28},{8,16},{12,20},{16,8},{20,12},{24,0},{28,4},{1,25},{... | collective-permute-start | bytes 1572872 | tf_op jit(solution)/shard_map/ppermute | solution.py:58
  16.3 51.9 %collective-permute-start.1 = (bf16[128,2048]{1,0:T(8,128)(2,1)S(1)}, bf16[128,2048]{1,0:T(8,128)(2,1)}, u32[]{:S(2)}, u32[]{:S(2)}) collective-permute-start(bf16[128,2048]{1,0:T(8,128)(2,1)S(1)} %bitcast.173), channel_id=1, source_target_pairs={{0,16},{4,20},{8,24},{12,28},{16,0},{20,4},{24,8},{28,12},{1,17},{... | collective-permute-start | bytes 1572872 | tf_op jit(solution)/shard_map/ppermute | solution.py:58
  26.8 27.6 %collective-permute-start.5 = (bf16[1,512,512]{2,1,0:T(8,128)(2,1)}, bf16[1,512,512]{2,1,0:T(8,128)(2,1)S(1)}, u32[]{:S(2)}, u32[]{:S(2)}) collective-permute-start(bf16[1,512,512]{2,1,0:T(8,128)(2,1)} %collective-permute-done.3), channel_id=1, source_target_pairs={{0,1},{1,0},{2,3},{3,2},{4,5},{5,4},{6,7},{7,6},{8,9},{9,8},{10,11... | collective-permute-start | bytes 1572872 | tf_op jit(solution)/shard_map/ppermute | solution.py:153
  70.4 47.5 %collective-permute-start.8 = (bf16[512,2048]{1,0:T(8,128)(2,1)S(1)}, bf16[512,2048]{1,0:T(8,128)(2,1)S(1)}, u32[]{:S(2)}, u32[]{:S(2)}) collective-permute-start(bf16[512,2048]{1,0:T(8,128)(2,1)S(1)} %get-tuple-element.201), channel_id=1, source_target_pairs={{0,4},{4,0},{8,12},{12,8},{16,20},{20,16},{24,28},{28,24},{1,5},{5... | collective-permute-start | bytes 6291464 | tf_op jit(solution)/shard_map/ppermute | solution.py:58
  104.7 64.5 %collective-permute-start.20 = (bf16[1,512,1024]{2,1,0:T(8,128)(2,1)}, bf16[1,512,1024]{2,1,0:T(8,128)(2,1)}, u32[]{:S(2)}, u32[]{:S(2)}) collective-permute-start(bf16[1,512,1024]{2,1,0:T(8,128)(2,1)} %bitcast.13), channel_id=1, source_target_pairs={{0,1},{1,0},{2,3},{3,2},{4,5},{5,4},{6,7},{7,6},{8,9},{9,8},{10,11... | collective-permute-start | bytes 3145736 | tf_op jit(solution)/shard_map/ppermute | solution.py:153
  106.5 46.9 %collective-permute-start.19 = (bf16[1,512,1024]{2,1,0:T(8,128)(2,1)}, bf16[1,512,1024]{2,1,0:T(8,128)(2,1)}, u32[]{:S(2)}, u32[]{:S(2)}) collective-permute-start(bf16[1,512,1024]{2,1,0:T(8,128)(2,1)} %bitcast.13), channel_id=1, source_target_pairs={{0,3},{1,2},{2,1},{3,0},{4,7},{5,6},{6,5},{7,4},{8,11},{9,10},{10,... | collective-permute-start | bytes 3145736 | tf_op jit(solution)/shard_map/ppermute | solution.py:153
  108.1 61.6 %collective-permute-start.23 = (bf16[2,2,512,256]{3,2,1,0:T(8,128)(2,1)S(1)}, bf16[2,2,512,256]{3,2,1,0:T(8,128)(2,1)}, u32[]{:S(2)}, u32[]{:S(2)}) collective-permute-start(bf16[2,2,512,256]{3,2,1,0:T(8,128)(2,1)S(1)} %pad_maximum_fusion.9.refs_0_), channel_id=1, source_target_pairs={{0,4},{4,0},{8,12},{12,8},{16,20},{20,16},{24,28},{28,24},{1,5},{5... | collective-permute-start | bytes 3145736 | tf_op jit(solution)/shard_map/ppermute | solution.py:58
  115.3 26.8 %collective-permute-start.22 = (bf16[2,2,512,256]{3,2,1,0:T(8,128)(2,1)S(1)}, bf16[2,2,512,256]{3,2,1,0:T(8,128)(2,1)}, u32[]{:S(2)}, u32[]{:S(2)}) collective-permute-start(bf16[2,2,512,256]{3,2,1,0:T(8,128)(2,1)S(1)} %pad_maximum_fusion.9.refs_0_), channel_id=1, source_target_pairs={{0,8},{4,12},{8,0},{12,4},{16,24},{20,28},{24,16},{28,20},{1,9},{5... | collective-permute-start | bytes 3145736 | tf_op jit(solution)/shard_map/ppermute | solution.py:58
  117.8 24.3 %collective-permute-start.26 = (bf16[2,2,512,256]{3,2,1,0:T(8,128)(2,1)}, bf16[2,2,512,256]{3,2,1,0:T(8,128)(2,1)}, u32[]{:S(2)}, u32[]{:S(2)}) collective-permute-start(bf16[2,2,512,256]{3,2,1,0:T(8,128)(2,1)} %pad_maximum_fusion.10.refs_4_), channel_id=1, source_target_pairs={{0,16},{4,20},{8,24},{12,28},{16,0},{20,4},{24,8},{28,12},{1,17},{... | collective-permute-start | bytes 3145736 | tf_op jit(solution)/shard_map/ppermute | solution.py:58
  142.1 27.7 %collective-permute-start.27 = (bf16[2,2,512,256]{3,2,1,0:T(8,128)(2,1)}, bf16[2,2,512,256]{3,2,1,0:T(8,128)(2,1)}, u32[]{:S(2)}, u32[]{:S(2)}) collective-permute-start(bf16[2,2,512,256]{3,2,1,0:T(8,128)(2,1)} %pad_maximum_fusion.10.refs_4_), channel_id=1, source_target_pairs={{0,4},{4,0},{8,12},{12,8},{16,20},{20,16},{24,28},{28,24},{1,5},{5... | collective-permute-start | bytes 3145736 | tf_op jit(solution)/shard_map/ppermute | solution.py:58
  142.1 27.7 %collective-permute-start.24 = (bf16[2,2,512,256]{3,2,1,0:T(8,128)(2,1)}, bf16[2,2,512,256]{3,2,1,0:T(8,128)(2,1)}, u32[]{:S(2)}, u32[]{:S(2)}) collective-permute-start(bf16[2,2,512,256]{3,2,1,0:T(8,128)(2,1)} %collective-permute-done.22.refs_1_), channel_id=1, source_target_pairs={{0,4},{4,0},{8,12},{12,8},{16,20},{20,16},{24,28},{28,24},{1,5},{5... | collective-permute-start | bytes 3145736 | tf_op jit(solution)/shard_map/ppermute | solution.py:58
  157.5 341.1 %reduce-scatter.11.cloned.1.call-start = ((), (), s32[]{:S(2)}) async-start(), calls=%async_computation.10 | async-start | bytes 2621440 | tf_op jit(solution)/shard_map/reduce_scatter | solution.py:194
  169.2 22.8 %collective-permute-start.29 = (bf16[1,512,1024]{2,1,0:T(8,128)(2,1)}, bf16[1,512,1024]{2,1,0:T(8,128)(2,1)S(1)}, u32[]{:S(2)}, u32[]{:S(2)}) collective-permute-start(bf16[1,512,1024]{2,1,0:T(8,128)(2,1)} %collective-permute-done.19), channel_id=1, source_target_pairs={{0,1},{1,0},{2,3},{3,2},{4,5},{5,4},{6,7},{7,6},{8,9},{9,8},{10,11... | collective-permute-start | bytes 3145736 | tf_op jit(solution)/shard_map/ppermute | solution.py:153
  195.1 24.0 %collective-permute-start.31 = (bf16[128,2048]{1,0:T(8,128)(2,1)S(1)}, bf16[128,2048]{1,0:T(8,128)(2,1)S(1)}, u32[]{:S(2)}, u32[]{:S(2)}) collective-permute-start(bf16[128,2048]{1,0:T(8,128)(2,1)S(1)} %add_convert_fusion), channel_id=1, source_target_pairs={{0,16},{4,20},{8,24},{12,28},{16,0},{20,4},{24,8},{28,12},{1,17},{... | collective-permute-start | bytes 1572872 | tf_op jit(solution)/shard_map/ppermute | solution.py:58
  198.2 25.9 %collective-permute-start.34 = (bf16[1,256,2048]{2,1,0:T(8,128)(2,1)}, bf16[1,256,2048]{2,1,0:T(8,128)(2,1)}, u32[]{:S(2)}, u32[]{:S(2)}) collective-permute-start(bf16[1,256,2048]{2,1,0:T(8,128)(2,1)} %bitcast.16), channel_id=1, source_target_pairs={{0,3},{1,2},{2,1},{3,0},{4,7},{5,6},{6,5},{7,4},{8,11},{9,10},{10,... | collective-permute-start | bytes 3145736 | tf_op jit(solution)/shard_map/ppermute | solution.py:153
  221.3 39.1 %collective-permute-start.33 = (bf16[512,2048]{1,0:T(8,128)(2,1)}, bf16[512,2048]{1,0:T(8,128)(2,1)}, u32[]{:S(2)}, u32[]{:S(2)}) collective-permute-start(bf16[512,2048]{1,0:T(8,128)(2,1)} %get-tuple-element.234), channel_id=1, source_target_pairs={{0,4},{4,0},{8,12},{12,8},{16,20},{20,16},{24,28},{28,24},{1,5},{5... | collective-permute-start | bytes 6291464 | tf_op jit(solution)/shard_map/ppermute | solution.py:58
  227.1 65.4 %collective-permute-start.43 = (bf16[2,256,2048]{2,1,0:T(8,128)(2,1)}, bf16[2,256,2048]{2,1,0:T(8,128)(2,1)}, u32[]{:S(2)}, u32[]{:S(2)}) collective-permute-start(bf16[2,256,2048]{2,1,0:T(8,128)(2,1)} %pad_maximum_fusion.2.refs_0_), channel_id=1, source_target_pairs={{0,1},{1,0},{2,3},{3,2},{4,5},{5,4},{6,7},{7,6},{8,9},{9,8},{10,11... | collective-permute-start | bytes 6291464 | tf_op jit(solution)/shard_map/ppermute | solution.py:153
  261.7 33.9 %collective-permute-start.41 = (bf16[2,128,2048]{2,1,0:T(8,128)(2,1)S(1)}, bf16[2,128,2048]{2,1,0:T(8,128)(2,1)S(1)}, u32[]{:S(2)}, u32[]{:S(2)}) collective-permute-start(bf16[2,128,2048]{2,1,0:T(8,128)(2,1)S(1)} %pad_maximum_fusion.12), channel_id=1, source_target_pairs={{0,4},{4,0},{8,12},{12,8},{16,20},{20,16},{24,28},{28,24},{1,5},{5... | collective-permute-start | bytes 3145736 | tf_op jit(solution)/shard_map/ppermute | solution.py:58
  261.8 31.5 %collective-permute-start.40 = (bf16[2,128,2048]{2,1,0:T(8,128)(2,1)S(1)}, bf16[2,128,2048]{2,1,0:T(8,128)(2,1)S(1)}, u32[]{:S(2)}, u32[]{:S(2)}) collective-permute-start(bf16[2,128,2048]{2,1,0:T(8,128)(2,1)S(1)} %pad_maximum_fusion.12), channel_id=1, source_target_pairs={{0,8},{4,12},{8,0},{12,4},{16,24},{20,28},{24,16},{28,20},{1,9},{5... | collective-permute-start | bytes 3145736 | tf_op jit(solution)/shard_map/ppermute | solution.py:58
  265.0 30.8 %collective-permute-start.37 = (bf16[2,128,2048]{2,1,0:T(8,128)(2,1)}, bf16[2,128,2048]{2,1,0:T(8,128)(2,1)}, u32[]{:S(2)}, u32[]{:S(2)}) collective-permute-start(bf16[2,128,2048]{2,1,0:T(8,128)(2,1)} %pad_maximum_fusion.11), channel_id=1, source_target_pairs={{0,4},{4,0},{8,12},{12,8},{16,20},{20,16},{24,28},{28,24},{1,5},{5... | collective-permute-start | bytes 3145736 | tf_op jit(solution)/shard_map/ppermute | solution.py:58
  265.0 28.4 %collective-permute-start.36 = (bf16[2,128,2048]{2,1,0:T(8,128)(2,1)}, bf16[2,128,2048]{2,1,0:T(8,128)(2,1)S(1)}, u32[]{:S(2)}, u32[]{:S(2)}) collective-permute-start(bf16[2,128,2048]{2,1,0:T(8,128)(2,1)} %pad_maximum_fusion.11), channel_id=1, source_target_pairs={{0,16},{4,20},{8,24},{12,28},{16,0},{20,4},{24,8},{28,12},{1,17},{... | collective-permute-start | bytes 3145736 | tf_op jit(solution)/shard_map/ppermute | solution.py:58
  310.9 187.7 %reduce-scatter.9.cloned.1.call-start = ((), (), s32[]{:S(2)}) async-start(), calls=%async_computation.9 | async-start | bytes 2621440 | tf_op jit(solution)/shard_map/reduce_scatter | solution.py:194
  317.0 203.6 %reduce-scatter.17.cloned.1.call-start = ((), (), s32[]{:S(2)}) async-start(), calls=%async_computation.13 | async-start | bytes 2621440 | tf_op jit(solution)/shard_map/reduce_scatter | solution.py:194
  359.3 161.3 %reduce-scatter.15.cloned.1.call-start = ((), (), s32[]{:S(2)}) async-start(), calls=%async_computation.12 | async-start | bytes 2621440 | tf_op jit(solution)/shard_map/reduce_scatter | solution.py:194
  368.8 53.7 %collective-permute-start.44 = (bf16[512,2048]{1,0:T(8,128)(2,1)}, bf16[512,2048]{1,0:T(8,128)(2,1)}, u32[]{:S(2)}, u32[]{:S(2)}) collective-permute-start(bf16[512,2048]{1,0:T(8,128)(2,1)} %feed_rows.3), channel_id=1, source_target_pairs={{0,4},{4,0},{8,12},{12,8},{16,20},{20,16},{24,28},{28,24},{1,5},{5... | collective-permute-start | bytes 6291464 | tf_op jit(solution)/shard_map/ppermute | solution.py:58
  376.1 25.8 %collective-permute-start.48 = (bf16[128,2048]{1,0:T(8,128)(2,1)}, bf16[128,2048]{1,0:T(8,128)(2,1)}, u32[]{:S(2)}, u32[]{:S(2)}) collective-permute-start(bf16[128,2048]{1,0:T(8,128)(2,1)} %get-tuple-element.221), channel_id=1, source_target_pairs={{0,24},{4,28},{8,16},{12,20},{16,8},{20,12},{24,0},{28,4},{1,25},{... | collective-permute-start | bytes 1572872 | tf_op jit(solution)/shard_map/ppermute | solution.py:58
  378.3 24.9 %collective-permute-start.47 = (bf16[128,2048]{1,0:T(8,128)(2,1)}, bf16[128,2048]{1,0:T(8,128)(2,1)}, u32[]{:S(2)}, u32[]{:S(2)}) collective-permute-start(bf16[128,2048]{1,0:T(8,128)(2,1)} %get-tuple-element.222), channel_id=1, source_target_pairs={{0,16},{4,20},{8,24},{12,28},{16,0},{20,4},{24,8},{28,12},{1,17},{... | collective-permute-start | bytes 1572872 | tf_op jit(solution)/shard_map/ppermute | solution.py:58
  422.2 187.7 %reduce-scatter.7.cloned.1.call-start = ((), (), s32[]{:S(2)}) async-start(), calls=%async_computation.8 | async-start | bytes 2621440 | tf_op jit(solution)/shard_map/reduce_scatter | solution.py:194
  432.9 25.3 %collective-permute-start.49 = (bf16[128,2048]{1,0:T(8,128)(2,1)}, bf16[128,2048]{1,0:T(8,128)(2,1)}, u32[]{:S(2)}, u32[]{:S(2)}) collective-permute-start(bf16[128,2048]{1,0:T(8,128)(2,1)} %get-tuple-element.217), channel_id=1, source_target_pairs={{0,8},{4,12},{8,0},{12,4},{16,24},{20,28},{24,16},{28,20},{1,9},{5... | collective-permute-start | bytes 1572872 | tf_op jit(solution)/shard_map/ppermute | solution.py:58
  434.7 25.5 %collective-permute-start.51 = (bf16[128,2048]{1,0:T(8,128)(2,1)}, bf16[128,2048]{1,0:T(8,128)(2,1)}, u32[]{:S(2)}, u32[]{:S(2)}) collective-permute-start(bf16[128,2048]{1,0:T(8,128)(2,1)} %get-tuple-element.218), channel_id=1, source_target_pairs={{0,24},{4,28},{8,16},{12,20},{16,8},{20,12},{24,0},{28,4},{1,25},{... | collective-permute-start | bytes 1572872 | tf_op jit(solution)/shard_map/ppermute | solution.py:58
  436.2 25.0 %collective-permute-start.50 = (bf16[128,2048]{1,0:T(8,128)(2,1)}, bf16[128,2048]{1,0:T(8,128)(2,1)}, u32[]{:S(2)}, u32[]{:S(2)}) collective-permute-start(bf16[128,2048]{1,0:T(8,128)(2,1)} %get-tuple-element.219), channel_id=1, source_target_pairs={{0,16},{4,20},{8,24},{12,28},{16,0},{20,4},{24,8},{28,12},{1,17},{... | collective-permute-start | bytes 1572872 | tf_op jit(solution)/shard_map/ppermute | solution.py:58
  461.2 42.2 %collective-permute-start.52 = (bf16[512,2048]{1,0:T(8,128)(2,1)}, bf16[512,2048]{1,0:T(8,128)(2,1)}, u32[]{:S(2)}, u32[]{:S(2)}) collective-permute-start(bf16[512,2048]{1,0:T(8,128)(2,1)} %convolution_convert_fusion.2), channel_id=1, source_target_pairs={{0,4},{4,0},{8,12},{12,8},{16,20},{20,16},{24,28},{28,24},{1,5},{5... | collective-permute-start | bytes 6291464 | tf_op jit(solution)/shard_map/ppermute | solution.py:58
  510.5 27.4 %collective-permute-start.64 = (bf16[128,2048]{1,0:T(8,128)(2,1)}, bf16[128,2048]{1,0:T(8,128)(2,1)}, u32[]{:S(2)}, u32[]{:S(2)}) collective-permute-start(bf16[128,2048]{1,0:T(8,128)(2,1)} %get-tuple-element.213), channel_id=1, source_target_pairs={{0,24},{4,28},{8,16},{12,20},{16,8},{20,12},{24,0},{28,4},{1,25},{... | collective-permute-start | bytes 1572872 | tf_op jit(solution)/shard_map/ppermute | solution.py:58
  513.5 24.7 %collective-permute-start.63 = (bf16[128,2048]{1,0:T(8,128)(2,1)}, bf16[128,2048]{1,0:T(8,128)(2,1)}, u32[]{:S(2)}, u32[]{:S(2)}) collective-permute-start(bf16[128,2048]{1,0:T(8,128)(2,1)} %get-tuple-element.214), channel_id=1, source_target_pairs={{0,16},{4,20},{8,24},{12,28},{16,0},{20,4},{24,8},{28,12},{1,17},{... | collective-permute-start | bytes 1572872 | tf_op jit(solution)/shard_map/ppermute | solution.py:58
  515.7 128.2 %reduce-scatter.13.cloned.1.call-start = ((), (), s32[]{:S(2)}) async-start(), calls=%async_computation.11 | async-start | bytes 1310720 | tf_op jit(solution)/shard_map/reduce_scatter | solution.py:194
  518.8 66.4 %collective-permute-start.68 = (bf16[2,256,1024]{2,1,0:T(8,128)(2,1)S(1)}, bf16[2,256,1024]{2,1,0:T(8,128)(2,1)}, u32[]{:S(2)}, u32[]{:S(2)}) collective-permute-start(bf16[2,256,1024]{2,1,0:T(8,128)(2,1)S(1)} %pad_maximum_fusion.13.refs_0_), channel_id=1, source_target_pairs={{0,4},{4,0},{8,12},{12,8},{16,20},{20,16},{24,28},{28,24},{1,5},{5... | collective-permute-start | bytes 3145736 | tf_op jit(solution)/shard_map/ppermute | solution.py:58
  522.5 57.4 %collective-permute-start.67 = (bf16[2,256,1024]{2,1,0:T(8,128)(2,1)S(1)}, bf16[2,256,1024]{2,1,0:T(8,128)(2,1)}, u32[]{:S(2)}, u32[]{:S(2)}) collective-permute-start(bf16[2,256,1024]{2,1,0:T(8,128)(2,1)S(1)} %pad_maximum_fusion.13.refs_0_), channel_id=1, source_target_pairs={{0,8},{4,12},{8,0},{12,4},{16,24},{20,28},{24,16},{28,20},{1,9},{5... | collective-permute-start | bytes 3145736 | tf_op jit(solution)/shard_map/ppermute | solution.py:58
  526.4 54.0 %collective-permute-start.71 = (bf16[2,256,1024]{2,1,0:T(8,128)(2,1)S(1)}, bf16[2,256,1024]{2,1,0:T(8,128)(2,1)}, u32[]{:S(2)}, u32[]{:S(2)}) collective-permute-start(bf16[2,256,1024]{2,1,0:T(8,128)(2,1)S(1)} %pad_maximum_fusion.14.refs_4_), channel_id=1, source_target_pairs={{0,16},{4,20},{8,24},{12,28},{16,0},{20,4},{24,8},{28,12},{1,17},{... | collective-permute-start | bytes 3145736 | tf_op jit(solution)/shard_map/ppermute | solution.py:58
  537.9 30.8 %collective-permute-start.85 = (bf16[1,512,512]{2,1,0:T(8,128)(2,1)}, bf16[1,512,512]{2,1,0:T(8,128)(2,1)}, u32[]{:S(2)}, u32[]{:S(2)}) collective-permute-start(bf16[1,512,512]{2,1,0:T(8,128)(2,1)} %bitcast.201), channel_id=1, source_target_pairs={{0,8},{4,12},{8,0},{12,4},{16,24},{20,28},{24,16},{28,20},{1,9},{5... | collective-permute-start | bytes 1572872 | tf_op jit(solution)/shard_map/ppermute | solution.py:58
  542.7 26.6 %collective-permute-start.89 = (bf16[2,1,5664]{2,1,0:T(2,128)(2,1)S(1)}, bf16[2,1,5664]{2,1,0:T(2,128)(2,1)S(1)}, u32[]{:S(2)}, u32[]{:S(2)}) collective-permute-start(bf16[2,1,5664]{2,1,0:T(2,128)(2,1)S(1)} %pad_maximum_fusion.26), channel_id=1, source_target_pairs={{0,1},{1,0},{2,3},{3,2},{4,5},{5,4},{6,7},{7,6},{8,9},{9,8},{10,11... | collective-permute-start | bytes 67976 | tf_op jit(solution)/shard_map/ppermute | solution.py:153
  579.9 31.1 %collective-permute-start.69 = (bf16[2,256,1024]{2,1,0:T(8,128)(2,1)}, bf16[2,256,1024]{2,1,0:T(8,128)(2,1)}, u32[]{:S(2)}, u32[]{:S(2)}) collective-permute-start(bf16[2,256,1024]{2,1,0:T(8,128)(2,1)} %collective-permute-done.67.refs_1_), channel_id=1, source_target_pairs={{0,4},{4,0},{8,12},{12,8},{16,20},{20,16},{24,28},{28,24},{1,5},{5... | collective-permute-start | bytes 3145736 | tf_op jit(solution)/shard_map/ppermute | solution.py:58
  580.4 31.9 %collective-permute-start.73 = (bf16[2,256,1024]{2,1,0:T(8,128)(2,1)}, bf16[2,256,1024]{2,1,0:T(8,128)(2,1)}, u32[]{:S(2)}, u32[]{:S(2)}) collective-permute-start(bf16[2,256,1024]{2,1,0:T(8,128)(2,1)} %collective-permute-done.71.refs_5_), channel_id=1, source_target_pairs={{0,4},{4,0},{8,12},{12,8},{16,20},{20,16},{24,28},{28,24},{1,5},{5... | collective-permute-start | bytes 3145736 | tf_op jit(solution)/shard_map/ppermute | solution.py:58
  584.4 39.5 %collective-permute-start.82 = (bf16[2,512,512]{2,1,0:T(8,128)(2,1)}, bf16[2,512,512]{2,1,0:T(8,128)(2,1)}, u32[]{:S(2)}, u32[]{:S(2)}) collective-permute-start(bf16[2,512,512]{2,1,0:T(8,128)(2,1)} %pad_maximum_fusion.15.refs_0_), channel_id=1, source_target_pairs={{0,8},{4,12},{8,0},{12,4},{16,24},{20,28},{24,16},{28,20},{1,9},{5... | collective-permute-start | bytes 3145736 | tf_op jit(solution)/shard_map/ppermute | solution.py:58
  585.2 39.2 %collective-permute-start.86 = (bf16[2,512,512]{2,1,0:T(8,128)(2,1)S(1)}, bf16[2,512,512]{2,1,0:T(8,128)(2,1)}, u32[]{:S(2)}, u32[]{:S(2)}) collective-permute-start(bf16[2,512,512]{2,1,0:T(8,128)(2,1)S(1)} %pad_maximum_fusion.16.refs_4_), channel_id=1, source_target_pairs={{0,16},{4,20},{8,24},{12,28},{16,0},{20,4},{24,8},{28,12},{1,17},{... | collective-permute-start | bytes 3145736 | tf_op jit(solution)/shard_map/ppermute | solution.py:58
  587.0 22.9 %collective-permute-start.92 = (bf16[2,5664]{1,0:T(2,128)(2,1)S(1)}, bf16[2,5664]{1,0:T(2,128)(2,1)S(1)}, u32[]{:S(2)}, u32[]{:S(2)}) collective-permute-start(bf16[2,5664]{1,0:T(2,128)(2,1)S(1)} %pad_maximum_fusion.29), channel_id=1, source_target_pairs={{0,16},{4,20},{8,24},{12,28},{16,0},{20,4},{24,8},{28,12},{1,17},{... | collective-permute-start | bytes 67976 | tf_op jit(solution)/shard_map/ppermute | solution.py:58
  631.1 24.1 %collective-permute-start.75 = (bf16[2,512,256]{2,1,0:T(8,128)(2,1)S(1)}, bf16[2,512,256]{2,1,0:T(8,128)(2,1)}, u32[]{:S(2)}, u32[]{:S(2)}) collective-permute-start(bf16[2,512,256]{2,1,0:T(8,128)(2,1)S(1)} %pad_maximum_fusion.20.refs_0_), channel_id=1, source_target_pairs={{0,4},{4,0},{8,12},{12,8},{16,20},{20,16},{24,28},{28,24},{1,5},{5... | collective-permute-start | bytes 1572872 | tf_op jit(solution)/shard_map/ppermute | solution.py:58
  631.2 24.0 %collective-permute-start.79 = (bf16[2,512,256]{2,1,0:T(8,128)(2,1)S(1)}, bf16[2,512,256]{2,1,0:T(8,128)(2,1)}, u32[]{:S(2)}, u32[]{:S(2)}) collective-permute-start(bf16[2,512,256]{2,1,0:T(8,128)(2,1)S(1)} %pad_maximum_fusion.21.refs_4_), channel_id=1, source_target_pairs={{0,4},{4,0},{8,12},{12,8},{16,20},{20,16},{24,28},{28,24},{1,5},{5... | collective-permute-start | bytes 1572872 | tf_op jit(solution)/shard_map/ppermute | solution.py:58
  (133 other events, 2662.3 us)
Sparse Core Ops, SparseCore 0:
  311.1 43.2 reduce-scatter.10
  356.8 43.1 reduce-scatter.8
  402.3 43.1 reduce-scatter.16
  447.8 45.9 reduce-scatter.14
  515.8 43.7 reduce-scatter.6
  591.0 27.2 reduce-scatter.12

commit v3 on v2

--- a/solution.py
+++ b/solution.py
@@ -4,6 +4,7 @@
 import jax
 import jax.numpy as jnp
 from jax import lax
+from jax.experimental.layout import Layout, with_layout_constraint
 from jax.experimental import pallas as pl
 from jax.experimental.pallas import tpu as pltpu
 from jax.sharding import PartitionSpec as P
@@ -70,24 +71,31 @@
 
 
 def ctx_scatter(even, odd, ready=(), finish=()):
-    chips = lax.axis_size("ctx") // 2
-    rows = even.shape[0] // chips
+    return ctx_scatter_chips(*ctx_scatter_cores(even, odd), ready, finish)
+
+
+def ctx_scatter_cores(even, odd):
+    rows = even.shape[0] // (lax.axis_size("ctx") // 2)
     both = even.astype(F32) + ctx_swap(odd.astype(BF16), 1).astype(F32)
-    total = both[:rows]
-    low = after(both.astype(BF16), *ready)
-    for at in range(1, chips):
-        got = ctx_swap(low[at * rows : (at + 1) * rows], 2 * at)
-        total = total + after(got, *finish).astype(F32)
+    return both[:rows], both[rows:].astype(BF16)
+
+
+def ctx_scatter_chips(total, low, ready=(), finish=()):
+    return ctx_scatter_sum(total, ctx_scatter_sent(low, total.shape[0], ready), finish)
+
+
+def ctx_scatter_sent(low, rows, ready=()):
+    low = after(low, *ready)
+    return [
+        ctx_swap(low[(at - 1) * rows : at * rows], 2 * at)
+        for at in range(1, lax.axis_size("ctx") // 2)
+    ]
+
+
+def ctx_scatter_sum(total, parts, finish=()):
+    for part in parts:
+        total = total + after(part, *finish).astype(F32)
     return total
-
-
-def ctx_gather_small(values):
-    chips = lax.axis_size("ctx") // 2
-    held, mask = values, 2
-    while mask < 2 * chips:
-        held = jnp.concatenate([held, ctx_swap(held, mask)], axis=0)
-        mask *= 2
-    return held, ctx_swap(held, 1)
 
 
 def chip_masks(side):
@@ -98,14 +106,17 @@
     return masks[1:] + masks[:1] if side else masks
 
 
-def ctx_gather_halves(first, second, wait=lambda values: values, last=lambda values: values):
+def ctx_gather_halves(
+    first, second, wait=lambda values: values, last=lambda values: values, begun=None
+):
     held, offsets = [first[None], second[None]], [[0], [0]]
     steps = len(chip_masks(0))
     for step in range(steps):
         sent = []
         for side in range(2):
             mask = chip_masks(side)[step]
-            sent.append((ctx_swap(held[side], mask), [at ^ mask for at in offsets[side]]))
+            got = begun[side] if begun and step == 0 else ctx_swap(held[side], mask)
+            sent.append((got, [at ^ mask for at in offsets[side]]))
         if step < steps - 1:
             for side in range(2):
                 held[side] = jnp.concatenate([held[side], wait(sent[side][0])], axis=0)
@@ -119,6 +130,25 @@
     return gathered
 
 
+def ctx_scatter_halves(even, odd, ready=(), finish=()):
+    chips = lax.axis_size("ctx") // 2
+    rows = even.shape[0] // chips
+    both = even.astype(F32) + ctx_swap(odd.astype(BF16), 1).astype(F32)
+    both = both.reshape(chips, 2, rows // 2, -1)
+    totals = []
+    for side in range(2):
+        blocks = {2 * at: both[at, side] for at in range(chips)}
+        for step, mask in enumerate(reversed(chip_masks(side))):
+            kept = [offset for offset in sorted(blocks) if not offset & mask]
+            sent = jnp.stack([blocks[offset ^ mask].astype(BF16) for offset in kept])
+            got = ctx_swap(after(sent, *ready) if step == 0 else sent, mask)
+            if len(kept) == 1:
+                got = after(got, *finish)
+            blocks = {offset: blocks[offset] + got[at].astype(F32) for at, offset in enumerate(kept)}
+        totals.append(blocks[0])
+    return jnp.concatenate(totals, axis=0)
+
+
 def in_order(parts, parity):
     blocks = {
         offset: values[at]
@@ -178,12 +208,8 @@
     return held
 
 
-def z_scatter_stacked(stacked):
-    for mask in reversed(z_masks(lax.axis_size("fsdp"))):
-        half = stacked.shape[0] // 2
-        sent = z_swap(stacked[half:].astype(BF16), mask)
-        stacked = stacked[:half].astype(F32) + sent.astype(F32)
-    return stacked[0]
+def z_sum_exchange(values):
+    return jnp.sum(lax.all_to_all(values, "fsdp", 0, 0, tiled=True), axis=0, dtype=F32)
 
 
 def z_gather_queued(values):
@@ -405,7 +431,7 @@
             ]
         for order in range(shape.fsdp_count):
             target = kv_target(shape, meta, block, order)
-            source = kv_source(shape, chip, order, slot, half)
+            source = kv_source(shape, chip, meta[1] ^ shape.offsets[order], slot, half)
             g_keys[parity][source, :HD] = (gkv_all[slot, target, :HD] * SCALE).astype(BF16)
             g_keys[parity][source, HD:] = gkv_all[slot, target, HD:].astype(BF16)
 
@@ -517,66 +543,31 @@
     )(meta, rows, bias, *parts)
 
 
-def hidden_grad_kernel(shape, meta, grads_ref, hidden_ref, *refs):
-    parts, (out_ref, sum_ref) = refs[:-2], refs[-2:]
-    at = pl.program_id(0)
-    weights = parts[0][0]
-    for part, start in zip(parts[1:], shape.part_starts(len(parts))[1:]):
-        weights = jnp.where(at < start, weights, part[0])
+def hidden_grad_kernel(grads_ref, hidden_ref, first, second, out_ref, sum_ref):
     values = hidden_ref[...]
     tanh = gelu_parts(values)
     root = math.sqrt(2.0 / math.pi)
     slope = 0.5 * (1.0 + tanh) + (0.5 * root) * values * (1.0 - tanh * tanh) * (
         1.0 + (3.0 * 0.044715) * (values * values)
     )
-    low = (mm_t(grads_ref[...], weights) * slope).astype(BF16)
+    width = first.shape[1]
+    grads = mm_t(grads_ref[:, :width], first[...]) + mm_t(grads_ref[:, width:], second[...])
+    low = (grads * slope).astype(BF16)
     out_ref[...] = low
     sum_ref[...] = jnp.sum(low.astype(F32), axis=0, keepdims=True)
 
 
-def relative(shape, meta, at):
-    place = shape.offsets[0]
-    for index, offset in enumerate(shape.offsets):
-        place = jnp.where(at == index, offset, place)
-    return meta[1] ^ place
-
-
-def feed_hidden_grad(shape, meta, grads, hidden, parts):
+def feed_hidden_grad(grads, hidden, weights):
     count, width = grads.shape
-    half, unit, _ = parts[0].shape
-    if unit % 128:
-        weights = jnp.zeros((2 * half, unit, width), BF16)
-        for at, offset in enumerate(shape.offsets):
-            weights = lax.dynamic_update_index_in_dim(
-                weights, block_of(shape, parts, at), meta[1] ^ offset, 0
-            )
-        pull = jax.vjp(gelu_tanh, hidden)[1]
-        out = pull(mm_t(grads, weights.reshape(-1, width)))[0].astype(BF16)
-        return out, jnp.sum(out, axis=0, dtype=F32, keepdims=True)
-    columns = 2 * half * unit
-    place = lambda i, m: (0, relative(shape, m, i))
+    columns = hidden.shape[1]
+    tile = 256
+    place = pl.BlockSpec((count, tile), lambda i: (0, i))
     return pl.pallas_call(
-        functools.partial(hidden_grad_kernel, shape),
-        grid_spec=pltpu.PrefetchScalarGridSpec(
-            num_scalar_prefetch=1,
-            grid=(2 * half,),
-            in_specs=[
-                pl.BlockSpec((count, width), lambda i, m: (0, 0)),
-                pl.BlockSpec((count, unit), place),
-                *[
-                    pl.BlockSpec(
-                        (1, unit, width),
-                        lambda i, m, start=start, last=part.shape[0] - 1: (
-                            jnp.clip(i - start, 0, last),
-                            0,
-                            0,
-                        ),
-                    )
-                    for part, start in zip(parts, shape.part_starts(len(parts)))
-                ],
-            ],
-            out_specs=[pl.BlockSpec((count, unit), place), pl.BlockSpec((1, unit), place)],
-        ),
+        hidden_grad_kernel,
+        grid=(columns // tile,),
+        in_specs=[pl.BlockSpec((count, width), lambda i: (0, 0)), place]
+        + [pl.BlockSpec((tile, width // 2), lambda i: (i, 0))] * 2,
+        out_specs=[place, pl.BlockSpec((1, tile), lambda i: (0, i))],
         out_shape=[
             jax.ShapeDtypeStruct((count, columns), BF16),
             jax.ShapeDtypeStruct((1, columns), F32),
@@ -588,47 +579,84 @@
             bytes_accessed=2 * (count * width + width * columns) + 6 * count * columns,
         ),
         name="feed_hidden_grad",
-    )(meta, grads, hidden, *parts)
-
-
-def feed_blocks_kernel(shape, grad, meta, rows_ref, *refs):
+    )(grads, hidden, *weights)
+
+
+def feed_late_kernel(steps, rows_ref, first, second, norm_ref, grads_ref, even_ref, odd_ref, *d_refs):
+    at = pl.program_id(0)
+    width = first.shape[1]
+    for side, out_ref in enumerate((even_ref, odd_ref)):
+
+        @pl.when(at // steps == side)
+        def _(out_ref=out_ref):
+            out_ref[:, :width] = mm(rows_ref[...], first[...]).astype(BF16)
+            out_ref[:, width:] = mm(rows_ref[...], second[...]).astype(BF16)
+
+    @pl.when(at >= 2 * steps)
+    def _():
+        columns = d_refs[0].shape[1]
+        for part, out_ref in enumerate(d_refs):
+            out_ref[...] = mm_rows(
+                norm_ref[...], grads_ref[:, part * columns : (part + 1) * columns]
+            ).astype(BF16)
+
+
+def feed_late(rows, weights, norm, grads):
+    depth, half_width = weights[0].shape
+    count, tile = rows.shape[0] // 2, 256
+    steps = count // tile
+    width, columns = norm.shape[1], grads.shape[1]
+    last = 2 * steps - 1
+    d_block = pl.BlockSpec((tile, columns // 2), lambda i: (jnp.maximum(i - last - 1, 0), 0))
+    return pl.pallas_call(
+        functools.partial(feed_late_kernel, steps),
+        grid=(2 * steps + width // tile,),
+        in_specs=[
+            pl.BlockSpec((tile, depth), lambda i: (jnp.minimum(i, last), 0)),
+            pl.BlockSpec((depth, half_width), lambda i: (0, 0)),
+            pl.BlockSpec((depth, half_width), lambda i: (0, 0)),
+            pl.BlockSpec((2 * count, tile), lambda i: (0, jnp.maximum(i - last - 1, 0))),
+            pl.BlockSpec((2 * count, columns), lambda i: (0, 0)),
+        ],
+        out_specs=[
+            pl.BlockSpec((tile, 2 * half_width), lambda i: (jnp.minimum(i, steps - 1), 0)),
+            pl.BlockSpec((tile, 2 * half_width), lambda i: (jnp.clip(i - steps, 0, steps - 1), 0)),
+            d_block,
+            d_block,
+        ],
+        out_shape=[jax.ShapeDtypeStruct((count, 2 * half_width), BF16)] * 2
+        + [jax.ShapeDtypeStruct((width, columns // 2), BF16)] * 2,
+        compiler_params=pltpu.CompilerParams(vmem_limit_bytes=56 * 2**20),
+        cost_estimate=pl.CostEstimate(
+            flops=8 * count * depth * half_width + 4 * count * width * columns,
+            transcendentals=0,
+            bytes_accessed=2 * (6 * count * half_width + 2 * depth * half_width + 4 * count * width),
+        ),
+        name="feed_late",
+    )(rows, *weights, norm, grads)
+
+
+def feed_grad_kernel(shape, meta, rows_ref, *refs):
     parts, out_ref = refs[:-1], refs[-1]
     for at, offset in enumerate(shape.offsets):
         block = block_of(shape, parts, at)
         size = block.shape[0]
         part = pl.ds(pl.multiple_of((meta[1] ^ offset) * size, size), size)
-        if grad:
-            out_ref[:, part] = mm_t(rows_ref[...], block).astype(BF16)
-        elif at == 0:
-            total = mm(rows_ref[:, part], block)
-        else:
-            total = total + mm(rows_ref[:, part], block)
-    if not grad:
-        out_ref[...] = total.astype(BF16)
-
-
-def feed_blocks(shape, meta, rows, parts, side, count, grad):
-    half, size, columns = parts[0].shape
-    width = 2 * half * size if grad else columns
+        out_ref[:, part] = mm_t(rows_ref[...], block).astype(BF16)
+
+
+def feed_grad(shape, meta, rows, parts, side, count):
+    width = shape.fsdp_count * parts[0].shape[1]
     tile = 256
-    if not grad and size % 128:
-        weights = jnp.zeros((2 * half, size, columns), BF16)
-        for at, offset in enumerate(shape.offsets):
-            weights = lax.dynamic_update_index_in_dim(
-                weights, block_of(shape, parts, at), meta[1] ^ offset, 0
-            )
-        rows = rows[side * count : (side + 1) * count]
-        return mm(rows, weights.reshape(-1, columns)).astype(BF16)
     steps = count // tile
-    weights = [pl.BlockSpec(part.shape, lambda i, m: (0, 0, 0)) for part in parts]
     return pl.pallas_call(
-        functools.partial(feed_blocks_kernel, shape, grad),
+        functools.partial(feed_grad_kernel, shape),
         grid_spec=pltpu.PrefetchScalarGridSpec(
             num_scalar_prefetch=1,
             grid=(steps,),
             in_specs=[
                 pl.BlockSpec((tile, rows.shape[1]), lambda i, m: (side * steps + i, 0)),
-                *weights,
+                *[pl.BlockSpec(part.shape, lambda i, m: (0, 0, 0)) for part in parts],
             ],
             out_specs=pl.BlockSpec((tile, width), lambda i, m: (i, 0)),
         ),
@@ -639,7 +667,7 @@
             transcendentals=0,
             bytes_accessed=2 * (count + width) * rows.shape[1] + 2 * count * width,
         ),
-        name="feed_grad_rows" if grad else "feed_rows",
+        name="feed_grad",
     )(meta, rows, *parts)
 
 
@@ -733,8 +761,8 @@
 
 def spread_columns(meta, gathered, groups, joined, extra=None):
     pieces = len(gathered)
-    rows = gathered[0][0][0].shape[1]
-    width = gathered[0][0][0].shape[2] // groups
+    rows, columns = gathered[0][0][0].shape[1:]
+    width = columns // groups if joined else columns // pieces
     count = sum(len(order) for _, order in gathered[0])
     if width % 128:
         results = []
@@ -748,19 +776,30 @@
         return [jnp.concatenate(results, axis=1)]
     members, moves = [], []
     for piece, parts in enumerate(gathered):
+        if not joined:
+            members = []
         for values, order in parts:
             for at, offset in enumerate(order):
                 for group in range(groups):
                     start = ((piece if joined else 0) * groups + group) * count * width
-                    columns = slice(group * width, (group + 1) * width)
-                    out = 0 if joined else piece
-                    moves.append((len(members), at, columns, offset, out, start, width, width))
+                    source = (group if joined else piece) * width
+                    moves.append(
+                        (
+                            len(members),
+                            at,
+                            slice(source, source + width),
+                            offset,
+                            0 if joined else piece,
+                            start,
+                            width,
+                            width,
+                        )
+                    )
             members.append(values)
-    sizes = [groups * count * width * pieces] if joined else [groups * count * width] * pieces
+    sizes = [groups * count * width * pieces] if joined else [count * width] * pieces
     tile = min(rows, 64)
     in_specs = [
-        pl.BlockSpec((member.shape[0], tile, groups * width), lambda i, m: (0, i, 0))
-        for member in members
+        pl.BlockSpec((member.shape[0], tile, columns), lambda i, m: (0, i, 0)) for member in members
     ]
     extras = []
     if extra is not None:
@@ -900,7 +939,7 @@
     ).astype(BF16)
     proj_own = lax.dynamic_slice_in_dim(w_proj, c_at * unit, unit, axis=0).astype(BF16)
     out_halves = out_parts[0], jnp.concatenate(out_parts[1:], axis=0)
-    fc_steps = z_gather_steps(after(fc_own, *out_parts))
+    fc_steps = z_gather_steps(after(fc_own, out_parts[0]))
 
     a_even = layer_norm(x_even.astype(F32), gain_one, shift_one)[0].astype(BF16)
     a_odd = layer_norm(x_odd.astype(F32), gain_one, shift_one)[0].astype(BF16)
@@ -921,7 +960,10 @@
     o_own = ctx_exchange(o_heads.reshape(ctx_count, tokens, q_width))
     o_own = jnp.transpose(o_own, (1, 0, 2)).reshape(tokens, width)
     fc_parts = z_gather_finish(*fc_steps)
-    proj_held = z_gather_held(after(proj_own, fc_parts[-1]))
+    proj_own = after(proj_own, fc_parts[-1])
+    w_p = [
+        z_gather_queued(proj_own[:, at * width // 2 : (at + 1) * width // 2]) for at in range(2)
+    ]
     o_own = after(o_own, *fc_steps)
     middle = x_own + (times_blocks(meta, o_own, out_blocks, out_layout, False) + out_bias)
     second_norm, normed_two, inverse_two = layer_norm(middle, gain_two, shift_two)
@@ -933,24 +975,24 @@
     o_even, o_odd = in_order(o_parts, 0), in_order(o_parts, 1)
     gm_all = jnp.concatenate([in_order(gm_parts, 0), in_order(gm_parts, 1)], axis=0)
     gm_all, o_even, o_odd = lax.optimization_barrier((gm_all, o_even, o_odd))
-    cn_all = after(jnp.concatenate([cn_even, cn_odd], axis=0), proj_held)
-    proj_parts = [proj_held, z_swap(proj_held, 1)]
+    cn_all = jnp.concatenate([cn_even, cn_odd], axis=0)
     half_rows = chips * tokens
     hidden, act = feed_hidden(shape, meta, cn_all, fc_parts, fc_bias.reshape(1, -1))
-    act_ready = after(act, *proj_parts)
-    parts = [slice(at * width // 2, (at + 1) * width // 2) for at in range(2)]
-    d_proj = [z_scatter_queued(mm_rows(act_ready, gm_all[:, part]).astype(BF16)) for part in parts]
-    g_hidden, g_bias_fc = feed_hidden_grad(
-        shape, meta, gm_all, hidden, proj_parts
-    )
-    g_odd = feed_blocks(shape, meta, g_hidden, fc_parts, 1, half_rows, True)
-    g_even = feed_blocks(shape, meta, after(g_hidden, g_odd), fc_parts, 0, half_rows, True)
-    grad_second = ctx_scatter(g_even, g_odd)
-    cn_late, act_late = after(cn_all, g_even), after(act, g_even)
-    own_width = fsdp_count * unit
-    parts = [slice(at * own_width // 2, (at + 1) * own_width // 2) for at in range(2)]
-    d_fc = [z_scatter_queued(mm_rows(cn_late, g_hidden[:, part]).astype(BF16)) for part in parts]
-    mlp = [feed_blocks(shape, meta, act_late, proj_parts, side, half_rows, False) for side in range(2)]
+    d_proj = mm_rows(act, gm_all).astype(BF16)
+    g_hidden, g_bias_fc = feed_hidden_grad(gm_all, hidden, w_p)
+    g_odd = feed_grad(shape, meta, g_hidden, fc_parts, 1, half_rows)
+    g_even = feed_grad(shape, meta, after(g_hidden, g_odd), fc_parts, 0, half_rows)
+    g_total, g_low = ctx_scatter_cores(g_even, g_odd)
+    cn_late, act_late, g_low = lax.optimization_barrier((cn_all, act, g_low))
+    g_parts = ctx_scatter_sent(g_low, tokens)
+    late = feed_late(act_late, w_p, cn_late, g_hidden)
+    g_parts, late = lax.optimization_barrier((g_parts, late))
+    grad_second = ctx_scatter_sum(g_total, g_parts)
+    d_proj = [
+        z_scatter_queued(after(part, *w_p)) for part in (d_proj[:, : width // 2], d_proj[:, width // 2 :])
+    ]
+    d_fc = [z_scatter_queued(part) for part in late[2:]]
+    r_total, r_low = ctx_scatter_cores(*late[:2])
 
     grad_mid_norm, grad_gain_two, grad_shift_two = norm_backward(
         grad_second, normed_two, inverse_two, gain_two
@@ -965,41 +1007,67 @@
         ],
         axis=2,
     )
-    grads = ctx_exchange(jnp.transpose(grads, (1, 0, 2))).reshape(ctx_count * tokens, 2 * q_width)
+    grads_sent = jnp.transpose(grads, (1, 0, 2))
+    grads = ctx_exchange(grads_sent).reshape(ctx_count * tokens, 2 * q_width)
+    grads, r_total = lax.optimization_barrier((grads, r_total))
 
     gq_even, gq_odd, gkv_even, gkv_odd, ga_even, ga_odd = attend_grad(
         shape, meta, q_all, kv_all, o_t, lse, grads
     )
-    result = ctx_scatter(*mlp, [grad_second], [gq_even])
-    result = (middle + (result + proj_bias)).astype(BF16)
-    gkv_plane = ctx_scatter(gkv_even, gkv_odd).reshape(fsdp_count, tokens, 2 * HD)
-    gkv_low = z_scatter_stacked(gkv_plane).astype(BF16)
-    gkv_even, gkv_odd = ctx_gather_small(gkv_low)
-    grad_first = ctx_scatter(
-        mm_t(gq_even, w_q), mm_t(gq_odd, w_q), [gkv_plane, result], [gkv_even, gkv_odd]
-    )
+    first_sent = [ctx_swap(part[None], chip_masks(side)[0]) for side, part in enumerate(d_proj)]
+    r_parts = ctx_scatter_sent(r_low, tokens, [grads_sent])
+    gkv_odd, first_sent, r_parts = lax.optimization_barrier((gkv_odd, first_sent, r_parts))
+    result = (middle + (ctx_scatter_sum(r_total, r_parts) + proj_bias)).astype(BF16)
+    gkv_plane = ctx_scatter(gkv_even, gkv_odd)
+    d_proj = ctx_gather_halves(
+        *d_proj, wait=lambda part: after(part, gkv_plane), begun=first_sent
+    )
+    gkv_low = z_sum_exchange(gkv_plane.astype(BF16).reshape(fsdp_count, tokens, 2 * HD)).astype(BF16)
+    gkv_all = ctx_exchange(jnp.broadcast_to(gkv_low[None], (ctx_count,) + gkv_low.shape))
+    gl_total, gl_low = ctx_scatter_cores(mm_t(gq_even, w_q), mm_t(gq_odd, w_q))
+    gl_parts = ctx_scatter_sent(gl_low, tokens, [gkv_plane])
+    gkv_all, gl_parts = lax.optimization_barrier((gkv_all, gl_parts))
+    (gkv_all,) = place_blocks(
+        meta,
+        [gkv_all],
+        [(ctx_count * tokens, 2 * HD)],
+        lambda ref: [
+            (
+                0,
+                (ref[0] ^ (2 * chip + parity),),
+                0,
+                (pl.ds((parity * chips + chip) * tokens, tokens),),
+            )
+            for parity in range(2)
+            for chip in range(chips)
+        ],
+        "place_keys",
+    )
+    gkv_even, gkv_odd = gkv_all[: chips * tokens], gkv_all[chips * tokens :]
+    grad_first = ctx_scatter_sum(gl_total, gl_parts)
     grad_in_norm, grad_gain_one, grad_shift_one = norm_backward(
         grad_first + mm_t(gkv_low, w_kv), normed_one, inverse_one, gain_one
     )
     grad_inputs = grad_middle + grad_in_norm
 
-    d_proj = ctx_gather_halves(
-        *[after(part, grads) for part in d_proj], wait=lambda part: after(part, gkv_plane)
-    )
     grad_w_proj = spread_rows(meta, d_proj)
     d_fc = ctx_gather_halves(
-        *[after(part, gkv_low) for part in d_fc], wait=lambda part: after(part, grad_first)
+        *[after(part, gkv_low) for part in d_fc], last=lambda part: after(part, grad_w_proj)
     )
     (grad_w_fc,) = spread_columns(meta, d_fc, fsdp_count // 2, True)
     d_q = mm_rows(a_even, gq_even) + mm_rows(a_odd, gq_odd)
     d_out = mm_rows(o_even, ga_even) + mm_rows(o_odd, ga_odd)
-    d_pair = z_scatter_queued(jnp.concatenate([d_q, d_out], axis=1).astype(BF16))
+    d_pair = with_layout_constraint(
+        jnp.concatenate([d_q, d_out], axis=1).astype(BF16), Layout(major_to_minor=(0, 1))
+    )
+    d_pair = z_scatter_queued(d_pair)
     d_kv = (mm_rows(a_even, gkv_even) + mm_rows(a_odd, gkv_odd)).astype(BF16)
     d_kv = z_scatter_queued(d_kv).astype(F32)
-    d_pair = ctx_gather_halves(
-        d_pair[:, :q_width], d_pair[:, q_width:], wait=lambda part: after(part, grad_w_proj)
-    )
-    grad_w_qkv, grad_w_out = spread_columns(meta, d_pair, 1, False, d_kv)
+    d_pair = [
+        (values.reshape(chips, shard, 2 * q_width), [2 * at + parity for at in range(chips)])
+        for parity, values in enumerate(ctx_gather(d_pair))
+    ]
+    grad_w_qkv, grad_w_out = spread_columns(meta, [d_pair] * 2, 1, False, d_kv)
 
     def column_sum(*parts):
         return sum(jnp.sum(part, axis=0, dtype=F32) for part in parts)
@@ -1024,11 +1092,9 @@
     stacked = jnp.concatenate(
         [member.reshape(fsdp_count, -1) for member in g_vectors], axis=1
     ).astype(BF16)
-    stacked = jnp.stack(
-        [lax.dynamic_index_in_dim(stacked, z_at ^ at, 0, keepdims=True) for at in shape.offsets]
-    )
-    own = z_scatter_stacked(stacked).astype(BF16)
-    summed = column_sum(*ctx_gather_small(own))
+    own = z_sum_exchange(stacked).astype(BF16)
+    own = ctx_exchange(jnp.broadcast_to(own[None], (ctx_count,) + own.shape))
+    summed = jnp.sum(own, axis=0, dtype=F32)
     vector_grads, start = [], 0
     for size in sizes:
         vector_grads.append(summed[start : start + size].astype(BF16).astype(F32))

time: 680 us -> 627 us (0.922)
  starting transfers between devices: 136 us -> 103 us
  matrix products: 46.2 us -> 26.5 us
  waiting for transfers between devices: 234 us -> 219 us
  local copies, waits for them, and re-layouts: 43.2 us -> 57.1 us
    reduce_scatter x6, waiting for transfers between devices: 0.1 us -> 46.2 us  [z_scatter_queued(): return lax.psum_scatter(values, 'fsdp', scatter_dimension=0, tiled=True)]
    ppermute x74 -> x64, waiting for transfers between devices: 148 us -> 105 us  [ctx_swap(): return lax.ppermute(values, 'ctx', [(at, at ^ mask) for at in range(count)])]
    ppermute x20 -> x14, starting transfers between devices: 61.1 us -> 26.3 us  [z_swap(): lax.ppermute(values, 'fsdp', [(at, at ^ mask) for at in range(count)])]
    ppermute x20 -> x14, waiting for transfers between devices: 77.7 us -> 50 us  [z_swap(): lax.ppermute(values, 'fsdp', [(at, at ^ mask) for at in range(count)])]
    dot_general x10 -> x7, matrix products: 32.9 us -> 14.6 us  [mm_rows(): lax.dot_general(left, right, (((0,), (0,)), ((), ())), preferred_element_...]
    unnamed x177 -> x148, local copies, waits for them, and re-layouts: 17.1 us -> 29.5 us
    all_to_all x0 -> x2, waiting for transfers between devices: none -> 11.5 us  [z_sum_exchange(): lax.all_to_all(values, 'fsdp', 0, 0, tiled=True)]
    reduce_scatter x6, starting transfers between devices: 11.8 us -> 0.88 us  [z_scatter_queued(): return lax.psum_scatter(values, 'fsdp', scatter_dimension=0, tiled=True)]
  transfers between devices with their start and end apart: 102 -> 92, of which waited for: 43 -> 36; matrix products, arithmetic and copies ran while one was open for 21% -> 21% of each run, Pallas kernels for 18% -> 20%
where the time goes in v3:
time: 627 us; the launch traced here: 616 us
  waiting for transfers between devices  219 us (35%)
  Pallas kernels  133 us (21%)
  starting transfers between devices  103 us (16%)
  other arithmetic  60.3 us (10%)
  local copies, waits for them, and re-layouts  57.1 us (9%)
  matrix products  26.5 us (4%)
  between operations  16.7 us (3%)
    ppermute x64, waiting for transfers between devices, ctx_swap(): return lax.ppermute(values, 'ctx', [(at, at ^ mask) for at in range(count)])  105 us
    ppermute x64, starting transfers between devices, ctx_swap(): return lax.ppermute(values, 'ctx', [(at, at ^ mask) for at in range(count)])  52.6 us
    ppermute x14, waiting for transfers between devices, z_swap(): lax.ppermute(values, 'fsdp', [(at, at ^ mask) for at in range(count)])  50 us
    reduce_scatter x6, waiting for transfers between devices, z_scatter_queued(): return lax.psum_scatter(values, 'fsdp', scatter_dimension=0, tiled=True)  46.2 us
    unnamed x148, local copies, waits for them, and re-layouts  29.5 us
    ppermute x14, starting transfers between devices, z_swap(): lax.ppermute(values, 'fsdp', [(at, at ^ mask) for at in range(count)])  26.3 us
    pallas_call x2, Pallas kernels, spread_columns(): pl.pallas_call(functools.partial(spread_kernel, moves, extras, len(sizes)...  18.2 us
    pallas_call x1, Pallas kernels, feed_late(): pl.pallas_call(functools.partial(feed_late_kernel, steps), grid=(2 * step...  18 us
  transfers between devices with their start and end apart: 92, of which 36 were waited for; matrix products, arithmetic and copies ran while one was open for 21% of the time, Pallas kernels for 20%

profile of v3, /device:TPU:0, one launch (start us, length us, event | category | flops | bytes accessed | tf_op | source)
XLA Modules:
  0.0 616.0 jit_solution(12382922797728831397)
XLA Ops:
  8.8 5.1 collective-permute-start.3
  17.3 9.5 %collective-permute-done.3 = bf16[1,512,512]{2,1,0:T(8,128)(2,1)} collective-permute-done((bf16[1,512,512]{2,1,0:T(8,128)(2,1)S(1)}, bf16[1,512,512]{2,1,0:T(8,128)(2,1)}, u32[]{:S(2)}, u32[]{:S(2)}) %collective-permute-start.3) | collective-permute-done | bytes 524320 | tf_op jit(solution)/shard_map/ppermute | solution.py:183
  26.8 10.0 %collective-permute-start.5 = (bf16[1,512,512]{2,1,0:T(8,128)(2,1)}, bf16[1,512,512]{2,1,0:T(8,128)(2,1)S(1)}, u32[]{:S(2)}, u32[]{:S(2)}) collective-permute-start(bf16[1,512,512]{2,1,0:T(8,128)(2,1)} %collective-permute-done.3), channel_id=1, source_target_pairs={{0,1},{1,0},{2,3},{3,2},{4,5},{5,4},{6,7},{7,6},{8,9},{9,8},{10,11... | collective-permute-start | bytes 1572872 | tf_op jit(solution)/shard_map/ppermute | solution.py:183
  43.5 7.1 %collective-permute-done.6 = bf16[1,48,128]{2,1,0:T(8,128)(2,1)S(1)} collective-permute-done((bf16[1,48,128]{2,1,0:T(8,128)(2,1)S(1)}, bf16[1,48,128]{2,1,0:T(8,128)(2,1)S(1)}, u32[]{:S(2)}, u32[]{:S(2)}) %collective-permute-start.6) | collective-permute-done | bytes 12320 | tf_op jit(solution)/shard_map/ppermute | solution.py:183
  55.8 3.7 place_first.1
  64.9 3.4 collective-permute-done.9
  78.8 4.0 collective-permute-done.14
  88.0 3.5 collective-permute-start.24
  93.8 25.5 %collective-permute-done.24 = bf16[1,512,256]{2,1,0:T(8,128)(2,1)S(1)} collective-permute-done((bf16[1,512,256]{2,1,0:T(8,128)(2,1)S(1)}, bf16[1,512,256]{2,1,0:T(8,128)(2,1)S(1)}, u32[]{:S(2)}, u32[]{:S(2)}) %collective-permute-start.24) | collective-permute-done | bytes 262176 | tf_op jit(solution)/shard_map/ppermute | solution.py:183
  122.9 10.4 %collective-permute-done.25 = bf16[1,2,512,256]{3,2,1,0:T(8,128)(2,1)S(1)} collective-permute-done((bf16[1,2,512,256]{3,2,1,0:T(8,128)(2,1)S(1)}, bf16[1,2,512,256]{3,2,1,0:T(8,128)(2,1)S(1)}, u32[]{:S(2)}, u32[]{:S(2)}) %collective-permute-start.25) | collective-permute-done | bytes 524320 | tf_op jit(solution)/shard_map/ppermute | solution.py:59
  141.7 14.4 %attend.1 = (bf16[1024,256]{1,0:T(8,128)(2,1)}, bf16[2,1024,128]{2,1,0:T(8,128)(2,1)}, bf16[2,2048,256]{2,1,0:T(8,128)(2,1)}, f32[8,128,256]{2,1,0:T(8,128)}, f32[8,1,256]{2,1,0:T(1,128)}) custom-call(s32[14]{0:T(128)} %pad_add_fusion.meta, bf16[512,256]{1,0:T(8,128)(2,1)} %fusion.15.q_even, bf16[512,256]{1,0:T(8,128)(2,1)} %fusion.16.q_odd, ...), custom_call_target="tpu_custom_call" | custom-call | flops 1073741824 | bytes 8388608 | tf_op jit(solution)/shard_map/attend/pallas_call | solution.py:444
  156.1 4.3 collective-permute-done.26.refs_5_
  160.9 4.1 all-to-all-start
  170.9 3.9 all-to-all-done
  179.5 6.9 %branch.1 = f32[128,2048]{1,0:T(8,128)} custom-call(s32[14]{0:T(128)} %pad_add_fusion.meta, bf16[128,2048]{1,0:T(8,128)(2,1)} %bitcast.157, bf16[2,2,512,256]{3,2,1,0:T(8,128)(2,1)} %copy-done.12, bf16[2,2,512,256]{3,2,1,0:T(8,128)(2,1)} %collective-permute-done.20.refs_1_, bf16[2,2,512,256]{3,2,1,0:T(8,128)(2,1)} %collective-permute-done.21.refs_2_, ...), custom_call_target="tpu_custom_call" | custom-call | flops 1073741824 | bytes 8388608 | tf_op jit(solution)/shard_map/branch/pallas_call | solution.py:690
  193.1 10.3 %collective-permute-done.30 = bf16[128,2048]{1,0:T(8,128)(2,1)S(1)} collective-permute-done((bf16[128,2048]{1,0:T(8,128)(2,1)S(1)}, bf16[128,2048]{1,0:T(8,128)(2,1)S(1)}, u32[]{:S(2)}, u32[]{:S(2)}) %collective-permute-start.30) | collective-permute-done | bytes 524320 | tf_op jit(solution)/shard_map/ppermute | solution.py:59
  204.5 9.4 %collective-permute-done.31 = bf16[128,2048]{1,0:T(8,128)(2,1)S(1)} collective-permute-done((bf16[128,2048]{1,0:T(8,128)(2,1)S(1)}, bf16[128,2048]{1,0:T(8,128)(2,1)S(1)}, u32[]{:S(2)}, u32[]{:S(2)}) %collective-permute-start.31) | collective-permute-done | bytes 524320 | tf_op jit(solution)/shard_map/ppermute | solution.py:59
  223.8 9.2 %collective-permute-done.38 = bf16[1,128,2048]{2,1,0:T(8,128)(2,1)} collective-permute-done((bf16[1,128,2048]{2,1,0:T(8,128)(2,1)}, bf16[1,128,2048]{2,1,0:T(8,128)(2,1)}, u32[]{:S(2)}, u32[]{:S(2)}) %collective-permute-start.38) | collective-permute-done | bytes 524320 | tf_op jit(solution)/shard_map/ppermute | solution.py:59
  242.3 10.7 %feed_hidden.1 = (f32[1024,1024]{1,0:T(8,128)}, bf16[1024,1024]{1,0:T(8,128)(2,1)}) custom-call(s32[14]{0:T(128)} %pad_add_fusion.meta, bf16[1024,2048]{1,0:T(8,128)(2,1)} %constant_dynamic-update-slice_fusion.5.rows_ref.norm_ref, f32[1,1024]{1,0:T(1,128)} %bitcast.219, bf16[2,512,1024]{2,1,0:T(8,128)(2,1)} %pad_maximum_fusion.1.refs_0_, ...), custom_call_target="tpu_custom_call" | custom-call | flops 4294967296 | bytes 14680064 | tf_op jit(solution)/shard_map/feed_hidden/pallas_call | solution.py:520
  254.9 5.1 collective-permute-done.39
  260.0 3.2 collective-permute-done.35
  275.5 4.9 convolution_convert_fusion
  283.7 10.7 %feed_hidden_grad.1 = (bf16[1024,1024]{1,0:T(8,128)(2,1)}, f32[1,1024]{1,0:T(1,128)}) custom-call(bf16[1024,2048]{1,0:T(8,128)(2,1)} %copy-done.45, f32[1024,1024]{1,0:T(8,128)} %get-tuple-element.111.hidden_ref, bf16[1024,1024]{1,0:T(8,128)(2,1)} %all-gather.3.cloned.1.call-done.first, bf16[1024,1024]{1,0:T(8,128)(2,1)} %all-gather.5.cloned.1.call-done.second), custom_call_target="tpu_custom_call" | custom-call | flops 4294967296 | bytes 14680064 | tf_op jit(solution)/shard_map/feed_hidden_grad/pallas_call | solution.py:565
  294.4 6.6 %feed_grad.2 = bf16[512,2048]{1,0:T(8,128)(2,1)} custom-call(s32[14]{0:T(128)} %pad_add_fusion.meta, bf16[1024,1024]{1,0:T(8,128)(2,1)} %get-tuple-element.114.rows_ref.grads_ref, bf16[2,512,1024]{2,1,0:T(8,128)(2,1)} %pad_maximum_fusion.1.refs_0_, bf16[1,512,1024]{2,1,0:T(8,128)(2,1)} %collective-permute-done.18.refs_1_, ...), custom_call_target="tpu_custom_call" | custom-call | flops 2147483648 | bytes 7340032 | tf_op jit(solution)/shard_map/feed_grad/pallas_call | solution.py:652
  301.6 6.6 %feed_grad.3 = bf16[512,2048]{1,0:T(8,128)(2,1)} custom-call(s32[14]{0:T(128)} %pad_add_fusion.meta, bf16[1024,1024]{1,0:T(8,128)(2,1)} %get-tuple-element.114.rows_ref.grads_ref, bf16[2,512,1024]{2,1,0:T(8,128)(2,1)} %pad_maximum_fusion.1.refs_0_, bf16[1,512,1024]{2,1,0:T(8,128)(2,1)} %collective-permute-done.18.refs_1_, ...), custom_call_target="tpu_custom_call" | custom-call | flops 2147483648 | bytes 7340032 | tf_op jit(solution)/shard_map/feed_grad/pallas_call | solution.py:652
  316.2 18.0 %feed_late.1 = (bf16[512,2048]{1,0:T(8,128)(2,1)}, bf16[512,2048]{1,0:T(8,128)(2,1)}, bf16[2048,512]{1,0:T(8,128)(2,1)}, bf16[2048,512]{1,0:T(8,128)(2,1)}) custom-call(bf16[1024,1024]{1,0:T(8,128)(2,1)} %get-tuple-element.117.rows_ref, bf16[1024,1024]{1,0:T(8,128)(2,1)} %all-gather.3.cloned.1.call-done.first, ...), custom_call_target="tpu_custom_call" | custom-call | flops 8589934592 | bytes 18874368 | tf_op jit(solution)/shard_map/feed_late/pallas_call | solution.py:611
  334.2 4.5 collective-permute-done.44
  343.8 8.2 %branch_grad.1 = f32[128,2048]{1,0:T(8,128)} custom-call(s32[14]{0:T(128)} %pad_add_fusion.meta, bf16[128,2048]{1,0:T(8,128)(2,1)} %get-tuple-element.251.rows_ref, bf16[2,2,512,256]{3,2,1,0:T(8,128)(2,1)} %copy-done.12, bf16[2,2,512,256]{3,2,1,0:T(8,128)(2,1)} %collective-permute-done.20.refs_1_, bf16[2,2,512,256]{3,2,1,0:T(8,128)(2,1)} %collective-permute-done.21.refs_2_, ...), custom_call_target="tpu_custom_call" | custom-call | flops 1073741824 | bytes 8388608 | tf_op jit(solution)/shard_map/branch_grad/pallas_call | solution.py:690
  354.5 3.6 all-to-all-start.1
  360.3 11.2 %reduce-scatter.7.cloned.1.call-done = bf16[256,1024]{1,0:T(8,128)(2,1)} async-done(((bf16[1024,1024]{1,0:T(8,128)(2,1)}), bf16[256,1024]{1,0:T(8,128)(2,1)}) %reduce-scatter.7.cloned.1.call-update) | async-done | bytes 524304 | tf_op jit(solution)/shard_map/reduce_scatter | solution.py:220
  383.9 16.3 %attend_grad.1 = (bf16[512,256]{1,0:T(8,128)(2,1)}, bf16[512,256]{1,0:T(8,128)(2,1)}, bf16[2048,256]{1,0:T(8,128)(2,1)}, bf16[2048,256]{1,0:T(8,128)(2,1)}, bf16...) custom-call(s32[14]{0:T(128)} %pad_add_fusion.meta, bf16[2,1024,128]{2,1,0:T(8,128)(2,1)} %get-tuple-element.129.q_all, ...), custom_call_target="tpu_custom_call" | custom-call | flops 2684354560 | bytes 10485760 | tf_op jit(solution)/shard_map/attend_grad/pallas_call | solution.py:471
  418.9 4.9 collective-permute-done.54
  423.8 4.9 collective-permute-done.56
  430.8 4.0 all-to-all-start.2
  445.3 5.8 all-to-all-done.2
  452.1 14.4 %reduce-scatter.15.cloned.1.call-done = bf16[512,512]{1,0:T(8,128)(2,1)} async-done(((bf16[2048,512]{1,0:T(8,128)(2,1)}), bf16[512,512]{1,0:T(8,128)(2,1)}) %reduce-scatter.15.cloned.1.call-update) | async-done | bytes 524304 | tf_op jit(solution)/shard_map/reduce_scatter | solution.py:220
  467.4 4.1 all-to-all-start.3
  484.3 7.8 %collective-permute-done.64 = bf16[1,512,512]{2,1,0:T(8,128)(2,1)} collective-permute-done((bf16[1,512,512]{2,1,0:T(8,128)(2,1)}, bf16[1,512,512]{2,1,0:T(8,128)(2,1)}, u32[]{:S(2)}, u32[]{:S(2)}) %collective-permute-start.64) | collective-permute-done | bytes 524320 | tf_op jit(solution)/shard_map/ppermute | solution.py:59
  492.1 20.6 %reduce-scatter.11.cloned.1.call-done = bf16[512,512]{1,0:T(8,128)(2,1)} async-done(((bf16[2048,512]{1,0:T(8,128)(2,1)}), bf16[512,512]{1,0:T(8,128)(2,1)}) %reduce-scatter.11.cloned.1.call-update) | async-done | bytes 524304 | tf_op jit(solution)/shard_map/reduce_scatter | solution.py:220
  521.8 6.0 collective-permute-done.60
  540.0 10.0 %collective-permute-done.61 = bf16[512,512]{1,0:T(8,128)(2,1)S(1)} collective-permute-done((bf16[512,512]{1,0:T(8,128)(2,1)}, bf16[512,512]{1,0:T(8,128)(2,1)S(1)}, u32[]{:S(2)}, u32[]{:S(2)}) %collective-permute-start.61) | collective-permute-done | bytes 524320 | tf_op jit(solution)/shard_map/ppermute | solution.py:59
  552.3 4.0 fusion.28
  558.4 3.3 all-to-all-start.4
  561.7 5.6 all-to-all-done.4
  569.6 3.4 all-to-all-start.5
  574.8 10.4 %spread_rows.1 = f32[2048,2048]{1,0:T(8,128)} custom-call(s32[14]{0:T(128)S(1)} %copy-done.2, bf16[2,256,1024]{2,1,0:T(8,128)(2,1)S(1)} %pad_maximum_fusion.13.refs_0_, bf16[2,256,1024]{2,1,0:T(8,128)(2,1)} %collective-permute-done.66.refs_1_, bf16[2,256,1024]{2,1,0:T(8,128)(2,1)S(1)} %copy-done.1, bf16[2,256,1024]{2,1,0:T(8,128)(2,1)} %collective-permute-done.68.refs_3_, ...), custom_call_target="tpu_custom_call" | custom-call | tf_op jit(solution)/shard_map/spread_rows/pallas_call | solution.py:738
  590.5 10.4 %spread_columns.3 = f32[512,8192]{1,0:T(8,128)} custom-call(s32[14]{0:T(128)S(1)} %copy-done.2, bf16[2,512,512]{2,1,0:T(8,128)(2,1)S(1)} %pad_maximum_fusion.12.refs_0_, bf16[2,512,512]{2,1,0:T(8,128)(2,1)} %collective-permute-done.65.refs_1_, bf16[2,512,512]{2,1,0:T(8,128)(2,1)} %collective-permute-done.72.refs_2_, ...), custom_call_target="tpu_custom_call" | custom-call | tf_op jit(solution)/shard_map/spread_columns/pallas_call | solution.py:810
  600.9 7.9 %spread_columns.2 = (f32[512,2304]{1,0:T(8,128)}, f32[512,2048]{1,0:T(8,128)}) custom-call(s32[14]{0:T(128)S(1)} %copy-done.2, bf16[4,512,512]{2,1,0:T(8,128)(2,1)} %bitcast.43.refs_0_, bf16[4,512,512]{2,1,0:T(8,128)(2,1)} %bitcast.44.refs_1_, f32[512,256]{1,0:T(8,128)S(1)} %convert_element_type.417.refs_2_), custom_call_target="tpu_custom_call" | custom-call | tf_op jit(solution)/shard_map/spread_columns/pallas_call | solution.py:810
  (457 shorter events, 217.3 us)
Async XLA Ops:
  13.9 37.5 %collective-permute-start.4 = (bf16[1,512,512]{2,1,0:T(8,128)(2,1)S(1)}, bf16[1,512,512]{2,1,0:T(8,128)(2,1)S(1)}, u32[]{:S(2)}, u32[]{:S(2)}) collective-permute-start(bf16[1,512,512]{2,1,0:T(8,128)(2,1)S(1)} %pad_maximum_fusion.16), channel_id=1, source_target_pairs={{0,1},{1,0},{2,3},{3,2},{4,5},{5,4},{6,7},{7,6},{8,9},{9,8},{10,11... | collective-permute-start | bytes 1572872 | tf_op jit(solution)/shard_map/ppermute | solution.py:183
  13.9 54.4 %collective-permute-start.2 = (bf16[128,2048]{1,0:T(8,128)(2,1)S(1)}, bf16[128,2048]{1,0:T(8,128)(2,1)}, u32[]{:S(2)}, u32[]{:S(2)}) collective-permute-start(bf16[128,2048]{1,0:T(8,128)(2,1)S(1)} %bitcast.152), channel_id=1, source_target_pairs={{0,24},{4,28},{8,16},{12,20},{16,8},{20,12},{24,0},{28,4},{1,25},{... | collective-permute-start | bytes 1572872 | tf_op jit(solution)/shard_map/ppermute | solution.py:59
  16.3 52.0 %collective-permute-start.1 = (bf16[128,2048]{1,0:T(8,128)(2,1)S(1)}, bf16[128,2048]{1,0:T(8,128)(2,1)}, u32[]{:S(2)}, u32[]{:S(2)}) collective-permute-start(bf16[128,2048]{1,0:T(8,128)(2,1)S(1)} %bitcast.153), channel_id=1, source_target_pairs={{0,16},{4,20},{8,24},{12,28},{16,0},{20,4},{24,8},{28,12},{1,17},{... | collective-permute-start | bytes 1572872 | tf_op jit(solution)/shard_map/ppermute | solution.py:59
  26.8 27.6 %collective-permute-start.5 = (bf16[1,512,512]{2,1,0:T(8,128)(2,1)}, bf16[1,512,512]{2,1,0:T(8,128)(2,1)S(1)}, u32[]{:S(2)}, u32[]{:S(2)}) collective-permute-start(bf16[1,512,512]{2,1,0:T(8,128)(2,1)} %collective-permute-done.3), channel_id=1, source_target_pairs={{0,1},{1,0},{2,3},{3,2},{4,5},{5,4},{6,7},{7,6},{8,9},{9,8},{10,11... | collective-permute-start | bytes 1572872 | tf_op jit(solution)/shard_map/ppermute | solution.py:183
  70.4 67.0 %collective-permute-start.8 = (bf16[512,2048]{1,0:T(8,128)(2,1)S(1)}, bf16[512,2048]{1,0:T(8,128)(2,1)S(1)}, u32[]{:S(2)}, u32[]{:S(2)}) collective-permute-start(bf16[512,2048]{1,0:T(8,128)(2,1)S(1)} %get-tuple-element.257), channel_id=1, source_target_pairs={{0,4},{4,0},{8,12},{12,8},{16,20},{20,16},{24,28},{28,24},{1,5},{5... | collective-permute-start | bytes 6291464 | tf_op jit(solution)/shard_map/ppermute | solution.py:59
  86.0 36.7 %collective-permute-start.15 = (bf16[2048,256]{1,0:T(8,128)(2,1)S(1)}, bf16[2048,256]{1,0:T(8,128)(2,1)S(1)}, u32[]{:S(2)}, u32[]{:S(2)}) collective-permute-start(bf16[2048,256]{1,0:T(8,128)(2,1)S(1)} %pad_maximum_fusion.6.kv_even), channel_id=1, source_target_pairs={{0,4},{4,0},{8,12},{12,8},{16,20},{20,16},{24,28},{28,24},{1,5},{5... | collective-permute-start | bytes 3145736 | tf_op jit(solution)/shard_map/ppermute | solution.py:59
  87.0 48.9 %collective-permute-start.17 = (bf16[1,512,1024]{2,1,0:T(8,128)(2,1)}, bf16[1,512,1024]{2,1,0:T(8,128)(2,1)}, u32[]{:S(2)}, u32[]{:S(2)}) collective-permute-start(bf16[1,512,1024]{2,1,0:T(8,128)(2,1)} %bitcast.13), channel_id=1, source_target_pairs={{0,3},{1,2},{2,1},{3,0},{4,7},{5,6},{6,5},{7,4},{8,11},{9,10},{10,... | collective-permute-start | bytes 3145736 | tf_op jit(solution)/shard_map/ppermute | solution.py:183
  88.0 31.4 %collective-permute-start.24 = (bf16[1,512,256]{2,1,0:T(8,128)(2,1)S(1)}, bf16[1,512,256]{2,1,0:T(8,128)(2,1)S(1)}, u32[]{:S(2)}, u32[]{:S(2)}) collective-permute-start(bf16[1,512,256]{2,1,0:T(8,128)(2,1)S(1)} %collective-permute-done.16), channel_id=1, source_target_pairs={{0,1},{1,0},{2,3},{3,2},{4,5},{5,4},{6,7},{7,6},{8,9},{9,8},{10,11... | collective-permute-start | bytes 786440 | tf_op jit(solution)/shard_map/ppermute | solution.py:183
  92.2 30.5 %collective-permute-start.19 = (bf16[1,2,512,256]{3,2,1,0:T(8,128)(2,1)S(1)}, bf16[1,2,512,256]{3,2,1,0:T(8,128)(2,1)S(1)}, u32[]{:S(2)}, u32[]{:S(2)}) collective-permute-start(bf16[1,2,512,256]{3,2,1,0:T(8,128)(2,1)S(1)} %bitcast.165), channel_id=1, source_target_pairs={{0,16},{4,20},{8,24},{12,28},{16,0},{20,4},{24,8},{28,12},{1,17},{... | collective-permute-start | bytes 1572872 | tf_op jit(solution)/shard_map/ppermute | solution.py:59
  122.7 38.1 %collective-permute-start.18 = (bf16[1,512,1024]{2,1,0:T(8,128)(2,1)}, bf16[1,512,1024]{2,1,0:T(8,128)(2,1)}, u32[]{:S(2)}, u32[]{:S(2)}) collective-permute-start(bf16[1,512,1024]{2,1,0:T(8,128)(2,1)} %bitcast.13), channel_id=1, source_target_pairs={{0,1},{1,0},{2,3},{3,2},{4,5},{5,4},{6,7},{7,6},{8,9},{9,8},{10,11... | collective-permute-start | bytes 3145736 | tf_op jit(solution)/shard_map/ppermute | solution.py:183
  122.9 56.6 %collective-permute-start.21 = (bf16[2,2,512,256]{3,2,1,0:T(8,128)(2,1)S(1)}, bf16[2,2,512,256]{3,2,1,0:T(8,128)(2,1)}, u32[]{:S(2)}, u32[]{:S(2)}) collective-permute-start(bf16[2,2,512,256]{3,2,1,0:T(8,128)(2,1)S(1)} %pad_maximum_fusion.8.refs_0_), channel_id=1, source_target_pairs={{0,4},{4,0},{8,12},{12,8},{16,20},{20,16},{24,28},{28,24},{1,5},{5... | collective-permute-start | bytes 3145736 | tf_op jit(solution)/shard_map/ppermute | solution.py:59
  133.4 27.0 %collective-permute-start.20 = (bf16[2,2,512,256]{3,2,1,0:T(8,128)(2,1)S(1)}, bf16[2,2,512,256]{3,2,1,0:T(8,128)(2,1)}, u32[]{:S(2)}, u32[]{:S(2)}) collective-permute-start(bf16[2,2,512,256]{3,2,1,0:T(8,128)(2,1)S(1)} %pad_maximum_fusion.8.refs_0_), channel_id=1, source_target_pairs={{0,8},{4,12},{8,0},{12,4},{16,24},{20,28},{24,16},{28,20},{1,9},{5... | collective-permute-start | bytes 3145736 | tf_op jit(solution)/shard_map/ppermute | solution.py:59
  135.9 24.4 %collective-permute-start.26 = (bf16[2,2,512,256]{3,2,1,0:T(8,128)(2,1)}, bf16[2,2,512,256]{3,2,1,0:T(8,128)(2,1)}, u32[]{:S(2)}, u32[]{:S(2)}) collective-permute-start(bf16[2,2,512,256]{3,2,1,0:T(8,128)(2,1)} %pad_maximum_fusion.9.refs_4_), channel_id=1, source_target_pairs={{0,16},{4,20},{8,24},{12,28},{16,0},{20,4},{24,8},{28,12},{1,17},{... | collective-permute-start | bytes 3145736 | tf_op jit(solution)/shard_map/ppermute | solution.py:59
  137.4 39.3 %collective-permute-start.29 = (bf16[1,512,1024]{2,1,0:T(8,128)(2,1)}, bf16[1,512,1024]{2,1,0:T(8,128)(2,1)}, u32[]{:S(2)}, u32[]{:S(2)}) collective-permute-start(bf16[1,512,1024]{2,1,0:T(8,128)(2,1)} %collective-permute-done.17), channel_id=1, source_target_pairs={{0,1},{1,0},{2,3},{3,2},{4,5},{5,4},{6,7},{7,6},{8,9},{9,8},{10,11... | collective-permute-start | bytes 3145736 | tf_op jit(solution)/shard_map/ppermute | solution.py:183
  165.1 117.8 %all-gather.5.cloned.1.call-start = ((), (), s32[]{:S(2)}) async-start(), calls=%async_computation.13 | async-start | bytes 2621440 | tf_op jit(solution)/shard_map/all_gather | solution.py:216
  179.0 103.9 %all-gather.3.cloned.1.call-start = ((), (), s32[]{:S(2)}) async-start(), calls=%async_computation.12 | async-start | bytes 2621440 | tf_op jit(solution)/shard_map/all_gather | solution.py:216
  189.0 24.9 %collective-permute-start.31 = (bf16[128,2048]{1,0:T(8,128)(2,1)S(1)}, bf16[128,2048]{1,0:T(8,128)(2,1)S(1)}, u32[]{:S(2)}, u32[]{:S(2)}) collective-permute-start(bf16[128,2048]{1,0:T(8,128)(2,1)S(1)} %add_convert_fusion.1), channel_id=1, source_target_pairs={{0,16},{4,20},{8,24},{12,28},{16,0},{20,4},{24,8},{28,12},{1,17},{... | collective-permute-start | bytes 1572872 | tf_op jit(solution)/shard_map/ppermute | solution.py:59
  189.5 25.4 %collective-permute-start.32 = (bf16[128,2048]{1,0:T(8,128)(2,1)S(1)}, bf16[128,2048]{1,0:T(8,128)(2,1)S(1)}, u32[]{:S(2)}, u32[]{:S(2)}) collective-permute-start(bf16[128,2048]{1,0:T(8,128)(2,1)S(1)} %add_convert_fusion.1), channel_id=1, source_target_pairs={{0,24},{4,28},{8,16},{12,20},{16,8},{20,12},{24,0},{28,4},{1,25},{... | collective-permute-start | bytes 1572872 | tf_op jit(solution)/shard_map/ppermute | solution.py:59
  221.8 136.6 %reduce-scatter.9.cloned.1.call-start = ((), (), s32[]{:S(2)}) async-start(), calls=%async_computation.15 | async-start | bytes 2621440 | tf_op jit(solution)/shard_map/reduce_scatter | solution.py:220
  234.3 30.7 %collective-permute-start.40 = (bf16[2,128,2048]{2,1,0:T(8,128)(2,1)S(1)}, bf16[2,128,2048]{2,1,0:T(8,128)(2,1)S(1)}, u32[]{:S(2)}, u32[]{:S(2)}) collective-permute-start(bf16[2,128,2048]{2,1,0:T(8,128)(2,1)S(1)} %pad_maximum_fusion.11), channel_id=1, source_target_pairs={{0,4},{4,0},{8,12},{12,8},{16,20},{20,16},{24,28},{28,24},{1,5},{5... | collective-permute-start | bytes 3145736 | tf_op jit(solution)/shard_map/ppermute | solution.py:59
  234.4 25.6 %collective-permute-start.39 = (bf16[2,128,2048]{2,1,0:T(8,128)(2,1)S(1)}, bf16[2,128,2048]{2,1,0:T(8,128)(2,1)S(1)}, u32[]{:S(2)}, u32[]{:S(2)}) collective-permute-start(bf16[2,128,2048]{2,1,0:T(8,128)(2,1)S(1)} %pad_maximum_fusion.11), channel_id=1, source_target_pairs={{0,8},{4,12},{8,0},{12,4},{16,24},{20,28},{24,16},{28,20},{1,9},{5... | collective-permute-start | bytes 3145736 | tf_op jit(solution)/shard_map/ppermute | solution.py:59
  237.4 27.7 %collective-permute-start.36 = (bf16[2,128,2048]{2,1,0:T(8,128)(2,1)}, bf16[2,128,2048]{2,1,0:T(8,128)(2,1)}, u32[]{:S(2)}, u32[]{:S(2)}) collective-permute-start(bf16[2,128,2048]{2,1,0:T(8,128)(2,1)} %pad_maximum_fusion.10), channel_id=1, source_target_pairs={{0,4},{4,0},{8,12},{12,8},{16,20},{20,16},{24,28},{28,24},{1,5},{5... | collective-permute-start | bytes 3145736 | tf_op jit(solution)/shard_map/ppermute | solution.py:59
  237.4 25.8 %collective-permute-start.35 = (bf16[2,128,2048]{2,1,0:T(8,128)(2,1)}, bf16[2,128,2048]{2,1,0:T(8,128)(2,1)S(1)}, u32[]{:S(2)}, u32[]{:S(2)}) collective-permute-start(bf16[2,128,2048]{2,1,0:T(8,128)(2,1)} %pad_maximum_fusion.10), channel_id=1, source_target_pairs={{0,16},{4,20},{8,24},{12,28},{16,0},{20,4},{24,8},{28,12},{1,17},{... | collective-permute-start | bytes 3145736 | tf_op jit(solution)/shard_map/ppermute | solution.py:59
  282.9 88.6 %reduce-scatter.7.cloned.1.call-start = ((), (), s32[]{:S(2)}) async-start(), calls=%async_computation.14 | async-start | bytes 2621440 | tf_op jit(solution)/shard_map/reduce_scatter | solution.py:220
  283.5 168.7 %reduce-scatter.17.cloned.1.call-start = ((), (), s32[]{:S(2)}) async-start(), calls=%async_computation.19 | async-start | bytes 2621440 | tf_op jit(solution)/shard_map/reduce_scatter | solution.py:220
  314.1 24.6 %collective-permute-start.44 = (bf16[128,2048]{1,0:T(8,128)(2,1)S(1)}, bf16[128,2048]{1,0:T(8,128)(2,1)}, u32[]{:S(2)}, u32[]{:S(2)}) collective-permute-start(bf16[128,2048]{1,0:T(8,128)(2,1)S(1)} %get-tuple-element.275), channel_id=1, source_target_pairs={{0,16},{4,20},{8,24},{12,28},{16,0},{20,4},{24,8},{28,12},{1,17},{... | collective-permute-start | bytes 1572872 | tf_op jit(solution)/shard_map/ppermute | solution.py:59
  339.0 127.5 %reduce-scatter.15.cloned.1.call-start = ((), (), s32[]{:S(2)}) async-start(), calls=%async_computation.18 | async-start | bytes 2621440 | tf_op jit(solution)/shard_map/reduce_scatter | solution.py:220
  339.1 33.9 %collective-permute-start.46 = (bf16[512,2048]{1,0:T(8,128)(2,1)}, bf16[512,2048]{1,0:T(8,128)(2,1)}, u32[]{:S(2)}, u32[]{:S(2)}) collective-permute-start(bf16[512,2048]{1,0:T(8,128)(2,1)} %get-tuple-element.127), channel_id=1, source_target_pairs={{0,4},{4,0},{8,12},{12,8},{16,20},{20,16},{24,28},{28,24},{1,5},{5... | collective-permute-start | bytes 6291464 | tf_op jit(solution)/shard_map/ppermute | solution.py:59
  358.1 154.6 %reduce-scatter.11.cloned.1.call-start = ((), (), s32[]{:S(2)}) async-start(), calls=%async_computation.16 | async-start | bytes 2621440 | tf_op jit(solution)/shard_map/reduce_scatter | solution.py:220
  358.4 48.2 %collective-permute-start.48 = (bf16[1,256,1024]{2,1,0:T(8,128)(2,1)}, bf16[1,256,1024]{2,1,0:T(8,128)(2,1)}, u32[]{:S(2)}, u32[]{:S(2)}) collective-permute-start(bf16[1,256,1024]{2,1,0:T(8,128)(2,1)} %bitcast.182), channel_id=1, source_target_pairs={{0,8},{4,12},{8,0},{12,4},{16,24},{20,28},{24,16},{28,20},{1,9},{5... | collective-permute-start | bytes 1572872 | tf_op jit(solution)/shard_map/ppermute | solution.py:59
  371.5 35.2 %collective-permute-start.47 = (bf16[1,256,1024]{2,1,0:T(8,128)(2,1)}, bf16[1,256,1024]{2,1,0:T(8,128)(2,1)}, u32[]{:S(2)}, u32[]{:S(2)}) collective-permute-start(bf16[1,256,1024]{2,1,0:T(8,128)(2,1)} %bitcast.188), channel_id=1, source_target_pairs={{0,16},{4,20},{8,24},{12,28},{16,0},{20,4},{24,8},{28,12},{1,17},{... | collective-permute-start | bytes 1572872 | tf_op jit(solution)/shard_map/ppermute | solution.py:59
  380.4 26.3 %collective-permute-start.51 = (bf16[128,2048]{1,0:T(8,128)(2,1)S(1)}, bf16[128,2048]{1,0:T(8,128)(2,1)S(1)}, u32[]{:S(2)}, u32[]{:S(2)}) collective-permute-start(bf16[128,2048]{1,0:T(8,128)(2,1)S(1)} %get-tuple-element.271), channel_id=1, source_target_pairs={{0,24},{4,28},{8,16},{12,20},{16,8},{20,12},{24,0},{28,4},{1,25},{... | collective-permute-start | bytes 1572872 | tf_op jit(solution)/shard_map/ppermute | solution.py:59
  381.9 25.8 %collective-permute-start.50 = (bf16[128,2048]{1,0:T(8,128)(2,1)S(1)}, bf16[128,2048]{1,0:T(8,128)(2,1)S(1)}, u32[]{:S(2)}, u32[]{:S(2)}) collective-permute-start(bf16[128,2048]{1,0:T(8,128)(2,1)S(1)} %get-tuple-element.272), channel_id=1, source_target_pairs={{0,16},{4,20},{8,24},{12,28},{16,0},{20,4},{24,8},{28,12},{1,17},{... | collective-permute-start | bytes 1572872 | tf_op jit(solution)/shard_map/ppermute | solution.py:59
  383.5 24.2 %collective-permute-start.49 = (bf16[128,2048]{1,0:T(8,128)(2,1)S(1)}, bf16[128,2048]{1,0:T(8,128)(2,1)S(1)}, u32[]{:S(2)}, u32[]{:S(2)}) collective-permute-start(bf16[128,2048]{1,0:T(8,128)(2,1)S(1)} %get-tuple-element.273), channel_id=1, source_target_pairs={{0,8},{4,12},{8,0},{12,4},{16,24},{20,28},{24,16},{28,20},{1,9},{5... | collective-permute-start | bytes 1572872 | tf_op jit(solution)/shard_map/ppermute | solution.py:59
  406.6 28.3 %collective-permute-start.52 = (bf16[512,2048]{1,0:T(8,128)(2,1)S(1)}, bf16[512,2048]{1,0:T(8,128)(2,1)}, u32[]{:S(2)}, u32[]{:S(2)}) collective-permute-start(bf16[512,2048]{1,0:T(8,128)(2,1)S(1)} %convolution_convert_fusion.1), channel_id=1, source_target_pairs={{0,4},{4,0},{8,12},{12,8},{16,20},{20,16},{24,28},{28,24},{1,5},{5... | collective-permute-start | bytes 6291464 | tf_op jit(solution)/shard_map/ppermute | solution.py:59
  439.8 34.0 %collective-permute-start.59 = (bf16[128,2048]{1,0:T(8,128)(2,1)}, bf16[128,2048]{1,0:T(8,128)(2,1)}, u32[]{:S(2)}, u32[]{:S(2)}) collective-permute-start(bf16[128,2048]{1,0:T(8,128)(2,1)} %get-tuple-element.268), channel_id=1, source_target_pairs={{0,24},{4,28},{8,16},{12,20},{16,8},{20,12},{24,0},{28,4},{1,25},{... | collective-permute-start | bytes 1572872 | tf_op jit(solution)/shard_map/ppermute | solution.py:59
  444.3 74.9 %collective-permute-start.67 = (bf16[2,256,1024]{2,1,0:T(8,128)(2,1)S(1)}, bf16[2,256,1024]{2,1,0:T(8,128)(2,1)S(1)}, u32[]{:S(2)}, u32[]{:S(2)}) collective-permute-start(bf16[2,256,1024]{2,1,0:T(8,128)(2,1)S(1)} %pad_maximum_fusion.13.refs_0_), channel_id=1, source_target_pairs={{0,4},{4,0},{8,12},{12,8},{16,20},{20,16},{24,28},{28,24},{1,5},{5... | collective-permute-start | bytes 3145736 | tf_op jit(solution)/shard_map/ppermute | solution.py:59
  444.3 35.0 %collective-permute-start.58 = (bf16[128,2048]{1,0:T(8,128)(2,1)}, bf16[128,2048]{1,0:T(8,128)(2,1)}, u32[]{:S(2)}, u32[]{:S(2)}) collective-permute-start(bf16[128,2048]{1,0:T(8,128)(2,1)} %get-tuple-element.269), channel_id=1, source_target_pairs={{0,16},{4,20},{8,24},{12,28},{16,0},{20,4},{24,8},{28,12},{1,17},{... | collective-permute-start | bytes 1572872 | tf_op jit(solution)/shard_map/ppermute | solution.py:59
  444.7 35.5 %collective-permute-start.57 = (bf16[128,2048]{1,0:T(8,128)(2,1)}, bf16[128,2048]{1,0:T(8,128)(2,1)}, u32[]{:S(2)}, u32[]{:S(2)}) collective-permute-start(bf16[128,2048]{1,0:T(8,128)(2,1)} %get-tuple-element.270), channel_id=1, source_target_pairs={{0,8},{4,12},{8,0},{12,4},{16,24},{20,28},{24,16},{28,20},{1,9},{5... | collective-permute-start | bytes 1572872 | tf_op jit(solution)/shard_map/ppermute | solution.py:59
  471.6 117.9 %reduce-scatter.13.cloned.1.call-start = ((), (), s32[]{:S(2)}) async-start(), calls=%async_computation.17 | async-start | bytes 1310720 | tf_op jit(solution)/shard_map/reduce_scatter | solution.py:220
  473.8 42.7 %collective-permute-start.74 = (bf16[1,512,512]{2,1,0:T(8,128)(2,1)}, bf16[1,512,512]{2,1,0:T(8,128)(2,1)}, u32[]{:S(2)}, u32[]{:S(2)}) collective-permute-start(bf16[1,512,512]{2,1,0:T(8,128)(2,1)} %bitcast.184), channel_id=1, source_target_pairs={{0,8},{4,12},{8,0},{12,4},{16,24},{20,28},{24,16},{28,20},{1,9},{5... | collective-permute-start | bytes 1572872 | tf_op jit(solution)/shard_map/ppermute | solution.py:59
  479.3 56.2 %collective-permute-start.66 = (bf16[2,256,1024]{2,1,0:T(8,128)(2,1)S(1)}, bf16[2,256,1024]{2,1,0:T(8,128)(2,1)}, u32[]{:S(2)}, u32[]{:S(2)}) collective-permute-start(bf16[2,256,1024]{2,1,0:T(8,128)(2,1)S(1)} %pad_maximum_fusion.13.refs_0_), channel_id=1, source_target_pairs={{0,8},{4,12},{8,0},{12,4},{16,24},{20,28},{24,16},{28,20},{1,9},{5... | collective-permute-start | bytes 3145736 | tf_op jit(solution)/shard_map/ppermute | solution.py:59
  480.2 55.8 %collective-permute-start.69 = (bf16[2,256,1024]{2,1,0:T(8,128)(2,1)S(1)}, bf16[2,256,1024]{2,1,0:T(8,128)(2,1)}, u32[]{:S(2)}, u32[]{:S(2)}) collective-permute-start(bf16[2,256,1024]{2,1,0:T(8,128)(2,1)S(1)} %pad_maximum_fusion.14.refs_4_), channel_id=1, source_target_pairs={{0,16},{4,20},{8,24},{12,28},{16,0},{20,4},{24,8},{28,12},{1,17},{... | collective-permute-start | bytes 3145736 | tf_op jit(solution)/shard_map/ppermute | solution.py:59
  516.5 35.1 %collective-permute-start.70 = (bf16[2,256,1024]{2,1,0:T(8,128)(2,1)S(1)}, bf16[2,256,1024]{2,1,0:T(8,128)(2,1)}, u32[]{:S(2)}, u32[]{:S(2)}) collective-permute-start(bf16[2,256,1024]{2,1,0:T(8,128)(2,1)S(1)} %pad_maximum_fusion.14.refs_4_), channel_id=1, source_target_pairs={{0,4},{4,0},{8,12},{12,8},{16,20},{20,16},{24,28},{28,24},{1,5},{5... | collective-permute-start | bytes 3145736 | tf_op jit(solution)/shard_map/ppermute | solution.py:59
  535.5 49.7 %collective-permute-start.75 = (bf16[2,512,512]{2,1,0:T(8,128)(2,1)}, bf16[2,512,512]{2,1,0:T(8,128)(2,1)}, u32[]{:S(2)}, u32[]{:S(2)}) collective-permute-start(bf16[2,512,512]{2,1,0:T(8,128)(2,1)} %pad_maximum_fusion.15.refs_4_), channel_id=1, source_target_pairs={{0,16},{4,20},{8,24},{12,28},{16,0},{20,4},{24,8},{28,12},{1,17},{... | collective-permute-start | bytes 3145736 | tf_op jit(solution)/shard_map/ppermute | solution.py:59
  536.1 49.2 %collective-permute-start.65 = (bf16[2,512,512]{2,1,0:T(8,128)(2,1)S(1)}, bf16[2,512,512]{2,1,0:T(8,128)(2,1)}, u32[]{:S(2)}, u32[]{:S(2)}) collective-permute-start(bf16[2,512,512]{2,1,0:T(8,128)(2,1)S(1)} %pad_maximum_fusion.12.refs_0_), channel_id=1, source_target_pairs={{0,8},{4,12},{8,0},{12,4},{16,24},{20,28},{24,16},{28,20},{1,9},{5... | collective-permute-start | bytes 3145736 | tf_op jit(solution)/shard_map/ppermute | solution.py:59
  539.9 33.0 %collective-permute-start.68 = (bf16[2,256,1024]{2,1,0:T(8,128)(2,1)}, bf16[2,256,1024]{2,1,0:T(8,128)(2,1)}, u32[]{:S(2)}, u32[]{:S(2)}) collective-permute-start(bf16[2,256,1024]{2,1,0:T(8,128)(2,1)} %collective-permute-done.66.refs_1_), channel_id=1, source_target_pairs={{0,4},{4,0},{8,12},{12,8},{16,20},{20,16},{24,28},{28,24},{1,5},{5... | collective-permute-start | bytes 3145736 | tf_op jit(solution)/shard_map/ppermute | solution.py:59
  551.7 49.2 %collective-permute-start.63 = (bf16[2048,512]{1,0:T(8,128)(2,1)}, bf16[2048,512]{1,0:T(8,128)(2,1)}, u32[]{:S(2)}, u32[]{:S(2)}) collective-permute-start(bf16[2048,512]{1,0:T(8,128)(2,1)} %constant_dynamic-update-slice_fusion.10), channel_id=1, source_target_pairs={{0,4},{4,0},{8,12},{12,8},{16,20},{20,16},{24,28},{28,24},{1,5},{5... | collective-permute-start | bytes 6291464 | tf_op jit(solution)/shard_map/ppermute | solution.py:59
  (105 other events, 1684.0 us)
Sparse Core Ops, SparseCore 0:
  179.1 43.7 all-gather.4
  224.4 44.6 all-gather.2
  283.0 42.9 reduce-scatter.8
  328.3 43.1 reduce-scatter.6
  373.6 43.1 reduce-scatter.16
  419.1 47.3 reduce-scatter.14
  469.4 43.2 reduce-scatter.10
  519.3 25.8 reduce-scatter.12

commit v4 on v3

--- a/solution.py
+++ b/solution.py
@@ -917,6 +917,18 @@
         fc_bias.reshape(fsdp_count, ctx_count, unit), c_at, 1, keepdims=False
     )
 
+    def relative_plan(ref):
+        return [
+            (
+                0,
+                (ref[0] ^ (2 * chip + parity),),
+                0,
+                (pl.ds((parity * chips + chip) * tokens, tokens),),
+            )
+            for parity in range(2)
+            for chip in range(chips)
+        ]
+
     x_own = x_low.astype(F32)
     first_norm, normed_one, inverse_one = layer_norm(x_own, gain_one, shift_one)
     kv_own = mm(first_norm.astype(BF16), w_kv)
@@ -968,13 +980,15 @@
     middle = x_own + (times_blocks(meta, o_own, out_blocks, out_layout, False) + out_bias)
     second_norm, normed_two, inverse_two = layer_norm(middle, gain_two, shift_two)
 
-    cn_even, cn_odd = ctx_gather(after(second_norm.astype(BF16), fc_parts[-1]))
-    o_parts, gm_parts = ctx_gather_halves(
-        after(o_own, cn_even), after(grad_mlp, cn_even), wait=lambda part: after(part, cn_odd)
-    )
-    o_even, o_odd = in_order(o_parts, 0), in_order(o_parts, 1)
-    gm_all = jnp.concatenate([in_order(gm_parts, 0), in_order(gm_parts, 1)], axis=0)
-    gm_all, o_even, o_odd = lax.optimization_barrier((gm_all, o_even, o_odd))
+    o_parts = [ctx_swap(o_own, 2 * at) for at in range(1, chips)]
+    cn_own, o_parts = lax.optimization_barrier((second_norm.astype(BF16), o_parts))
+    cn_even, cn_odd = ctx_gather(cn_own)
+    o_even = jnp.concatenate([o_own, *o_parts], axis=0)
+    o_odd = ctx_swap(o_even, 1)
+    gm_all = lax.all_gather(grad_mlp, "ctx", axis=0, tiled=False)
+    (gm_all,) = place_blocks(
+        meta, [gm_all], [(ctx_count * tokens, width)], relative_plan, "place_rows"
+    )
     cn_all = jnp.concatenate([cn_even, cn_odd], axis=0)
     half_rows = chips * tokens
     hidden, act = feed_hidden(shape, meta, cn_all, fc_parts, fc_bias.reshape(1, -1))
@@ -1031,16 +1045,7 @@
         meta,
         [gkv_all],
         [(ctx_count * tokens, 2 * HD)],
-        lambda ref: [
-            (
-                0,
-                (ref[0] ^ (2 * chip + parity),),
-                0,
-                (pl.ds((parity * chips + chip) * tokens, tokens),),
-            )
-            for parity in range(2)
-            for chip in range(chips)
-        ],
+        relative_plan,
         "place_keys",
     )
     gkv_even, gkv_odd = gkv_all[: chips * tokens], gkv_all[chips * tokens :]

time: 627 us -> 623 us (level)
  local copies, waits for them, and re-layouts: 57.1 us -> 49.6 us
  other arithmetic: 60.3 us -> 53.1 us
    all_gather x2, waiting for transfers between devices: 0.01 us -> 13.4 us  [z_gather_queued(): return lax.all_gather(values, 'fsdp', axis=0, tiled=True)]
    reduce_scatter x6, waiting for transfers between devices: 46.2 us -> 35.1 us  [z_scatter_queued(): return lax.psum_scatter(values, 'fsdp', scatter_dimension=0, tiled=True)]
    unnamed x148 -> x155, local copies, waits for them, and re-layouts: 29.5 us -> 23.1 us
    ppermute x64 -> x60, waiting for transfers between devices: 105 us -> 103 us  [ctx_swap(): return lax.ppermute(values, 'ctx', [(at, at ^ mask) for at in range(count)])]
    ppermute x64 -> x60, starting transfers between devices: 52.6 us -> 51.7 us  [ctx_swap(): return lax.ppermute(values, 'ctx', [(at, at ^ mask) for at in range(count)])]
  transfers between devices with their start and end apart: 92 -> 89, of which waited for: 36 -> 37; matrix products, arithmetic and copies ran while one was open for 21% -> 20% of each run, Pallas kernels for 20% -> 21%
where the time goes in v4:
time: 623 us; the launch traced here: 612 us
  waiting for transfers between devices  222 us (36%)
  Pallas kernels  139 us (22%)
  starting transfers between devices  101 us (16%)
  other arithmetic  53.1 us (9%)
  local copies, waits for them, and re-layouts  49.6 us (8%)
  matrix products  32.1 us (5%)
  between operations  16.4 us (3%)
    ppermute x60, waiting for transfers between devices, ctx_swap(): return lax.ppermute(values, 'ctx', [(at, at ^ mask) for at in range(count)])  103 us
    ppermute x60, starting transfers between devices, ctx_swap(): return lax.ppermute(values, 'ctx', [(at, at ^ mask) for at in range(count)])  51.7 us
    ppermute x14, waiting for transfers between devices, z_swap(): lax.ppermute(values, 'fsdp', [(at, at ^ mask) for at in range(count)])  51.3 us
    reduce_scatter x6, waiting for transfers between devices, z_scatter_queued(): return lax.psum_scatter(values, 'fsdp', scatter_dimension=0, tiled=True)  35.1 us
    ppermute x14, starting transfers between devices, z_swap(): lax.ppermute(values, 'fsdp', [(at, at ^ mask) for at in range(count)])  24.8 us
    unnamed x155, local copies, waits for them, and re-layouts  23.1 us
    dot_general x7, matrix products, mm_rows(): lax.dot_general(left, right, (((0,), (0,)), ((), ())), preferred_element_...  20.1 us
    pallas_call x2, Pallas kernels, spread_columns(): pl.pallas_call(functools.partial(spread_kernel, moves, extras, len(sizes)...  18.2 us
  transfers between devices with their start and end apart: 89, of which 37 were waited for; matrix products, arithmetic and copies ran while one was open for 20% of the time, Pallas kernels for 21%

profile of v4, /device:TPU:0, one launch (start us, length us, event | category | flops | bytes accessed | tf_op | source)
XLA Modules:
  0.0 612.3 jit_solution(9815859408786903613)
XLA Ops:
  8.8 3.1 collective-permute-start.4
  21.0 16.4 %collective-permute-done.3 = bf16[1,512,512]{2,1,0:T(8,128)(2,1)} collective-permute-done((bf16[1,512,512]{2,1,0:T(8,128)(2,1)S(1)}, bf16[1,512,512]{2,1,0:T(8,128)(2,1)}, u32[]{:S(2)}, u32[]{:S(2)}) %collective-permute-start.3) | collective-permute-done | bytes 524320 | tf_op jit(solution)/shard_map/ppermute | solution.py:183
  44.7 5.6 collective-permute-done.6
  55.6 3.7 place_first.1
  77.6 3.4 collective-permute-start.16
  84.5 3.7 collective-permute-done.13
  88.5 3.6 collective-permute-start.17
  96.5 25.3 %collective-permute-done.24 = bf16[1,512,256]{2,1,0:T(8,128)(2,1)S(1)} collective-permute-done((bf16[1,512,256]{2,1,0:T(8,128)(2,1)S(1)}, bf16[1,512,256]{2,1,0:T(8,128)(2,1)S(1)}, u32[]{:S(2)}, u32[]{:S(2)}) %collective-permute-start.24) | collective-permute-done | bytes 262176 | tf_op jit(solution)/shard_map/ppermute | solution.py:183
  125.9 9.9 %collective-permute-done.25 = bf16[1,2,512,256]{3,2,1,0:T(8,128)(2,1)S(1)} collective-permute-done((bf16[1,2,512,256]{3,2,1,0:T(8,128)(2,1)S(1)}, bf16[1,2,512,256]{3,2,1,0:T(8,128)(2,1)S(1)}, u32[]{:S(2)}, u32[]{:S(2)}) %collective-permute-start.25) | collective-permute-done | bytes 524320 | tf_op jit(solution)/shard_map/ppermute | solution.py:59
  143.5 14.4 %attend.1 = (bf16[1024,256]{1,0:T(8,128)(2,1)}, bf16[2,1024,128]{2,1,0:T(8,128)(2,1)}, bf16[2,2048,256]{2,1,0:T(8,128)(2,1)}, f32[8,128,256]{2,1,0:T(8,128)}, f32[8,1,256]{2,1,0:T(1,128)}) custom-call(s32[14]{0:T(128)} %pad_add_fusion.meta, bf16[512,256]{1,0:T(8,128)(2,1)} %fusion.15.q_even, bf16[512,256]{1,0:T(8,128)(2,1)} %fusion.16.q_odd, ...), custom_call_target="tpu_custom_call" | custom-call | flops 1073741824 | bytes 8388608 | tf_op jit(solution)/shard_map/attend/pallas_call | solution.py:444
  157.8 3.9 collective-permute-done.26.refs_5_
  162.4 4.2 all-to-all-start
  169.3 3.1 pad_maximum_fusion.1.refs_0_
  172.4 3.9 all-to-all-done
  184.5 6.7 %branch.1 = f32[128,2048]{1,0:T(8,128)} custom-call(s32[14]{0:T(128)} %pad_add_fusion.meta, bf16[128,2048]{1,0:T(8,128)(2,1)} %bitcast.42.rows_ref, bf16[2,2,512,256]{3,2,1,0:T(8,128)(2,1)} %copy-done.11, bf16[2,2,512,256]{3,2,1,0:T(8,128)(2,1)} %collective-permute-done.20.refs_1_, bf16[2,2,512,256]{3,2,1,0:T(8,128)(2,1)} %collective-permute-done.21.refs_2_, ...), custom_call_target="tpu_custom_call" | custom-call | flops 1073741824 | bytes 8388608 | tf_op jit(solution)/shard_map/branch/pallas_call | solution.py:690
  194.3 7.8 %collective-permute-done.30 = bf16[128,2048]{1,0:T(8,128)(2,1)S(1)} collective-permute-done((bf16[128,2048]{1,0:T(8,128)(2,1)}, bf16[128,2048]{1,0:T(8,128)(2,1)S(1)}, u32[]{:S(2)}, u32[]{:S(2)}) %collective-permute-start.30) | collective-permute-done | bytes 524320 | tf_op jit(solution)/shard_map/ppermute | solution.py:59
  206.5 11.6 %collective-permute-done.34 = bf16[128,2048]{1,0:T(8,128)(2,1)S(1)} collective-permute-done((bf16[128,2048]{1,0:T(8,128)(2,1)S(1)}, bf16[128,2048]{1,0:T(8,128)(2,1)S(1)}, u32[]{:S(2)}, u32[]{:S(2)}) %collective-permute-start.34) | collective-permute-done | bytes 524320 | tf_op jit(solution)/shard_map/ppermute | solution.py:59
  218.1 10.1 %collective-permute-done.33 = bf16[128,2048]{1,0:T(8,128)(2,1)S(1)} collective-permute-done((bf16[128,2048]{1,0:T(8,128)(2,1)S(1)}, bf16[128,2048]{1,0:T(8,128)(2,1)S(1)}, u32[]{:S(2)}, u32[]{:S(2)}) %collective-permute-start.33) | collective-permute-done | bytes 524320 | tf_op jit(solution)/shard_map/ppermute | solution.py:59
  238.5 10.9 %feed_hidden.1 = (f32[1024,1024]{1,0:T(8,128)}, bf16[1024,1024]{1,0:T(8,128)(2,1)}) custom-call(s32[14]{0:T(128)} %pad_add_fusion.meta, bf16[1024,2048]{1,0:T(8,128)(2,1)} %copy-done.50, f32[1,1024]{1,0:T(1,128)} %bitcast.173, bf16[2,512,1024]{2,1,0:T(8,128)(2,1)} %pad_maximum_fusion.1.refs_0_, bf16[1,512,1024]{2,1,0:T(8,128)(2,1)} %collective-permute-done.18.refs_1_, ...), custom_call_target="tpu_custom_call" | custom-call | flops 4294967296 | bytes 14680064 | tf_op jit(solution)/shard_map/feed_hidden/pallas_call | solution.py:520
  249.4 5.3 place_rows.1.grads_ref
  254.7 7.0 %convolution_convert_fusion = bf16[1024,2048]{1,0:T(8,128)(2,1)S(1)} fusion(bf16[1024,1024]{1,0:T(8,128)(2,1)S(1)} %copy-done.65, bf16[1024,2048]{1,0:T(8,128)(2,1)} %place_rows.1.grads_ref), kind=kOutput, calls=%fused_computation.19 | convolution fusion | flops 4297064448 | bytes 10485760 | tf_op jit(solution)/shard_map/dot_general | solution.py:50
  264.2 13.4 %all-gather.6.cloned.1.call-done.first = bf16[1024,1024]{1,0:T(8,128)(2,1)} async-done(((bf16[256,1024]{1,0:T(8,128)(2,1)}), bf16[1024,1024]{1,0:T(8,128)(2,1)}) %all-gather.6.cloned.1.call-update) | async-done | bytes 2097168 | tf_op jit(solution)/shard_map/all_gather | solution.py:216
  278.5 11.0 %feed_hidden_grad.1 = (bf16[1024,1024]{1,0:T(8,128)(2,1)}, f32[1,1024]{1,0:T(1,128)}) custom-call(bf16[1024,2048]{1,0:T(8,128)(2,1)} %place_rows.1.grads_ref, f32[1024,1024]{1,0:T(8,128)} %get-tuple-element.102.hidden_ref, bf16[1024,1024]{1,0:T(8,128)(2,1)} %all-gather.6.cloned.1.call-done.first, bf16[1024,1024]{1,0:T(8,128)(2,1)} %all-gather.8.cloned.1.call-done.second), custom_call_target="tpu_custom_call" | custom-call | flops 4294967296 | bytes 14680064 | tf_op jit(solution)/shard_map/feed_hidden_grad/pallas_call | solution.py:565
  289.5 6.6 %feed_grad.2 = bf16[512,2048]{1,0:T(8,128)(2,1)} custom-call(s32[14]{0:T(128)} %pad_add_fusion.meta, bf16[1024,1024]{1,0:T(8,128)(2,1)} %get-tuple-element.105.rows_ref.grads_ref, bf16[2,512,1024]{2,1,0:T(8,128)(2,1)} %pad_maximum_fusion.1.refs_0_, bf16[1,512,1024]{2,1,0:T(8,128)(2,1)} %collective-permute-done.18.refs_1_, ...), custom_call_target="tpu_custom_call" | custom-call | flops 2147483648 | bytes 7340032 | tf_op jit(solution)/shard_map/feed_grad/pallas_call | solution.py:652
  296.1 6.6 %feed_grad.3 = bf16[512,2048]{1,0:T(8,128)(2,1)} custom-call(s32[14]{0:T(128)} %pad_add_fusion.meta, bf16[1024,1024]{1,0:T(8,128)(2,1)} %get-tuple-element.105.rows_ref.grads_ref, bf16[2,512,1024]{2,1,0:T(8,128)(2,1)} %pad_maximum_fusion.1.refs_0_, bf16[1,512,1024]{2,1,0:T(8,128)(2,1)} %collective-permute-done.18.refs_1_, ...), custom_call_target="tpu_custom_call" | custom-call | flops 2147483648 | bytes 7340032 | tf_op jit(solution)/shard_map/feed_grad/pallas_call | solution.py:652
  310.6 18.0 %feed_late.1 = (bf16[512,2048]{1,0:T(8,128)(2,1)}, bf16[512,2048]{1,0:T(8,128)(2,1)}, bf16[2048,512]{1,0:T(8,128)(2,1)}, bf16[2048,512]{1,0:T(8,128)(2,1)}) custom-call(bf16[1024,1024]{1,0:T(8,128)(2,1)} %get-tuple-element.108.rows_ref, bf16[1024,1024]{1,0:T(8,128)(2,1)} %all-gather.6.cloned.1.call-done.first, ...), custom_call_target="tpu_custom_call" | custom-call | flops 8589934592 | bytes 18874368 | tf_op jit(solution)/shard_map/feed_late/pallas_call | solution.py:611
  328.6 5.1 collective-permute-done.39
  345.1 8.2 %branch_grad.1 = f32[128,2048]{1,0:T(8,128)} custom-call(s32[14]{0:T(128)} %pad_add_fusion.meta, bf16[128,2048]{1,0:T(8,128)(2,1)} %get-tuple-element.243.rows_ref, bf16[2,2,512,256]{3,2,1,0:T(8,128)(2,1)} %copy-done.11, bf16[2,2,512,256]{3,2,1,0:T(8,128)(2,1)} %collective-permute-done.20.refs_1_, bf16[2,2,512,256]{3,2,1,0:T(8,128)(2,1)} %collective-permute-done.21.refs_2_, ...), custom_call_target="tpu_custom_call" | custom-call | flops 1073741824 | bytes 8388608 | tf_op jit(solution)/shard_map/branch_grad/pallas_call | solution.py:690
  355.8 3.6 all-to-all-start.1
  361.6 6.2 %reduce-scatter.7.cloned.1.call-done = bf16[256,1024]{1,0:T(8,128)(2,1)} async-done(((bf16[1024,1024]{1,0:T(8,128)(2,1)}), bf16[256,1024]{1,0:T(8,128)(2,1)}) %reduce-scatter.7.cloned.1.call-update) | async-done | bytes 524304 | tf_op jit(solution)/shard_map/reduce_scatter | solution.py:220
  379.9 16.3 %attend_grad.1 = (bf16[512,256]{1,0:T(8,128)(2,1)}, bf16[512,256]{1,0:T(8,128)(2,1)}, bf16[2048,256]{1,0:T(8,128)(2,1)}, bf16[2048,256]{1,0:T(8,128)(2,1)}, bf16...) custom-call(s32[14]{0:T(128)} %pad_add_fusion.meta, bf16[2,1024,128]{2,1,0:T(8,128)(2,1)} %get-tuple-element.120.q_all, ...), custom_call_target="tpu_custom_call" | custom-call | flops 2684354560 | bytes 10485760 | tf_op jit(solution)/shard_map/attend_grad/pallas_call | solution.py:471
  420.9 4.9 collective-permute-done.49
  425.8 5.0 collective-permute-done.51
  433.1 4.0 all-to-all-start.2
  447.5 6.4 %all-to-all-done.2 = bf16[4,128,256]{2,1,0:T(8,128)(2,1)} async-done(((bf16[4,128,256]{2,1,0:T(8,128)(2,1)}), bf16[4,128,256]{2,1,0:T(8,128)(2,1)}, u32[]{:S(2)}, u32[]{:S(2)}) %all-to-all-start.2) | async-done | bytes 262176 | tf_op jit(solution)/shard_map/all_to_all | solution.py:212
  455.0 8.1 %reduce-scatter.15.cloned.1.call-done = bf16[512,512]{1,0:T(8,128)(2,1)} async-done(((bf16[2048,512]{1,0:T(8,128)(2,1)}), bf16[512,512]{1,0:T(8,128)(2,1)}) %reduce-scatter.15.cloned.1.call-update) | async-done | bytes 524304 | tf_op jit(solution)/shard_map/reduce_scatter | solution.py:220
  463.9 4.1 all-to-all-start.3
  480.8 7.8 %collective-permute-done.60 = bf16[1,512,512]{2,1,0:T(8,128)(2,1)} collective-permute-done((bf16[1,512,512]{2,1,0:T(8,128)(2,1)}, bf16[1,512,512]{2,1,0:T(8,128)(2,1)}, u32[]{:S(2)}, u32[]{:S(2)}) %collective-permute-start.60) | collective-permute-done | bytes 524320 | tf_op jit(solution)/shard_map/ppermute | solution.py:59
  488.6 20.7 %reduce-scatter.11.cloned.1.call-done = bf16[512,512]{1,0:T(8,128)(2,1)} async-done(((bf16[2048,512]{1,0:T(8,128)(2,1)}), bf16[512,512]{1,0:T(8,128)(2,1)}) %reduce-scatter.11.cloned.1.call-update) | async-done | bytes 524304 | tf_op jit(solution)/shard_map/reduce_scatter | solution.py:220
  518.4 6.0 collective-permute-done.56
  536.5 10.0 %collective-permute-done.57 = bf16[512,512]{1,0:T(8,128)(2,1)S(1)} collective-permute-done((bf16[512,512]{1,0:T(8,128)(2,1)}, bf16[512,512]{1,0:T(8,128)(2,1)S(1)}, u32[]{:S(2)}, u32[]{:S(2)}) %collective-permute-start.57) | collective-permute-done | bytes 524320 | tf_op jit(solution)/shard_map/ppermute | solution.py:59
  548.8 4.0 fusion.28
  554.9 3.3 all-to-all-start.4
  558.2 5.6 all-to-all-done.4
  566.2 3.4 all-to-all-start.5
  571.4 10.4 %spread_rows.1 = f32[2048,2048]{1,0:T(8,128)} custom-call(s32[14]{0:T(128)S(1)} %copy-done.2, bf16[2,256,1024]{2,1,0:T(8,128)(2,1)S(1)} %pad_maximum_fusion.10.refs_0_, bf16[2,256,1024]{2,1,0:T(8,128)(2,1)} %collective-permute-done.62.refs_1_, bf16[2,256,1024]{2,1,0:T(8,128)(2,1)S(1)} %copy-done.1, bf16[2,256,1024]{2,1,0:T(8,128)(2,1)} %collective-permute-done.64.refs_3_, ...), custom_call_target="tpu_custom_call" | custom-call | tf_op jit(solution)/shard_map/spread_rows/pallas_call | solution.py:738
  587.1 10.4 %spread_columns.3 = f32[512,8192]{1,0:T(8,128)} custom-call(s32[14]{0:T(128)S(1)} %copy-done.2, bf16[2,512,512]{2,1,0:T(8,128)(2,1)S(1)} %pad_maximum_fusion.9.refs_0_, bf16[2,512,512]{2,1,0:T(8,128)(2,1)} %collective-permute-done.61.refs_1_, bf16[2,512,512]{2,1,0:T(8,128)(2,1)} %collective-permute-done.68.refs_2_, ...), custom_call_target="tpu_custom_call" | custom-call | tf_op jit(solution)/shard_map/spread_columns/pallas_call | solution.py:810
  597.4 7.9 %spread_columns.2 = (f32[512,2304]{1,0:T(8,128)}, f32[512,2048]{1,0:T(8,128)}) custom-call(s32[14]{0:T(128)S(1)} %copy-done.2, bf16[4,512,512]{2,1,0:T(8,128)(2,1)} %bitcast.28.refs_0_, bf16[4,512,512]{2,1,0:T(8,128)(2,1)} %bitcast.29.refs_1_, f32[512,256]{1,0:T(8,128)S(1)} %convert_element_type.438.refs_2_), custom_call_target="tpu_custom_call" | custom-call | tf_op jit(solution)/shard_map/spread_columns/pallas_call | solution.py:810
  (453 shorter events, 215.3 us)
Async XLA Ops:
  7.2 242.2 %all-gather.4.cloned.1.call-start = ((), (), s32[]{:S(2)}) async-start(), calls=%async_computation.12 | async-start | bytes 4718592 | tf_op jit(solution)/shard_map/all_gather | solution.py:988
  8.8 42.3 %collective-permute-start.4 = (bf16[1,512,512]{2,1,0:T(8,128)(2,1)S(1)}, bf16[1,512,512]{2,1,0:T(8,128)(2,1)S(1)}, u32[]{:S(2)}, u32[]{:S(2)}) collective-permute-start(bf16[1,512,512]{2,1,0:T(8,128)(2,1)S(1)} %pad_maximum_fusion.13), channel_id=1, source_target_pairs={{0,1},{1,0},{2,3},{3,2},{4,5},{5,4},{6,7},{7,6},{8,9},{9,8},{10,11... | collective-permute-start | bytes 1572872 | tf_op jit(solution)/shard_map/ppermute | solution.py:183
  11.9 25.6 %collective-permute-start.3 = (bf16[1,512,512]{2,1,0:T(8,128)(2,1)S(1)}, bf16[1,512,512]{2,1,0:T(8,128)(2,1)}, u32[]{:S(2)}, u32[]{:S(2)}) collective-permute-start(bf16[1,512,512]{2,1,0:T(8,128)(2,1)S(1)} %pad_maximum_fusion.13), channel_id=1, source_target_pairs={{0,3},{1,2},{2,1},{3,0},{4,7},{5,6},{6,5},{7,4},{8,11},{9,10},{10,... | collective-permute-start | bytes 1572872 | tf_op jit(solution)/shard_map/ppermute | solution.py:183
  14.3 54.0 %collective-permute-start.2 = (bf16[128,2048]{1,0:T(8,128)(2,1)S(1)}, bf16[128,2048]{1,0:T(8,128)(2,1)}, u32[]{:S(2)}, u32[]{:S(2)}) collective-permute-start(bf16[128,2048]{1,0:T(8,128)(2,1)S(1)} %bitcast.111), channel_id=1, source_target_pairs={{0,24},{4,28},{8,16},{12,20},{16,8},{20,12},{24,0},{28,4},{1,25},{... | collective-permute-start | bytes 1572872 | tf_op jit(solution)/shard_map/ppermute | solution.py:59
  16.8 51.6 %collective-permute-start.1 = (bf16[128,2048]{1,0:T(8,128)(2,1)S(1)}, bf16[128,2048]{1,0:T(8,128)(2,1)}, u32[]{:S(2)}, u32[]{:S(2)}) collective-permute-start(bf16[128,2048]{1,0:T(8,128)(2,1)S(1)} %bitcast.112), channel_id=1, source_target_pairs={{0,16},{4,20},{8,24},{12,28},{16,0},{20,4},{24,8},{28,12},{1,17},{... | collective-permute-start | bytes 1572872 | tf_op jit(solution)/shard_map/ppermute | solution.py:59
  72.8 66.0 %collective-permute-start.8 = (bf16[512,2048]{1,0:T(8,128)(2,1)S(1)}, bf16[512,2048]{1,0:T(8,128)(2,1)S(1)}, u32[]{:S(2)}, u32[]{:S(2)}) collective-permute-start(bf16[512,2048]{1,0:T(8,128)(2,1)S(1)} %get-tuple-element.249), channel_id=1, source_target_pairs={{0,4},{4,0},{8,12},{12,8},{16,20},{20,16},{24,28},{28,24},{1,5},{5... | collective-permute-start | bytes 6291464 | tf_op jit(solution)/shard_map/ppermute | solution.py:59
  88.4 37.4 %collective-permute-start.15 = (bf16[2048,256]{1,0:T(8,128)(2,1)S(1)}, bf16[2048,256]{1,0:T(8,128)(2,1)S(1)}, u32[]{:S(2)}, u32[]{:S(2)}) collective-permute-start(bf16[2048,256]{1,0:T(8,128)(2,1)S(1)} %pad_maximum_fusion.5.kv_even), channel_id=1, source_target_pairs={{0,4},{4,0},{8,12},{12,8},{16,20},{20,16},{24,28},{28,24},{1,5},{5... | collective-permute-start | bytes 3145736 | tf_op jit(solution)/shard_map/ppermute | solution.py:59
  88.5 48.9 %collective-permute-start.17 = (bf16[1,512,1024]{2,1,0:T(8,128)(2,1)}, bf16[1,512,1024]{2,1,0:T(8,128)(2,1)}, u32[]{:S(2)}, u32[]{:S(2)}) collective-permute-start(bf16[1,512,1024]{2,1,0:T(8,128)(2,1)} %bitcast.13), channel_id=1, source_target_pairs={{0,3},{1,2},{2,1},{3,0},{4,7},{5,6},{6,5},{7,4},{8,11},{9,10},{10,... | collective-permute-start | bytes 3145736 | tf_op jit(solution)/shard_map/ppermute | solution.py:183
  92.1 29.7 %collective-permute-start.24 = (bf16[1,512,256]{2,1,0:T(8,128)(2,1)S(1)}, bf16[1,512,256]{2,1,0:T(8,128)(2,1)S(1)}, u32[]{:S(2)}, u32[]{:S(2)}) collective-permute-start(bf16[1,512,256]{2,1,0:T(8,128)(2,1)S(1)} %collective-permute-done.16), channel_id=1, source_target_pairs={{0,1},{1,0},{2,3},{3,2},{4,5},{5,4},{6,7},{7,6},{8,9},{9,8},{10,11... | collective-permute-start | bytes 786440 | tf_op jit(solution)/shard_map/ppermute | solution.py:183
  94.9 29.3 %collective-permute-start.19 = (bf16[1,2,512,256]{3,2,1,0:T(8,128)(2,1)S(1)}, bf16[1,2,512,256]{3,2,1,0:T(8,128)(2,1)S(1)}, u32[]{:S(2)}, u32[]{:S(2)}) collective-permute-start(bf16[1,2,512,256]{3,2,1,0:T(8,128)(2,1)S(1)} %bitcast.119), channel_id=1, source_target_pairs={{0,16},{4,20},{8,24},{12,28},{16,0},{20,4},{24,8},{28,12},{1,17},{... | collective-permute-start | bytes 1572872 | tf_op jit(solution)/shard_map/ppermute | solution.py:59
  124.2 38.1 %collective-permute-start.18 = (bf16[1,512,1024]{2,1,0:T(8,128)(2,1)}, bf16[1,512,1024]{2,1,0:T(8,128)(2,1)}, u32[]{:S(2)}, u32[]{:S(2)}) collective-permute-start(bf16[1,512,1024]{2,1,0:T(8,128)(2,1)} %bitcast.13), channel_id=1, source_target_pairs={{0,1},{1,0},{2,3},{3,2},{4,5},{5,4},{6,7},{7,6},{8,9},{9,8},{10,11... | collective-permute-start | bytes 3145736 | tf_op jit(solution)/shard_map/ppermute | solution.py:183
  125.8 55.7 %collective-permute-start.21 = (bf16[2,2,512,256]{3,2,1,0:T(8,128)(2,1)S(1)}, bf16[2,2,512,256]{3,2,1,0:T(8,128)(2,1)}, u32[]{:S(2)}, u32[]{:S(2)}) collective-permute-start(bf16[2,2,512,256]{3,2,1,0:T(8,128)(2,1)S(1)} %pad_maximum_fusion.7.refs_0_), channel_id=1, source_target_pairs={{0,4},{4,0},{8,12},{12,8},{16,20},{20,16},{24,28},{28,24},{1,5},{5... | collective-permute-start | bytes 3145736 | tf_op jit(solution)/shard_map/ppermute | solution.py:59
  135.8 26.0 %collective-permute-start.20 = (bf16[2,2,512,256]{3,2,1,0:T(8,128)(2,1)S(1)}, bf16[2,2,512,256]{3,2,1,0:T(8,128)(2,1)}, u32[]{:S(2)}, u32[]{:S(2)}) collective-permute-start(bf16[2,2,512,256]{3,2,1,0:T(8,128)(2,1)S(1)} %pad_maximum_fusion.7.refs_0_), channel_id=1, source_target_pairs={{0,8},{4,12},{8,0},{12,4},{16,24},{20,28},{24,16},{28,20},{1,9},{5... | collective-permute-start | bytes 3145736 | tf_op jit(solution)/shard_map/ppermute | solution.py:59
  137.4 24.4 %collective-permute-start.26 = (bf16[2,2,512,256]{3,2,1,0:T(8,128)(2,1)}, bf16[2,2,512,256]{3,2,1,0:T(8,128)(2,1)}, u32[]{:S(2)}, u32[]{:S(2)}) collective-permute-start(bf16[2,2,512,256]{3,2,1,0:T(8,128)(2,1)} %pad_maximum_fusion.8.refs_4_), channel_id=1, source_target_pairs={{0,16},{4,20},{8,24},{12,28},{16,0},{20,4},{24,8},{28,12},{1,17},{... | collective-permute-start | bytes 3145736 | tf_op jit(solution)/shard_map/ppermute | solution.py:59
  138.8 39.3 %collective-permute-start.36 = (bf16[1,512,1024]{2,1,0:T(8,128)(2,1)}, bf16[1,512,1024]{2,1,0:T(8,128)(2,1)}, u32[]{:S(2)}, u32[]{:S(2)}) collective-permute-start(bf16[1,512,1024]{2,1,0:T(8,128)(2,1)} %collective-permute-done.17), channel_id=1, source_target_pairs={{0,1},{1,0},{2,3},{3,2},{4,5},{5,4},{6,7},{7,6},{8,9},{9,8},{10,11... | collective-permute-start | bytes 3145736 | tf_op jit(solution)/shard_map/ppermute | solution.py:183
  161.8 22.7 %collective-permute-start.22 = (bf16[2,2,512,256]{3,2,1,0:T(8,128)(2,1)}, bf16[2,2,512,256]{3,2,1,0:T(8,128)(2,1)}, u32[]{:S(2)}, u32[]{:S(2)}) collective-permute-start(bf16[2,2,512,256]{3,2,1,0:T(8,128)(2,1)} %collective-permute-done.20.refs_1_), channel_id=1, source_target_pairs={{0,4},{4,0},{8,12},{12,8},{16,20},{20,16},{24,28},{28,24},{1,5},{5... | collective-permute-start | bytes 3145736 | tf_op jit(solution)/shard_map/ppermute | solution.py:59
  162.3 22.2 %collective-permute-start.28 = (bf16[2,2,512,256]{3,2,1,0:T(8,128)(2,1)}, bf16[2,2,512,256]{3,2,1,0:T(8,128)(2,1)}, u32[]{:S(2)}, u32[]{:S(2)}) collective-permute-start(bf16[2,2,512,256]{3,2,1,0:T(8,128)(2,1)} %collective-permute-done.26.refs_5_), channel_id=1, source_target_pairs={{0,4},{4,0},{8,12},{12,8},{16,20},{20,16},{24,28},{28,24},{1,5},{5... | collective-permute-start | bytes 3145736 | tf_op jit(solution)/shard_map/ppermute | solution.py:59
  166.5 97.7 %all-gather.8.cloned.1.call-start = ((), (), s32[]{:S(2)}) async-start(), calls=%async_computation.14 | async-start | bytes 2621440 | tf_op jit(solution)/shard_map/all_gather | solution.py:216
  181.0 96.7 %all-gather.6.cloned.1.call-start = ((), (), s32[]{:S(2)}) async-start(), calls=%async_computation.13 | async-start | bytes 2621440 | tf_op jit(solution)/shard_map/all_gather | solution.py:216
  205.0 23.2 %collective-permute-start.33 = (bf16[128,2048]{1,0:T(8,128)(2,1)S(1)}, bf16[128,2048]{1,0:T(8,128)(2,1)S(1)}, u32[]{:S(2)}, u32[]{:S(2)}) collective-permute-start(bf16[128,2048]{1,0:T(8,128)(2,1)S(1)} %add_convert_fusion.1), channel_id=1, source_target_pairs={{0,16},{4,20},{8,24},{12,28},{16,0},{20,4},{24,8},{28,12},{1,17},{... | collective-permute-start | bytes 1572872 | tf_op jit(solution)/shard_map/ppermute | solution.py:59
  230.2 129.5 %reduce-scatter.9.cloned.1.call-start = ((), (), s32[]{:S(2)}) async-start(), calls=%async_computation.16 | async-start | bytes 2621440 | tf_op jit(solution)/shard_map/reduce_scatter | solution.py:220
  277.7 90.2 %reduce-scatter.7.cloned.1.call-start = ((), (), s32[]{:S(2)}) async-start(), calls=%async_computation.15 | async-start | bytes 2621440 | tf_op jit(solution)/shard_map/reduce_scatter | solution.py:220
  278.2 176.7 %reduce-scatter.17.cloned.1.call-start = ((), (), s32[]{:S(2)}) async-start(), calls=%async_computation.20 | async-start | bytes 2621440 | tf_op jit(solution)/shard_map/reduce_scatter | solution.py:220
  309.3 24.4 %collective-permute-start.39 = (bf16[128,2048]{1,0:T(8,128)(2,1)S(1)}, bf16[128,2048]{1,0:T(8,128)(2,1)}, u32[]{:S(2)}, u32[]{:S(2)}) collective-permute-start(bf16[128,2048]{1,0:T(8,128)(2,1)S(1)} %get-tuple-element.267), channel_id=1, source_target_pairs={{0,16},{4,20},{8,24},{12,28},{16,0},{20,4},{24,8},{28,12},{1,17},{... | collective-permute-start | bytes 1572872 | tf_op jit(solution)/shard_map/ppermute | solution.py:59
  309.9 23.9 %collective-permute-start.38 = (bf16[128,2048]{1,0:T(8,128)(2,1)S(1)}, bf16[128,2048]{1,0:T(8,128)(2,1)}, u32[]{:S(2)}, u32[]{:S(2)}) collective-permute-start(bf16[128,2048]{1,0:T(8,128)(2,1)S(1)} %get-tuple-element.268), channel_id=1, source_target_pairs={{0,8},{4,12},{8,0},{12,4},{16,24},{20,28},{24,16},{28,20},{1,9},{5... | collective-permute-start | bytes 1572872 | tf_op jit(solution)/shard_map/ppermute | solution.py:59
  333.8 129.3 %reduce-scatter.15.cloned.1.call-start = ((), (), s32[]{:S(2)}) async-start(), calls=%async_computation.19 | async-start | bytes 2621440 | tf_op jit(solution)/shard_map/reduce_scatter | solution.py:220
  335.8 33.6 %collective-permute-start.41 = (bf16[512,2048]{1,0:T(8,128)(2,1)}, bf16[512,2048]{1,0:T(8,128)(2,1)}, u32[]{:S(2)}, u32[]{:S(2)}) collective-permute-start(bf16[512,2048]{1,0:T(8,128)(2,1)} %get-tuple-element.118), channel_id=1, source_target_pairs={{0,4},{4,0},{8,12},{12,8},{16,20},{20,16},{24,28},{28,24},{1,5},{5... | collective-permute-start | bytes 6291464 | tf_op jit(solution)/shard_map/ppermute | solution.py:59
  340.4 57.5 %collective-permute-start.55 = (bf16[512,2048]{1,0:T(8,128)(2,1)}, bf16[512,2048]{1,0:T(8,128)(2,1)}, u32[]{:S(2)}, u32[]{:S(2)}) collective-permute-start(bf16[512,2048]{1,0:T(8,128)(2,1)} %constant_dynamic-update-slice_fusion.5), channel_id=1, source_target_pairs={{0,4},{4,0},{8,12},{12,8},{16,20},{20,16},{24,28},{28,24},{1,5},{5... | collective-permute-start | bytes 6291464 | tf_op jit(solution)/shard_map/ppermute | solution.py:59
  359.4 149.9 %reduce-scatter.11.cloned.1.call-start = ((), (), s32[]{:S(2)}) async-start(), calls=%async_computation.17 | async-start | bytes 2621440 | tf_op jit(solution)/shard_map/reduce_scatter | solution.py:220
  359.7 44.8 %collective-permute-start.43 = (bf16[1,256,1024]{2,1,0:T(8,128)(2,1)}, bf16[1,256,1024]{2,1,0:T(8,128)(2,1)}, u32[]{:S(2)}, u32[]{:S(2)}) collective-permute-start(bf16[1,256,1024]{2,1,0:T(8,128)(2,1)} %bitcast.136), channel_id=1, source_target_pairs={{0,8},{4,12},{8,0},{12,4},{16,24},{20,28},{24,16},{28,20},{1,9},{5... | collective-permute-start | bytes 1572872 | tf_op jit(solution)/shard_map/ppermute | solution.py:59
  367.9 36.7 %collective-permute-start.42 = (bf16[1,256,1024]{2,1,0:T(8,128)(2,1)}, bf16[1,256,1024]{2,1,0:T(8,128)(2,1)}, u32[]{:S(2)}, u32[]{:S(2)}) collective-permute-start(bf16[1,256,1024]{2,1,0:T(8,128)(2,1)} %bitcast.142), channel_id=1, source_target_pairs={{0,16},{4,20},{8,24},{12,28},{16,0},{20,4},{24,8},{28,12},{1,17},{... | collective-permute-start | bytes 1572872 | tf_op jit(solution)/shard_map/ppermute | solution.py:59
  377.2 27.4 %collective-permute-start.46 = (bf16[128,2048]{1,0:T(8,128)(2,1)S(1)}, bf16[128,2048]{1,0:T(8,128)(2,1)S(1)}, u32[]{:S(2)}, u32[]{:S(2)}) collective-permute-start(bf16[128,2048]{1,0:T(8,128)(2,1)S(1)} %get-tuple-element.263), channel_id=1, source_target_pairs={{0,24},{4,28},{8,16},{12,20},{16,8},{20,12},{24,0},{28,4},{1,25},{... | collective-permute-start | bytes 1572872 | tf_op jit(solution)/shard_map/ppermute | solution.py:59
  378.3 29.2 %collective-permute-start.45 = (bf16[128,2048]{1,0:T(8,128)(2,1)S(1)}, bf16[128,2048]{1,0:T(8,128)(2,1)S(1)}, u32[]{:S(2)}, u32[]{:S(2)}) collective-permute-start(bf16[128,2048]{1,0:T(8,128)(2,1)S(1)} %get-tuple-element.264), channel_id=1, source_target_pairs={{0,16},{4,20},{8,24},{12,28},{16,0},{20,4},{24,8},{28,12},{1,17},{... | collective-permute-start | bytes 1572872 | tf_op jit(solution)/shard_map/ppermute | solution.py:59
  404.5 32.6 %collective-permute-start.47 = (bf16[512,2048]{1,0:T(8,128)(2,1)S(1)}, bf16[512,2048]{1,0:T(8,128)(2,1)}, u32[]{:S(2)}, u32[]{:S(2)}) collective-permute-start(bf16[512,2048]{1,0:T(8,128)(2,1)S(1)} %convolution_convert_fusion.1), channel_id=1, source_target_pairs={{0,4},{4,0},{8,12},{12,8},{16,20},{20,16},{24,28},{28,24},{1,5},{5... | collective-permute-start | bytes 6291464 | tf_op jit(solution)/shard_map/ppermute | solution.py:59
  442.0 28.2 %collective-permute-start.54 = (bf16[128,2048]{1,0:T(8,128)(2,1)}, bf16[128,2048]{1,0:T(8,128)(2,1)}, u32[]{:S(2)}, u32[]{:S(2)}) collective-permute-start(bf16[128,2048]{1,0:T(8,128)(2,1)} %get-tuple-element.260), channel_id=1, source_target_pairs={{0,24},{4,28},{8,16},{12,20},{16,8},{20,12},{24,0},{28,4},{1,25},{... | collective-permute-start | bytes 1572872 | tf_op jit(solution)/shard_map/ppermute | solution.py:59
  445.5 70.2 %collective-permute-start.63 = (bf16[2,256,1024]{2,1,0:T(8,128)(2,1)S(1)}, bf16[2,256,1024]{2,1,0:T(8,128)(2,1)S(1)}, u32[]{:S(2)}, u32[]{:S(2)}) collective-permute-start(bf16[2,256,1024]{2,1,0:T(8,128)(2,1)S(1)} %pad_maximum_fusion.10.refs_0_), channel_id=1, source_target_pairs={{0,4},{4,0},{8,12},{12,8},{16,20},{20,16},{24,28},{28,24},{1,5},{5... | collective-permute-start | bytes 3145736 | tf_op jit(solution)/shard_map/ppermute | solution.py:59
  445.6 30.2 %collective-permute-start.53 = (bf16[128,2048]{1,0:T(8,128)(2,1)}, bf16[128,2048]{1,0:T(8,128)(2,1)}, u32[]{:S(2)}, u32[]{:S(2)}) collective-permute-start(bf16[128,2048]{1,0:T(8,128)(2,1)} %get-tuple-element.261), channel_id=1, source_target_pairs={{0,16},{4,20},{8,24},{12,28},{16,0},{20,4},{24,8},{28,12},{1,17},{... | collective-permute-start | bytes 1572872 | tf_op jit(solution)/shard_map/ppermute | solution.py:59
  446.1 30.6 %collective-permute-start.52 = (bf16[128,2048]{1,0:T(8,128)(2,1)}, bf16[128,2048]{1,0:T(8,128)(2,1)}, u32[]{:S(2)}, u32[]{:S(2)}) collective-permute-start(bf16[128,2048]{1,0:T(8,128)(2,1)} %get-tuple-element.262), channel_id=1, source_target_pairs={{0,8},{4,12},{8,0},{12,4},{16,24},{20,28},{24,16},{28,20},{1,9},{5... | collective-permute-start | bytes 1572872 | tf_op jit(solution)/shard_map/ppermute | solution.py:59
  468.0 118.0 %reduce-scatter.13.cloned.1.call-start = ((), (), s32[]{:S(2)}) async-start(), calls=%async_computation.18 | async-start | bytes 1310720 | tf_op jit(solution)/shard_map/reduce_scatter | solution.py:220
  470.3 42.8 %collective-permute-start.70 = (bf16[1,512,512]{2,1,0:T(8,128)(2,1)}, bf16[1,512,512]{2,1,0:T(8,128)(2,1)}, u32[]{:S(2)}, u32[]{:S(2)}) collective-permute-start(bf16[1,512,512]{2,1,0:T(8,128)(2,1)} %bitcast.138), channel_id=1, source_target_pairs={{0,8},{4,12},{8,0},{12,4},{16,24},{20,28},{24,16},{28,20},{1,9},{5... | collective-permute-start | bytes 1572872 | tf_op jit(solution)/shard_map/ppermute | solution.py:59
  475.8 56.3 %collective-permute-start.62 = (bf16[2,256,1024]{2,1,0:T(8,128)(2,1)S(1)}, bf16[2,256,1024]{2,1,0:T(8,128)(2,1)}, u32[]{:S(2)}, u32[]{:S(2)}) collective-permute-start(bf16[2,256,1024]{2,1,0:T(8,128)(2,1)S(1)} %pad_maximum_fusion.10.refs_0_), channel_id=1, source_target_pairs={{0,8},{4,12},{8,0},{12,4},{16,24},{20,28},{24,16},{28,20},{1,9},{5... | collective-permute-start | bytes 3145736 | tf_op jit(solution)/shard_map/ppermute | solution.py:59
  476.7 55.9 %collective-permute-start.65 = (bf16[2,256,1024]{2,1,0:T(8,128)(2,1)S(1)}, bf16[2,256,1024]{2,1,0:T(8,128)(2,1)}, u32[]{:S(2)}, u32[]{:S(2)}) collective-permute-start(bf16[2,256,1024]{2,1,0:T(8,128)(2,1)S(1)} %pad_maximum_fusion.11.refs_4_), channel_id=1, source_target_pairs={{0,16},{4,20},{8,24},{12,28},{16,0},{20,4},{24,8},{28,12},{1,17},{... | collective-permute-start | bytes 3145736 | tf_op jit(solution)/shard_map/ppermute | solution.py:59
  513.1 35.1 %collective-permute-start.66 = (bf16[2,256,1024]{2,1,0:T(8,128)(2,1)S(1)}, bf16[2,256,1024]{2,1,0:T(8,128)(2,1)}, u32[]{:S(2)}, u32[]{:S(2)}) collective-permute-start(bf16[2,256,1024]{2,1,0:T(8,128)(2,1)S(1)} %pad_maximum_fusion.11.refs_4_), channel_id=1, source_target_pairs={{0,4},{4,0},{8,12},{12,8},{16,20},{20,16},{24,28},{28,24},{1,5},{5... | collective-permute-start | bytes 3145736 | tf_op jit(solution)/shard_map/ppermute | solution.py:59
  532.0 49.7 %collective-permute-start.71 = (bf16[2,512,512]{2,1,0:T(8,128)(2,1)}, bf16[2,512,512]{2,1,0:T(8,128)(2,1)}, u32[]{:S(2)}, u32[]{:S(2)}) collective-permute-start(bf16[2,512,512]{2,1,0:T(8,128)(2,1)} %pad_maximum_fusion.12.refs_4_), channel_id=1, source_target_pairs={{0,16},{4,20},{8,24},{12,28},{16,0},{20,4},{24,8},{28,12},{1,17},{... | collective-permute-start | bytes 3145736 | tf_op jit(solution)/shard_map/ppermute | solution.py:59
  532.6 49.2 %collective-permute-start.61 = (bf16[2,512,512]{2,1,0:T(8,128)(2,1)S(1)}, bf16[2,512,512]{2,1,0:T(8,128)(2,1)}, u32[]{:S(2)}, u32[]{:S(2)}) collective-permute-start(bf16[2,512,512]{2,1,0:T(8,128)(2,1)S(1)} %pad_maximum_fusion.9.refs_0_), channel_id=1, source_target_pairs={{0,8},{4,12},{8,0},{12,4},{16,24},{20,28},{24,16},{28,20},{1,9},{5... | collective-permute-start | bytes 3145736 | tf_op jit(solution)/shard_map/ppermute | solution.py:59
  536.5 33.0 %collective-permute-start.64 = (bf16[2,256,1024]{2,1,0:T(8,128)(2,1)}, bf16[2,256,1024]{2,1,0:T(8,128)(2,1)}, u32[]{:S(2)}, u32[]{:S(2)}) collective-permute-start(bf16[2,256,1024]{2,1,0:T(8,128)(2,1)} %collective-permute-done.62.refs_1_), channel_id=1, source_target_pairs={{0,4},{4,0},{8,12},{12,8},{16,20},{20,16},{24,28},{28,24},{1,5},{5... | collective-permute-start | bytes 3145736 | tf_op jit(solution)/shard_map/ppermute | solution.py:59
  546.5 23.4 %collective-permute-start.67 = (bf16[2,256,1024]{2,1,0:T(8,128)(2,1)}, bf16[2,256,1024]{2,1,0:T(8,128)(2,1)}, u32[]{:S(2)}, u32[]{:S(2)}) collective-permute-start(bf16[2,256,1024]{2,1,0:T(8,128)(2,1)} %collective-permute-done.65.refs_5_), channel_id=1, source_target_pairs={{0,4},{4,0},{8,12},{12,8},{16,20},{20,16},{24,28},{28,24},{1,5},{5... | collective-permute-start | bytes 3145736 | tf_op jit(solution)/shard_map/ppermute | solution.py:59
  548.2 49.2 %collective-permute-start.59 = (bf16[2048,512]{1,0:T(8,128)(2,1)}, bf16[2048,512]{1,0:T(8,128)(2,1)}, u32[]{:S(2)}, u32[]{:S(2)}) collective-permute-start(bf16[2048,512]{1,0:T(8,128)(2,1)} %constant_dynamic-update-slice_fusion.9), channel_id=1, source_target_pairs={{0,4},{4,0},{8,12},{12,8},{16,20},{20,16},{24,28},{28,24},{1,5},{5... | collective-permute-start | bytes 6291464 | tf_op jit(solution)/shard_map/ppermute | solution.py:59
  (107 other events, 1739.5 us)
Sparse Core Ops, SparseCore 0:
  20.7 48.8 all-gather.3
  181.1 46.8 all-gather.7
  230.3 47.2 all-gather.5
  279.8 42.5 reduce-scatter.8
  324.6 43.2 reduce-scatter.6
  370.0 43.1 reduce-scatter.16
  415.7 47.3 reduce-scatter.14
  465.9 43.3 reduce-scatter.10
  515.8 25.8 reduce-scatter.12

commit v5 on v4

--- a/solution.py
+++ b/solution.py
@@ -107,7 +107,7 @@
 
 
 def ctx_gather_halves(
-    first, second, wait=lambda values: values, last=lambda values: values, begun=None
+    first, second, wait=lambda values: values, last=lambda values: values, begun=None, finish=None
 ):
     held, offsets = [first[None], second[None]], [[0], [0]]
     steps = len(chip_masks(0))
@@ -121,6 +121,9 @@
             for side in range(2):
                 held[side] = jnp.concatenate([held[side], wait(sent[side][0])], axis=0)
                 offsets[side] = offsets[side] + sent[side][1]
+    if finish:
+        came = finish([got for got, _ in sent])
+        sent = [(got, order) for got, (_, order) in zip(came, sent)]
     gathered = []
     for side in range(2):
         parts = [(held[side], offsets[side]), (last(sent[side][0]), sent[side][1])]
@@ -1033,9 +1036,23 @@
     gkv_odd, first_sent, r_parts = lax.optimization_barrier((gkv_odd, first_sent, r_parts))
     result = (middle + (ctx_scatter_sum(r_total, r_parts) + proj_bias)).astype(BF16)
     gkv_plane = ctx_scatter(gkv_even, gkv_odd)
+    d_q = mm_rows(a_even, gq_even) + mm_rows(a_odd, gq_odd)
+    d_out = mm_rows(o_even, ga_even) + mm_rows(o_odd, ga_odd)
+    d_pair = with_layout_constraint(
+        jnp.concatenate([d_q, d_out], axis=1).astype(BF16), Layout(major_to_minor=(0, 1))
+    )
+    d_pair = z_scatter_queued(d_pair)
+    pair = []
+
+    def finish(parts):
+        parts, d_done = lax.optimization_barrier((parts, d_pair))
+        pair.append(d_done)
+        return parts
+
     d_proj = ctx_gather_halves(
-        *d_proj, wait=lambda part: after(part, gkv_plane), begun=first_sent
-    )
+        *d_proj, wait=lambda part: after(part, gkv_plane), begun=first_sent, finish=finish
+    )
+    (d_pair,) = pair
     gkv_low = z_sum_exchange(gkv_plane.astype(BF16).reshape(fsdp_count, tokens, 2 * HD)).astype(BF16)
     gkv_all = ctx_exchange(jnp.broadcast_to(gkv_low[None], (ctx_count,) + gkv_low.shape))
     gl_total, gl_low = ctx_scatter_cores(mm_t(gq_even, w_q), mm_t(gq_odd, w_q))
@@ -1060,12 +1077,6 @@
         *[after(part, gkv_low) for part in d_fc], last=lambda part: after(part, grad_w_proj)
     )
     (grad_w_fc,) = spread_columns(meta, d_fc, fsdp_count // 2, True)
-    d_q = mm_rows(a_even, gq_even) + mm_rows(a_odd, gq_odd)
-    d_out = mm_rows(o_even, ga_even) + mm_rows(o_odd, ga_odd)
-    d_pair = with_layout_constraint(
-        jnp.concatenate([d_q, d_out], axis=1).astype(BF16), Layout(major_to_minor=(0, 1))
-    )
-    d_pair = z_scatter_queued(d_pair)
     d_kv = (mm_rows(a_even, gkv_even) + mm_rows(a_odd, gkv_odd)).astype(BF16)
     d_kv = z_scatter_queued(d_kv).astype(F32)
     d_pair = [
@@ -1097,6 +1108,7 @@
     stacked = jnp.concatenate(
         [member.reshape(fsdp_count, -1) for member in g_vectors], axis=1
     ).astype(BF16)
+    stacked, grad_w_proj = lax.optimization_barrier((stacked, grad_w_proj))
     own = z_sum_exchange(stacked).astype(BF16)
     own = ctx_exchange(jnp.broadcast_to(own[None], (ctx_count,) + own.shape))
     summed = jnp.sum(own, axis=0, dtype=F32)

time: 623 us -> 622 us (level)
  waiting for transfers between devices: 222 us -> 211 us
    reduce_scatter x6, waiting for transfers between devices: 35.1 us -> 7.12 us  [z_scatter_queued(): return lax.psum_scatter(values, 'fsdp', scatter_dimension=0, tiled=True)]
    ppermute x60, waiting for transfers between devices: 103 us -> 125 us  [ctx_swap(): return lax.ppermute(values, 'ctx', [(at, at ^ mask) for at in range(count)])]
    unnamed x155 -> x140, local copies, waits for them, and re-layouts: 23.1 us -> 23 us
  transfers between devices with their start and end apart: 89 -> 89, of which waited for: 37 -> 37; matrix products, arithmetic and copies ran while one was open for 20% -> 22% of each run, Pallas kernels for 21% -> 21%
where the time goes in v5:
time: 622 us; the launch traced here: 611 us
  waiting for transfers between devices  211 us (34%)
  Pallas kernels  139 us (22%)
  starting transfers between devices  101 us (16%)
  other arithmetic  55.7 us (9%)
  local copies, waits for them, and re-layouts  50.3 us (8%)
  matrix products  36.8 us (6%)
  between operations  16.2 us (3%)
    ppermute x60, waiting for transfers between devices, ctx_swap(): return lax.ppermute(values, 'ctx', [(at, at ^ mask) for at in range(count)])  125 us
    ppermute x60, starting transfers between devices, ctx_swap(): return lax.ppermute(values, 'ctx', [(at, at ^ mask) for at in range(count)])  51.8 us
    ppermute x14, waiting for transfers between devices, z_swap(): lax.ppermute(values, 'fsdp', [(at, at ^ mask) for at in range(count)])  51.3 us
    ppermute x14, starting transfers between devices, z_swap(): lax.ppermute(values, 'fsdp', [(at, at ^ mask) for at in range(count)])  24.9 us
    dot_general x7, matrix products, mm_rows(): lax.dot_general(left, right, (((0,), (0,)), ((), ())), preferred_element_...  23.6 us
    unnamed x140, local copies, waits for them, and re-layouts  23 us
    pallas_call x2, Pallas kernels, spread_columns(): pl.pallas_call(functools.partial(spread_kernel, moves, extras, len(sizes)...  18.2 us
    pallas_call x1, Pallas kernels, feed_late(): pl.pallas_call(functools.partial(feed_late_kernel, steps), grid=(2 * step...  18 us
  transfers between devices with their start and end apart: 89, of which 37 were waited for; matrix products, arithmetic and copies ran while one was open for 22% of the time, Pallas kernels for 21%

profile of v5, /device:TPU:0, one launch (start us, length us, event | category | flops | bytes accessed | tf_op | source)
XLA Modules:
  0.0 610.6 jit_solution(5423727276367083928)
XLA Ops:
  21.0 16.4 %collective-permute-done.3 = bf16[1,512,512]{2,1,0:T(8,128)(2,1)} collective-permute-done((bf16[1,512,512]{2,1,0:T(8,128)(2,1)S(1)}, bf16[1,512,512]{2,1,0:T(8,128)(2,1)}, u32[]{:S(2)}, u32[]{:S(2)}) %collective-permute-start.3) | collective-permute-done | bytes 524320 | tf_op jit(solution)/shard_map/ppermute | solution.py:186
  44.7 5.6 collective-permute-done.6
  55.6 3.7 place_first.1
  77.5 3.4 collective-permute-start.16
  84.5 3.7 collective-permute-done.13
  88.5 3.6 collective-permute-start.17
  96.5 25.3 %collective-permute-done.24 = bf16[1,512,256]{2,1,0:T(8,128)(2,1)S(1)} collective-permute-done((bf16[1,512,256]{2,1,0:T(8,128)(2,1)S(1)}, bf16[1,512,256]{2,1,0:T(8,128)(2,1)S(1)}, u32[]{:S(2)}, u32[]{:S(2)}) %collective-permute-start.24) | collective-permute-done | bytes 262176 | tf_op jit(solution)/shard_map/ppermute | solution.py:186
  125.9 9.9 %collective-permute-done.25 = bf16[1,2,512,256]{3,2,1,0:T(8,128)(2,1)S(1)} collective-permute-done((bf16[1,2,512,256]{3,2,1,0:T(8,128)(2,1)S(1)}, bf16[1,2,512,256]{3,2,1,0:T(8,128)(2,1)S(1)}, u32[]{:S(2)}, u32[]{:S(2)}) %collective-permute-start.25) | collective-permute-done | bytes 524320 | tf_op jit(solution)/shard_map/ppermute | solution.py:59
  143.4 14.4 %attend.1 = (bf16[1024,256]{1,0:T(8,128)(2,1)}, bf16[2,1024,128]{2,1,0:T(8,128)(2,1)}, bf16[2,2048,256]{2,1,0:T(8,128)(2,1)}, f32[8,128,256]{2,1,0:T(8,128)}, f32[8,1,256]{2,1,0:T(1,128)}) custom-call(s32[14]{0:T(128)} %pad_add_fusion.meta, bf16[512,256]{1,0:T(8,128)(2,1)} %fusion.15.q_even, bf16[512,256]{1,0:T(8,128)(2,1)} %fusion.16.q_odd, ...), custom_call_target="tpu_custom_call" | custom-call | flops 1073741824 | bytes 8388608 | tf_op jit(solution)/shard_map/attend/pallas_call | solution.py:447
  157.8 3.9 collective-permute-done.26.refs_5_
  162.3 4.1 all-to-all-start
  172.3 3.9 all-to-all-done
  184.5 6.7 %branch.1 = f32[128,2048]{1,0:T(8,128)} custom-call(s32[14]{0:T(128)} %pad_add_fusion.meta, bf16[128,2048]{1,0:T(8,128)(2,1)} %bitcast.43.rows_ref, bf16[2,2,512,256]{3,2,1,0:T(8,128)(2,1)} %copy-done.6, bf16[2,2,512,256]{3,2,1,0:T(8,128)(2,1)} %collective-permute-done.20.refs_1_, bf16[2,2,512,256]{3,2,1,0:T(8,128)(2,1)} %collective-permute-done.21.refs_2_, ...), custom_call_target="tpu_custom_call" | custom-call | flops 1073741824 | bytes 8388608 | tf_op jit(solution)/shard_map/branch/pallas_call | solution.py:693
  194.2 7.8 %collective-permute-done.30 = bf16[128,2048]{1,0:T(8,128)(2,1)S(1)} collective-permute-done((bf16[128,2048]{1,0:T(8,128)(2,1)}, bf16[128,2048]{1,0:T(8,128)(2,1)S(1)}, u32[]{:S(2)}, u32[]{:S(2)}) %collective-permute-start.30) | collective-permute-done | bytes 524320 | tf_op jit(solution)/shard_map/ppermute | solution.py:59
  206.4 11.6 %collective-permute-done.34 = bf16[128,2048]{1,0:T(8,128)(2,1)S(1)} collective-permute-done((bf16[128,2048]{1,0:T(8,128)(2,1)S(1)}, bf16[128,2048]{1,0:T(8,128)(2,1)S(1)}, u32[]{:S(2)}, u32[]{:S(2)}) %collective-permute-start.34) | collective-permute-done | bytes 524320 | tf_op jit(solution)/shard_map/ppermute | solution.py:59
  218.0 10.1 %collective-permute-done.33 = bf16[128,2048]{1,0:T(8,128)(2,1)S(1)} collective-permute-done((bf16[128,2048]{1,0:T(8,128)(2,1)S(1)}, bf16[128,2048]{1,0:T(8,128)(2,1)S(1)}, u32[]{:S(2)}, u32[]{:S(2)}) %collective-permute-start.33) | collective-permute-done | bytes 524320 | tf_op jit(solution)/shard_map/ppermute | solution.py:59
  238.5 10.9 %feed_hidden.1 = (f32[1024,1024]{1,0:T(8,128)}, bf16[1024,1024]{1,0:T(8,128)(2,1)}) custom-call(s32[14]{0:T(128)} %pad_add_fusion.meta, bf16[1024,2048]{1,0:T(8,128)(2,1)} %copy-done.42, f32[1,1024]{1,0:T(1,128)} %bitcast.180, bf16[2,512,1024]{2,1,0:T(8,128)(2,1)} %pad_maximum_fusion.1.refs_0_, bf16[1,512,1024]{2,1,0:T(8,128)(2,1)} %collective-permute-done.18.refs_1_, ...), custom_call_target="tpu_custom_call" | custom-call | flops 4294967296 | bytes 14680064 | tf_op jit(solution)/shard_map/feed_hidden/pallas_call | solution.py:523
  249.4 5.3 place_rows.1.grads_ref
  254.7 7.0 %convolution_convert_fusion = bf16[1024,2048]{1,0:T(8,128)(2,1)S(1)} fusion(bf16[1024,1024]{1,0:T(8,128)(2,1)S(1)} %copy-done.57, bf16[1024,2048]{1,0:T(8,128)(2,1)} %place_rows.1.grads_ref), kind=kOutput, calls=%fused_computation.19 | convolution fusion | flops 4297064448 | bytes 10485760 | tf_op jit(solution)/shard_map/dot_general | solution.py:50
  264.2 13.4 %all-gather.6.cloned.1.call-done.first = bf16[1024,1024]{1,0:T(8,128)(2,1)} async-done(((bf16[256,1024]{1,0:T(8,128)(2,1)}), bf16[1024,1024]{1,0:T(8,128)(2,1)}) %all-gather.6.cloned.1.call-update) | async-done | bytes 2097168 | tf_op jit(solution)/shard_map/all_gather | solution.py:219
  278.4 11.1 %feed_hidden_grad.1 = (bf16[1024,1024]{1,0:T(8,128)(2,1)}, f32[1,1024]{1,0:T(1,128)}) custom-call(bf16[1024,2048]{1,0:T(8,128)(2,1)} %place_rows.1.grads_ref, f32[1024,1024]{1,0:T(8,128)} %get-tuple-element.107.hidden_ref, bf16[1024,1024]{1,0:T(8,128)(2,1)} %all-gather.6.cloned.1.call-done.first, bf16[1024,1024]{1,0:T(8,128)(2,1)} %all-gather.8.cloned.1.call-done.second), custom_call_target="tpu_custom_call" | custom-call | flops 4294967296 | bytes 14680064 | tf_op jit(solution)/shard_map/feed_hidden_grad/pallas_call | solution.py:568
  289.5 6.6 %feed_grad.2 = bf16[512,2048]{1,0:T(8,128)(2,1)} custom-call(s32[14]{0:T(128)} %pad_add_fusion.meta, bf16[1024,1024]{1,0:T(8,128)(2,1)} %get-tuple-element.110.rows_ref.grads_ref, bf16[2,512,1024]{2,1,0:T(8,128)(2,1)} %pad_maximum_fusion.1.refs_0_, bf16[1,512,1024]{2,1,0:T(8,128)(2,1)} %collective-permute-done.18.refs_1_, ...), custom_call_target="tpu_custom_call" | custom-call | flops 2147483648 | bytes 7340032 | tf_op jit(solution)/shard_map/feed_grad/pallas_call | solution.py:655
  296.1 6.6 %feed_grad.3 = bf16[512,2048]{1,0:T(8,128)(2,1)} custom-call(s32[14]{0:T(128)} %pad_add_fusion.meta, bf16[1024,1024]{1,0:T(8,128)(2,1)} %get-tuple-element.110.rows_ref.grads_ref, bf16[2,512,1024]{2,1,0:T(8,128)(2,1)} %pad_maximum_fusion.1.refs_0_, bf16[1,512,1024]{2,1,0:T(8,128)(2,1)} %collective-permute-done.18.refs_1_, ...), custom_call_target="tpu_custom_call" | custom-call | flops 2147483648 | bytes 7340032 | tf_op jit(solution)/shard_map/feed_grad/pallas_call | solution.py:655
  310.6 18.0 %feed_late.1 = (bf16[512,2048]{1,0:T(8,128)(2,1)}, bf16[512,2048]{1,0:T(8,128)(2,1)}, bf16[2048,512]{1,0:T(8,128)(2,1)}, bf16[2048,512]{1,0:T(8,128)(2,1)}) custom-call(bf16[1024,1024]{1,0:T(8,128)(2,1)} %get-tuple-element.113.rows_ref, bf16[1024,1024]{1,0:T(8,128)(2,1)} %all-gather.6.cloned.1.call-done.first, ...), custom_call_target="tpu_custom_call" | custom-call | flops 8589934592 | bytes 18874368 | tf_op jit(solution)/shard_map/feed_late/pallas_call | solution.py:614
  328.6 5.1 collective-permute-done.39
  345.1 8.2 %branch_grad.1 = f32[128,2048]{1,0:T(8,128)} custom-call(s32[14]{0:T(128)} %pad_add_fusion.meta, bf16[128,2048]{1,0:T(8,128)(2,1)} %get-tuple-element.253.rows_ref, bf16[2,2,512,256]{3,2,1,0:T(8,128)(2,1)} %copy-done.6, bf16[2,2,512,256]{3,2,1,0:T(8,128)(2,1)} %collective-permute-done.20.refs_1_, bf16[2,2,512,256]{3,2,1,0:T(8,128)(2,1)} %collective-permute-done.21.refs_2_, ...), custom_call_target="tpu_custom_call" | custom-call | flops 1073741824 | bytes 8388608 | tf_op jit(solution)/shard_map/branch_grad/pallas_call | solution.py:693
  355.8 4.3 all-to-all-start.1
  362.2 5.6 reduce-scatter.7.cloned.1.call-done
  379.6 16.3 %attend_grad.1 = (bf16[512,256]{1,0:T(8,128)(2,1)}, bf16[512,256]{1,0:T(8,128)(2,1)}, bf16[2048,256]{1,0:T(8,128)(2,1)}, bf16[2048,256]{1,0:T(8,128)(2,1)}, bf16...) custom-call(s32[14]{0:T(128)} %pad_add_fusion.meta, bf16[2,1024,128]{2,1,0:T(8,128)(2,1)} %get-tuple-element.125.q_all, ...), custom_call_target="tpu_custom_call" | custom-call | flops 2684354560 | bytes 10485760 | tf_op jit(solution)/shard_map/attend_grad/pallas_call | solution.py:474
  403.3 4.8 collective-permute-done.45
  427.6 4.5 collective-permute-done.49
  432.1 4.6 collective-permute-done.51
  440.0 3.4 all-to-all-start.2
  456.6 3.3 all-to-all-done.2
  460.8 4.1 all-to-all-start.3
  468.1 15.5 %collective-permute-done.54 = bf16[128,2048]{1,0:T(8,128)(2,1)} collective-permute-done((bf16[128,2048]{1,0:T(8,128)(2,1)}, bf16[128,2048]{1,0:T(8,128)(2,1)}, u32[]{:S(2)}, u32[]{:S(2)}) %collective-permute-start.54) | collective-permute-done | bytes 524320 | tf_op jit(solution)/shard_map/ppermute | solution.py:59
  483.6 14.0 %collective-permute-done.53 = bf16[128,2048]{1,0:T(8,128)(2,1)} collective-permute-done((bf16[128,2048]{1,0:T(8,128)(2,1)}, bf16[128,2048]{1,0:T(8,128)(2,1)}, u32[]{:S(2)}, u32[]{:S(2)}) %collective-permute-start.53) | collective-permute-done | bytes 524320 | tf_op jit(solution)/shard_map/ppermute | solution.py:59
  504.1 3.7 fusion.47
  510.7 4.6 fusion.14
  526.3 8.9 %collective-permute-done.60 = bf16[512,512]{1,0:T(8,128)(2,1)S(1)} collective-permute-done((bf16[512,512]{1,0:T(8,128)(2,1)}, bf16[512,512]{1,0:T(8,128)(2,1)S(1)}, u32[]{:S(2)}, u32[]{:S(2)}) %collective-permute-start.60) | collective-permute-done | bytes 524320 | tf_op jit(solution)/shard_map/ppermute | solution.py:59
  535.8 7.4 %collective-permute-done.59 = bf16[512,512]{1,0:T(8,128)(2,1)S(1)} collective-permute-done((bf16[512,512]{1,0:T(8,128)(2,1)}, bf16[512,512]{1,0:T(8,128)(2,1)S(1)}, u32[]{:S(2)}, u32[]{:S(2)}) %collective-permute-start.59) | collective-permute-done | bytes 524320 | tf_op jit(solution)/shard_map/ppermute | solution.py:59
  546.4 3.9 fusion.28
  550.6 10.6 %spread_rows.1 = f32[2048,2048]{1,0:T(8,128)} custom-call(s32[14]{0:T(128)S(1)} %copy-done, bf16[2,256,1024]{2,1,0:T(8,128)(2,1)S(1)} %pad_maximum_fusion.9.refs_0_, bf16[2,256,1024]{2,1,0:T(8,128)(2,1)} %collective-permute-done.55.refs_1_, bf16[2,256,1024]{2,1,0:T(8,128)(2,1)} %collective-permute-done.64.refs_2_, ...), custom_call_target="tpu_custom_call" | custom-call | tf_op jit(solution)/shard_map/spread_rows/pallas_call | solution.py:741
  563.2 3.5 all-to-all-start.4
  567.7 4.7 all-to-all-done.4
  574.7 3.4 all-to-all-start.5
  585.4 10.4 %spread_columns.3 = f32[512,8192]{1,0:T(8,128)} custom-call(s32[14]{0:T(128)S(1)} %copy-done, bf16[2,512,512]{2,1,0:T(8,128)(2,1)S(1)} %pad_maximum_fusion.11.refs_0_, bf16[2,512,512]{2,1,0:T(8,128)(2,1)} %collective-permute-done.63.refs_1_, bf16[2,512,512]{2,1,0:T(8,128)(2,1)S(1)} %collective-permute-done.68.refs_2_, ...), custom_call_target="tpu_custom_call" | custom-call | tf_op jit(solution)/shard_map/spread_columns/pallas_call | solution.py:813
  595.8 7.9 %spread_columns.2 = (f32[512,2304]{1,0:T(8,128)}, f32[512,2048]{1,0:T(8,128)}) custom-call(s32[14]{0:T(128)S(1)} %copy-done, bf16[4,512,512]{2,1,0:T(8,128)(2,1)} %bitcast.28.refs_0_, bf16[4,512,512]{2,1,0:T(8,128)(2,1)} %bitcast.29.refs_1_, f32[512,256]{1,0:T(8,128)S(1)} %convert_element_type.431.refs_2_), custom_call_target="tpu_custom_call" | custom-call | tf_op jit(solution)/shard_map/spread_columns/pallas_call | solution.py:813
  (437 shorter events, 218.7 us)
Async XLA Ops:
  7.2 242.2 %all-gather.4.cloned.1.call-start = ((), (), s32[]{:S(2)}) async-start(), calls=%async_computation.12 | async-start | bytes 4718592 | tf_op jit(solution)/shard_map/all_gather | solution.py:991
  8.8 42.3 %collective-permute-start.4 = (bf16[1,512,512]{2,1,0:T(8,128)(2,1)S(1)}, bf16[1,512,512]{2,1,0:T(8,128)(2,1)S(1)}, u32[]{:S(2)}, u32[]{:S(2)}) collective-permute-start(bf16[1,512,512]{2,1,0:T(8,128)(2,1)S(1)} %pad_maximum_fusion.13), channel_id=1, source_target_pairs={{0,1},{1,0},{2,3},{3,2},{4,5},{5,4},{6,7},{7,6},{8,9},{9,8},{10,11... | collective-permute-start | bytes 1572872 | tf_op jit(solution)/shard_map/ppermute | solution.py:186
  11.9 25.6 %collective-permute-start.3 = (bf16[1,512,512]{2,1,0:T(8,128)(2,1)S(1)}, bf16[1,512,512]{2,1,0:T(8,128)(2,1)}, u32[]{:S(2)}, u32[]{:S(2)}) collective-permute-start(bf16[1,512,512]{2,1,0:T(8,128)(2,1)S(1)} %pad_maximum_fusion.13), channel_id=1, source_target_pairs={{0,3},{1,2},{2,1},{3,0},{4,7},{5,6},{6,5},{7,4},{8,11},{9,10},{10,... | collective-permute-start | bytes 1572872 | tf_op jit(solution)/shard_map/ppermute | solution.py:186
  14.3 54.1 %collective-permute-start.2 = (bf16[128,2048]{1,0:T(8,128)(2,1)S(1)}, bf16[128,2048]{1,0:T(8,128)(2,1)}, u32[]{:S(2)}, u32[]{:S(2)}) collective-permute-start(bf16[128,2048]{1,0:T(8,128)(2,1)S(1)} %bitcast.116), channel_id=1, source_target_pairs={{0,24},{4,28},{8,16},{12,20},{16,8},{20,12},{24,0},{28,4},{1,25},{... | collective-permute-start | bytes 1572872 | tf_op jit(solution)/shard_map/ppermute | solution.py:59
  16.8 51.6 %collective-permute-start.1 = (bf16[128,2048]{1,0:T(8,128)(2,1)S(1)}, bf16[128,2048]{1,0:T(8,128)(2,1)}, u32[]{:S(2)}, u32[]{:S(2)}) collective-permute-start(bf16[128,2048]{1,0:T(8,128)(2,1)S(1)} %bitcast.117), channel_id=1, source_target_pairs={{0,16},{4,20},{8,24},{12,28},{16,0},{20,4},{24,8},{28,12},{1,17},{... | collective-permute-start | bytes 1572872 | tf_op jit(solution)/shard_map/ppermute | solution.py:59
  72.8 66.0 %collective-permute-start.8 = (bf16[512,2048]{1,0:T(8,128)(2,1)S(1)}, bf16[512,2048]{1,0:T(8,128)(2,1)S(1)}, u32[]{:S(2)}, u32[]{:S(2)}) collective-permute-start(bf16[512,2048]{1,0:T(8,128)(2,1)S(1)} %get-tuple-element.259), channel_id=1, source_target_pairs={{0,4},{4,0},{8,12},{12,8},{16,20},{20,16},{24,28},{28,24},{1,5},{5... | collective-permute-start | bytes 6291464 | tf_op jit(solution)/shard_map/ppermute | solution.py:59
  88.3 37.4 %collective-permute-start.15 = (bf16[2048,256]{1,0:T(8,128)(2,1)S(1)}, bf16[2048,256]{1,0:T(8,128)(2,1)S(1)}, u32[]{:S(2)}, u32[]{:S(2)}) collective-permute-start(bf16[2048,256]{1,0:T(8,128)(2,1)S(1)} %pad_maximum_fusion.5.kv_even), channel_id=1, source_target_pairs={{0,4},{4,0},{8,12},{12,8},{16,20},{20,16},{24,28},{28,24},{1,5},{5... | collective-permute-start | bytes 3145736 | tf_op jit(solution)/shard_map/ppermute | solution.py:59
  88.5 48.9 %collective-permute-start.17 = (bf16[1,512,1024]{2,1,0:T(8,128)(2,1)}, bf16[1,512,1024]{2,1,0:T(8,128)(2,1)}, u32[]{:S(2)}, u32[]{:S(2)}) collective-permute-start(bf16[1,512,1024]{2,1,0:T(8,128)(2,1)} %bitcast.13), channel_id=1, source_target_pairs={{0,3},{1,2},{2,1},{3,0},{4,7},{5,6},{6,5},{7,4},{8,11},{9,10},{10,... | collective-permute-start | bytes 3145736 | tf_op jit(solution)/shard_map/ppermute | solution.py:186
  92.1 29.7 %collective-permute-start.24 = (bf16[1,512,256]{2,1,0:T(8,128)(2,1)S(1)}, bf16[1,512,256]{2,1,0:T(8,128)(2,1)S(1)}, u32[]{:S(2)}, u32[]{:S(2)}) collective-permute-start(bf16[1,512,256]{2,1,0:T(8,128)(2,1)S(1)} %collective-permute-done.16), channel_id=1, source_target_pairs={{0,1},{1,0},{2,3},{3,2},{4,5},{5,4},{6,7},{7,6},{8,9},{9,8},{10,11... | collective-permute-start | bytes 786440 | tf_op jit(solution)/shard_map/ppermute | solution.py:186
  94.9 29.3 %collective-permute-start.19 = (bf16[1,2,512,256]{3,2,1,0:T(8,128)(2,1)S(1)}, bf16[1,2,512,256]{3,2,1,0:T(8,128)(2,1)S(1)}, u32[]{:S(2)}, u32[]{:S(2)}) collective-permute-start(bf16[1,2,512,256]{3,2,1,0:T(8,128)(2,1)S(1)} %bitcast.124), channel_id=1, source_target_pairs={{0,16},{4,20},{8,24},{12,28},{16,0},{20,4},{24,8},{28,12},{1,17},{... | collective-permute-start | bytes 1572872 | tf_op jit(solution)/shard_map/ppermute | solution.py:59
  124.2 38.1 %collective-permute-start.18 = (bf16[1,512,1024]{2,1,0:T(8,128)(2,1)}, bf16[1,512,1024]{2,1,0:T(8,128)(2,1)}, u32[]{:S(2)}, u32[]{:S(2)}) collective-permute-start(bf16[1,512,1024]{2,1,0:T(8,128)(2,1)} %bitcast.13), channel_id=1, source_target_pairs={{0,1},{1,0},{2,3},{3,2},{4,5},{5,4},{6,7},{7,6},{8,9},{9,8},{10,11... | collective-permute-start | bytes 3145736 | tf_op jit(solution)/shard_map/ppermute | solution.py:186
  125.8 55.6 %collective-permute-start.21 = (bf16[2,2,512,256]{3,2,1,0:T(8,128)(2,1)S(1)}, bf16[2,2,512,256]{3,2,1,0:T(8,128)(2,1)}, u32[]{:S(2)}, u32[]{:S(2)}) collective-permute-start(bf16[2,2,512,256]{3,2,1,0:T(8,128)(2,1)S(1)} %pad_maximum_fusion.7.refs_0_), channel_id=1, source_target_pairs={{0,4},{4,0},{8,12},{12,8},{16,20},{20,16},{24,28},{28,24},{1,5},{5... | collective-permute-start | bytes 3145736 | tf_op jit(solution)/shard_map/ppermute | solution.py:59
  135.8 26.0 %collective-permute-start.20 = (bf16[2,2,512,256]{3,2,1,0:T(8,128)(2,1)S(1)}, bf16[2,2,512,256]{3,2,1,0:T(8,128)(2,1)}, u32[]{:S(2)}, u32[]{:S(2)}) collective-permute-start(bf16[2,2,512,256]{3,2,1,0:T(8,128)(2,1)S(1)} %pad_maximum_fusion.7.refs_0_), channel_id=1, source_target_pairs={{0,8},{4,12},{8,0},{12,4},{16,24},{20,28},{24,16},{28,20},{1,9},{5... | collective-permute-start | bytes 3145736 | tf_op jit(solution)/shard_map/ppermute | solution.py:59
  137.4 24.4 %collective-permute-start.26 = (bf16[2,2,512,256]{3,2,1,0:T(8,128)(2,1)}, bf16[2,2,512,256]{3,2,1,0:T(8,128)(2,1)}, u32[]{:S(2)}, u32[]{:S(2)}) collective-permute-start(bf16[2,2,512,256]{3,2,1,0:T(8,128)(2,1)} %pad_maximum_fusion.8.refs_4_), channel_id=1, source_target_pairs={{0,16},{4,20},{8,24},{12,28},{16,0},{20,4},{24,8},{28,12},{1,17},{... | collective-permute-start | bytes 3145736 | tf_op jit(solution)/shard_map/ppermute | solution.py:59
  138.8 39.3 %collective-permute-start.36 = (bf16[1,512,1024]{2,1,0:T(8,128)(2,1)}, bf16[1,512,1024]{2,1,0:T(8,128)(2,1)}, u32[]{:S(2)}, u32[]{:S(2)}) collective-permute-start(bf16[1,512,1024]{2,1,0:T(8,128)(2,1)} %collective-permute-done.17), channel_id=1, source_target_pairs={{0,1},{1,0},{2,3},{3,2},{4,5},{5,4},{6,7},{7,6},{8,9},{9,8},{10,11... | collective-permute-start | bytes 3145736 | tf_op jit(solution)/shard_map/ppermute | solution.py:186
  161.7 22.7 %collective-permute-start.22 = (bf16[2,2,512,256]{3,2,1,0:T(8,128)(2,1)}, bf16[2,2,512,256]{3,2,1,0:T(8,128)(2,1)}, u32[]{:S(2)}, u32[]{:S(2)}) collective-permute-start(bf16[2,2,512,256]{3,2,1,0:T(8,128)(2,1)} %collective-permute-done.20.refs_1_), channel_id=1, source_target_pairs={{0,4},{4,0},{8,12},{12,8},{16,20},{20,16},{24,28},{28,24},{1,5},{5... | collective-permute-start | bytes 3145736 | tf_op jit(solution)/shard_map/ppermute | solution.py:59
  166.5 97.7 %all-gather.8.cloned.1.call-start = ((), (), s32[]{:S(2)}) async-start(), calls=%async_computation.14 | async-start | bytes 2621440 | tf_op jit(solution)/shard_map/all_gather | solution.py:219
  180.9 96.7 %all-gather.6.cloned.1.call-start = ((), (), s32[]{:S(2)}) async-start(), calls=%async_computation.13 | async-start | bytes 2621440 | tf_op jit(solution)/shard_map/all_gather | solution.py:219
  204.9 23.2 %collective-permute-start.33 = (bf16[128,2048]{1,0:T(8,128)(2,1)S(1)}, bf16[128,2048]{1,0:T(8,128)(2,1)S(1)}, u32[]{:S(2)}, u32[]{:S(2)}) collective-permute-start(bf16[128,2048]{1,0:T(8,128)(2,1)S(1)} %add_convert_fusion.1), channel_id=1, source_target_pairs={{0,16},{4,20},{8,24},{12,28},{16,0},{20,4},{24,8},{28,12},{1,17},{... | collective-permute-start | bytes 1572872 | tf_op jit(solution)/shard_map/ppermute | solution.py:59
  230.2 130.1 %reduce-scatter.9.cloned.1.call-start = ((), (), s32[]{:S(2)}) async-start(), calls=%async_computation.16 | async-start | bytes 2621440 | tf_op jit(solution)/shard_map/reduce_scatter | solution.py:223
  277.6 90.2 %reduce-scatter.7.cloned.1.call-start = ((), (), s32[]{:S(2)}) async-start(), calls=%async_computation.15 | async-start | bytes 2621440 | tf_op jit(solution)/shard_map/reduce_scatter | solution.py:223
  278.2 189.9 %reduce-scatter.17.cloned.1.call-start = ((), (), s32[]{:S(2)}) async-start(), calls=%async_computation.20 | async-start | bytes 2621440 | tf_op jit(solution)/shard_map/reduce_scatter | solution.py:223
  309.3 24.4 %collective-permute-start.39 = (bf16[128,2048]{1,0:T(8,128)(2,1)S(1)}, bf16[128,2048]{1,0:T(8,128)(2,1)}, u32[]{:S(2)}, u32[]{:S(2)}) collective-permute-start(bf16[128,2048]{1,0:T(8,128)(2,1)S(1)} %get-tuple-element.277), channel_id=1, source_target_pairs={{0,16},{4,20},{8,24},{12,28},{16,0},{20,4},{24,8},{28,12},{1,17},{... | collective-permute-start | bytes 1572872 | tf_op jit(solution)/shard_map/ppermute | solution.py:59
  309.8 23.9 %collective-permute-start.38 = (bf16[128,2048]{1,0:T(8,128)(2,1)S(1)}, bf16[128,2048]{1,0:T(8,128)(2,1)}, u32[]{:S(2)}, u32[]{:S(2)}) collective-permute-start(bf16[128,2048]{1,0:T(8,128)(2,1)S(1)} %get-tuple-element.278), channel_id=1, source_target_pairs={{0,8},{4,12},{8,0},{12,4},{16,24},{20,28},{24,16},{28,20},{1,9},{5... | collective-permute-start | bytes 1572872 | tf_op jit(solution)/shard_map/ppermute | solution.py:59
  333.7 134.4 %reduce-scatter.15.cloned.1.call-start = ((), (), s32[]{:S(2)}) async-start(), calls=%async_computation.19 | async-start | bytes 2621440 | tf_op jit(solution)/shard_map/reduce_scatter | solution.py:223
  335.7 33.6 %collective-permute-start.41 = (bf16[512,2048]{1,0:T(8,128)(2,1)}, bf16[512,2048]{1,0:T(8,128)(2,1)}, u32[]{:S(2)}, u32[]{:S(2)}) collective-permute-start(bf16[512,2048]{1,0:T(8,128)(2,1)} %get-tuple-element.123), channel_id=1, source_target_pairs={{0,4},{4,0},{8,12},{12,8},{16,20},{20,16},{24,28},{28,24},{1,5},{5... | collective-permute-start | bytes 6291464 | tf_op jit(solution)/shard_map/ppermute | solution.py:59
  340.4 57.3 %collective-permute-start.57 = (bf16[512,2048]{1,0:T(8,128)(2,1)}, bf16[512,2048]{1,0:T(8,128)(2,1)}, u32[]{:S(2)}, u32[]{:S(2)}) collective-permute-start(bf16[512,2048]{1,0:T(8,128)(2,1)} %constant_dynamic-update-slice_fusion.5), channel_id=1, source_target_pairs={{0,4},{4,0},{8,12},{12,8},{16,20},{20,16},{24,28},{28,24},{1,5},{5... | collective-permute-start | bytes 6291464 | tf_op jit(solution)/shard_map/ppermute | solution.py:59
  360.0 149.2 %reduce-scatter.11.cloned.1.call-start = ((), (), s32[]{:S(2)}) async-start(), calls=%async_computation.17 | async-start | bytes 2621440 | tf_op jit(solution)/shard_map/reduce_scatter | solution.py:223
  360.3 42.9 %collective-permute-start.43 = (bf16[1,256,1024]{2,1,0:T(8,128)(2,1)}, bf16[1,256,1024]{2,1,0:T(8,128)(2,1)}, u32[]{:S(2)}, u32[]{:S(2)}) collective-permute-start(bf16[1,256,1024]{2,1,0:T(8,128)(2,1)} %bitcast.144), channel_id=1, source_target_pairs={{0,8},{4,12},{8,0},{12,4},{16,24},{20,28},{24,16},{28,20},{1,9},{5... | collective-permute-start | bytes 1572872 | tf_op jit(solution)/shard_map/ppermute | solution.py:59
  367.9 35.4 %collective-permute-start.42 = (bf16[1,256,1024]{2,1,0:T(8,128)(2,1)}, bf16[1,256,1024]{2,1,0:T(8,128)(2,1)}, u32[]{:S(2)}, u32[]{:S(2)}) collective-permute-start(bf16[1,256,1024]{2,1,0:T(8,128)(2,1)} %bitcast.146), channel_id=1, source_target_pairs={{0,16},{4,20},{8,24},{12,28},{16,0},{20,4},{24,8},{28,12},{1,17},{... | collective-permute-start | bytes 1572872 | tf_op jit(solution)/shard_map/ppermute | solution.py:59
  377.5 25.8 %collective-permute-start.46 = (bf16[128,2048]{1,0:T(8,128)(2,1)S(1)}, bf16[128,2048]{1,0:T(8,128)(2,1)S(1)}, u32[]{:S(2)}, u32[]{:S(2)}) collective-permute-start(bf16[128,2048]{1,0:T(8,128)(2,1)S(1)} %get-tuple-element.273), channel_id=1, source_target_pairs={{0,24},{4,28},{8,16},{12,20},{16,8},{20,12},{24,0},{28,4},{1,25},{... | collective-permute-start | bytes 1572872 | tf_op jit(solution)/shard_map/ppermute | solution.py:59
  378.1 30.0 %collective-permute-start.45 = (bf16[128,2048]{1,0:T(8,128)(2,1)S(1)}, bf16[128,2048]{1,0:T(8,128)(2,1)S(1)}, u32[]{:S(2)}, u32[]{:S(2)}) collective-permute-start(bf16[128,2048]{1,0:T(8,128)(2,1)S(1)} %get-tuple-element.274), channel_id=1, source_target_pairs={{0,16},{4,20},{8,24},{12,28},{16,0},{20,4},{24,8},{28,12},{1,17},{... | collective-permute-start | bytes 1572872 | tf_op jit(solution)/shard_map/ppermute | solution.py:59
  417.9 30.4 %collective-permute-start.47 = (bf16[512,2048]{1,0:T(8,128)(2,1)}, bf16[512,2048]{1,0:T(8,128)(2,1)}, u32[]{:S(2)}, u32[]{:S(2)}) collective-permute-start(bf16[512,2048]{1,0:T(8,128)(2,1)} %convolution_convert_fusion.1), channel_id=1, source_target_pairs={{0,4},{4,0},{8,12},{12,8},{16,20},{20,16},{24,28},{28,24},{1,5},{5... | collective-permute-start | bytes 6291464 | tf_op jit(solution)/shard_map/ppermute | solution.py:59
  444.8 63.0 %collective-permute-start.55 = (bf16[2,256,1024]{2,1,0:T(8,128)(2,1)S(1)}, bf16[2,256,1024]{2,1,0:T(8,128)(2,1)}, u32[]{:S(2)}, u32[]{:S(2)}) collective-permute-start(bf16[2,256,1024]{2,1,0:T(8,128)(2,1)S(1)} %pad_maximum_fusion.9.refs_0_), channel_id=1, source_target_pairs={{0,8},{4,12},{8,0},{12,4},{16,24},{20,28},{24,16},{28,20},{1,9},{5... | collective-permute-start | bytes 3145736 | tf_op jit(solution)/shard_map/ppermute | solution.py:59
  446.8 61.0 %collective-permute-start.56 = (bf16[2,256,1024]{2,1,0:T(8,128)(2,1)S(1)}, bf16[2,256,1024]{2,1,0:T(8,128)(2,1)}, u32[]{:S(2)}, u32[]{:S(2)}) collective-permute-start(bf16[2,256,1024]{2,1,0:T(8,128)(2,1)S(1)} %pad_maximum_fusion.10.refs_4_), channel_id=1, source_target_pairs={{0,16},{4,20},{8,24},{12,28},{16,0},{20,4},{24,8},{28,12},{1,17},{... | collective-permute-start | bytes 3145736 | tf_op jit(solution)/shard_map/ppermute | solution.py:59
  453.1 30.4 %collective-permute-start.54 = (bf16[128,2048]{1,0:T(8,128)(2,1)}, bf16[128,2048]{1,0:T(8,128)(2,1)}, u32[]{:S(2)}, u32[]{:S(2)}) collective-permute-start(bf16[128,2048]{1,0:T(8,128)(2,1)} %get-tuple-element.270), channel_id=1, source_target_pairs={{0,24},{4,28},{8,16},{12,20},{16,8},{20,12},{24,0},{28,4},{1,25},{... | collective-permute-start | bytes 1572872 | tf_op jit(solution)/shard_map/ppermute | solution.py:59
  454.6 43.0 %collective-permute-start.53 = (bf16[128,2048]{1,0:T(8,128)(2,1)}, bf16[128,2048]{1,0:T(8,128)(2,1)}, u32[]{:S(2)}, u32[]{:S(2)}) collective-permute-start(bf16[128,2048]{1,0:T(8,128)(2,1)} %get-tuple-element.271), channel_id=1, source_target_pairs={{0,16},{4,20},{8,24},{12,28},{16,0},{20,4},{24,8},{28,12},{1,17},{... | collective-permute-start | bytes 1572872 | tf_op jit(solution)/shard_map/ppermute | solution.py:59
  456.4 42.7 %collective-permute-start.52 = (bf16[128,2048]{1,0:T(8,128)(2,1)}, bf16[128,2048]{1,0:T(8,128)(2,1)}, u32[]{:S(2)}, u32[]{:S(2)}) collective-permute-start(bf16[128,2048]{1,0:T(8,128)(2,1)} %get-tuple-element.272), channel_id=1, source_target_pairs={{0,8},{4,12},{8,0},{12,4},{16,24},{20,28},{24,16},{28,20},{1,9},{5... | collective-permute-start | bytes 1572872 | tf_op jit(solution)/shard_map/ppermute | solution.py:59
  460.8 40.7 %all-to-all-start.3 = ((bf16[8,128,256]{2,1,0:T(8,128)(2,1)}), bf16[8,128,256]{2,1,0:T(8,128)(2,1)}, u32[]{:S(2)}, u32[]{:S(2)}) async-start(bf16[8,128,256]{2,1,0:T(8,128)(2,1)} %broadcast_in_dim.61), calls=%async_computation.5 | async-start | bytes 1048576 | tf_op jit(solution)/shard_map/all_to_all | solution.py:166
  465.0 115.9 %reduce-scatter.13.cloned.1.call-start = ((), (), s32[]{:S(2)}) async-start(), calls=%async_computation.18 | async-start | bytes 1310720 | tf_op jit(solution)/shard_map/reduce_scatter | solution.py:223
  483.6 39.5 %collective-permute-start.64 = (bf16[2,256,1024]{2,1,0:T(8,128)(2,1)S(1)}, bf16[2,256,1024]{2,1,0:T(8,128)(2,1)}, u32[]{:S(2)}, u32[]{:S(2)}) collective-permute-start(bf16[2,256,1024]{2,1,0:T(8,128)(2,1)S(1)} %pad_maximum_fusion.9.refs_0_), channel_id=1, source_target_pairs={{0,4},{4,0},{8,12},{12,8},{16,20},{20,16},{24,28},{28,24},{1,5},{5... | collective-permute-start | bytes 3145736 | tf_op jit(solution)/shard_map/ppermute | solution.py:59
  507.8 38.5 %collective-permute-start.66 = (bf16[2,256,1024]{2,1,0:T(8,128)(2,1)S(1)}, bf16[2,256,1024]{2,1,0:T(8,128)(2,1)}, u32[]{:S(2)}, u32[]{:S(2)}) collective-permute-start(bf16[2,256,1024]{2,1,0:T(8,128)(2,1)S(1)} %pad_maximum_fusion.10.refs_4_), channel_id=1, source_target_pairs={{0,4},{4,0},{8,12},{12,8},{16,20},{20,16},{24,28},{28,24},{1,5},{5... | collective-permute-start | bytes 3145736 | tf_op jit(solution)/shard_map/ppermute | solution.py:59
  516.9 26.3 %collective-permute-start.59 = (bf16[512,512]{1,0:T(8,128)(2,1)}, bf16[512,512]{1,0:T(8,128)(2,1)S(1)}, u32[]{:S(2)}, u32[]{:S(2)}) collective-permute-start(bf16[512,512]{1,0:T(8,128)(2,1)} %reduce-scatter.11.cloned.1.call-done), channel_id=1, source_target_pairs={{0,16},{4,20},{8,24},{12,28},{16,0},{20,4},{24,8},{28,12},{1,17},{... | collective-permute-start | bytes 1572872 | tf_op jit(solution)/shard_map/ppermute | solution.py:59
  523.0 27.5 %collective-permute-start.65 = (bf16[2,256,1024]{2,1,0:T(8,128)(2,1)}, bf16[2,256,1024]{2,1,0:T(8,128)(2,1)}, u32[]{:S(2)}, u32[]{:S(2)}) collective-permute-start(bf16[2,256,1024]{2,1,0:T(8,128)(2,1)} %collective-permute-done.55.refs_1_), channel_id=1, source_target_pairs={{0,4},{4,0},{8,12},{12,8},{16,20},{20,16},{24,28},{28,24},{1,5},{5... | collective-permute-start | bytes 3145736 | tf_op jit(solution)/shard_map/ppermute | solution.py:59
  524.4 26.2 %collective-permute-start.67 = (bf16[2,256,1024]{2,1,0:T(8,128)(2,1)}, bf16[2,256,1024]{2,1,0:T(8,128)(2,1)}, u32[]{:S(2)}, u32[]{:S(2)}) collective-permute-start(bf16[2,256,1024]{2,1,0:T(8,128)(2,1)} %collective-permute-done.56.refs_5_), channel_id=1, source_target_pairs={{0,4},{4,0},{8,12},{12,8},{16,20},{20,16},{24,28},{28,24},{1,5},{5... | collective-permute-start | bytes 3145736 | tf_op jit(solution)/shard_map/ppermute | solution.py:59
  535.2 32.0 %collective-permute-start.71 = (bf16[2,512,512]{2,1,0:T(8,128)(2,1)}, bf16[2,512,512]{2,1,0:T(8,128)(2,1)}, u32[]{:S(2)}, u32[]{:S(2)}) collective-permute-start(bf16[2,512,512]{2,1,0:T(8,128)(2,1)} %pad_maximum_fusion.12.refs_4_), channel_id=1, source_target_pairs={{0,16},{4,20},{8,24},{12,28},{16,0},{20,4},{24,8},{28,12},{1,17},{... | collective-permute-start | bytes 3145736 | tf_op jit(solution)/shard_map/ppermute | solution.py:59
  543.2 24.0 %collective-permute-start.63 = (bf16[2,512,512]{2,1,0:T(8,128)(2,1)S(1)}, bf16[2,512,512]{2,1,0:T(8,128)(2,1)}, u32[]{:S(2)}, u32[]{:S(2)}) collective-permute-start(bf16[2,512,512]{2,1,0:T(8,128)(2,1)S(1)} %pad_maximum_fusion.11.refs_0_), channel_id=1, source_target_pairs={{0,8},{4,12},{8,0},{12,4},{16,24},{20,28},{24,16},{28,20},{1,9},{5... | collective-permute-start | bytes 3145736 | tf_op jit(solution)/shard_map/ppermute | solution.py:59
  546.3 49.5 %collective-permute-start.61 = (bf16[2048,512]{1,0:T(8,128)(2,1)}, bf16[2048,512]{1,0:T(8,128)(2,1)}, u32[]{:S(2)}, u32[]{:S(2)}) collective-permute-start(bf16[2048,512]{1,0:T(8,128)(2,1)} %constant_dynamic-update-slice_fusion.9), channel_id=1, source_target_pairs={{0,4},{4,0},{8,12},{12,8},{16,20},{20,16},{24,28},{28,24},{1,5},{5... | collective-permute-start | bytes 6291464 | tf_op jit(solution)/shard_map/ppermute | solution.py:59
  (99 other events, 1529.8 us)
Sparse Core Ops, SparseCore 0:
  20.7 48.8 all-gather.3
  181.0 46.8 all-gather.7
  230.3 47.2 all-gather.5
  279.7 42.5 reduce-scatter.8
  324.6 43.2 reduce-scatter.6
  370.0 43.1 reduce-scatter.16
  415.6 47.3 reduce-scatter.14
  465.9 43.3 reduce-scatter.10
  515.4 26.0 reduce-scatter.12

commit v6 on v5

--- a/solution.py
+++ b/solution.py
@@ -1108,8 +1108,8 @@
     stacked = jnp.concatenate(
         [member.reshape(fsdp_count, -1) for member in g_vectors], axis=1
     ).astype(BF16)
-    stacked, grad_w_proj = lax.optimization_barrier((stacked, grad_w_proj))
     own = z_sum_exchange(stacked).astype(BF16)
+    own, grad_w_proj = lax.optimization_barrier((own, grad_w_proj))
     own = ctx_exchange(jnp.broadcast_to(own[None], (ctx_count,) + own.shape))
     summed = jnp.sum(own, axis=0, dtype=F32)
     vector_grads, start = [], 0

time: 622 us -> 621 us (level)
    unnamed x140 -> x137, local copies, waits for them, and re-layouts: 23 us -> 23 us
  transfers between devices with their start and end apart: 89 -> 89, of which waited for: 37 -> 37; matrix products, arithmetic and copies ran while one was open for 22% -> 22% of each run, Pallas kernels for 21% -> 22%
where the time goes in v6:
time: 621 us; the launch traced here: 610 us
  waiting for transfers between devices  209 us (34%)
  Pallas kernels  139 us (22%)
  starting transfers between devices  102 us (16%)
  other arithmetic  56.1 us (9%)
  local copies, waits for them, and re-layouts  50.4 us (8%)
  matrix products  36.8 us (6%)
  between operations  16.2 us (3%)
    ppermute x60, waiting for transfers between devices, ctx_swap(): return lax.ppermute(values, 'ctx', [(at, at ^ mask) for at in range(count)])  122 us
    ppermute x60, starting transfers between devices, ctx_swap(): return lax.ppermute(values, 'ctx', [(at, at ^ mask) for at in range(count)])  53.4 us
    ppermute x14, waiting for transfers between devices, z_swap(): lax.ppermute(values, 'fsdp', [(at, at ^ mask) for at in range(count)])  51.3 us
    ppermute x14, starting transfers between devices, z_swap(): lax.ppermute(values, 'fsdp', [(at, at ^ mask) for at in range(count)])  24.9 us
    dot_general x7, matrix products, mm_rows(): lax.dot_general(left, right, (((0,), (0,)), ((), ())), preferred_element_...  23.6 us
    unnamed x137, local copies, waits for them, and re-layouts  23 us
    pallas_call x2, Pallas kernels, spread_columns(): pl.pallas_call(functools.partial(spread_kernel, moves, extras, len(sizes)...  18.2 us
    pallas_call x1, Pallas kernels, feed_late(): pl.pallas_call(functools.partial(feed_late_kernel, steps), grid=(2 * step...  18 us
  transfers between devices with their start and end apart: 89, of which 37 were waited for; matrix products, arithmetic and copies ran while one was open for 22% of the time, Pallas kernels for 22%

profile of v6, /device:TPU:0, one launch (start us, length us, event | category | flops | bytes accessed | tf_op | source)
XLA Modules:
  0.0 610.0 jit_solution(849809996274141186)
XLA Ops:
  21.0 16.4 %collective-permute-done.3 = bf16[1,512,512]{2,1,0:T(8,128)(2,1)} collective-permute-done((bf16[1,512,512]{2,1,0:T(8,128)(2,1)S(1)}, bf16[1,512,512]{2,1,0:T(8,128)(2,1)}, u32[]{:S(2)}, u32[]{:S(2)}) %collective-permute-start.3) | collective-permute-done | bytes 524320 | tf_op jit(solution)/shard_map/ppermute | solution.py:186
  44.7 5.6 collective-permute-done.6
  55.6 3.7 place_first.1
  77.5 3.4 collective-permute-start.16
  84.5 3.7 collective-permute-done.13
  88.5 3.6 collective-permute-start.17
  96.5 25.3 %collective-permute-done.24 = bf16[1,512,256]{2,1,0:T(8,128)(2,1)S(1)} collective-permute-done((bf16[1,512,256]{2,1,0:T(8,128)(2,1)S(1)}, bf16[1,512,256]{2,1,0:T(8,128)(2,1)S(1)}, u32[]{:S(2)}, u32[]{:S(2)}) %collective-permute-start.24) | collective-permute-done | bytes 262176 | tf_op jit(solution)/shard_map/ppermute | solution.py:186
  125.9 9.9 %collective-permute-done.25 = bf16[1,2,512,256]{3,2,1,0:T(8,128)(2,1)S(1)} collective-permute-done((bf16[1,2,512,256]{3,2,1,0:T(8,128)(2,1)S(1)}, bf16[1,2,512,256]{3,2,1,0:T(8,128)(2,1)S(1)}, u32[]{:S(2)}, u32[]{:S(2)}) %collective-permute-start.25) | collective-permute-done | bytes 524320 | tf_op jit(solution)/shard_map/ppermute | solution.py:59
  143.5 14.4 %attend.1 = (bf16[1024,256]{1,0:T(8,128)(2,1)}, bf16[2,1024,128]{2,1,0:T(8,128)(2,1)}, bf16[2,2048,256]{2,1,0:T(8,128)(2,1)}, f32[8,128,256]{2,1,0:T(8,128)}, f32[8,1,256]{2,1,0:T(1,128)}) custom-call(s32[14]{0:T(128)} %pad_add_fusion.meta, bf16[512,256]{1,0:T(8,128)(2,1)} %fusion.15.q_even, bf16[512,256]{1,0:T(8,128)(2,1)} %fusion.16.q_odd, ...), custom_call_target="tpu_custom_call" | custom-call | flops 1073741824 | bytes 8388608 | tf_op jit(solution)/shard_map/attend/pallas_call | solution.py:447
  157.8 3.9 collective-permute-done.26.refs_5_
  162.3 4.2 all-to-all-start
  172.3 3.9 all-to-all-done
  184.5 6.7 %branch.1 = f32[128,2048]{1,0:T(8,128)} custom-call(s32[14]{0:T(128)} %pad_add_fusion.meta, bf16[128,2048]{1,0:T(8,128)(2,1)} %bitcast.42.rows_ref, bf16[2,2,512,256]{3,2,1,0:T(8,128)(2,1)} %copy-done.6, bf16[2,2,512,256]{3,2,1,0:T(8,128)(2,1)} %collective-permute-done.20.refs_1_, bf16[2,2,512,256]{3,2,1,0:T(8,128)(2,1)} %collective-permute-done.21.refs_2_, ...), custom_call_target="tpu_custom_call" | custom-call | flops 1073741824 | bytes 8388608 | tf_op jit(solution)/shard_map/branch/pallas_call | solution.py:693
  194.2 7.8 %collective-permute-done.30 = bf16[128,2048]{1,0:T(8,128)(2,1)S(1)} collective-permute-done((bf16[128,2048]{1,0:T(8,128)(2,1)}, bf16[128,2048]{1,0:T(8,128)(2,1)S(1)}, u32[]{:S(2)}, u32[]{:S(2)}) %collective-permute-start.30) | collective-permute-done | bytes 524320 | tf_op jit(solution)/shard_map/ppermute | solution.py:59
  206.4 11.6 %collective-permute-done.34 = bf16[128,2048]{1,0:T(8,128)(2,1)S(1)} collective-permute-done((bf16[128,2048]{1,0:T(8,128)(2,1)S(1)}, bf16[128,2048]{1,0:T(8,128)(2,1)S(1)}, u32[]{:S(2)}, u32[]{:S(2)}) %collective-permute-start.34) | collective-permute-done | bytes 524320 | tf_op jit(solution)/shard_map/ppermute | solution.py:59
  218.1 10.1 %collective-permute-done.33 = bf16[128,2048]{1,0:T(8,128)(2,1)S(1)} collective-permute-done((bf16[128,2048]{1,0:T(8,128)(2,1)S(1)}, bf16[128,2048]{1,0:T(8,128)(2,1)S(1)}, u32[]{:S(2)}, u32[]{:S(2)}) %collective-permute-start.33) | collective-permute-done | bytes 524320 | tf_op jit(solution)/shard_map/ppermute | solution.py:59
  238.5 10.9 %feed_hidden.1 = (f32[1024,1024]{1,0:T(8,128)}, bf16[1024,1024]{1,0:T(8,128)(2,1)}) custom-call(s32[14]{0:T(128)} %pad_add_fusion.meta, bf16[1024,2048]{1,0:T(8,128)(2,1)} %copy-done.41, f32[1,1024]{1,0:T(1,128)} %bitcast.172, bf16[2,512,1024]{2,1,0:T(8,128)(2,1)} %pad_maximum_fusion.1.refs_0_, bf16[1,512,1024]{2,1,0:T(8,128)(2,1)} %collective-permute-done.18.refs_1_, ...), custom_call_target="tpu_custom_call" | custom-call | flops 4294967296 | bytes 14680064 | tf_op jit(solution)/shard_map/feed_hidden/pallas_call | solution.py:523
  249.4 5.3 place_rows.1.grads_ref
  254.7 7.0 %convolution_convert_fusion = bf16[1024,2048]{1,0:T(8,128)(2,1)S(1)} fusion(bf16[1024,1024]{1,0:T(8,128)(2,1)S(1)} %copy-done.56, bf16[1024,2048]{1,0:T(8,128)(2,1)} %place_rows.1.grads_ref), kind=kOutput, calls=%fused_computation.19 | convolution fusion | flops 4297064448 | bytes 10485760 | tf_op jit(solution)/shard_map/dot_general | solution.py:50
  264.2 13.4 %all-gather.6.cloned.1.call-done.first = bf16[1024,1024]{1,0:T(8,128)(2,1)} async-done(((bf16[256,1024]{1,0:T(8,128)(2,1)}), bf16[1024,1024]{1,0:T(8,128)(2,1)}) %all-gather.6.cloned.1.call-update) | async-done | bytes 2097168 | tf_op jit(solution)/shard_map/all_gather | solution.py:219
  278.4 11.1 %feed_hidden_grad.1 = (bf16[1024,1024]{1,0:T(8,128)(2,1)}, f32[1,1024]{1,0:T(1,128)}) custom-call(bf16[1024,2048]{1,0:T(8,128)(2,1)} %place_rows.1.grads_ref, f32[1024,1024]{1,0:T(8,128)} %get-tuple-element.107.hidden_ref, bf16[1024,1024]{1,0:T(8,128)(2,1)} %all-gather.6.cloned.1.call-done.first, bf16[1024,1024]{1,0:T(8,128)(2,1)} %all-gather.8.cloned.1.call-done.second), custom_call_target="tpu_custom_call" | custom-call | flops 4294967296 | bytes 14680064 | tf_op jit(solution)/shard_map/feed_hidden_grad/pallas_call | solution.py:568
  289.5 6.6 %feed_grad.2 = bf16[512,2048]{1,0:T(8,128)(2,1)} custom-call(s32[14]{0:T(128)} %pad_add_fusion.meta, bf16[1024,1024]{1,0:T(8,128)(2,1)} %get-tuple-element.110.rows_ref.grads_ref, bf16[2,512,1024]{2,1,0:T(8,128)(2,1)} %pad_maximum_fusion.1.refs_0_, bf16[1,512,1024]{2,1,0:T(8,128)(2,1)} %collective-permute-done.18.refs_1_, ...), custom_call_target="tpu_custom_call" | custom-call | flops 2147483648 | bytes 7340032 | tf_op jit(solution)/shard_map/feed_grad/pallas_call | solution.py:655
  296.1 6.6 %feed_grad.3 = bf16[512,2048]{1,0:T(8,128)(2,1)} custom-call(s32[14]{0:T(128)} %pad_add_fusion.meta, bf16[1024,1024]{1,0:T(8,128)(2,1)} %get-tuple-element.110.rows_ref.grads_ref, bf16[2,512,1024]{2,1,0:T(8,128)(2,1)} %pad_maximum_fusion.1.refs_0_, bf16[1,512,1024]{2,1,0:T(8,128)(2,1)} %collective-permute-done.18.refs_1_, ...), custom_call_target="tpu_custom_call" | custom-call | flops 2147483648 | bytes 7340032 | tf_op jit(solution)/shard_map/feed_grad/pallas_call | solution.py:655
  310.6 18.0 %feed_late.1 = (bf16[512,2048]{1,0:T(8,128)(2,1)}, bf16[512,2048]{1,0:T(8,128)(2,1)}, bf16[2048,512]{1,0:T(8,128)(2,1)}, bf16[2048,512]{1,0:T(8,128)(2,1)}) custom-call(bf16[1024,1024]{1,0:T(8,128)(2,1)} %get-tuple-element.113.rows_ref, bf16[1024,1024]{1,0:T(8,128)(2,1)} %all-gather.6.cloned.1.call-done.first, ...), custom_call_target="tpu_custom_call" | custom-call | flops 8589934592 | bytes 18874368 | tf_op jit(solution)/shard_map/feed_late/pallas_call | solution.py:614
  328.6 5.1 collective-permute-done.39
  345.1 8.2 %branch_grad.1 = f32[128,2048]{1,0:T(8,128)} custom-call(s32[14]{0:T(128)} %pad_add_fusion.meta, bf16[128,2048]{1,0:T(8,128)(2,1)} %get-tuple-element.253.rows_ref, bf16[2,2,512,256]{3,2,1,0:T(8,128)(2,1)} %copy-done.6, bf16[2,2,512,256]{3,2,1,0:T(8,128)(2,1)} %collective-permute-done.20.refs_1_, bf16[2,2,512,256]{3,2,1,0:T(8,128)(2,1)} %collective-permute-done.21.refs_2_, ...), custom_call_target="tpu_custom_call" | custom-call | flops 1073741824 | bytes 8388608 | tf_op jit(solution)/shard_map/branch_grad/pallas_call | solution.py:693
  355.8 4.2 all-to-all-start.1
  362.2 5.6 reduce-scatter.7.cloned.1.call-done
  379.6 16.3 %attend_grad.1 = (bf16[512,256]{1,0:T(8,128)(2,1)}, bf16[512,256]{1,0:T(8,128)(2,1)}, bf16[2048,256]{1,0:T(8,128)(2,1)}, bf16[2048,256]{1,0:T(8,128)(2,1)}, bf16...) custom-call(s32[14]{0:T(128)} %pad_add_fusion.meta, bf16[2,1024,128]{2,1,0:T(8,128)(2,1)} %get-tuple-element.125.q_all, ...), custom_call_target="tpu_custom_call" | custom-call | flops 2684354560 | bytes 10485760 | tf_op jit(solution)/shard_map/attend_grad/pallas_call | solution.py:474
  403.3 4.8 collective-permute-done.45
  427.7 4.4 collective-permute-done.49
  432.1 4.5 collective-permute-done.51
  440.1 3.4 all-to-all-start.2
  456.7 3.2 all-to-all-done.2
  460.8 4.1 all-to-all-start.3
  468.1 15.5 %collective-permute-done.54 = bf16[128,2048]{1,0:T(8,128)(2,1)} collective-permute-done((bf16[128,2048]{1,0:T(8,128)(2,1)}, bf16[128,2048]{1,0:T(8,128)(2,1)}, u32[]{:S(2)}, u32[]{:S(2)}) %collective-permute-start.54) | collective-permute-done | bytes 524320 | tf_op jit(solution)/shard_map/ppermute | solution.py:59
  483.6 14.0 %collective-permute-done.53 = bf16[128,2048]{1,0:T(8,128)(2,1)} collective-permute-done((bf16[128,2048]{1,0:T(8,128)(2,1)}, bf16[128,2048]{1,0:T(8,128)(2,1)}, u32[]{:S(2)}, u32[]{:S(2)}) %collective-permute-start.53) | collective-permute-done | bytes 524320 | tf_op jit(solution)/shard_map/ppermute | solution.py:59
  504.1 3.7 fusion.47
  510.7 4.6 fusion.14
  529.2 7.3 %collective-permute-done.60 = bf16[512,512]{1,0:T(8,128)(2,1)S(1)} collective-permute-done((bf16[512,512]{1,0:T(8,128)(2,1)}, bf16[512,512]{1,0:T(8,128)(2,1)S(1)}, u32[]{:S(2)}, u32[]{:S(2)}) %collective-permute-start.60) | collective-permute-done | bytes 524320 | tf_op jit(solution)/shard_map/ppermute | solution.py:59
  536.4 6.7 %collective-permute-done.59 = bf16[512,512]{1,0:T(8,128)(2,1)S(1)} collective-permute-done((bf16[512,512]{1,0:T(8,128)(2,1)}, bf16[512,512]{1,0:T(8,128)(2,1)S(1)}, u32[]{:S(2)}, u32[]{:S(2)}) %collective-permute-start.59) | collective-permute-done | bytes 524320 | tf_op jit(solution)/shard_map/ppermute | solution.py:59
  545.4 3.9 fusion.28
  551.5 3.3 all-to-all-start.4
  554.8 5.7 all-to-all-done.4
  561.4 10.6 %spread_rows.1 = f32[2048,2048]{1,0:T(8,128)} custom-call(s32[14]{0:T(128)S(1)} %copy-done, bf16[2,256,1024]{2,1,0:T(8,128)(2,1)S(1)} %pad_maximum_fusion.9.refs_0_, bf16[2,256,1024]{2,1,0:T(8,128)(2,1)} %collective-permute-done.55.refs_1_, bf16[2,256,1024]{2,1,0:T(8,128)(2,1)} %collective-permute-done.64.refs_2_, ...), custom_call_target="tpu_custom_call" | custom-call | tf_op jit(solution)/shard_map/spread_rows/pallas_call | solution.py:741
  574.1 3.4 all-to-all-start.5
  584.8 10.4 %spread_columns.3 = f32[512,8192]{1,0:T(8,128)} custom-call(s32[14]{0:T(128)S(1)} %copy-done, bf16[2,512,512]{2,1,0:T(8,128)(2,1)S(1)} %pad_maximum_fusion.11.refs_0_, bf16[2,512,512]{2,1,0:T(8,128)(2,1)} %collective-permute-done.63.refs_1_, bf16[2,512,512]{2,1,0:T(8,128)(2,1)} %collective-permute-done.68.refs_2_, ...), custom_call_target="tpu_custom_call" | custom-call | tf_op jit(solution)/shard_map/spread_columns/pallas_call | solution.py:813
  595.1 7.9 %spread_columns.2 = (f32[512,2304]{1,0:T(8,128)}, f32[512,2048]{1,0:T(8,128)}) custom-call(s32[14]{0:T(128)S(1)} %copy-done, bf16[4,512,512]{2,1,0:T(8,128)(2,1)} %bitcast.28.refs_0_, bf16[4,512,512]{2,1,0:T(8,128)(2,1)} %bitcast.29.refs_1_, f32[512,256]{1,0:T(8,128)S(1)} %convert_element_type.438.refs_2_), custom_call_target="tpu_custom_call" | custom-call | tf_op jit(solution)/shard_map/spread_columns/pallas_call | solution.py:813
  (435 shorter events, 219.7 us)
Async XLA Ops:
  7.2 242.2 %all-gather.4.cloned.1.call-start = ((), (), s32[]{:S(2)}) async-start(), calls=%async_computation.12 | async-start | bytes 4718592 | tf_op jit(solution)/shard_map/all_gather | solution.py:991
  8.8 42.3 %collective-permute-start.4 = (bf16[1,512,512]{2,1,0:T(8,128)(2,1)S(1)}, bf16[1,512,512]{2,1,0:T(8,128)(2,1)S(1)}, u32[]{:S(2)}, u32[]{:S(2)}) collective-permute-start(bf16[1,512,512]{2,1,0:T(8,128)(2,1)S(1)} %pad_maximum_fusion.13), channel_id=1, source_target_pairs={{0,1},{1,0},{2,3},{3,2},{4,5},{5,4},{6,7},{7,6},{8,9},{9,8},{10,11... | collective-permute-start | bytes 1572872 | tf_op jit(solution)/shard_map/ppermute | solution.py:186
  11.9 25.6 %collective-permute-start.3 = (bf16[1,512,512]{2,1,0:T(8,128)(2,1)S(1)}, bf16[1,512,512]{2,1,0:T(8,128)(2,1)}, u32[]{:S(2)}, u32[]{:S(2)}) collective-permute-start(bf16[1,512,512]{2,1,0:T(8,128)(2,1)S(1)} %pad_maximum_fusion.13), channel_id=1, source_target_pairs={{0,3},{1,2},{2,1},{3,0},{4,7},{5,6},{6,5},{7,4},{8,11},{9,10},{10,... | collective-permute-start | bytes 1572872 | tf_op jit(solution)/shard_map/ppermute | solution.py:186
  14.3 54.1 %collective-permute-start.2 = (bf16[128,2048]{1,0:T(8,128)(2,1)S(1)}, bf16[128,2048]{1,0:T(8,128)(2,1)}, u32[]{:S(2)}, u32[]{:S(2)}) collective-permute-start(bf16[128,2048]{1,0:T(8,128)(2,1)S(1)} %bitcast.111), channel_id=1, source_target_pairs={{0,24},{4,28},{8,16},{12,20},{16,8},{20,12},{24,0},{28,4},{1,25},{... | collective-permute-start | bytes 1572872 | tf_op jit(solution)/shard_map/ppermute | solution.py:59
  16.8 51.6 %collective-permute-start.1 = (bf16[128,2048]{1,0:T(8,128)(2,1)S(1)}, bf16[128,2048]{1,0:T(8,128)(2,1)}, u32[]{:S(2)}, u32[]{:S(2)}) collective-permute-start(bf16[128,2048]{1,0:T(8,128)(2,1)S(1)} %bitcast.112), channel_id=1, source_target_pairs={{0,16},{4,20},{8,24},{12,28},{16,0},{20,4},{24,8},{28,12},{1,17},{... | collective-permute-start | bytes 1572872 | tf_op jit(solution)/shard_map/ppermute | solution.py:59
  72.8 66.0 %collective-permute-start.8 = (bf16[512,2048]{1,0:T(8,128)(2,1)S(1)}, bf16[512,2048]{1,0:T(8,128)(2,1)S(1)}, u32[]{:S(2)}, u32[]{:S(2)}) collective-permute-start(bf16[512,2048]{1,0:T(8,128)(2,1)S(1)} %get-tuple-element.259), channel_id=1, source_target_pairs={{0,4},{4,0},{8,12},{12,8},{16,20},{20,16},{24,28},{28,24},{1,5},{5... | collective-permute-start | bytes 6291464 | tf_op jit(solution)/shard_map/ppermute | solution.py:59
  88.3 37.4 %collective-permute-start.15 = (bf16[2048,256]{1,0:T(8,128)(2,1)S(1)}, bf16[2048,256]{1,0:T(8,128)(2,1)S(1)}, u32[]{:S(2)}, u32[]{:S(2)}) collective-permute-start(bf16[2048,256]{1,0:T(8,128)(2,1)S(1)} %pad_maximum_fusion.5.kv_even), channel_id=1, source_target_pairs={{0,4},{4,0},{8,12},{12,8},{16,20},{20,16},{24,28},{28,24},{1,5},{5... | collective-permute-start | bytes 3145736 | tf_op jit(solution)/shard_map/ppermute | solution.py:59
  88.5 48.9 %collective-permute-start.17 = (bf16[1,512,1024]{2,1,0:T(8,128)(2,1)}, bf16[1,512,1024]{2,1,0:T(8,128)(2,1)}, u32[]{:S(2)}, u32[]{:S(2)}) collective-permute-start(bf16[1,512,1024]{2,1,0:T(8,128)(2,1)} %bitcast.13), channel_id=1, source_target_pairs={{0,3},{1,2},{2,1},{3,0},{4,7},{5,6},{6,5},{7,4},{8,11},{9,10},{10,... | collective-permute-start | bytes 3145736 | tf_op jit(solution)/shard_map/ppermute | solution.py:186
  92.1 29.7 %collective-permute-start.24 = (bf16[1,512,256]{2,1,0:T(8,128)(2,1)S(1)}, bf16[1,512,256]{2,1,0:T(8,128)(2,1)S(1)}, u32[]{:S(2)}, u32[]{:S(2)}) collective-permute-start(bf16[1,512,256]{2,1,0:T(8,128)(2,1)S(1)} %collective-permute-done.16), channel_id=1, source_target_pairs={{0,1},{1,0},{2,3},{3,2},{4,5},{5,4},{6,7},{7,6},{8,9},{9,8},{10,11... | collective-permute-start | bytes 786440 | tf_op jit(solution)/shard_map/ppermute | solution.py:186
  94.9 29.3 %collective-permute-start.19 = (bf16[1,2,512,256]{3,2,1,0:T(8,128)(2,1)S(1)}, bf16[1,2,512,256]{3,2,1,0:T(8,128)(2,1)S(1)}, u32[]{:S(2)}, u32[]{:S(2)}) collective-permute-start(bf16[1,2,512,256]{3,2,1,0:T(8,128)(2,1)S(1)} %bitcast.119), channel_id=1, source_target_pairs={{0,16},{4,20},{8,24},{12,28},{16,0},{20,4},{24,8},{28,12},{1,17},{... | collective-permute-start | bytes 1572872 | tf_op jit(solution)/shard_map/ppermute | solution.py:59
  124.2 38.1 %collective-permute-start.18 = (bf16[1,512,1024]{2,1,0:T(8,128)(2,1)}, bf16[1,512,1024]{2,1,0:T(8,128)(2,1)}, u32[]{:S(2)}, u32[]{:S(2)}) collective-permute-start(bf16[1,512,1024]{2,1,0:T(8,128)(2,1)} %bitcast.13), channel_id=1, source_target_pairs={{0,1},{1,0},{2,3},{3,2},{4,5},{5,4},{6,7},{7,6},{8,9},{9,8},{10,11... | collective-permute-start | bytes 3145736 | tf_op jit(solution)/shard_map/ppermute | solution.py:186
  125.8 55.6 %collective-permute-start.21 = (bf16[2,2,512,256]{3,2,1,0:T(8,128)(2,1)S(1)}, bf16[2,2,512,256]{3,2,1,0:T(8,128)(2,1)}, u32[]{:S(2)}, u32[]{:S(2)}) collective-permute-start(bf16[2,2,512,256]{3,2,1,0:T(8,128)(2,1)S(1)} %pad_maximum_fusion.7.refs_0_), channel_id=1, source_target_pairs={{0,4},{4,0},{8,12},{12,8},{16,20},{20,16},{24,28},{28,24},{1,5},{5... | collective-permute-start | bytes 3145736 | tf_op jit(solution)/shard_map/ppermute | solution.py:59
  135.8 26.0 %collective-permute-start.20 = (bf16[2,2,512,256]{3,2,1,0:T(8,128)(2,1)S(1)}, bf16[2,2,512,256]{3,2,1,0:T(8,128)(2,1)}, u32[]{:S(2)}, u32[]{:S(2)}) collective-permute-start(bf16[2,2,512,256]{3,2,1,0:T(8,128)(2,1)S(1)} %pad_maximum_fusion.7.refs_0_), channel_id=1, source_target_pairs={{0,8},{4,12},{8,0},{12,4},{16,24},{20,28},{24,16},{28,20},{1,9},{5... | collective-permute-start | bytes 3145736 | tf_op jit(solution)/shard_map/ppermute | solution.py:59
  137.4 24.4 %collective-permute-start.26 = (bf16[2,2,512,256]{3,2,1,0:T(8,128)(2,1)}, bf16[2,2,512,256]{3,2,1,0:T(8,128)(2,1)}, u32[]{:S(2)}, u32[]{:S(2)}) collective-permute-start(bf16[2,2,512,256]{3,2,1,0:T(8,128)(2,1)} %pad_maximum_fusion.8.refs_4_), channel_id=1, source_target_pairs={{0,16},{4,20},{8,24},{12,28},{16,0},{20,4},{24,8},{28,12},{1,17},{... | collective-permute-start | bytes 3145736 | tf_op jit(solution)/shard_map/ppermute | solution.py:59
  138.8 39.3 %collective-permute-start.36 = (bf16[1,512,1024]{2,1,0:T(8,128)(2,1)}, bf16[1,512,1024]{2,1,0:T(8,128)(2,1)}, u32[]{:S(2)}, u32[]{:S(2)}) collective-permute-start(bf16[1,512,1024]{2,1,0:T(8,128)(2,1)} %collective-permute-done.17), channel_id=1, source_target_pairs={{0,1},{1,0},{2,3},{3,2},{4,5},{5,4},{6,7},{7,6},{8,9},{9,8},{10,11... | collective-permute-start | bytes 3145736 | tf_op jit(solution)/shard_map/ppermute | solution.py:186
  166.5 97.7 %all-gather.8.cloned.1.call-start = ((), (), s32[]{:S(2)}) async-start(), calls=%async_computation.14 | async-start | bytes 2621440 | tf_op jit(solution)/shard_map/all_gather | solution.py:219
  180.9 96.7 %all-gather.6.cloned.1.call-start = ((), (), s32[]{:S(2)}) async-start(), calls=%async_computation.13 | async-start | bytes 2621440 | tf_op jit(solution)/shard_map/all_gather | solution.py:219
  205.0 23.2 %collective-permute-start.33 = (bf16[128,2048]{1,0:T(8,128)(2,1)S(1)}, bf16[128,2048]{1,0:T(8,128)(2,1)S(1)}, u32[]{:S(2)}, u32[]{:S(2)}) collective-permute-start(bf16[128,2048]{1,0:T(8,128)(2,1)S(1)} %add_convert_fusion.1), channel_id=1, source_target_pairs={{0,16},{4,20},{8,24},{12,28},{16,0},{20,4},{24,8},{28,12},{1,17},{... | collective-permute-start | bytes 1572872 | tf_op jit(solution)/shard_map/ppermute | solution.py:59
  230.2 130.1 %reduce-scatter.9.cloned.1.call-start = ((), (), s32[]{:S(2)}) async-start(), calls=%async_computation.16 | async-start | bytes 2621440 | tf_op jit(solution)/shard_map/reduce_scatter | solution.py:223
  277.6 90.2 %reduce-scatter.7.cloned.1.call-start = ((), (), s32[]{:S(2)}) async-start(), calls=%async_computation.15 | async-start | bytes 2621440 | tf_op jit(solution)/shard_map/reduce_scatter | solution.py:223
  278.2 189.9 %reduce-scatter.17.cloned.1.call-start = ((), (), s32[]{:S(2)}) async-start(), calls=%async_computation.20 | async-start | bytes 2621440 | tf_op jit(solution)/shard_map/reduce_scatter | solution.py:223
  309.3 24.4 %collective-permute-start.39 = (bf16[128,2048]{1,0:T(8,128)(2,1)S(1)}, bf16[128,2048]{1,0:T(8,128)(2,1)}, u32[]{:S(2)}, u32[]{:S(2)}) collective-permute-start(bf16[128,2048]{1,0:T(8,128)(2,1)S(1)} %get-tuple-element.277), channel_id=1, source_target_pairs={{0,16},{4,20},{8,24},{12,28},{16,0},{20,4},{24,8},{28,12},{1,17},{... | collective-permute-start | bytes 1572872 | tf_op jit(solution)/shard_map/ppermute | solution.py:59
  309.9 23.9 %collective-permute-start.38 = (bf16[128,2048]{1,0:T(8,128)(2,1)S(1)}, bf16[128,2048]{1,0:T(8,128)(2,1)}, u32[]{:S(2)}, u32[]{:S(2)}) collective-permute-start(bf16[128,2048]{1,0:T(8,128)(2,1)S(1)} %get-tuple-element.278), channel_id=1, source_target_pairs={{0,8},{4,12},{8,0},{12,4},{16,24},{20,28},{24,16},{28,20},{1,9},{5... | collective-permute-start | bytes 1572872 | tf_op jit(solution)/shard_map/ppermute | solution.py:59
  333.7 134.3 %reduce-scatter.15.cloned.1.call-start = ((), (), s32[]{:S(2)}) async-start(), calls=%async_computation.19 | async-start | bytes 2621440 | tf_op jit(solution)/shard_map/reduce_scatter | solution.py:223
  335.7 33.6 %collective-permute-start.41 = (bf16[512,2048]{1,0:T(8,128)(2,1)}, bf16[512,2048]{1,0:T(8,128)(2,1)}, u32[]{:S(2)}, u32[]{:S(2)}) collective-permute-start(bf16[512,2048]{1,0:T(8,128)(2,1)} %get-tuple-element.123), channel_id=1, source_target_pairs={{0,4},{4,0},{8,12},{12,8},{16,20},{20,16},{24,28},{28,24},{1,5},{5... | collective-permute-start | bytes 6291464 | tf_op jit(solution)/shard_map/ppermute | solution.py:59
  340.4 57.2 %collective-permute-start.57 = (bf16[512,2048]{1,0:T(8,128)(2,1)}, bf16[512,2048]{1,0:T(8,128)(2,1)}, u32[]{:S(2)}, u32[]{:S(2)}) collective-permute-start(bf16[512,2048]{1,0:T(8,128)(2,1)} %constant_dynamic-update-slice_fusion.5), channel_id=1, source_target_pairs={{0,4},{4,0},{8,12},{12,8},{16,20},{20,16},{24,28},{28,24},{1,5},{5... | collective-permute-start | bytes 6291464 | tf_op jit(solution)/shard_map/ppermute | solution.py:59
  360.0 149.2 %reduce-scatter.11.cloned.1.call-start = ((), (), s32[]{:S(2)}) async-start(), calls=%async_computation.17 | async-start | bytes 2621440 | tf_op jit(solution)/shard_map/reduce_scatter | solution.py:223
  360.3 42.9 %collective-permute-start.43 = (bf16[1,256,1024]{2,1,0:T(8,128)(2,1)}, bf16[1,256,1024]{2,1,0:T(8,128)(2,1)}, u32[]{:S(2)}, u32[]{:S(2)}) collective-permute-start(bf16[1,256,1024]{2,1,0:T(8,128)(2,1)} %bitcast.139), channel_id=1, source_target_pairs={{0,8},{4,12},{8,0},{12,4},{16,24},{20,28},{24,16},{28,20},{1,9},{5... | collective-permute-start | bytes 1572872 | tf_op jit(solution)/shard_map/ppermute | solution.py:59
  367.8 35.4 %collective-permute-start.42 = (bf16[1,256,1024]{2,1,0:T(8,128)(2,1)}, bf16[1,256,1024]{2,1,0:T(8,128)(2,1)}, u32[]{:S(2)}, u32[]{:S(2)}) collective-permute-start(bf16[1,256,1024]{2,1,0:T(8,128)(2,1)} %bitcast.141), channel_id=1, source_target_pairs={{0,16},{4,20},{8,24},{12,28},{16,0},{20,4},{24,8},{28,12},{1,17},{... | collective-permute-start | bytes 1572872 | tf_op jit(solution)/shard_map/ppermute | solution.py:59
  377.5 25.8 %collective-permute-start.46 = (bf16[128,2048]{1,0:T(8,128)(2,1)S(1)}, bf16[128,2048]{1,0:T(8,128)(2,1)S(1)}, u32[]{:S(2)}, u32[]{:S(2)}) collective-permute-start(bf16[128,2048]{1,0:T(8,128)(2,1)S(1)} %get-tuple-element.273), channel_id=1, source_target_pairs={{0,24},{4,28},{8,16},{12,20},{16,8},{20,12},{24,0},{28,4},{1,25},{... | collective-permute-start | bytes 1572872 | tf_op jit(solution)/shard_map/ppermute | solution.py:59
  378.1 30.0 %collective-permute-start.45 = (bf16[128,2048]{1,0:T(8,128)(2,1)S(1)}, bf16[128,2048]{1,0:T(8,128)(2,1)S(1)}, u32[]{:S(2)}, u32[]{:S(2)}) collective-permute-start(bf16[128,2048]{1,0:T(8,128)(2,1)S(1)} %get-tuple-element.274), channel_id=1, source_target_pairs={{0,16},{4,20},{8,24},{12,28},{16,0},{20,4},{24,8},{28,12},{1,17},{... | collective-permute-start | bytes 1572872 | tf_op jit(solution)/shard_map/ppermute | solution.py:59
  417.9 30.4 %collective-permute-start.47 = (bf16[512,2048]{1,0:T(8,128)(2,1)}, bf16[512,2048]{1,0:T(8,128)(2,1)}, u32[]{:S(2)}, u32[]{:S(2)}) collective-permute-start(bf16[512,2048]{1,0:T(8,128)(2,1)} %convolution_convert_fusion.1), channel_id=1, source_target_pairs={{0,4},{4,0},{8,12},{12,8},{16,20},{20,16},{24,28},{28,24},{1,5},{5... | collective-permute-start | bytes 6291464 | tf_op jit(solution)/shard_map/ppermute | solution.py:59
  444.9 62.9 %collective-permute-start.55 = (bf16[2,256,1024]{2,1,0:T(8,128)(2,1)S(1)}, bf16[2,256,1024]{2,1,0:T(8,128)(2,1)}, u32[]{:S(2)}, u32[]{:S(2)}) collective-permute-start(bf16[2,256,1024]{2,1,0:T(8,128)(2,1)S(1)} %pad_maximum_fusion.9.refs_0_), channel_id=1, source_target_pairs={{0,8},{4,12},{8,0},{12,4},{16,24},{20,28},{24,16},{28,20},{1,9},{5... | collective-permute-start | bytes 3145736 | tf_op jit(solution)/shard_map/ppermute | solution.py:59
  446.8 61.0 %collective-permute-start.56 = (bf16[2,256,1024]{2,1,0:T(8,128)(2,1)S(1)}, bf16[2,256,1024]{2,1,0:T(8,128)(2,1)}, u32[]{:S(2)}, u32[]{:S(2)}) collective-permute-start(bf16[2,256,1024]{2,1,0:T(8,128)(2,1)S(1)} %pad_maximum_fusion.10.refs_4_), channel_id=1, source_target_pairs={{0,16},{4,20},{8,24},{12,28},{16,0},{20,4},{24,8},{28,12},{1,17},{... | collective-permute-start | bytes 3145736 | tf_op jit(solution)/shard_map/ppermute | solution.py:59
  453.2 30.4 %collective-permute-start.54 = (bf16[128,2048]{1,0:T(8,128)(2,1)}, bf16[128,2048]{1,0:T(8,128)(2,1)}, u32[]{:S(2)}, u32[]{:S(2)}) collective-permute-start(bf16[128,2048]{1,0:T(8,128)(2,1)} %get-tuple-element.270), channel_id=1, source_target_pairs={{0,24},{4,28},{8,16},{12,20},{16,8},{20,12},{24,0},{28,4},{1,25},{... | collective-permute-start | bytes 1572872 | tf_op jit(solution)/shard_map/ppermute | solution.py:59
  454.7 43.0 %collective-permute-start.53 = (bf16[128,2048]{1,0:T(8,128)(2,1)}, bf16[128,2048]{1,0:T(8,128)(2,1)}, u32[]{:S(2)}, u32[]{:S(2)}) collective-permute-start(bf16[128,2048]{1,0:T(8,128)(2,1)} %get-tuple-element.271), channel_id=1, source_target_pairs={{0,16},{4,20},{8,24},{12,28},{16,0},{20,4},{24,8},{28,12},{1,17},{... | collective-permute-start | bytes 1572872 | tf_op jit(solution)/shard_map/ppermute | solution.py:59
  456.4 42.7 %collective-permute-start.52 = (bf16[128,2048]{1,0:T(8,128)(2,1)}, bf16[128,2048]{1,0:T(8,128)(2,1)}, u32[]{:S(2)}, u32[]{:S(2)}) collective-permute-start(bf16[128,2048]{1,0:T(8,128)(2,1)} %get-tuple-element.272), channel_id=1, source_target_pairs={{0,8},{4,12},{8,0},{12,4},{16,24},{20,28},{24,16},{28,20},{1,9},{5... | collective-permute-start | bytes 1572872 | tf_op jit(solution)/shard_map/ppermute | solution.py:59
  460.8 40.8 %all-to-all-start.3 = ((bf16[8,128,256]{2,1,0:T(8,128)(2,1)}), bf16[8,128,256]{2,1,0:T(8,128)(2,1)}, u32[]{:S(2)}, u32[]{:S(2)}) async-start(bf16[8,128,256]{2,1,0:T(8,128)(2,1)} %broadcast_in_dim.61), calls=%async_computation.5 | async-start | bytes 1048576 | tf_op jit(solution)/shard_map/all_to_all | solution.py:166
  465.0 116.2 %reduce-scatter.13.cloned.1.call-start = ((), (), s32[]{:S(2)}) async-start(), calls=%async_computation.18 | async-start | bytes 1310720 | tf_op jit(solution)/shard_map/reduce_scatter | solution.py:223
  483.6 44.1 %collective-permute-start.64 = (bf16[2,256,1024]{2,1,0:T(8,128)(2,1)S(1)}, bf16[2,256,1024]{2,1,0:T(8,128)(2,1)}, u32[]{:S(2)}, u32[]{:S(2)}) collective-permute-start(bf16[2,256,1024]{2,1,0:T(8,128)(2,1)S(1)} %pad_maximum_fusion.9.refs_0_), channel_id=1, source_target_pairs={{0,4},{4,0},{8,12},{12,8},{16,20},{20,16},{24,28},{28,24},{1,5},{5... | collective-permute-start | bytes 3145736 | tf_op jit(solution)/shard_map/ppermute | solution.py:59
  507.8 37.0 %collective-permute-start.66 = (bf16[2,256,1024]{2,1,0:T(8,128)(2,1)S(1)}, bf16[2,256,1024]{2,1,0:T(8,128)(2,1)}, u32[]{:S(2)}, u32[]{:S(2)}) collective-permute-start(bf16[2,256,1024]{2,1,0:T(8,128)(2,1)S(1)} %pad_maximum_fusion.10.refs_4_), channel_id=1, source_target_pairs={{0,4},{4,0},{8,12},{12,8},{16,20},{20,16},{24,28},{28,24},{1,5},{5... | collective-permute-start | bytes 3145736 | tf_op jit(solution)/shard_map/ppermute | solution.py:59
  516.8 26.3 %collective-permute-start.59 = (bf16[512,512]{1,0:T(8,128)(2,1)}, bf16[512,512]{1,0:T(8,128)(2,1)S(1)}, u32[]{:S(2)}, u32[]{:S(2)}) collective-permute-start(bf16[512,512]{1,0:T(8,128)(2,1)} %reduce-scatter.11.cloned.1.call-done), channel_id=1, source_target_pairs={{0,16},{4,20},{8,24},{12,28},{16,0},{20,4},{24,8},{28,12},{1,17},{... | collective-permute-start | bytes 1572872 | tf_op jit(solution)/shard_map/ppermute | solution.py:59
  524.4 47.6 %collective-permute-start.71 = (bf16[2,512,512]{2,1,0:T(8,128)(2,1)}, bf16[2,512,512]{2,1,0:T(8,128)(2,1)}, u32[]{:S(2)}, u32[]{:S(2)}) collective-permute-start(bf16[2,512,512]{2,1,0:T(8,128)(2,1)} %pad_maximum_fusion.12.refs_4_), channel_id=1, source_target_pairs={{0,16},{4,20},{8,24},{12,28},{16,0},{20,4},{24,8},{28,12},{1,17},{... | collective-permute-start | bytes 3145736 | tf_op jit(solution)/shard_map/ppermute | solution.py:59
  527.7 44.3 %collective-permute-start.63 = (bf16[2,512,512]{2,1,0:T(8,128)(2,1)S(1)}, bf16[2,512,512]{2,1,0:T(8,128)(2,1)}, u32[]{:S(2)}, u32[]{:S(2)}) collective-permute-start(bf16[2,512,512]{2,1,0:T(8,128)(2,1)S(1)} %pad_maximum_fusion.11.refs_0_), channel_id=1, source_target_pairs={{0,8},{4,12},{8,0},{12,4},{16,24},{20,28},{24,16},{28,20},{1,9},{5... | collective-permute-start | bytes 3145736 | tf_op jit(solution)/shard_map/ppermute | solution.py:59
  536.4 24.3 %collective-permute-start.65 = (bf16[2,256,1024]{2,1,0:T(8,128)(2,1)}, bf16[2,256,1024]{2,1,0:T(8,128)(2,1)}, u32[]{:S(2)}, u32[]{:S(2)}) collective-permute-start(bf16[2,256,1024]{2,1,0:T(8,128)(2,1)} %collective-permute-done.55.refs_1_), channel_id=1, source_target_pairs={{0,4},{4,0},{8,12},{12,8},{16,20},{20,16},{24,28},{28,24},{1,5},{5... | collective-permute-start | bytes 3145736 | tf_op jit(solution)/shard_map/ppermute | solution.py:59
  544.8 50.3 %collective-permute-start.61 = (bf16[2048,512]{1,0:T(8,128)(2,1)}, bf16[2048,512]{1,0:T(8,128)(2,1)}, u32[]{:S(2)}, u32[]{:S(2)}) collective-permute-start(bf16[2048,512]{1,0:T(8,128)(2,1)} %constant_dynamic-update-slice_fusion.9), channel_id=1, source_target_pairs={{0,4},{4,0},{8,12},{12,8},{16,20},{20,16},{24,28},{28,24},{1,5},{5... | collective-permute-start | bytes 6291464 | tf_op jit(solution)/shard_map/ppermute | solution.py:59
  560.8 24.0 %collective-permute-start.72 = (bf16[2,512,512]{2,1,0:T(8,128)(2,1)}, bf16[2,512,512]{2,1,0:T(8,128)(2,1)}, u32[]{:S(2)}, u32[]{:S(2)}) collective-permute-start(bf16[2,512,512]{2,1,0:T(8,128)(2,1)} %pad_maximum_fusion.12.refs_4_), channel_id=1, source_target_pairs={{0,4},{4,0},{8,12},{12,8},{16,20},{20,16},{24,28},{28,24},{1,5},{5... | collective-permute-start | bytes 3145736 | tf_op jit(solution)/shard_map/ppermute | solution.py:59
  560.9 23.9 %collective-permute-start.68 = (bf16[2,512,512]{2,1,0:T(8,128)(2,1)S(1)}, bf16[2,512,512]{2,1,0:T(8,128)(2,1)}, u32[]{:S(2)}, u32[]{:S(2)}) collective-permute-start(bf16[2,512,512]{2,1,0:T(8,128)(2,1)S(1)} %pad_maximum_fusion.11.refs_0_), channel_id=1, source_target_pairs={{0,4},{4,0},{8,12},{12,8},{16,20},{20,16},{24,28},{28,24},{1,5},{5... | collective-permute-start | bytes 3145736 | tf_op jit(solution)/shard_map/ppermute | solution.py:59
  (98 other events, 1507.3 us)
Sparse Core Ops, SparseCore 0:
  20.7 48.8 all-gather.3
  181.0 46.8 all-gather.7
  230.3 47.2 all-gather.5
  279.8 42.5 reduce-scatter.8
  324.6 43.1 reduce-scatter.6
  370.0 43.1 reduce-scatter.16
  415.6 47.3 reduce-scatter.14
  465.8 43.3 reduce-scatter.10
  515.4 26.0 reduce-scatter.12
